TPU v7x, 128 devices: a whole 4x4x4 slice. The times are simulated.
128 devices in a mesh: req: 16 (over z, x), mlp: 8 (over y, core).
Axes of the slice: x: 4, y: 4, z: 4, core: 2. Of those that a mesh axis runs over, the one named last changes fastest.
Arguments:
- tokens: bfloat16 [65536, 1024], P(('req', 'mlp')), may hold values from -72 to 72
- attend_weight: bfloat16 [1024, 3072], replicated, may hold values from -0.1875 to 0.1875
- output_weight: bfloat16 [1024, 1024], replicated, may hold values from -0.1875 to 0.1875
- attend_gain: float32 [1024], replicated, may hold values from 0.1 to 1.9
- up_weight: bfloat16 [1024, 4096], P(None, 'mlp'), may hold values from -0.1875 to 0.1875
- down_weight: bfloat16 [1024, 4096], P(None, 'mlp'), may hold values from -0.09375 to 0.09375
- mlp_gain: float32 [1024], replicated, may hold values from 0.1 to 1.9
- embed_weight: bfloat16 [1024, 128], replicated, may hold values from -0.1875 to 0.1875
- query_length: int32 [512], P(('req', 'mlp')), may hold values from 1 to 128, 49152 in all
- documents: bfloat16 [128, 256, 128], P('req', 'mlp'), may hold values from -0.54 to 0.54
- document_length: int32 [128], P('req'), may hold values from 1 to 256, 16512 in all
- candidates: int32 [512, 8], P(('req', 'mlp')), may hold values from 0 to 127
Outputs:
- embedded: bfloat16 [65536, 128], P(('req', 'mlp'))
- scores: float32 [512, 8], P(('req', 'mlp'))
All inputs are finite; a program needn't handle non-finite values. No bound on the sum of `query_length` or of `document_length` on one device may be relied on, other than what follows from the above.
Results may differ from a plain program's by a relative error of at most 0.015.
The roundings to bfloat16 on the way count: a program that leaves them out, or rounds other values in their place, can miss the bound.
Values may be sent and summed in bfloat16 or wider, within the bound.
No kernel may reach another device: no remote copies, remote signals or barrier semaphores. Data moves between devices by JAX's collectives and lax.ppermute only.
A program may use at most 128 MiB of HBM per device.

v0:
```python
import jax
import jax.numpy as jnp
from jax import lax
from jax.sharding import PartitionSpec as P

D = 1024
HEADS = 16
HD = 64
P_SIZE = 128
SEQ = 128


def norm_rows(values, scaling):
    average = jnp.mean(values, axis=-1, keepdims=True)
    centred = values - average
    variance = jnp.mean(centred * centred, axis=-1, keepdims=True)
    return centred * lax.rsqrt(variance + 1e-05) * scaling


def best_match(piece, flat_docs, live_doc):
    sims = lax.dot_general(
        piece, flat_docs, (((1,), (1,)), ((), ())), preferred_element_type=jnp.float32
    )
    sims = sims.reshape(piece.shape[0], live_doc.shape[0], live_doc.shape[1])
    sims = jnp.where(live_doc[None], sims, -1e30)
    return jnp.max(sims, axis=2)


def on_device(
    tokens,
    attend_weight,
    output_weight,
    attend_gain,
    up_weight,
    down_weight,
    mlp_gain,
    embed_weight,
    query_length,
    documents,
    document_length,
    candidates,
):
    rows = tokens.shape[0]
    requests = query_length.shape[0]
    held_docs = documents.shape[0]
    packed = jnp.dot(tokens, attend_weight, preferred_element_type=jnp.float32).astype(jnp.bfloat16)
    packed = packed.reshape(requests, SEQ, 3, HEADS, HD)
    live_slot = jnp.arange(SEQ)[None, :] < query_length[:, None]
    logits = jnp.einsum(
        "rqhd,rkhd->rhqk", packed[:, :, 0], packed[:, :, 1], preferred_element_type=jnp.float32
    ) * HD ** (-0.5)
    logits = jnp.where(live_slot[:, None, None, :], logits, -1e30)
    highest = jnp.max(logits, axis=-1, keepdims=True)
    weights = jnp.exp(logits - highest)
    probs = (weights / jnp.sum(weights, axis=-1, keepdims=True)).astype(jnp.bfloat16)
    context = jnp.einsum(
        "rhqk,rkhd->rqhd", probs, packed[:, :, 2], preferred_element_type=jnp.float32
    )
    context = context.astype(jnp.bfloat16).reshape(rows, D)
    attended = jnp.dot(context, output_weight, preferred_element_type=jnp.float32)
    normed = norm_rows(tokens.astype(jnp.float32) + attended, attend_gain).astype(jnp.bfloat16)
    hidden = jax.nn.gelu(
        jnp.dot(
            normed,
            lax.all_gather(up_weight, "mlp", axis=1, tiled=True),
            preferred_element_type=jnp.float32,
        ),
        approximate=False,
    ).astype(jnp.bfloat16)
    reduced = lax.dot_general(
        hidden,
        lax.all_gather(down_weight, "mlp", axis=1, tiled=True),
        (((1,), (1,)), ((), ())),
        preferred_element_type=jnp.float32,
    )
    layer_out = norm_rows(normed.astype(jnp.float32) + reduced, mlp_gain).astype(jnp.bfloat16)
    projected = jnp.dot(layer_out, embed_weight, preferred_element_type=jnp.float32)
    unit = projected * lax.rsqrt(jnp.sum(projected * projected, axis=-1, keepdims=True) + 1e-06)
    embedded = jnp.where(live_slot.reshape(rows, 1), unit, 0.0).astype(jnp.bfloat16)
    shard_rows = documents.shape[1]
    positions = lax.axis_index("mlp") * shard_rows + jnp.arange(shard_rows)
    live_doc = positions[None, :] < document_length[:, None]
    flat_docs = documents.reshape(held_docs * shard_rows, P_SIZE)
    partial_best = best_match(
        lax.all_gather(embedded, ("req", "mlp"), axis=0, tiled=True), flat_docs, live_doc
    )
    best = lax.pmax(partial_best.astype(jnp.bfloat16), "mlp").astype(partial_best.dtype)
    totals = jnp.sum(best.reshape(best.shape[0] // SEQ, SEQ, held_docs), axis=1)
    swapped = lax.all_to_all(totals, "req", split_axis=0, concat_axis=1, tiled=True)
    swapped = lax.dynamic_slice_in_dim(swapped, lax.axis_index("mlp") * requests, requests, 0)
    all_docs = swapped.shape[1]
    matches = candidates[:, :, None] == jnp.arange(all_docs, dtype=jnp.int32)[None, None, :]
    scores = jnp.sum(jnp.where(matches, swapped[:, None, :], 0.0), axis=2)
    return (embedded, scores)


def solution(mesh):
    return jax.shard_map(
        on_device,
        mesh=mesh,
        in_specs=(
            P(("req", "mlp"), None),
            P(),
            P(),
            P(),
            P(None, "mlp"),
            P(None, "mlp"),
            P(),
            P(),
            P(("req", "mlp")),
            P("req", "mlp", None),
            P("req"),
            P(("req", "mlp"), None),
        ),
        out_specs=(P(("req", "mlp"), None), P(("req", "mlp"), None)),
        check_vma=False,
    )
```

profile of v0, /device:TPU:1, one launch (start us, length us, event | category | flops | bytes accessed | tf_op | source)
XLA Modules:
  0.0 351.6 jit_solution(13701282405548366960)
XLA Ops:
  7.2 0.7 all-gather.4.cloned.1.call-update
  8.0 0.7 all-gather.6.cloned.1.call-update
  8.7 8.2 %convolution_convert_fusion = bf16[512,3072]{1,0:T(8,128)(2,1)} fusion(bf16[512,1024]{1,0:T(8,128)(2,1)} %param.12, bf16[1024,3072]{1,0:T(8,128)(2,1)} %param.13), kind=kOutput, calls=%fused_computation.23 | convolution fusion | flops 3222798336 | bytes 10485760 | tf_op jit(solution)/shard_map/dot_general | solution.py:46
  17.0 8.7 %reshape.125 = bf16[4,128,3,16,64]{4,3,2,1,0:T(8,128)(2,1)} reshape(bf16[512,3072]{1,0:T(8,128)(2,1)} %convolution_convert_fusion) | data formatting | bytes 6291456 | tf_op jit(solution)/shard_map/reshape | solution.py:47
  25.7 6.1 %fusion.70 = (bf16[4,128,1,16,64]{4,3,2,1,0:T(8,128)(2,1)}, bf16[4,128,1,16,64]{4,3,2,1,0:T(8,128)(2,1)}, bf16[4,128,1,16,64]{4,3,2,1,0:T(8,128)(2,1)}) fusion(bf16[4,128,3,16,64]{4,3,2,1,0:T(8,128)(2,1)} %reshape.125), kind=kLoop, calls=%fused_computation.100 | loop fusion | bytes 6291456 | tf_op jit(solution)/shard_map/slice | solution.py:57
  31.8 2.8 copy.70
  34.6 3.5 %copy.71 = bf16[4,128,1,16,64]{1,4,3,0,2:T(8,128)(2,1)} copy(bf16[4,128,1,16,64]{4,3,2,1,0:T(8,128)(2,1)} %get-tuple-element.14) | data formatting | bytes 2097152
  38.2 3.6 %copy.69 = bf16[4,128,1,16,64]{1,4,3,0,2:T(8,128)(2,1)} copy(bf16[4,128,1,16,64]{4,3,2,1,0:T(8,128)(2,1)} %get-tuple-element.12) | data formatting | bytes 2097152
  41.8 2.1 fusion.29
  43.9 1.7 fusion.71
  45.6 0.7 fusion.25
  46.4 0.9 copy.56
  47.3 1.4 fusion.72
  48.7 1.3 copy-done.2
  50.0 0.3 multiply_reduce_fusion.1
  50.4 12.7 %all-gather.4.cloned.1.call-done = bf16[1024,4096]{1,0:T(8,128)(2,1)} async-done(((bf16[1024,512]{1,0:T(8,128)(2,1)}), bf16[1024,4096]{1,0:T(8,128)(2,1)}) %all-gather.4.cloned.1.call-update) | async-done | bytes 8388624 | tf_op jit(solution)/shard_map/all_gather | solution.py:65
  63.1 51.6 %all-gather.6.cloned.1.call-done = bf16[1024,4096]{1,0:T(8,128)(2,1)} async-done(((bf16[1024,512]{1,0:T(8,128)(2,1)}), bf16[1024,4096]{1,0:T(8,128)(2,1)}) %all-gather.6.cloned.1.call-update) | async-done | bytes 8388624 | tf_op jit(solution)/shard_map/all_gather | solution.py:72
  114.7 32.1 %fusion.73 = (f32[512]{0:T(512)S(1)}, f32[512,1024]{1,0:T(8,128)S(1)}) fusion(bf16[1024,4096]{1,0:T(8,128)(2,1)} %all-gather.6.cloned.1.call-done, f32[1024]{0:T(1024)S(1)} %copy-done.11, f32[512]{0:T(512)S(1)} %add_rsqrt_fusion.2, f32[512,1024]{1,0:T(8,128)} %copy-done.2, f32[512]{0:T(512)S(1)} %broadcast_multiply_fusion.1, ...), kind=kOutput, calls=%fused_computation.103 | convolution fusion | flops 8732016640 | bytes 20981760 | tf_op jit(solution)/shard_map/dot_general | solution.py:70
  146.8 0.3 multiply_reduce_fusion
  147.2 0.7 multiply_reduce_fusion.2
  147.9 0.7 select_convert_fusion
  148.7 91.0 %all-gather.8.cloned.1.call-done = bf16[65536,128]{0,1:T(8,128)(2,1)} async-done(((bf16[512,128]{0,1:T(8,128)(2,1)}), bf16[65536,128]{0,1:T(8,128)(2,1)}) %all-gather.8.cloned.1.call-update) | async-done | bytes 16777232 | tf_op jit(solution)/shard_map/all_gather | solution.py:85
  239.7 27.4 %fusion.2 = bf16[65536,8]{0,1:T(8,128)(2,1)} fusion(bf16[8,32,128]{2,1,0:T(8,128)(2,1)S(1)} %copy-done.10, bf16[65536,128]{0,1:T(8,128)(2,1)} %all-gather.8.cloned.1.call-done, pred[8,32]{1,0:T(8,128)(4,1)S(1)} %broadcast_compare_fusion), kind=kOutput, calls=%fused_computation.4 | convolution fusion | flops 4327997440 | bytes 17891584 | tf_op jit(solution)/shard_map/dot_general | solution.py:21
  267.2 59.9 %all-reduce.2.cloned.1.call-done = bf16[512,128,8]{1,2,0:T(8,128)(2,1)} async-done(((bf16[512,128,8]{1,2,0:T(8,128)(2,1)}), bf16[512,128,8]{1,2,0:T(8,128)(2,1)}) %all-reduce.2.cloned.1.call-update) | async-done | bytes 1048592 | tf_op jit(solution)/shard_map/pmax | solution.py:87
  327.1 1.8 convert_reduce_fusion
  329.1 0.7 reshape.127
  329.8 6.7 %all-to-all-start = ((f32[16,1,256]{2,1,0:T(1,128)}), f32[16,1,256]{2,1,0:T(1,128)S(1)}, u32[]{:S(2)}, u32[]{:S(2)}) async-start(f32[16,1,256]{2,1,0:T(1,128)} %reshape.127), calls=%async_computation | async-start | bytes 32768 | tf_op jit(solution)/shard_map/all_to_all | solution.py:89
  336.5 0.8 copy.61
  337.2 5.7 %all-to-all-done = f32[16,1,256]{2,1,0:T(1,128)S(1)} async-done(((f32[16,1,256]{2,1,0:T(1,128)}), f32[16,1,256]{2,1,0:T(1,128)S(1)}, u32[]{:S(2)}, u32[]{:S(2)}) %all-to-all-start) | async-done | bytes 16416 | tf_op jit(solution)/shard_map/all_to_all | solution.py:89
  342.9 0.5 broadcast.105
  343.4 0.7 reduce
  344.3 0.8 select_reduce_fusion
  (44 shorter events, 0.8 us)
Async XLA Ops:
  7.2 40.1 %copy-start = (bf16[1024,1024]{1,0:T(8,128)(2,1)S(1)}, bf16[1024,1024]{1,0:T(8,128)(2,1)}, u32[]{:S(2)}) copy-start(bf16[1024,1024]{1,0:T(8,128)(2,1)} %param.14) | copy-start | bytes 6291460
  7.2 55.9 %all-gather.4.cloned.1.call-start = ((), (), s32[]{:S(2)}) async-start(), calls=%async_computation.1 | async-start | bytes 9437184 | tf_op jit(solution)/shard_map/all_gather | solution.py:65
  7.9 106.8 %all-gather.6.cloned.1.call-start = ((), (), s32[]{:S(2)}) async-start(), calls=%async_computation.2 | async-start | bytes 9437184 | tf_op jit(solution)/shard_map/all_gather | solution.py:72
  8.7 231.1 %all-gather.8.cloned.1.call-start = ((), (), s32[]{:S(2)}) async-start(), calls=%async_computation.3 | async-start | bytes 16908288 | tf_op jit(solution)/shard_map/all_gather | solution.py:85
  25.7 16.0 %copy-start.12 = (s32[4]{0:T(128)S(1)}, s32[4]{0:T(128)}, u32[]{:S(2)}) copy-start(s32[4]{0:T(128)} %param.20) | copy-start | bytes 52
  41.7 3.9 %copy-start.4 = (bf16[4,128,1,16,64]{1,4,3,0,2:T(8,128)(2,1)S(1)}, bf16[4,128,1,16,64]{1,4,3,0,2:T(8,128)(2,1)}, u32[]{:S(2)}) copy-start(bf16[4,128,1,16,64]{1,4,3,0,2:T(8,128)(2,1)} %copy.69) | copy-start | bytes 3145732
  45.6 1.7 copy-start.5
  46.3 68.3 %copy-start.11 = (f32[1024]{0:T(1024)S(1)}, f32[1024]{0:T(1024)}, u32[]{:S(2)}) copy-start(f32[1024]{0:T(1024)} %param.15) | copy-start | bytes 12292
  48.7 1.4 copy-start.2
  50.4 96.8 %copy-start.6 = (bf16[1024,128]{1,0:T(8,128)(2,1)S(1)}, bf16[1024,128]{1,0:T(8,128)(2,1)}, u32[]{:S(2)}) copy-start(bf16[1024,128]{1,0:T(8,128)(2,1)} %param.19) | copy-start | bytes 786436
  50.4 96.8 %copy-start.7 = (f32[1024]{0:T(1024)S(1)}, f32[1024]{0:T(1024)}, u32[]{:S(2)}) copy-start(f32[1024]{0:T(1024)} %param.18) | copy-start | bytes 12292
  50.4 98.3 %copy-start.9 = (s32[8]{0:T(128)S(1)}, s32[8]{0:T(128)}, u32[]{:S(2)}) copy-start(s32[8]{0:T(128)} %param.22) | copy-start | bytes 100
  50.4 189.3 %copy-start.10 = (bf16[8,32,128]{2,1,0:T(8,128)(2,1)S(1)}, bf16[8,32,128]{2,1,0:T(8,128)(2,1)}, u32[]{:S(2)}) copy-start(bf16[8,32,128]{2,1,0:T(8,128)(2,1)} %param.21) | copy-start | bytes 196612
  148.6 178.5 %all-reduce.2.cloned.1.call-start = ((), (), s32[]{:S(2)}) async-start(), calls=%async_computation.4 | async-start | bytes 2097152 | tf_op jit(solution)/shard_map/pmax | solution.py:87
  148.7 187.7 %copy-start.3 = (bf16[512,128]{0,1:T(8,128)(2,1)S(1)}, bf16[512,128]{0,1:T(8,128)(2,1)}, u32[]{:S(2)}) copy-start(bf16[512,128]{0,1:T(8,128)(2,1)} %select_convert_fusion) | copy-start | bytes 393220
  148.7 195.6 %copy-start.8 = (s32[4,8]{1,0:T(4,128)S(1)}, s32[4,8]{1,0:T(4,128)}, u32[]{:S(2)}) copy-start(s32[4,8]{1,0:T(4,128)} %param.23) | copy-start | bytes 388
  239.7 105.3 %copy-start.1 = (bf16[1024,1024]{1,0:T(8,128)(2,1)S(1)}, bf16[1024,1024]{1,0:T(8,128)(2,1)}, u32[]{:S(2)}) copy-start(bf16[1024,1024]{1,0:T(8,128)(2,1)} %param.14) | copy-start | bytes 6291460
  329.8 13.1 %all-to-all-start = ((f32[16,1,256]{2,1,0:T(1,128)}), f32[16,1,256]{2,1,0:T(1,128)S(1)}, u32[]{:S(2)}, u32[]{:S(2)}) async-start(f32[16,1,256]{2,1,0:T(1,128)} %reshape.127), calls=%async_computation | async-start | bytes 32768 | tf_op jit(solution)/shard_map/all_to_all | solution.py:89
Sparse Core Ops, SparseCore 0:
  9.7 53.3 all-gather.3
  64.8 49.8 all-gather.5
  148.7 90.9 all-gather.7
  267.3 59.7 all-reduce.1
where the time goes:
time: 355 us; the launch traced here: 352 us
  waiting for transfers between devices  222 us (63%)
  matrix products  72.6 us (20%)
  local copies, waits for them, and re-layouts  29.4 us (8%)
  between operations  14 us (4%)
  starting transfers between devices  6.82 us (2%)
  other arithmetic  6.53 us (2%)
    all_gather x1, waiting for transfers between devices, on_device(): lax.all_gather(embedded, ('req', 'mlp'), axis=0, tiled=True)  91 us
    pmax x1, waiting for transfers between devices, on_device(): lax.pmax(partial_best.astype(jnp.bfloat16), 'mlp')  59.9 us
    all_gather x1, waiting for transfers between devices, on_device(): lax.all_gather(down_weight, 'mlp', axis=1, tiled=True)  51.6 us
    dot_general x1, matrix products, on_device(): lax.dot_general(hidden, lax.all_gather(down_weight, 'mlp', axis=1, tiled=...  32.1 us
    dot_general x1, matrix products, best_match(): lax.dot_general(piece, flat_docs, (((1,), (1,)), ((), ())), preferred_ele...  27.4 us
    unnamed x32, local copies, waits for them, and re-layouts  12.9 us
    all_gather x1, waiting for transfers between devices, on_device(): lax.all_gather(up_weight, 'mlp', axis=1, tiled=True)  12.7 us
    reshape x1, local copies, waits for them, and re-layouts, on_device(): packed = packed.reshape(requests, SEQ, 3, HEADS, HD)  8.73 us
  transfers between devices with their start and end apart: 5, of which 5 were waited for; matrix products, arithmetic and copies ran while one was open for 12% of the time, Pallas kernels for 0%

commit v1 on v0

v1 whole, which is shorter than its diff:
```python
import functools

import jax
import jax.numpy as jnp
from jax import lax
from jax.experimental import pallas as pl
from jax.experimental.pallas import tpu as pltpu
from jax.sharding import PartitionSpec as P

D = 1024
HEADS = 16
HD = 64
P_SIZE = 128
SEQ = 128
LANES = 128
SLABS = 2 * D // LANES
DEAD = -1e30
VMEM_LIMIT = 56 * 1024 * 1024
f32 = jnp.float32
bf16 = jnp.bfloat16


def dot(a, b):
    return jnp.dot(a, b, preferred_element_type=f32)


def dot_t(a, b):
    return lax.dot_general(a, b, (((1,), (1,)), ((), ())), preferred_element_type=f32)


def norm_rows(values, scaling):
    average = jnp.mean(values, axis=-1, keepdims=True)
    centred = values - average
    variance = jnp.mean(centred * centred, axis=-1, keepdims=True)
    return centred * lax.rsqrt(variance + 1e-05) * scaling


def gelu(x):
    return 0.5 * x * (1.0 + lax.erf(x * (0.5 ** 0.5)))


def params(**kw):
    return pltpu.CompilerParams(vmem_limit_bytes=VMEM_LIMIT, **kw)


def vmem(n=1):
    return [pl.BlockSpec(memory_space=pltpu.VMEM)] * n


def pack_body(up, down, out):
    for j in range(SLABS // 2):
        rows = slice(j * LANES, (j + 1) * LANES)
        out[j] = up[rows, :].T
        out[SLABS // 2 + j] = down[rows, :].T


def attend_body(length, tok, qkv, wo, gain, out, packed, context):
    rows_all = tok.shape[0]
    for c in range(0, 3 * D, 512):
        packed[:, c : c + 512] = dot(tok[...], qkv[:, c : c + 512]).astype(bf16)
    lane = lax.broadcasted_iota(jnp.int32, (2 * SEQ, LANES), 1)
    low = lax.broadcasted_iota(jnp.int32, (SEQ, LANES), 1) < HD

    def request(r, carry):
        rows = pl.ds(pl.multiple_of(r * SEQ, SEQ), SEQ)
        live = lane < length[r]
        for p in range(HEADS // 2):
            at = p * LANES
            q = packed[rows, at : at + LANES]
            k = packed[rows, D + at : D + at + LANES]
            v = packed[rows, 2 * D + at : 2 * D + at + LANES]
            zero = jnp.zeros_like(q)
            both = jnp.concatenate([jnp.where(low, q, zero), jnp.where(low, zero, q)], axis=0)
            logits = jnp.where(live, dot_t(both, k) * HD ** (-0.5), DEAD)
            weights = jnp.exp(logits - jnp.max(logits, axis=-1, keepdims=True))
            probs = (weights * (1.0 / jnp.sum(weights, axis=-1, keepdims=True))).astype(bf16)
            ctx = dot(probs, v)
            context[rows, at : at + LANES] = jnp.where(low, ctx[:SEQ], ctx[SEQ:]).astype(bf16)
        return carry

    lax.fori_loop(0, rows_all // SEQ, request, 0)
    attended = dot(context[...], wo[...])
    out[...] = norm_rows(tok[...].astype(f32) + attended, gain[...]).astype(bf16)


def attend(tokens, qkv, wo, gain, length):
    rows = tokens.shape[0]
    return pl.pallas_call(
        attend_body,
        out_shape=jax.ShapeDtypeStruct((rows, D), bf16),
        in_specs=[pl.BlockSpec(memory_space=pltpu.SMEM)] + vmem(4),
        out_specs=vmem()[0],
        scratch_shapes=[pltpu.VMEM((rows, 3 * D), bf16), pltpu.VMEM((rows, D), bf16)],
        compiler_params=params(),
        name="attend",
    )(length, tokens, qkv, wo, gain.reshape(1, D))


def pack(up, down):
    return pl.pallas_call(
        pack_body,
        out_shape=jax.ShapeDtypeStruct((SLABS, up.shape[1], LANES), bf16),
        in_specs=vmem(2),
        out_specs=vmem()[0],
        compiler_params=params(),
        name="pack",
    )(up, down)


def ffn_body(length, normed, piece, gain, we, out, acc):
    step = pl.program_id(0)

    @pl.when(step == 0)
    def _():
        acc[...] = jnp.zeros_like(acc)

    n = piece.shape[2]
    half = SLABS // 2
    sub = 256
    x = normed[...]
    for s in range(0, n, sub):
        wu = jnp.concatenate([piece[0, j, s : s + sub] for j in range(half)], axis=1)
        wd = jnp.concatenate([piece[0, half + j, s : s + sub] for j in range(half)], axis=1)
        acc[...] += dot(gelu(dot_t(x, wu)).astype(bf16), wd)

    @pl.when(step == pl.num_programs(0) - 1)
    def _():
        layer = norm_rows(normed[...].astype(f32) + acc[...], gain[...]).astype(bf16)
        projected = dot(layer, we[...])
        unit = projected * lax.rsqrt(jnp.sum(projected * projected, axis=-1, keepdims=True) + 1e-06)
        slot = lax.broadcasted_iota(jnp.int32, (SEQ, P_SIZE), 0)
        for r in range(normed.shape[0] // SEQ):
            rows = slice(r * SEQ, (r + 1) * SEQ)
            out[rows, :] = jnp.where(slot < length[r], unit[rows], 0.0).astype(bf16)


def ffn(normed, pieces, gain, we, length):
    rows = normed.shape[0]
    return pl.pallas_call(
        ffn_body,
        grid=(pieces.shape[0],),
        out_shape=jax.ShapeDtypeStruct((rows, P_SIZE), bf16),
        in_specs=[
            pl.BlockSpec(memory_space=pltpu.SMEM),
            pl.BlockSpec((rows, D), lambda i: (0, 0)),
            pl.BlockSpec((1,) + pieces.shape[1:], lambda i: (i, 0, 0, 0)),
            pl.BlockSpec((1, D), lambda i: (0, 0)),
            pl.BlockSpec((D, P_SIZE), lambda i: (0, 0)),
        ],
        out_specs=pl.BlockSpec((rows, P_SIZE), lambda i: (0, 0)),
        scratch_shapes=[pltpu.VMEM((rows, D), f32)],
        compiler_params=params(),
        name="ffn",
    )(length, normed, pieces, gain.reshape(1, D), we)


def score_body(cand, emb, docs, out, held, lens, best, sem, lsem):
    groups, slices = docs.shape[0], docs.shape[1]
    picks = cand.shape[0]
    per = 8
    toks = 32

    def fetch(i):
        e = cand[i]
        return pltpu.make_async_copy(
            docs.at[e // per, :, pl.ds(pl.multiple_of((e % per) * toks, toks), toks), :], held.at[i], sem.at[i]
        )

    lencopy = pltpu.make_async_copy(docs.at[:, 0, pl.ds(per * toks, 16), :], lens, lsem)
    lencopy.start()
    for i in range(picks):
        fetch(i).start()
    lencopy.wait()
    pos = lax.broadcasted_iota(jnp.int32, (slices * toks, LANES), 0).astype(f32)
    row = lax.broadcasted_iota(jnp.int32, (16, LANES), 0)
    for i in range(picks):
        fetch(i).wait()
        e = cand[i]
        block = lens[e // per].astype(f32)
        limit = jnp.sum(jnp.where(row == e % per, block, 0.0), axis=0, keepdims=True)
        q = emb[(i // 8) * SEQ : (i // 8 + 1) * SEQ, :]
        sims = dot_t(held[i].reshape(slices * toks, P_SIZE), q)
        best[i // 8, pl.ds(i % 8, 1), :] = jnp.max(jnp.where(pos < limit, sims, DEAD), axis=0, keepdims=True)
    out[...] = jnp.sum(best[...], axis=-1)


def score(cand, emb, docs):
    requests, picks = cand.shape
    total = requests * picks
    return pl.pallas_call(
        score_body,
        out_shape=jax.ShapeDtypeStruct((requests, picks), f32),
        in_specs=[
            pl.BlockSpec(memory_space=pltpu.SMEM),
            pl.BlockSpec(memory_space=pltpu.VMEM),
            pl.BlockSpec(memory_space=pl.ANY),
        ],
        out_specs=vmem()[0],
        scratch_shapes=[
            pltpu.VMEM((total, 8, 32, P_SIZE), bf16),
            pltpu.VMEM((16, 16, LANES), bf16),
            pltpu.VMEM((requests, picks, LANES), f32),
            pltpu.SemaphoreType.DMA((total,)),
            pltpu.SemaphoreType.DMA(()),
        ],
        compiler_params=params(),
        name="score",
    )(cand.reshape(-1), emb, docs)


def on_device(
    tokens,
    attend_weight,
    output_weight,
    attend_gain,
    up_weight,
    down_weight,
    mlp_gain,
    embed_weight,
    query_length,
    documents,
    document_length,
    candidates,
):
    held = documents.shape[0]
    weights = pack(up_weight, down_weight)
    pieces = lax.all_gather(weights, "mlp", axis=0, tiled=False)
    limits = jnp.broadcast_to(document_length.astype(bf16)[:, None], (held, P_SIZE))
    block = jnp.concatenate(
        [documents.reshape(-1, P_SIZE), limits, jnp.zeros((16 - held, P_SIZE), bf16)], axis=0
    )
    docs = lax.all_gather(block, ("req", "mlp"), axis=0, tiled=False)
    docs = docs.reshape(16, 8, block.shape[0], P_SIZE)
    normed = attend(tokens, attend_weight, output_weight, attend_gain, query_length)
    embedded = ffn(normed, pieces, mlp_gain, embed_weight, query_length)
    scores = score(candidates, embedded, docs)
    return (embedded, scores)


def solution(mesh):
    return jax.shard_map(
        on_device,
        mesh=mesh,
        in_specs=(
            P(("req", "mlp"), None),
            P(),
            P(),
            P(),
            P(None, "mlp"),
            P(None, "mlp"),
            P(),
            P(),
            P(("req", "mlp")),
            P("req", "mlp", None),
            P("req"),
            P(("req", "mlp"), None),
        ),
        out_specs=(P(("req", "mlp"), None), P(("req", "mlp"), None)),
        check_vma=False,
    )
```

time: 355 us -> 190 us (0.54)
  waiting for transfers between devices: 222 us -> 128 us
  matrix products: 72.6 us -> 0 us
  Pallas kernels: 0 us -> 46.3 us
  local copies, waits for them, and re-layouts: 29.4 us -> 0.71 us
  starting transfers between devices: 6.82 us -> 0.08 us
  other arithmetic: 6.53 us -> 0.77 us
    dot_general x7 -> x0, matrix products: 72.6 us -> none  [the longest x1 32.1 us: on_device(): lax.dot_general(hidden, lax.all_gather(down_weight, 'mlp', axis=1, tiled=...]
    pmax x1 -> x0, waiting for transfers between devices: 59.9 us -> none  [on_device(): lax.pmax(partial_best.astype(jnp.bfloat16), 'mlp')]
    pallas_call x0 -> x4, Pallas kernels: none -> 46.3 us  [the longest x1 18.6 us: ffn(): pl.pallas_call(ffn_body, grid=(pieces.shape[0],), out_shape=jax.ShapeDtyp...]
    all_gather x3 -> x2, waiting for transfers between devices: 155 us -> 128 us  [the longest x1 72.7 us: on_device(): pieces = lax.all_gather(weights, 'mlp', axis=0, tiled=False)]
    unnamed x32 -> x6, local copies, waits for them, and re-layouts: 12.9 us -> 0.01 us
    reshape x1, local copies, waits for them, and re-layouts: 8.73 us -> 0.61 us  [score(): cand.reshape(-1)]
    all_to_all x1 -> x0, starting transfers between devices: 6.66 us -> none  [on_device(): lax.all_to_all(totals, 'req', split_axis=0, concat_axis=1, tiled=True)]
    slice x1 -> x0, local copies, waits for them, and re-layouts: 6.09 us -> none  [on_device(): packed[:, :, 2]]
  transfers between devices with their start and end apart: 5 -> 2, of which waited for: 5 -> 2; matrix products, arithmetic and copies ran while one was open for 12% -> 1% of each run, Pallas kernels for 0% -> 17%
where the time goes in v1:
time: 190 us
  waiting for transfers between devices  128 us (67%)
  Pallas kernels  46.3 us (24%)
  between operations  14.1 us (7%)
    all_gather x1, waiting for transfers between devices, on_device(): pieces = lax.all_gather(weights, 'mlp', axis=0, tiled=False)  72.7 us
    all_gather x1, waiting for transfers between devices, on_device(): docs = lax.all_gather(block, ('req', 'mlp'), axis=0, tiled=False)  55.4 us
    pallas_call x1, Pallas kernels, ffn(): pl.pallas_call(ffn_body, grid=(pieces.shape[0],), out_shape=jax.ShapeDtyp...  18.6 us
    pallas_call x1, Pallas kernels, attend(): pl.pallas_call(attend_body, out_shape=jax.ShapeDtypeStruct((rows, D), bf1...  14.5 us
    pallas_call x1, Pallas kernels, score(): pl.pallas_call(score_body, out_shape=jax.ShapeDtypeStruct((requests, pick...  9.67 us
  transfers between devices with their start and end apart: 2, of which 2 were waited for; matrix products, arithmetic and copies ran while one was open for 1% of the time, Pallas kernels for 17%

profile of v1, /device:TPU:1, one launch (start us, length us, event | category | flops | bytes accessed | tf_op | source)
XLA Modules:
  0.0 190.1 jit_solution(3736953958449594492)
XLA Ops:
  7.2 0.0 copy-start.2
  7.2 0.0 copy-start
  7.2 0.0 copy-start.1
  7.2 0.0 all-gather.5.cloned.1.call-start
  7.2 3.5 %pack.1 = bf16[16,512,128]{2,1,0:T(8,128)(2,1)} custom-call(bf16[1024,512]{1,0:T(8,128)(2,1)} %up.1, bf16[1024,512]{1,0:T(8,128)(2,1)} %down.1), custom_call_target="tpu_custom_call" | custom-call | tf_op jit(solution)/shard_map/pack/pallas_call | solution.py:100
  10.7 0.0 all-gather.5.cloned.1.call-update
  10.8 0.0 all-gather.7.cloned.1.call-start
  10.8 0.0 copy-done.2
  10.9 0.1 pad.2.clone
  10.9 0.0 copy-done
  10.9 0.8 maximum_maximum_fusion
  11.7 0.0 all-gather.7.cloned.1.call-update
  11.7 0.0 copy-done.1
  11.7 0.6 reshape.22.cand
  12.4 14.5 %attend.1.normed = bf16[512,1024]{1,0:T(8,128)(2,1)} custom-call(s32[4]{0:T(128)} %length.3, bf16[512,1024]{1,0:T(8,128)(2,1)} %tok.1, bf16[1024,3072]{1,0:T(8,128)(2,1)} %qkv.1, bf16[1024,1024]{1,0:T(8,128)(2,1)} %wo.1, f32[1,1024]{1,0:T(1,128)} %bitcast.8), custom_call_target="tpu_custom_call" | custom-call | tf_op jit(solution)/shard_map/attend/pallas_call | solution.py:88
  26.8 72.7 %all-gather.5.cloned.1.call-done = bf16[128,512,128]{2,1,0:T(8,128)(2,1)} async-done(((bf16[16,512,128]{2,1,0:T(8,128)(2,1)}), bf16[128,512,128]{2,1,0:T(8,128)(2,1)}) %all-gather.5.cloned.1.call-update) | async-done | bytes 16777232 | tf_op jit(solution)/shard_map/all_gather | solution.py:227
  99.6 18.6 %ffn.1.emb = bf16[512,128]{1,0:T(8,128)(2,1)} custom-call(s32[4]{0:T(128)} %length.3, bf16[512,1024]{1,0:T(8,128)(2,1)} %attend.1.normed, bf16[8,16,512,128]{3,2,1,0:T(8,128)(2,1)} %bitcast.5, f32[1,1024]{1,0:T(1,128)} %bitcast.9, bf16[1024,128]{1,0:T(8,128)(2,1)} %we.1), custom_call_target="tpu_custom_call" | custom-call | tf_op jit(solution)/shard_map/ffn/pallas_call | solution.py:139
  118.2 55.4 %all-gather.7.cloned.1.call-done = bf16[34816,128]{1,0:T(8,128)(2,1)} async-done(((bf16[272,128]{1,0:T(8,128)(2,1)}), bf16[34816,128]{1,0:T(8,128)(2,1)}) %all-gather.7.cloned.1.call-update) | async-done | bytes 8912912 | tf_op jit(solution)/shard_map/all_gather | solution.py:232
  173.6 9.7 %score.1 = f32[4,8]{1,0:T(4,128)} custom-call(s32[32]{0:T(128)} %reshape.22.cand, bf16[512,128]{1,0:T(8,128)(2,1)} %ffn.1.emb, bf16[16,8,272,128]{3,2,1,0:T(8,128)(2,1)} %bitcast.6), custom_call_target="tpu_custom_call" | custom-call | tf_op jit(solution)/shard_map/score/pallas_call | solution.py:190
  (3 shorter events, 0.0 us)
Async XLA Ops:
  7.2 3.7 %copy-start.2 = (s32[8]{0:T(128)S(1)}, s32[8]{0:T(128)}, u32[]{:S(2)}) copy-start(s32[8]{0:T(128)} %param.22) | copy-start | bytes 100
  7.2 3.8 %copy-start = (bf16[8,32,128]{2,1,0:T(8,128)(2,1)S(1)}, bf16[8,32,128]{2,1,0:T(8,128)(2,1)}, u32[]{:S(2)}) copy-start(bf16[8,32,128]{2,1,0:T(8,128)(2,1)} %param.21) | copy-start | bytes 196612
  7.2 4.6 %copy-start.1 = (s32[4,8]{1,0:T(4,128)S(1)}, s32[4,8]{1,0:T(4,128)}, u32[]{:S(2)}) copy-start(s32[4,8]{1,0:T(4,128)} %param.23) | copy-start | bytes 388
  7.2 92.4 %all-gather.5.cloned.1.call-start = ((), (), s32[]{:S(2)}) async-start(), calls=%async_computation | async-start | bytes 18874368 | tf_op jit(solution)/shard_map/all_gather | solution.py:227
  10.8 162.8 %all-gather.7.cloned.1.call-start = ((), (), s32[]{:S(2)}) async-start(), calls=%async_computation.1 | async-start | bytes 8982528 | tf_op jit(solution)/shard_map/all_gather | solution.py:232
Sparse Core Ops, SparseCore 0:
  10.9 88.6 all-gather.4
  102.5 71.0 all-gather.6

commit v2 on v1

v2 whole, which is shorter than its diff:
```python
import functools

import jax
import jax.numpy as jnp
from jax import lax
from jax.experimental import pallas as pl
from jax.experimental.pallas import tpu as pltpu
from jax.sharding import PartitionSpec as P

D = 1024
HEADS = 16
HD = 64
P_SIZE = 128
SEQ = 128
LANES = 128
SLABS = 2 * D // LANES
HALF = SLABS // 2
TOKS = 32
DOC_ROWS = 144
SLICE = 32
AROUND = (0, 3, 1, 2)
DEAD = -1e30
f32 = jnp.float32
bf16 = jnp.bfloat16


def dot(a, b):
    return jnp.dot(a, b, preferred_element_type=f32)


def dot_t(a, b):
    return lax.dot_general(a, b, (((1,), (1,)), ((), ())), preferred_element_type=f32)


def norm_rows(values, scaling):
    average = jnp.mean(values, axis=-1, keepdims=True)
    centred = values - average
    variance = jnp.mean(centred * centred, axis=-1, keepdims=True)
    return centred * lax.rsqrt(variance + 1e-05) * scaling


def gelu(x):
    return 0.5 * x * (1.0 + lax.erf(x * (0.5 ** 0.5)))


def params(mib):
    return pltpu.CompilerParams(vmem_limit_bytes=mib * 1024 * 1024)


def vmem(n=1):
    return [pl.BlockSpec(memory_space=pltpu.VMEM)] * n


def place(z, x, y, c):
    return ((z % 4) * 4 + x % 4) * 8 + (y % 4) * 2 + c % 2


def shift(dz=0, dx=0, dy=0, dc=0):
    return [
        (place(z, x, y, c), place(z + dz, x + dx, y + dy, c + dc))
        for z in range(4)
        for x in range(4)
        for y in range(4)
        for c in range(2)
    ]


STEPS = {
    "y+": shift(dy=1),
    "y-": shift(dy=-1),
    "y2": shift(dy=2),
    "x+": shift(dx=1),
    "x-": shift(dx=-1),
    "x2": shift(dx=2),
    "z+": shift(dz=1),
    "z-": shift(dz=-1),
    "z2": shift(dz=2),
    "c": shift(dc=1),
}


def send(value, way):
    return lax.ppermute(value, ("req", "mlp"), STEPS[way])


def after(value, *first):
    return lax.optimization_barrier((value, first))[0]


def first_body(where, up, down, docs, limits, out, turned):
    for part in range(2):
        lanes = slice(256 + part * LANES, 256 + (part + 1) * LANES)
        start = pl.multiple_of(where[1 - part] * SLICE, SLICE)
        for j in range(HALF):
            rows = slice(j * LANES, (j + 1) * LANES)
            for k, w in ((j, up), (HALF + j, down)):
                turned[...] = w[rows, lanes].T
                at = k * 2 * SLICE + part * SLICE
                out[at : at + SLICE, :] = turned[pl.ds(start, SLICE), :]
    base = SLABS * 2 * SLICE
    for h in range(2):
        at = base + h * DOC_ROWS
        out[at : at + 4 * TOKS, :] = docs[h * 4 * TOKS : (h + 1) * 4 * TOKS, :]
        row = lax.broadcasted_iota(jnp.int32, (16, LANES), 0)
        limit = jnp.zeros((16, LANES), f32)
        for j in range(4):
            limit = jnp.where(row == j, limits[h * 4 + j].astype(f32), limit)
        out[at + 4 * TOKS : at + DOC_ROWS, :] = limit.astype(bf16)


def first(where, up, down, docs, limits):
    smem = pl.BlockSpec(memory_space=pltpu.SMEM)
    return pl.pallas_call(
        first_body,
        out_shape=jax.ShapeDtypeStruct((SLABS * 2 * SLICE + 2 * DOC_ROWS, LANES), bf16),
        in_specs=[smem] + vmem(3) + [smem],
        out_specs=vmem()[0],
        scratch_shapes=[pltpu.VMEM((LANES, LANES), bf16)],
        compiler_params=params(16),
        name="first",
    )(where, up, down, docs, limits)


def pack_body(up, down, low, high):
    for j in range(HALF):
        rows = slice(j * LANES, (j + 1) * LANES)
        low[j] = up[rows, :256].T
        low[HALF + j] = down[rows, :256].T
        high[j] = up[rows, 256:].T
        high[HALF + j] = down[rows, 256:].T


def pack(up, down):
    piece = jax.ShapeDtypeStruct((SLABS, 256, LANES), bf16)
    return pl.pallas_call(
        pack_body,
        out_shape=(piece, piece),
        in_specs=vmem(2),
        out_specs=tuple(vmem(2)),
        compiler_params=params(16),
        name="pack",
    )(up, down)


def units(refs, half, start, size):
    slabs = []
    for j in range(HALF):
        parts, at = [], 0
        for ref, count in refs:
            low, high = max(start, at), min(start + size, at + count)
            if low < high:
                parts.append(ref[half * HALF + j, low - at : high - at])
            at += count
        slabs.append(parts[0] if len(parts) == 1 else jnp.concatenate(parts, axis=0))
    return jnp.concatenate(slabs, axis=1)


def attend_body(length, tok, qkv, wo, gain, out, packed, context):
    rows_all = tok.shape[0]
    for c in range(0, 3 * D, 512):
        packed[:, c : c + 512] = dot(tok[...], qkv[:, c : c + 512]).astype(bf16)
    lane = lax.broadcasted_iota(jnp.int32, (2 * SEQ, LANES), 1)
    low = lax.broadcasted_iota(jnp.int32, (SEQ, LANES), 1) < HD

    def request(r, carry):
        rows = pl.ds(pl.multiple_of(r * SEQ, SEQ), SEQ)
        live = lane < length[r]
        for p in range(HEADS // 2):
            at = p * LANES
            q = packed[rows, at : at + LANES]
            k = packed[rows, D + at : D + at + LANES]
            v = packed[rows, 2 * D + at : 2 * D + at + LANES]
            zero = jnp.zeros_like(q)
            both = jnp.concatenate([jnp.where(low, q, zero), jnp.where(low, zero, q)], axis=0)
            logits = jnp.where(live, dot_t(both, k) * HD ** (-0.5), DEAD)
            weights = jnp.exp(logits - jnp.max(logits, axis=-1, keepdims=True))
            probs = (weights * (1.0 / jnp.sum(weights, axis=-1, keepdims=True))).astype(bf16)
            ctx = dot(probs, v)
            context[rows, at : at + LANES] = jnp.where(low, ctx[:SEQ], ctx[SEQ:]).astype(bf16)
        return carry

    lax.fori_loop(0, rows_all // SEQ, request, 0)
    attended = dot(context[...], wo[...])
    out[...] = norm_rows(tok[...].astype(f32) + attended, gain[...]).astype(bf16)


def attend(tokens, qkv, wo, gain, length):
    rows = tokens.shape[0]
    return pl.pallas_call(
        attend_body,
        out_shape=jax.ShapeDtypeStruct((rows, D), bf16),
        in_specs=[pl.BlockSpec(memory_space=pltpu.SMEM)] + vmem(4),
        out_specs=vmem()[0],
        scratch_shapes=[pltpu.VMEM((rows, 3 * D), bf16), pltpu.VMEM((rows, D), bf16)],
        compiler_params=params(32),
        cost_estimate=pl.CostEstimate(flops=8 * rows * D * D, transcendentals=0, bytes_accessed=8 * D * D),
        name="attend",
    )(length, tokens, qkv, wo, gain.reshape(1, D))


def ffn_body(counts, sub, fresh, *refs):
    tokens = refs[0]
    old = None if fresh else refs[1]
    pieces = list(zip(refs[1 if fresh else 2 : -1], counts))
    out = refs[-1]
    total = sum(counts)
    x = tokens[...]
    acc = None if fresh else old[...]
    for s in range(0, total, sub):
        n = min(sub, total - s)
        inner = gelu(dot_t(x, units(pieces, 0, s, n))).astype(bf16)
        more = dot(inner, units(pieces, 1, s, n))
        acc = more if acc is None else acc + more
    out[...] = acc


def ffn(tokens, old, pieces, name, sub=256):
    rows = tokens.shape[0]
    counts = tuple(p.shape[1] for p in pieces)
    tail = ((tokens,) if old is None else (tokens, old)) + tuple(pieces)
    return pl.pallas_call(
        functools.partial(ffn_body, counts, sub, old is None),
        out_shape=jax.ShapeDtypeStruct((rows, D), f32),
        in_specs=vmem(len(tail)),
        out_specs=vmem()[0],
        input_output_aliases={} if old is None else {1: 0},
        compiler_params=params(32),
        cost_estimate=pl.CostEstimate(flops=4 * rows * D * sum(counts), transcendentals=0, bytes_accessed=4 * D * sum(counts)),
        name=name,
    )(*tail)


def embed_body(length, normed, mine, other, gain, we, out):
    layer = norm_rows(normed[...].astype(f32) + (mine[...] + other[...]), gain[...]).astype(bf16)
    projected = dot(layer, we[...])
    unit = projected * lax.rsqrt(jnp.sum(projected * projected, axis=-1, keepdims=True) + 1e-06)
    slot = lax.broadcasted_iota(jnp.int32, (SEQ, P_SIZE), 0)
    for r in range(normed.shape[0] // SEQ):
        rows = slice(r * SEQ, (r + 1) * SEQ)
        out[rows, :] = jnp.where(slot < length[r], unit[rows], 0.0).astype(bf16)


def embed(length, normed, mine, other, gain, we):
    return pl.pallas_call(
        embed_body,
        out_shape=jax.ShapeDtypeStruct((normed.shape[0], P_SIZE), bf16),
        in_specs=[pl.BlockSpec(memory_space=pltpu.SMEM)] + vmem(5),
        out_specs=vmem()[0],
        compiler_params=params(24),
        name="embed",
    )(length, normed, mine, other, gain.reshape(1, D), we)


def score_body(where, cand, pair, emb, sib, *refs):
    docs, out, held, sem = refs[:8], refs[8], refs[9], refs[10]
    copies = [pltpu.make_async_copy(docs[i], held.at[i], sem.at[i]) for i in range(8)]
    for copy in copies:
        copy.start()
    z, x, y, c = where[0], where[1], where[2], where[3]
    local = lax.broadcasted_iota(jnp.int32, (TOKS, LANES), 0)
    pos = jnp.concatenate(
        [local + TOKS * (2 * ((y + d) & 3) + c) for d in AROUND], axis=0
    ).astype(f32)
    row = lax.broadcasted_iota(jnp.int32, (16, LANES), 0)

    def slot(d):
        return jnp.where(d == 0, 0, jnp.where(d == 3, 1, d + 1))

    for copy in copies:
        copy.wait()
    per = cand.shape[0]
    for i in range(2 * per):
        e = cand[i] if i < per else pair[i - per]
        tokens = emb if i < per else sib
        j, req = e & 7, e >> 3
        sz, sx = slot(((req >> 2) - z) & 3), slot(((req & 3) - x) & 3)
        h, j4 = j >> 2, j & 3
        outer = h * 4 + jnp.where(h == 0, sz, sx)
        within = jnp.where(h == 0, sx, sz)
        block = held[outer, within, :, pl.ds(pl.multiple_of(j4 * TOKS, TOKS), TOKS), :]
        lens = held[outer, within, 0, 4 * TOKS : DOC_ROWS, :].astype(f32)
        limit = jnp.sum(jnp.where(row == j4, lens, 0.0), axis=0, keepdims=True)
        r = (i % per) // 8
        sims = dot_t(block.reshape(4 * TOKS, P_SIZE), tokens[r * SEQ : (r + 1) * SEQ, :])
        out[i : i + 1, :] = jnp.max(jnp.where(pos < limit, sims, DEAD), axis=0, keepdims=True)


def score(where, cand, pair, emb, sib, docs):
    smem = pl.BlockSpec(memory_space=pltpu.SMEM)
    total = 2 * cand.size
    docs = [d.reshape(4, 4, DOC_ROWS, P_SIZE) for d in docs]
    return pl.pallas_call(
        score_body,
        out_shape=jax.ShapeDtypeStruct((total, SEQ), f32),
        in_specs=[smem] * 3 + vmem(2) + [pl.BlockSpec(memory_space=pl.ANY)] * 8,
        out_specs=vmem()[0],
        scratch_shapes=[
            pltpu.VMEM((8, 4, 4, DOC_ROWS, P_SIZE), bf16),
            pltpu.SemaphoreType.DMA((8,)),
        ],
        compiler_params=params(16),
        name="score",
    )(where, cand.reshape(-1), pair.reshape(-1), emb, sib, *docs)


def on_device(
    tokens,
    attend_weight,
    output_weight,
    attend_gain,
    up_weight,
    down_weight,
    mlp_gain,
    embed_weight,
    query_length,
    documents,
    document_length,
    candidates,
):
    req, mlp = lax.axis_index("req"), lax.axis_index("mlp")
    where = jnp.stack([req // 4, req % 4, mlp // 2, mlp % 2]).astype(jnp.int32)
    pair = send(candidates, "c")
    start = first(where, up_weight, down_weight, documents.reshape(-1, P_SIZE), document_length)
    near = [send(start, way) for way in ("y+", "y-", "y2")]
    low, high = pack(up_weight, down_weight)
    normed = attend(tokens, attend_weight, output_weight, attend_gain, query_length)
    pair_normed = send(normed, "c")
    both = jnp.concatenate([normed, pair_normed], axis=0)

    size = SLABS * 2 * SLICE
    slices = [n[:size].reshape(SLABS, 2 * SLICE, LANES) for n in near]
    blocks = [start] + near
    halves = [[b[size + h * DOC_ROWS : size + (h + 1) * DOC_ROWS] for b in blocks] for h in range(2)]
    flat = SLABS * 3 * SLICE
    go = [
        jnp.concatenate(
            [jnp.concatenate([s[:, h * SLICE : (h + 1) * SLICE] for s in slices], axis=1).reshape(flat, LANES)]
            + halves[h],
            axis=0,
        )
        for h in range(2)
    ]
    axes = ("x", "z")
    came = [[send(go[h], axes[h] + way) for way in ("+", "-")] for h in range(2)]
    low_go = after(low, *near)
    low_far = send(low_go, "y2")
    for h in range(2):
        came[h].append(send(go[h], axes[h] + "2"))
    low_go = after(low, *came[0][:2], *came[1][:2])
    low_near = [send(low_go, "y+"), send(low_go, "y-")]
    wide = [[a[:flat].reshape(SLABS, 3 * SLICE, LANES) for a in came[h]] for h in range(2)]
    total = ffn(both, None, [low, high], "ffn1")
    total = ffn(both, total, slices + wide[0][:2] + wide[1][:2], "ffn2")
    docs = [jnp.concatenate([go[h][flat:]] + [a[flat:] for a in came[h]], axis=0) for h in range(2)]
    last = [[send(docs[h], axes[1 - h] + way) for way in ("+", "-", "2")] for h in range(2)]
    total = ffn(both, total, [wide[0][2], wide[1][2], low_far], "ffn3")
    rows = normed.shape[0]
    away = ffn(pair_normed, total[rows:], low_near, "ffn4")
    other = send(away, "c")
    mine = ffn(normed, total[:rows], low_near, "ffn5")
    embedded = embed(query_length, normed, mine, other, mlp_gain, embed_weight)
    sib = send(embedded, "c")
    best = score(where, candidates, pair, embedded, sib, [docs[0]] + last[0] + [docs[1]] + last[1])
    half = best.shape[0] // 2
    best = jnp.maximum(best[:half], send(best[half:], "c"))
    scores = jnp.sum(best, axis=1).reshape(candidates.shape)
    return (embedded, scores)


def solution(mesh):
    return jax.shard_map(
        on_device,
        mesh=mesh,
        in_specs=(
            P(("req", "mlp"), None),
            P(),
            P(),
            P(),
            P(None, "mlp"),
            P(None, "mlp"),
            P(),
            P(),
            P(("req", "mlp")),
            P("req", "mlp", None),
            P("req"),
            P(("req", "mlp"), None),
        ),
        out_specs=(P(("req", "mlp"), None), P(("req", "mlp"), None)),
        check_vma=False,
    )
```

time: 190 us -> 162 us (0.85); the launches traced: 190 us -> 159 us
  waiting for transfers between devices: 128 us -> 68.4 us
  starting transfers between devices: 0.08 us -> 46.2 us
  between operations: 14.1 us -> 1.04 us
  Pallas kernels: 46.3 us -> 35.9 us
  local copies, waits for them, and re-layouts: 0.71 us -> 6.89 us
    all_gather x2 -> x0, waiting for transfers between devices: 128 us -> none  [the longest x1 72.7 us: on_device(): pieces = lax.all_gather(weights, 'mlp', axis=0, tiled=False)]
    ppermute x0 -> x23, waiting for transfers between devices: none -> 68.4 us  [send(): return lax.ppermute(value, ('req', 'mlp'), STEPS[way])]
    ppermute x0 -> x23, starting transfers between devices: none -> 46.2 us  [send(): return lax.ppermute(value, ('req', 'mlp'), STEPS[way])]
    pallas_call x3 -> x9, Pallas kernels: 31.8 us -> 25.5 us  [the longest x5 17.2 us: ffn(): pl.pallas_call(functools.partial(ffn_body, counts, sub, old is None), out...]
    unnamed x6 -> x40, local copies, waits for them, and re-layouts: 0.01 us -> 5.16 us
    pallas_call x1, Pallas kernels: 14.5 us -> 10.4 us  [attend(): pl.pallas_call(attend_body, out_shape=jax.ShapeDtypeStruct((rows, D), bf1...]
  transfers between devices with their start and end apart: 2 -> 23, of which waited for: 2 -> 11; matrix products, arithmetic and copies ran while one was open for 1% -> 1% of each run, Pallas kernels for 17% -> 18%
where the time goes in v2:
time: 162 us; the launch traced here: 159 us
  waiting for transfers between devices  68.4 us (42%)
  starting transfers between devices  46.2 us (29%)
  Pallas kernels  35.9 us (22%)
  local copies, waits for them, and re-layouts  6.89 us (4%)
    ppermute x23, waiting for transfers between devices, send(): return lax.ppermute(value, ('req', 'mlp'), STEPS[way])  68.4 us
    ppermute x23, starting transfers between devices, send(): return lax.ppermute(value, ('req', 'mlp'), STEPS[way])  46.2 us
    pallas_call x5, Pallas kernels, ffn(): pl.pallas_call(functools.partial(ffn_body, counts, sub, old is None), out...  17.2 us
    pallas_call x1, Pallas kernels, attend(): pl.pallas_call(attend_body, out_shape=jax.ShapeDtypeStruct((rows, D), bf1...  10.4 us
    unnamed x40, local copies, waits for them, and re-layouts  5.16 us
    pallas_call x1, Pallas kernels, score(): pl.pallas_call(score_body, out_shape=jax.ShapeDtypeStruct((total, SEQ), f...  4.53 us
  transfers between devices with their start and end apart: 23, of which 11 were waited for; matrix products, arithmetic and copies ran while one was open for 1% of the time, Pallas kernels for 18%

profile of v2, /device:TPU:1, one launch (start us, length us, event | category | flops | bytes accessed | tf_op | source)
XLA Modules:
  0.0 158.9 jit_solution(4996342165208313081)
XLA Ops:
  0.7 1.2 copy-done
  2.0 1.2 copy-done.2
  5.6 3.8 %collective-permute-start.3 = (bf16[1312,128]{1,0:T(8,128)(2,1)S(1)}, bf16[1312,128]{1,0:T(8,128)(2,1)S(1)}, u32[]{:S(2)}, u32[]{:S(2)}) collective-permute-start(bf16[1312,128]{1,0:T(8,128)(2,1)S(1)} %first.1), channel_id=1, source_target_pairs={{0,4},{1,5},{2,6},{3,7},{4,0},{5,1},{6,2},{7,3},{8,12},{9,13},{10,... | collective-permute-start | bytes 1007624 | tf_op jit(solution)/shard_map/ppermute | solution.py:83
  10.9 5.9 %collective-permute-done.3 = bf16[1312,128]{1,0:T(8,128)(2,1)S(1)} collective-permute-done((bf16[1312,128]{1,0:T(8,128)(2,1)S(1)}, bf16[1312,128]{1,0:T(8,128)(2,1)S(1)}, u32[]{:S(2)}, u32[]{:S(2)}) %collective-permute-start.3) | collective-permute-done | bytes 335904 | tf_op jit(solution)/shard_map/ppermute | solution.py:83
  16.9 7.5 %collective-permute-done.2 = bf16[1312,128]{1,0:T(8,128)(2,1)S(1)} collective-permute-done((bf16[1312,128]{1,0:T(8,128)(2,1)S(1)}, bf16[1312,128]{1,0:T(8,128)(2,1)S(1)}, u32[]{:S(2)}, u32[]{:S(2)}) %collective-permute-start.2) | collective-permute-done | bytes 335904 | tf_op jit(solution)/shard_map/ppermute | solution.py:83
  25.3 1.3 collective-permute-start.4
  26.7 1.4 collective-permute-start.5
  28.1 10.4 %attend.1.refs_0_.normed = bf16[512,1024]{1,0:T(8,128)(2,1)S(1)} custom-call(s32[4]{0:T(128)S(1)} %copy-done.9, bf16[512,1024]{1,0:T(8,128)(2,1)S(1)} %copy-done.12, bf16[1024,3072]{1,0:T(8,128)(2,1)S(1)} %copy-done.10, bf16[1024,1024]{1,0:T(8,128)(2,1)S(1)} %copy-done.11, f32[1,1024]{1,0:T(1,128)S(1)} %bitcast.46), custom_call_target="tpu_custom_call" | custom-call | flops 4294967296 | bytes 8388608 | tf_op jit(solution)/shard_map/attend/pallas_call | solution.py:189
  38.5 1.6 %collective-permute-start = (bf16[512,1024]{1,0:T(8,128)(2,1)S(1)}, bf16[512,1024]{1,0:T(8,128)(2,1)S(1)}, u32[]{:S(2)}, u32[]{:S(2)}) collective-permute-start(bf16[512,1024]{1,0:T(8,128)(2,1)S(1)} %attend.1.refs_0_.normed), channel_id=1, source_target_pairs={{0,1},{1,0},{2,3},{3,2},{4,5},{5,4},{6,7},{7,6},{8,9},{9,8},{10,11... | collective-permute-start | bytes 3145736 | tf_op jit(solution)/shard_map/ppermute | solution.py:83
  40.2 1.6 %collective-permute-start.6 = (bf16[2112,128]{1,0:T(8,128)(2,1)S(1)}, bf16[2112,128]{1,0:T(8,128)(2,1)S(1)}, u32[]{:S(2)}, u32[]{:S(2)}) collective-permute-start(bf16[2112,128]{1,0:T(8,128)(2,1)S(1)} %get-tuple-element.14), channel_id=1, source_target_pairs={{0,32},{1,33},{2,34},{3,35},{4,36},{5,37},{6,38},{7,39},{8,40},{9,... | collective-permute-start | bytes 1622024 | tf_op jit(solution)/shard_map/ppermute | solution.py:83
  41.8 2.1 %collective-permute-start.7 = (bf16[2112,128]{1,0:T(8,128)(2,1)S(1)}, bf16[2112,128]{1,0:T(8,128)(2,1)S(1)}, u32[]{:S(2)}, u32[]{:S(2)}) collective-permute-start(bf16[2112,128]{1,0:T(8,128)(2,1)S(1)} %get-tuple-element.14), channel_id=1, source_target_pairs={{0,96},{1,97},{2,98},{3,99},{4,100},{5,101},{6,102},{7,103},{8,104... | collective-permute-start | bytes 1622024 | tf_op jit(solution)/shard_map/ppermute | solution.py:83
  43.9 1.5 collective-permute-start.8
  45.5 1.3 collective-permute-start.9
  47.4 9.1 %collective-permute-done.6 = bf16[2112,128]{1,0:T(8,128)(2,1)S(1)} collective-permute-done((bf16[2112,128]{1,0:T(8,128)(2,1)S(1)}, bf16[2112,128]{1,0:T(8,128)(2,1)S(1)}, u32[]{:S(2)}, u32[]{:S(2)}) %collective-permute-start.6) | collective-permute-done | bytes 540704 | tf_op jit(solution)/shard_map/ppermute | solution.py:83
  56.5 2.5 %collective-permute-start.10 = (bf16[16,256,128]{2,1,0:T(8,128)(2,1)S(1)}, bf16[16,256,128]{2,1,0:T(8,128)(2,1)S(1)}, u32[]{:S(2)}, u32[]{:S(2)}) collective-permute-start(bf16[16,256,128]{2,1,0:T(8,128)(2,1)S(1)} %get-tuple-element.9.refs_1_), channel_id=1, source_target_pairs={{0,4},{1,5},{2,6},{3,7},{4,0},{5,1},{6,2},{7,3},{8,12},{9,13},{10,... | collective-permute-start | bytes 3145736 | tf_op jit(solution)/shard_map/ppermute | solution.py:83
  59.6 2.5 %collective-permute-start.12 = (bf16[16,256,128]{2,1,0:T(8,128)(2,1)S(1)}, bf16[16,256,128]{2,1,0:T(8,128)(2,1)S(1)}, u32[]{:S(2)}, u32[]{:S(2)}) collective-permute-start(bf16[16,256,128]{2,1,0:T(8,128)(2,1)S(1)} %get-tuple-element.9.refs_1_), channel_id=1, source_target_pairs={{0,6},{1,7},{2,0},{3,1},{4,2},{5,3},{6,4},{7,5},{8,14},{9,15},{10,... | collective-permute-start | bytes 3145736 | tf_op jit(solution)/shard_map/ppermute | solution.py:83
  62.1 7.0 %collective-permute-done.9 = bf16[2112,128]{1,0:T(8,128)(2,1)S(1)} collective-permute-done((bf16[2112,128]{1,0:T(8,128)(2,1)S(1)}, bf16[2112,128]{1,0:T(8,128)(2,1)S(1)}, u32[]{:S(2)}, u32[]{:S(2)}) %collective-permute-start.9) | collective-permute-done | bytes 540704 | tf_op jit(solution)/shard_map/ppermute | solution.py:83
  69.3 2.4 %ffn1.1.refs_1_ = f32[1024,1024]{1,0:T(8,128)S(1)} custom-call(bf16[1024,1024]{1,0:T(8,128)(2,1)S(1)} %pad_maximum_fusion.refs_0_, bf16[16,256,128]{2,1,0:T(8,128)(2,1)S(1)} %get-tuple-element.9.refs_1_, bf16[16,256,128]{2,1,0:T(8,128)(2,1)S(1)} %get-tuple-element.7.refs_2_), custom_call_target="tpu_custom_call" | custom-call | flops 2147483648 | bytes 2097152 | tf_op jit(solution)/shard_map/ffn1/pallas_call | solution.py:221
  71.7 5.1 %ffn2.1.refs_1_ = f32[1024,1024]{1,0:T(8,128)S(1)} custom-call(bf16[1024,1024]{1,0:T(8,128)(2,1)S(1)} %pad_maximum_fusion.refs_0_, f32[1024,1024]{1,0:T(8,128)S(1)} %ffn1.1.refs_1_, bf16[16,64,128]{2,1,0:T(8,128)(2,1)S(1)} %bitcast.31, bf16[16,64,128]{2,1,0:T(8,128)(2,1)S(1)} %bitcast.29, ...), custom_call_target="tpu_custom_call", output_to_operand_aliasing={{}: (1, {})} | custom-call | flops 2415919104 | bytes 2359296 | tf_op jit(solution)/shard_map/ffn2/pallas_call | solution.py:221
  76.8 5.3 %collective-permute-done.10.refs_4_ = bf16[16,256,128]{2,1,0:T(8,128)(2,1)S(1)} collective-permute-done((bf16[16,256,128]{2,1,0:T(8,128)(2,1)S(1)}, bf16[16,256,128]{2,1,0:T(8,128)(2,1)S(1)}, u32[]{:S(2)}, u32[]{:S(2)}) %collective-permute-start.10) | collective-permute-done | bytes 1048608 | tf_op jit(solution)/shard_map/ppermute | solution.py:83
  82.1 4.6 %ffn3.1 = f32[1024,1024]{1,0:T(8,128)S(1)} custom-call(bf16[1024,1024]{1,0:T(8,128)(2,1)S(1)} %pad_maximum_fusion.refs_0_, f32[1024,1024]{1,0:T(8,128)S(1)} %ffn2.1.refs_1_, bf16[16,96,128]{2,1,0:T(8,128)(2,1)S(1)} %bitcast.36, bf16[16,96,128]{2,1,0:T(8,128)(2,1)S(1)} %bitcast.37, ...), custom_call_target="tpu_custom_call", output_to_operand_aliasing={{}: (1, {})} | custom-call | flops 1879048192 | bytes 1835008 | tf_op jit(solution)/shard_map/ffn3/pallas_call | solution.py:221
  87.2 18.3 %collective-permute-done.11.refs_2_ = bf16[16,256,128]{2,1,0:T(8,128)(2,1)S(1)} collective-permute-done((bf16[16,256,128]{2,1,0:T(8,128)(2,1)S(1)}, bf16[16,256,128]{2,1,0:T(8,128)(2,1)S(1)}, u32[]{:S(2)}, u32[]{:S(2)}) %collective-permute-start.11) | collective-permute-done | bytes 1048608 | tf_op jit(solution)/shard_map/ppermute | solution.py:83
  105.5 2.7 %ffn4.1 = f32[512,1024]{1,0:T(8,128)S(1)} custom-call(bf16[512,1024]{1,0:T(8,128)(2,1)S(1)} %collective-permute-done.refs_0_, f32[512,1024]{1,0:T(8,128)S(1)} %get-tuple-element.10.refs_1_, bf16[16,256,128]{2,1,0:T(8,128)(2,1)S(1)} %collective-permute-done.11.refs_2_, ...), custom_call_target="tpu_custom_call", output_to_operand_aliasing={{}: (1, {})} | custom-call | flops 1073741824 | bytes 2097152 | tf_op jit(solution)/shard_map/ffn4/pallas_call | solution.py:221
  109.1 2.7 %collective-permute-start.17 = (bf16[2304,128]{1,0:T(8,128)(2,1)S(1)}, bf16[2304,128]{1,0:T(8,128)(2,1)S(1)}, u32[]{:S(2)}, u32[]{:S(2)}) collective-permute-start(bf16[2304,128]{1,0:T(8,128)(2,1)S(1)} %slice_dynamic-update-slice_fusion.3), channel_id=1, source_target_pairs={{0,96},{1,97},{2,98},{3,99},{4,100},{5,101},{6,102},{7,103},{8,104... | collective-permute-start | bytes 1769480 | tf_op jit(solution)/shard_map/ppermute | solution.py:83
  112.6 12.4 %collective-permute-done.16 = bf16[2304,128]{1,0:T(8,128)(2,1)S(1)} collective-permute-done((bf16[2304,128]{1,0:T(8,128)(2,1)S(1)}, bf16[2304,128]{1,0:T(8,128)(2,1)S(1)}, u32[]{:S(2)}, u32[]{:S(2)}) %collective-permute-start.16) | collective-permute-done | bytes 589856 | tf_op jit(solution)/shard_map/ppermute | solution.py:83
  125.0 1.3 collective-permute-start.20
  126.8 2.5 %ffn5.1.mine = f32[512,1024]{1,0:T(8,128)S(1)} custom-call(bf16[512,1024]{1,0:T(8,128)(2,1)S(1)} %attend.1.refs_0_.normed, f32[512,1024]{1,0:T(8,128)S(1)} %get-tuple-element.11.refs_1_, bf16[16,256,128]{2,1,0:T(8,128)(2,1)S(1)} %collective-permute-done.11.refs_2_, ...), custom_call_target="tpu_custom_call", output_to_operand_aliasing={{}: (1, {})} | custom-call | flops 1073741824 | bytes 2097152 | tf_op jit(solution)/shard_map/ffn5/pallas_call | solution.py:221
  129.3 2.3 %embed.1.emb = bf16[512,128]{1,0:T(8,128)(2,1)} custom-call(s32[4]{0:T(128)S(1)} %copy-done.9, bf16[512,1024]{1,0:T(8,128)(2,1)S(1)} %attend.1.refs_0_.normed, f32[512,1024]{1,0:T(8,128)S(1)} %ffn5.1.mine, f32[512,1024]{1,0:T(8,128)S(1)} %collective-permute-done.13.other, f32[1,1024]{1,0:T(1,128)S(1)} %bitcast.45, bf16[1024,128]{1,0:T(8,128)(2,1)S(1)} %copy-done.5), custom_call_target="tpu_custom_call" | custom-call | tf_op jit(solution)/shard_map/embed/pallas_call | solution.py:244
  131.6 14.2 %collective-permute-start.15 = (bf16[512,128]{1,0:T(8,128)(2,1)}, bf16[512,128]{1,0:T(8,128)(2,1)}, u32[]{:S(2)}, u32[]{:S(2)}) collective-permute-start(bf16[512,128]{1,0:T(8,128)(2,1)} %embed.1.emb), channel_id=1, source_target_pairs={{0,1},{1,0},{2,3},{3,2},{4,5},{5,4},{6,7},{7,6},{8,9},{9,8},{10,11... | collective-permute-start | bytes 393224 | tf_op jit(solution)/shard_map/ppermute | solution.py:83
  146.0 1.1 collective-permute-done.15.sib
  148.0 4.5 %score.1 = f32[64,128]{1,0:T(8,128)S(1)} custom-call(s32[4]{0:T(128)S(1)} %pad_add_fusion.where, s32[32]{0:T(128)S(1)} %reshape.93.cand, s32[32]{0:T(128)S(1)} %reshape.94.pair, bf16[512,128]{1,0:T(8,128)(2,1)S(1)} %copy-done.4, bf16[512,128]{1,0:T(8,128)(2,1)} %collective-permute-done.15.sib, bf16[4,4,144,128]{3,2,1,0:T(8,128)(2,1)S(1)} %bitcast.39, ...), custom_call_target="tpu_custom_call" | custom-call | tf_op jit(solution)/shard_map/score/pallas_call | solution.py:292
  152.6 4.7 %collective-permute-start.22 = (f32[32,128]{1,0:T(8,128)S(1)}, f32[32,128]{1,0:T(8,128)S(1)}, u32[]{:S(2)}, u32[]{:S(2)}) collective-permute-start(f32[32,128]{1,0:T(8,128)S(1)} %slice.168), channel_id=1, source_target_pairs={{0,1},{1,0},{2,3},{3,2},{4,5},{5,4},{6,7},{7,6},{8,9},{9,8},{10,11... | collective-permute-start | bytes 49160 | tf_op jit(solution)/shard_map/ppermute | solution.py:83
  (87 shorter events, 11.7 us)
Async XLA Ops:
  4.7 23.4 %copy-start.11 = (bf16[1024,1024]{1,0:T(8,128)(2,1)S(1)}, bf16[1024,1024]{1,0:T(8,128)(2,1)}, u32[]{:S(2)}) copy-start(bf16[1024,1024]{1,0:T(8,128)(2,1)} %wo.1) | copy-start | bytes 6291460
  4.7 23.4 %copy-start.12 = (bf16[512,1024]{1,0:T(8,128)(2,1)S(1)}, bf16[512,1024]{1,0:T(8,128)(2,1)}, u32[]{:S(2)}) copy-start(bf16[512,1024]{1,0:T(8,128)(2,1)} %tok.1) | copy-start | bytes 3145732
  5.6 11.2 %collective-permute-start.3 = (bf16[1312,128]{1,0:T(8,128)(2,1)S(1)}, bf16[1312,128]{1,0:T(8,128)(2,1)S(1)}, u32[]{:S(2)}, u32[]{:S(2)}) collective-permute-start(bf16[1312,128]{1,0:T(8,128)(2,1)S(1)} %first.1), channel_id=1, source_target_pairs={{0,4},{1,5},{2,6},{3,7},{4,0},{5,1},{6,2},{7,3},{8,12},{9,13},{10,... | collective-permute-start | bytes 1007624 | tf_op jit(solution)/shard_map/ppermute | solution.py:83
  9.4 14.9 %collective-permute-start.2 = (bf16[1312,128]{1,0:T(8,128)(2,1)S(1)}, bf16[1312,128]{1,0:T(8,128)(2,1)S(1)}, u32[]{:S(2)}, u32[]{:S(2)}) collective-permute-start(bf16[1312,128]{1,0:T(8,128)(2,1)S(1)} %first.1), channel_id=1, source_target_pairs={{0,6},{1,7},{2,0},{3,1},{4,2},{5,3},{6,4},{7,5},{8,14},{9,15},{10,... | collective-permute-start | bytes 1007624 | tf_op jit(solution)/shard_map/ppermute | solution.py:83
  10.2 14.8 %collective-permute-start.1 = (bf16[1312,128]{1,0:T(8,128)(2,1)S(1)}, bf16[1312,128]{1,0:T(8,128)(2,1)S(1)}, u32[]{:S(2)}, u32[]{:S(2)}) collective-permute-start(bf16[1312,128]{1,0:T(8,128)(2,1)S(1)} %first.1), channel_id=1, source_target_pairs={{0,2},{1,3},{2,4},{3,5},{4,6},{5,7},{6,0},{7,1},{8,10},{9,11},{10,... | collective-permute-start | bytes 1007624 | tf_op jit(solution)/shard_map/ppermute | solution.py:83
  16.8 11.3 %copy-start.10 = (bf16[1024,3072]{1,0:T(8,128)(2,1)S(1)}, bf16[1024,3072]{1,0:T(8,128)(2,1)}, u32[]{:S(2)}) copy-start(bf16[1024,3072]{1,0:T(8,128)(2,1)} %qkv.1) | copy-start | bytes 18874372
  25.0 3.1 %copy-start.9 = (s32[4]{0:T(128)S(1)}, s32[4]{0:T(128)}, u32[]{:S(2)}) copy-start(s32[4]{0:T(128)} %length.3) | copy-start | bytes 52
  25.0 3.1 %copy-start.13 = (f32[1024]{0:T(1024)S(1)}, f32[1024]{0:T(1024)}, u32[]{:S(2)}) copy-start(f32[1024]{0:T(1024)} %param.15) | copy-start | bytes 12292
  25.3 18.6 %collective-permute-start.4 = (bf16[2112,128]{1,0:T(8,128)(2,1)S(1)}, bf16[2112,128]{1,0:T(8,128)(2,1)S(1)}, u32[]{:S(2)}, u32[]{:S(2)}) collective-permute-start(bf16[2112,128]{1,0:T(8,128)(2,1)S(1)} %get-tuple-element.15), channel_id=1, source_target_pairs={{0,8},{1,9},{2,10},{3,11},{4,12},{5,13},{6,14},{7,15},{8,16},{9,17... | collective-permute-start | bytes 1622024 | tf_op jit(solution)/shard_map/ppermute | solution.py:83
  26.7 18.8 %collective-permute-start.5 = (bf16[2112,128]{1,0:T(8,128)(2,1)S(1)}, bf16[2112,128]{1,0:T(8,128)(2,1)S(1)}, u32[]{:S(2)}, u32[]{:S(2)}) collective-permute-start(bf16[2112,128]{1,0:T(8,128)(2,1)S(1)} %get-tuple-element.15), channel_id=1, source_target_pairs={{0,24},{1,25},{2,26},{3,27},{4,28},{5,29},{6,30},{7,31},{8,0},{9,1... | collective-permute-start | bytes 1622024 | tf_op jit(solution)/shard_map/ppermute | solution.py:83
  28.1 18.7 %copy-start.1 = (bf16[1024,512]{1,0:T(8,128)(2,1)S(1)}, bf16[1024,512]{1,0:T(8,128)(2,1)}, u32[]{:S(2)}) copy-start(bf16[1024,512]{1,0:T(8,128)(2,1)} %up.3) | copy-start | bytes 3145732
  28.1 18.7 %copy-start.3 = (bf16[1024,512]{1,0:T(8,128)(2,1)S(1)}, bf16[1024,512]{1,0:T(8,128)(2,1)}, u32[]{:S(2)}) copy-start(bf16[1024,512]{1,0:T(8,128)(2,1)} %down.3) | copy-start | bytes 3145732
  38.5 30.6 %collective-permute-start = (bf16[512,1024]{1,0:T(8,128)(2,1)S(1)}, bf16[512,1024]{1,0:T(8,128)(2,1)S(1)}, u32[]{:S(2)}, u32[]{:S(2)}) collective-permute-start(bf16[512,1024]{1,0:T(8,128)(2,1)S(1)} %attend.1.refs_0_.normed), channel_id=1, source_target_pairs={{0,1},{1,0},{2,3},{3,2},{4,5},{5,4},{6,7},{7,6},{8,9},{9,8},{10,11... | collective-permute-start | bytes 3145736 | tf_op jit(solution)/shard_map/ppermute | solution.py:83
  40.2 16.3 %collective-permute-start.6 = (bf16[2112,128]{1,0:T(8,128)(2,1)S(1)}, bf16[2112,128]{1,0:T(8,128)(2,1)S(1)}, u32[]{:S(2)}, u32[]{:S(2)}) collective-permute-start(bf16[2112,128]{1,0:T(8,128)(2,1)S(1)} %get-tuple-element.14), channel_id=1, source_target_pairs={{0,32},{1,33},{2,34},{3,35},{4,36},{5,37},{6,38},{7,39},{8,40},{9,... | collective-permute-start | bytes 1622024 | tf_op jit(solution)/shard_map/ppermute | solution.py:83
  41.8 17.2 %collective-permute-start.7 = (bf16[2112,128]{1,0:T(8,128)(2,1)S(1)}, bf16[2112,128]{1,0:T(8,128)(2,1)S(1)}, u32[]{:S(2)}, u32[]{:S(2)}) collective-permute-start(bf16[2112,128]{1,0:T(8,128)(2,1)S(1)} %get-tuple-element.14), channel_id=1, source_target_pairs={{0,96},{1,97},{2,98},{3,99},{4,100},{5,101},{6,102},{7,103},{8,104... | collective-permute-start | bytes 1622024 | tf_op jit(solution)/shard_map/ppermute | solution.py:83
  43.9 15.6 %collective-permute-start.8 = (bf16[2112,128]{1,0:T(8,128)(2,1)S(1)}, bf16[2112,128]{1,0:T(8,128)(2,1)S(1)}, u32[]{:S(2)}, u32[]{:S(2)}) collective-permute-start(bf16[2112,128]{1,0:T(8,128)(2,1)S(1)} %get-tuple-element.15), channel_id=1, source_target_pairs={{0,16},{1,17},{2,18},{3,19},{4,20},{5,21},{6,22},{7,23},{8,24},{9,... | collective-permute-start | bytes 1622024 | tf_op jit(solution)/shard_map/ppermute | solution.py:83
  45.5 23.6 %collective-permute-start.9 = (bf16[2112,128]{1,0:T(8,128)(2,1)S(1)}, bf16[2112,128]{1,0:T(8,128)(2,1)S(1)}, u32[]{:S(2)}, u32[]{:S(2)}) collective-permute-start(bf16[2112,128]{1,0:T(8,128)(2,1)S(1)} %get-tuple-element.14), channel_id=1, source_target_pairs={{0,64},{1,65},{2,66},{3,67},{4,68},{5,69},{6,70},{7,71},{8,72},{9,... | collective-permute-start | bytes 1622024 | tf_op jit(solution)/shard_map/ppermute | solution.py:83
  56.5 25.6 %collective-permute-start.10 = (bf16[16,256,128]{2,1,0:T(8,128)(2,1)S(1)}, bf16[16,256,128]{2,1,0:T(8,128)(2,1)S(1)}, u32[]{:S(2)}, u32[]{:S(2)}) collective-permute-start(bf16[16,256,128]{2,1,0:T(8,128)(2,1)S(1)} %get-tuple-element.9.refs_1_), channel_id=1, source_target_pairs={{0,4},{1,5},{2,6},{3,7},{4,0},{5,1},{6,2},{7,3},{8,12},{9,13},{10,... | collective-permute-start | bytes 3145736 | tf_op jit(solution)/shard_map/ppermute | solution.py:83
  59.0 46.6 %collective-permute-start.11 = (bf16[16,256,128]{2,1,0:T(8,128)(2,1)S(1)}, bf16[16,256,128]{2,1,0:T(8,128)(2,1)S(1)}, u32[]{:S(2)}, u32[]{:S(2)}) collective-permute-start(bf16[16,256,128]{2,1,0:T(8,128)(2,1)S(1)} %get-tuple-element.9.refs_1_), channel_id=1, source_target_pairs={{0,2},{1,3},{2,4},{3,5},{4,6},{5,7},{6,0},{7,1},{8,10},{9,11},{10,... | collective-permute-start | bytes 3145736 | tf_op jit(solution)/shard_map/ppermute | solution.py:83
  59.6 46.0 %collective-permute-start.12 = (bf16[16,256,128]{2,1,0:T(8,128)(2,1)S(1)}, bf16[16,256,128]{2,1,0:T(8,128)(2,1)S(1)}, u32[]{:S(2)}, u32[]{:S(2)}) collective-permute-start(bf16[16,256,128]{2,1,0:T(8,128)(2,1)S(1)} %get-tuple-element.9.refs_1_), channel_id=1, source_target_pairs={{0,6},{1,7},{2,0},{3,1},{4,2},{5,3},{6,4},{7,5},{8,14},{9,15},{10,... | collective-permute-start | bytes 3145736 | tf_op jit(solution)/shard_map/ppermute | solution.py:83
  105.5 3.3 %copy-start.14 = (s32[4,8]{1,0:T(4,128)S(1)}, s32[4,8]{1,0:T(4,128)}, u32[]{:S(2)}) copy-start(s32[4,8]{1,0:T(4,128)} %param.23) | copy-start | bytes 388
  108.2 18.0 %collective-permute-start.13 = (f32[512,1024]{1,0:T(8,128)S(1)}, f32[512,1024]{1,0:T(8,128)S(1)}, u32[]{:S(2)}, u32[]{:S(2)}) collective-permute-start(f32[512,1024]{1,0:T(8,128)S(1)} %ffn4.1), channel_id=1, source_target_pairs={{0,1},{1,0},{2,3},{3,2},{4,5},{5,4},{6,7},{7,6},{8,9},{9,8},{10,11... | collective-permute-start | bytes 6291464 | tf_op jit(solution)/shard_map/ppermute | solution.py:83
  108.8 3.8 %collective-permute-start.14 = (s32[4,8]{1,0:T(4,128)S(1)}, s32[4,8]{1,0:T(4,128)S(1)}, u32[]{:S(2)}, u32[]{:S(2)}) collective-permute-start(s32[4,8]{1,0:T(4,128)S(1)} %copy-done.14), channel_id=1, source_target_pairs={{0,1},{1,0},{2,3},{3,2},{4,5},{5,4},{6,7},{7,6},{8,9},{9,8},{10,11... | collective-permute-start | bytes 392 | tf_op jit(solution)/shard_map/ppermute | solution.py:83
  109.0 16.0 %collective-permute-start.16 = (bf16[2304,128]{1,0:T(8,128)(2,1)S(1)}, bf16[2304,128]{1,0:T(8,128)(2,1)S(1)}, u32[]{:S(2)}, u32[]{:S(2)}) collective-permute-start(bf16[2304,128]{1,0:T(8,128)(2,1)S(1)} %slice_dynamic-update-slice_fusion.3), channel_id=1, source_target_pairs={{0,32},{1,33},{2,34},{3,35},{4,36},{5,37},{6,38},{7,39},{8,40},{9,... | collective-permute-start | bytes 1769480 | tf_op jit(solution)/shard_map/ppermute | solution.py:83
  109.1 22.5 %collective-permute-start.17 = (bf16[2304,128]{1,0:T(8,128)(2,1)S(1)}, bf16[2304,128]{1,0:T(8,128)(2,1)S(1)}, u32[]{:S(2)}, u32[]{:S(2)}) collective-permute-start(bf16[2304,128]{1,0:T(8,128)(2,1)S(1)} %slice_dynamic-update-slice_fusion.3), channel_id=1, source_target_pairs={{0,96},{1,97},{2,98},{3,99},{4,100},{5,101},{6,102},{7,103},{8,104... | collective-permute-start | bytes 1769480 | tf_op jit(solution)/shard_map/ppermute | solution.py:83
  111.7 34.2 %collective-permute-start.18 = (bf16[2304,128]{1,0:T(8,128)(2,1)S(1)}, bf16[2304,128]{1,0:T(8,128)(2,1)S(1)}, u32[]{:S(2)}, u32[]{:S(2)}) collective-permute-start(bf16[2304,128]{1,0:T(8,128)(2,1)S(1)} %slice_dynamic-update-slice_fusion.3), channel_id=1, source_target_pairs={{0,64},{1,65},{2,66},{3,67},{4,68},{5,69},{6,70},{7,71},{8,72},{9,... | collective-permute-start | bytes 1769480 | tf_op jit(solution)/shard_map/ppermute | solution.py:83
  112.6 33.4 %collective-permute-start.19 = (bf16[2304,128]{1,0:T(8,128)(2,1)S(1)}, bf16[2304,128]{1,0:T(8,128)(2,1)S(1)}, u32[]{:S(2)}, u32[]{:S(2)}) collective-permute-start(bf16[2304,128]{1,0:T(8,128)(2,1)S(1)} %slice_dynamic-update-slice_fusion), channel_id=1, source_target_pairs={{0,8},{1,9},{2,10},{3,11},{4,12},{5,13},{6,14},{7,15},{8,16},{9,17... | collective-permute-start | bytes 1769480 | tf_op jit(solution)/shard_map/ppermute | solution.py:83
  125.0 21.0 %collective-permute-start.20 = (bf16[2304,128]{1,0:T(8,128)(2,1)S(1)}, bf16[2304,128]{1,0:T(8,128)(2,1)}, u32[]{:S(2)}, u32[]{:S(2)}) collective-permute-start(bf16[2304,128]{1,0:T(8,128)(2,1)S(1)} %slice_dynamic-update-slice_fusion), channel_id=1, source_target_pairs={{0,24},{1,25},{2,26},{3,27},{4,28},{5,29},{6,30},{7,31},{8,0},{9,1... | collective-permute-start | bytes 1769480 | tf_op jit(solution)/shard_map/ppermute | solution.py:83
  126.3 19.7 %collective-permute-start.21 = (bf16[2304,128]{1,0:T(8,128)(2,1)S(1)}, bf16[2304,128]{1,0:T(8,128)(2,1)}, u32[]{:S(2)}, u32[]{:S(2)}) collective-permute-start(bf16[2304,128]{1,0:T(8,128)(2,1)S(1)} %slice_dynamic-update-slice_fusion), channel_id=1, source_target_pairs={{0,16},{1,17},{2,18},{3,19},{4,20},{5,21},{6,22},{7,23},{8,24},{9,... | collective-permute-start | bytes 1769480 | tf_op jit(solution)/shard_map/ppermute | solution.py:83
  126.8 2.5 %copy-start.7 = (f32[1024]{0:T(1024)S(1)}, f32[1024]{0:T(1024)}, u32[]{:S(2)}) copy-start(f32[1024]{0:T(1024)} %param.18) | copy-start | bytes 12292
  131.6 15.6 %collective-permute-start.15 = (bf16[512,128]{1,0:T(8,128)(2,1)}, bf16[512,128]{1,0:T(8,128)(2,1)}, u32[]{:S(2)}, u32[]{:S(2)}) collective-permute-start(bf16[512,128]{1,0:T(8,128)(2,1)} %embed.1.emb), channel_id=1, source_target_pairs={{0,1},{1,0},{2,3},{3,2},{4,5},{5,4},{6,7},{7,6},{8,9},{9,8},{10,11... | collective-permute-start | bytes 393224 | tf_op jit(solution)/shard_map/ppermute | solution.py:83
  152.6 5.5 %collective-permute-start.22 = (f32[32,128]{1,0:T(8,128)S(1)}, f32[32,128]{1,0:T(8,128)S(1)}, u32[]{:S(2)}, u32[]{:S(2)}) collective-permute-start(f32[32,128]{1,0:T(8,128)S(1)} %slice.168), channel_id=1, source_target_pairs={{0,1},{1,0},{2,3},{3,2},{4,5},{5,4},{6,7},{7,6},{8,9},{9,8},{10,11... | collective-permute-start | bytes 49160 | tf_op jit(solution)/shard_map/ppermute | solution.py:83
  (6 other events, 7.3 us)

commit v3 on v2

v3 whole, which is shorter than its diff:
```python
import functools

import jax
import jax.numpy as jnp
from jax import lax
from jax.experimental import pallas as pl
from jax.experimental.pallas import tpu as pltpu
from jax.sharding import PartitionSpec as P

D = 1024
HEADS = 16
HD = 64
P_SIZE = 128
SEQ = 128
LANES = 128
SLABS = 2 * D // LANES
HALF = SLABS // 2
TOKS = 32
DOC_ROWS = 272
SLICE = 64
PART = SLABS * SLICE
BLOCK = PART + DOC_ROWS
AROUND = (0, 3, 1, 2)
AROUND_Y = (3, 1, 2, 0)
DEAD = -1e30
f32 = jnp.float32
bf16 = jnp.bfloat16


def dot(a, b):
    return jnp.dot(a, b, preferred_element_type=f32)


def dot_t(a, b):
    return lax.dot_general(a, b, (((1,), (1,)), ((), ())), preferred_element_type=f32)


def norm_rows(values, scaling):
    average = jnp.mean(values, axis=-1, keepdims=True)
    centred = values - average
    variance = jnp.mean(centred * centred, axis=-1, keepdims=True)
    return centred * lax.rsqrt(variance + 1e-05) * scaling


def gelu(x):
    return 0.5 * x * (1.0 + lax.erf(x * (0.5 ** 0.5)))


LIGHT = pl.CostEstimate(flops=1, transcendentals=0, bytes_accessed=1)


def params(mib):
    return pltpu.CompilerParams(vmem_limit_bytes=mib * 1024 * 1024)


def vmem(n=1):
    return [pl.BlockSpec(memory_space=pltpu.VMEM)] * n


def place(z, x, y, c):
    return ((z % 4) * 4 + x % 4) * 8 + (y % 4) * 2 + c % 2


def shift(move):
    return [
        (place(z, x, y, c), place(*move(z, x, y, c)))
        for z in range(4)
        for x in range(4)
        for y in range(4)
        for c in range(2)
    ]


def along_y(d):
    return shift(lambda z, x, y, c: (z, x, y + d, c))


def crossed(d, first):
    return shift(lambda z, x, y, c: (z, x + d, y, c) if c == first else (z + d, x, y, c))


STEPS = {"y+": along_y(1), "y-": along_y(-1), "y2": along_y(2)}
for name, d in (("+", 1), ("-", -1), ("2", 2)):
    STEPS["f" + name] = crossed(d, 0)
    STEPS["g" + name] = crossed(d, 1)
STEPS["c"] = shift(lambda z, x, y, c: (z, x, y, c + 1))


def send(value, way):
    return lax.ppermute(value, ("req", "mlp"), STEPS[way])


def after(value, *first):
    return lax.optimization_barrier((value, first))[0]


def any_spec(n=1):
    return [pl.BlockSpec(memory_space=pl.ANY)] * n


SMEM = pl.BlockSpec(memory_space=pltpu.SMEM)


def first_body(where, limits, up, down, docs, out, held, turned, sems):
    index = where[4]
    lanes = pl.ds(pl.multiple_of(256 + (index >> 1) * LANES, LANES), LANES)
    copies = [pltpu.make_async_copy(w.at[:, lanes], held.at[k], sems.at[k]) for k, w in enumerate((up, down))]
    tokens = DOC_ROWS - 16
    copies.append(pltpu.make_async_copy(docs, out.at[PART : PART + tokens], sems.at[2]))
    for copy in copies:
        copy.start()
    row = lax.broadcasted_iota(jnp.int32, (16, LANES), 0)
    limit = jnp.zeros((16, LANES), f32)
    for j in range(8):
        limit = jnp.where(row == j, limits[j].astype(f32), limit)
    out[PART + tokens : BLOCK, :] = limit.astype(bf16)
    start = pl.multiple_of((index & 1) * SLICE, SLICE)
    for k in range(2):
        copies[k].wait()
        for j in range(HALF):
            slab = k * HALF + j
            turned[slab] = held[k, j * LANES : (j + 1) * LANES, :].T
            out[slab * SLICE : (slab + 1) * SLICE, :] = turned[slab, pl.ds(start, SLICE), :]
    copies[2].wait()


def first(where, up, down, docs, limits):
    return pl.pallas_call(
        first_body,
        out_shape=jax.ShapeDtypeStruct((BLOCK, LANES), bf16),
        in_specs=[SMEM] * 2 + any_spec(3),
        out_specs=vmem()[0],
        scratch_shapes=[
            pltpu.VMEM((2, D, LANES), bf16),
            pltpu.VMEM((SLABS, LANES, LANES), bf16),
            pltpu.SemaphoreType.DMA((3,)),
        ],
        compiler_params=params(16),
        cost_estimate=LIGHT,
        name="first",
    )(where, limits, up, down, docs)


def pack_body(up, down, low, high):
    for j in range(HALF):
        rows = slice(j * LANES, (j + 1) * LANES)
        low[j] = up[rows, :256].T
        low[HALF + j] = down[rows, :256].T
        high[j] = up[rows, 256:].T
        high[HALF + j] = down[rows, 256:].T


def pack(up, down):
    piece = jax.ShapeDtypeStruct((SLABS, 256, LANES), bf16)
    low, high = pl.pallas_call(
        pack_body,
        out_shape=(piece, piece),
        in_specs=vmem(2),
        out_specs=tuple(vmem(2)),
        compiler_params=params(16),
        cost_estimate=LIGHT,
        name="pack",
    )(up, down)
    return low.reshape(-1, LANES), high.reshape(-1, LANES)


def join_body(takes, *refs):
    out, at = refs[-1], 0
    for k, start, size in takes:
        out[at : at + size, :] = refs[k][start : start + size, :]
        at += size


def join(arrays, takes, name):
    return pl.pallas_call(
        functools.partial(join_body, takes),
        out_shape=jax.ShapeDtypeStruct((sum(t[2] for t in takes), LANES), bf16),
        in_specs=vmem(len(arrays)),
        out_specs=vmem()[0],
        compiler_params=params(16),
        cost_estimate=LIGHT,
        name=name,
    )(*arrays)


def attend_body(length, tok, qkv, wo, gain, out, packed, context):
    rows_all = tok.shape[0]
    for c in range(0, 3 * D, 512):
        packed[:, c : c + 512] = dot(tok[...], qkv[:, c : c + 512]).astype(bf16)
    lane = lax.broadcasted_iota(jnp.int32, (2 * SEQ, LANES), 1)
    low = lax.broadcasted_iota(jnp.int32, (SEQ, LANES), 1) < HD

    def request(r, carry):
        rows = pl.ds(pl.multiple_of(r * SEQ, SEQ), SEQ)
        live = lane < length[r]
        for p in range(HEADS // 2):
            at = p * LANES
            q = packed[rows, at : at + LANES]
            k = packed[rows, D + at : D + at + LANES]
            v = packed[rows, 2 * D + at : 2 * D + at + LANES]
            zero = jnp.zeros_like(q)
            both = jnp.concatenate([jnp.where(low, q, zero), jnp.where(low, zero, q)], axis=0)
            logits = jnp.where(live, dot_t(both, k) * HD ** (-0.5), DEAD)
            weights = jnp.exp(logits - jnp.max(logits, axis=-1, keepdims=True))
            probs = (weights * (1.0 / jnp.sum(weights, axis=-1, keepdims=True))).astype(bf16)
            ctx = dot(probs, v)
            context[rows, at : at + LANES] = jnp.where(low, ctx[:SEQ], ctx[SEQ:]).astype(bf16)
        return carry

    lax.fori_loop(0, rows_all // SEQ, request, 0)
    attended = dot(context[...], wo[...])
    out[...] = norm_rows(tok[...].astype(f32) + attended, gain[...]).astype(bf16)


def attend(tokens, qkv, wo, gain, length):
    rows = tokens.shape[0]
    return pl.pallas_call(
        attend_body,
        out_shape=jax.ShapeDtypeStruct((rows, D), bf16),
        in_specs=[pl.BlockSpec(memory_space=pltpu.SMEM)] + vmem(4),
        out_specs=vmem()[0],
        scratch_shapes=[pltpu.VMEM((rows, 3 * D), bf16), pltpu.VMEM((rows, D), bf16)],
        compiler_params=params(32),
        cost_estimate=LIGHT,
        name="attend",
    )(length, tokens, qkv, wo, gain.reshape(1, D))


def units(refs, half, start, size):
    slabs = []
    for j in range(HALF):
        parts, at = [], 0
        for ref, base, count in refs:
            low, high = max(start, at), min(start + size, at + count)
            if low < high:
                row = base + (half * HALF + j) * count
                parts.append(ref[row + low - at : row + high - at, :])
            at += count
        slabs.append(parts[0] if len(parts) == 1 else jnp.concatenate(parts, axis=0))
    return jnp.concatenate(slabs, axis=1)


def ffn_body(pieces, arrays, fresh, *refs):
    tokens, out = refs[0], refs[-1]
    held = refs[-1 - arrays : -1]
    laid = [(held[k], base, count) for k, base, count in pieces]
    total = sum(count for _, _, count in pieces)
    x = tokens[...]
    acc = None if fresh else refs[1][...]
    for s in range(0, total, 256):
        n = min(256, total - s)
        inner = gelu(dot_t(x, units(laid, 0, s, n))).astype(bf16)
        more = dot(inner, units(laid, 1, s, n))
        acc = more if acc is None else acc + more
    out[...] = acc


def ffn(tokens, old, arrays, pieces, name):
    rows = tokens.shape[0]
    tail = ((tokens,) if old is None else (tokens, old)) + tuple(arrays)
    return pl.pallas_call(
        functools.partial(ffn_body, tuple(pieces), len(arrays), old is None),
        out_shape=jax.ShapeDtypeStruct((rows, D), f32),
        in_specs=vmem(len(tail)),
        out_specs=vmem()[0],
        input_output_aliases={} if old is None else {1: 0},
        compiler_params=params(32),
        cost_estimate=LIGHT,
        name=name,
    )(*tail)


def embed_body(length, normed, mine, other, gain, we, out):
    layer = norm_rows(normed[...].astype(f32) + (mine[...] + other[...]), gain[...]).astype(bf16)
    projected = dot(layer, we[...])
    unit = projected * lax.rsqrt(jnp.sum(projected * projected, axis=-1, keepdims=True) + 1e-06)
    slot = lax.broadcasted_iota(jnp.int32, (SEQ, P_SIZE), 0)
    for r in range(normed.shape[0] // SEQ):
        rows = slice(r * SEQ, (r + 1) * SEQ)
        out[rows, :] = jnp.where(slot < length[r], unit[rows], 0.0).astype(bf16)


def embed(length, normed, mine, other, gain, we):
    return pl.pallas_call(
        embed_body,
        out_shape=jax.ShapeDtypeStruct((normed.shape[0], P_SIZE), bf16),
        in_specs=[pl.BlockSpec(memory_space=pltpu.SMEM)] + vmem(5),
        out_specs=vmem()[0],
        compiler_params=params(24),
        cost_estimate=LIGHT,
        name="embed",
    )(length, normed, mine, other, gain.reshape(1, D), we)


def score_body(where, cand, pair, emb, sib, *refs):
    docs, out, held, sem = refs[:5], refs[5], refs[6], refs[7]
    copies = [pltpu.make_async_copy(docs[i], held.at[i], sem.at[i]) for i in range(3)]
    copies += [
        pltpu.make_async_copy(docs[3 + i], held.at[3, 2 * i : 2 * i + 2], sem.at[3 + i]) for i in range(2)
    ]
    for copy in copies:
        copy.start()
    z, x, y, c = where[0], where[1], where[2], where[3]
    local = lax.broadcasted_iota(jnp.int32, (TOKS, LANES), 0)
    pos = jnp.concatenate(
        [local + TOKS * (2 * ((y + d) & 3) + c) for d in AROUND_Y], axis=0
    ).astype(f32)
    row = lax.broadcasted_iota(jnp.int32, (16, LANES), 0)

    def slot(d):
        return jnp.where(d == 0, 0, jnp.where(d == 3, 1, d + 1))

    for copy in copies:
        copy.wait()
    per = cand.shape[0]
    for i in range(2 * per):
        e = cand[i] if i < per else pair[i - per]
        tokens = emb if i < per else sib
        j, req = e & 7, e >> 3
        sz, sx = slot(((req >> 2) - z) & 3), slot(((req & 3) - x) & 3)
        outer = jnp.where(c == 0, sz, sx)
        within = jnp.where(c == 0, sx, sz)
        block = held[outer, within, :, pl.ds(pl.multiple_of(j * TOKS, TOKS), TOKS), :]
        lens = held[outer, within, 0, 8 * TOKS : DOC_ROWS, :].astype(f32)
        limit = jnp.sum(jnp.where(row == j, lens, 0.0), axis=0, keepdims=True)
        r = (i % per) // 8
        sims = dot_t(block.reshape(4 * TOKS, P_SIZE), tokens[r * SEQ : (r + 1) * SEQ, :])
        out[i : i + 1, :] = jnp.max(jnp.where(pos < limit, sims, DEAD), axis=0, keepdims=True)


def score(where, cand, pair, emb, sib, docs):
    total = 2 * cand.size
    docs = [d.reshape(-1, 4, DOC_ROWS, P_SIZE) for d in docs]
    return pl.pallas_call(
        score_body,
        out_shape=jax.ShapeDtypeStruct((total, SEQ), f32),
        in_specs=[SMEM] * 3 + vmem(2) + any_spec(5),
        out_specs=vmem()[0],
        scratch_shapes=[
            pltpu.VMEM((4, 4, 4, DOC_ROWS, P_SIZE), bf16),
            pltpu.SemaphoreType.DMA((5,)),
        ],
        compiler_params=params(16),
        cost_estimate=LIGHT,
        name="score",
    )(where, cand.reshape(-1), pair.reshape(-1), emb, sib, *docs)


def on_device(
    tokens,
    attend_weight,
    output_weight,
    attend_gain,
    up_weight,
    down_weight,
    mlp_gain,
    embed_weight,
    query_length,
    documents,
    document_length,
    candidates,
):
    req, mlp = lax.axis_index("req"), lax.axis_index("mlp")
    z, x, y, c = req // 4, req % 4, mlp // 2, mlp % 2
    where = jnp.stack([z, x, y, c, jnp.where(c == 0, x, z)]).astype(jnp.int32)
    start = first(where, up_weight, down_weight, documents.reshape(-1, P_SIZE), document_length)
    near = [send(start, way) for way in ("y+", "y-", "y2")]
    low, high = pack(up_weight, down_weight)
    normed = attend(after(tokens, start), attend_weight, output_weight, attend_gain, query_length)
    near = after(tuple(near), normed, high)

    whole = [(k, 0, BLOCK) for k in range(3)] + [(3, PART, DOC_ROWS)]
    go = join([*near, start], whole, "join1")
    came = [send(go, way) for way in ("f+", "f-", "f2")]
    low_go = after(low, go)
    low_near = [send(low_go, "y+"), send(low_go, "y-")]
    parts = [(k, i * BLOCK, SLICE) for k in range(3) for i in range(3)]
    takes = [(k, at, DOC_ROWS) for k in range(4) for at in [i * BLOCK + PART for i in range(3)] + [3 * BLOCK]]
    docs = join([go, *came], takes, "join2")
    last = [send(docs, way) for way in ("g+", "g-")]
    pair_normed = send(after(normed, docs), "c")
    both = jnp.concatenate([normed, pair_normed], axis=0)
    low_near = after(tuple(low_near), docs)
    mid = 128
    ahead = join([low_near[0]], [(0, k * 256, mid) for k in range(SLABS)], "join3")
    behind = join([low_near[1]], [(0, k * 256 + mid, mid) for k in range(SLABS)], "join4")
    low_far = [send(ahead, "y+"), send(behind, "y-")]
    total = ffn(both, None, [low, high], [(0, 0, 256), (1, 0, 256)], "ffn1")
    total = ffn(both, total, tuple(near) + tuple(came), [(k, 0, SLICE) for k in range(3)] + [(k + 3, b, n) for k, b, n in parts], "ffn2")
    total = ffn(both, total, low_near, [(0, 0, 256), (1, 0, 256)], "ffn3")
    cut = docs.shape[0] // 2
    low_far = after(tuple(low_far), *last)
    last += [send(last[0][:cut], "g+"), send(last[1][cut:], "g-")]
    rows = normed.shape[0]
    rest = [(0, 0, mid), (1, 0, mid)]
    away = ffn(pair_normed, total[rows:], low_far, rest, "ffn4")
    other = send(away, "c")
    mine = ffn(normed, total[:rows], low_far, rest, "ffn5")
    embedded = embed(query_length, normed, mine, other, mlp_gain, embed_weight)
    sib = send(embedded, "c")
    pair = send(after(candidates, total), "c")
    best = score(where, candidates, pair, embedded, sib, [docs] + last)
    half = best.shape[0] // 2
    best = jnp.maximum(best[:half], send(best[half:], "c"))
    scores = jnp.sum(best, axis=1).reshape(candidates.shape)
    return (embedded, scores)


def solution(mesh):
    return jax.shard_map(
        on_device,
        mesh=mesh,
        in_specs=(
            P(("req", "mlp"), None),
            P(),
            P(),
            P(),
            P(None, "mlp"),
            P(None, "mlp"),
            P(),
            P(),
            P(("req", "mlp")),
            P("req", "mlp", None),
            P("req"),
            P(("req", "mlp"), None),
        ),
        out_specs=(P(("req", "mlp"), None), P(("req", "mlp"), None)),
        check_vma=False,
    )
```

time: 162 us -> 96.7 us (0.60); the launches traced: 159 us -> 96.4 us
  waiting for transfers between devices: 68.4 us -> 25 us
  starting transfers between devices: 46.2 us -> 26.2 us
  local copies, waits for them, and re-layouts: 6.89 us -> 10.8 us
  Pallas kernels: 35.9 us -> 33.2 us
    ppermute x23 -> x19, waiting for transfers between devices: 68.4 us -> 25 us  [send(): return lax.ppermute(value, ('req', 'mlp'), STEPS[way])]
    ppermute x23 -> x19, starting transfers between devices: 46.2 us -> 26.2 us  [send(): return lax.ppermute(value, ('req', 'mlp'), STEPS[way])]
    unnamed x40 -> x26, local copies, waits for them, and re-layouts: 5.16 us -> 7.66 us
    pallas_call x6 -> x10, Pallas kernels: 18.1 us -> 16.1 us  [the longest x5 14.8 us: ffn(): pl.pallas_call(functools.partial(ffn_body, tuple(pieces), len(arrays), ol...]
  transfers between devices with their start and end apart: 23 -> 19, of which waited for: 11 -> 8; matrix products, arithmetic and copies ran while one was open for 1% -> 3% of each run, Pallas kernels for 18% -> 28%
where the time goes in v3:
time: 96.7 us; the launch traced here: 96.4 us
  Pallas kernels  33.2 us (34%)
  starting transfers between devices  26.2 us (27%)
  waiting for transfers between devices  25 us (26%)
  local copies, waits for them, and re-layouts  10.8 us (11%)
    ppermute x19, starting transfers between devices, send(): return lax.ppermute(value, ('req', 'mlp'), STEPS[way])  26.2 us
    ppermute x19, waiting for transfers between devices, send(): return lax.ppermute(value, ('req', 'mlp'), STEPS[way])  25 us
    pallas_call x5, Pallas kernels, ffn(): pl.pallas_call(functools.partial(ffn_body, tuple(pieces), len(arrays), ol...  14.8 us
    pallas_call x1, Pallas kernels, attend(): pl.pallas_call(attend_body, out_shape=jax.ShapeDtypeStruct((rows, D), bf1...  10.3 us
    unnamed x26, local copies, waits for them, and re-layouts  7.66 us
    pallas_call x1, Pallas kernels, score(): pl.pallas_call(score_body, out_shape=jax.ShapeDtypeStruct((total, SEQ), f...  3.88 us
    pallas_call x1, Pallas kernels, embed(): pl.pallas_call(embed_body, out_shape=jax.ShapeDtypeStruct((normed.shape[0...  2.32 us
  transfers between devices with their start and end apart: 19, of which 8 were waited for; matrix products, arithmetic and copies ran while one was open for 3% of the time, Pallas kernels for 28%

profile of v3, /device:TPU:1, one launch (start us, length us, event | category | flops | bytes accessed | tf_op | source)
XLA Modules:
  0.0 96.4 jit_solution(16786235695739015447)
XLA Ops:
  0.8 1.2 %copy-done.1 = bf16[1024,512]{1,0:T(8,128)(2,1)S(1)} copy-done((bf16[1024,512]{1,0:T(8,128)(2,1)S(1)}, bf16[1024,512]{1,0:T(8,128)(2,1)}, u32[]{:S(2)}) %copy-start.1) | copy-done | bytes 1048600
  2.0 1.2 %copy-done.2 = bf16[1024,512]{1,0:T(8,128)(2,1)S(1)} copy-done((bf16[1024,512]{1,0:T(8,128)(2,1)S(1)}, bf16[1024,512]{1,0:T(8,128)(2,1)}, u32[]{:S(2)}) %copy-start.2) | copy-done | bytes 1048600
  4.7 1.1 %first.1.refs_3_ = bf16[1296,128]{1,0:T(8,128)(2,1)S(1)} custom-call(s32[5]{0:T(128)S(1)} %stack.23.where, s32[8]{0:T(128)S(1)} %copy-done.11, bf16[1024,512]{1,0:T(8,128)(2,1)S(1)} %copy-done.1, bf16[1024,512]{1,0:T(8,128)(2,1)S(1)} %copy-done.2, bf16[256,128]{1,0:T(8,128)(2,1)S(1)} %bitcast.22), custom_call_target="tpu_custom_call" | custom-call | flops 1 | bytes 1 | tf_op jit(solution)/shard_map/first/pallas_call | solution.py:128
  5.8 2.2 %collective-permute-start = (bf16[1296,128]{1,0:T(8,128)(2,1)S(1)}, bf16[1296,128]{1,0:T(8,128)(2,1)S(1)}, u32[]{:S(2)}, u32[]{:S(2)}) collective-permute-start(bf16[1296,128]{1,0:T(8,128)(2,1)S(1)} %first.1.refs_3_), channel_id=1, source_target_pairs={{0,2},{1,3},{2,4},{3,5},{4,6},{5,7},{6,0},{7,1},{8,10},{9,11},{10,... | collective-permute-start | bytes 995336 | tf_op jit(solution)/shard_map/ppermute | solution.py:90
  8.0 1.5 %collective-permute-start.1 = (bf16[1296,128]{1,0:T(8,128)(2,1)S(1)}, bf16[1296,128]{1,0:T(8,128)(2,1)S(1)}, u32[]{:S(2)}, u32[]{:S(2)}) collective-permute-start(bf16[1296,128]{1,0:T(8,128)(2,1)S(1)} %first.1.refs_3_), channel_id=1, source_target_pairs={{0,6},{1,7},{2,0},{3,1},{4,2},{5,3},{6,4},{7,5},{8,14},{9,15},{10,... | collective-permute-start | bytes 995336 | tf_op jit(solution)/shard_map/ppermute | solution.py:90
  9.5 1.6 %collective-permute-start.2 = (bf16[1296,128]{1,0:T(8,128)(2,1)S(1)}, bf16[1296,128]{1,0:T(8,128)(2,1)S(1)}, u32[]{:S(2)}, u32[]{:S(2)}) collective-permute-start(bf16[1296,128]{1,0:T(8,128)(2,1)S(1)} %first.1.refs_3_), channel_id=1, source_target_pairs={{0,4},{1,5},{2,6},{3,7},{4,0},{5,1},{6,2},{7,3},{8,12},{9,13},{10,... | collective-permute-start | bytes 995336 | tf_op jit(solution)/shard_map/ppermute | solution.py:90
  11.7 2.8 %copy-done = bf16[1024,3072]{1,0:T(8,128)(2,1)S(1)} copy-done((bf16[1024,3072]{1,0:T(8,128)(2,1)S(1)}, bf16[1024,3072]{1,0:T(8,128)(2,1)}, u32[]{:S(2)}) %copy-start) | copy-done | bytes 6291480
  14.5 10.3 %attend.1.refs_0_.normed = bf16[512,1024]{1,0:T(8,128)(2,1)S(1)} custom-call(s32[4]{0:T(128)S(1)} %copy-done.10, bf16[512,1024]{1,0:T(8,128)(2,1)S(1)} %copy-done.4, bf16[1024,3072]{1,0:T(8,128)(2,1)S(1)} %copy-done, bf16[1024,1024]{1,0:T(8,128)(2,1)S(1)} %copy-done.3, f32[1,1024]{1,0:T(1,128)S(1)} %bitcast.23), custom_call_target="tpu_custom_call" | custom-call | flops 1 | bytes 1 | tf_op jit(solution)/shard_map/attend/pallas_call | solution.py:217
  25.0 1.7 %collective-permute-start.3 = (bf16[4160,128]{1,0:T(8,128)(2,1)S(1)}, bf16[4160,128]{1,0:T(8,128)(2,1)S(1)}, u32[]{:S(2)}, u32[]{:S(2)}) collective-permute-start(bf16[4160,128]{1,0:T(8,128)(2,1)S(1)} %join1.1.refs_0_), channel_id=1, source_target_pairs={{0,8},{1,33},{2,10},{3,35},{4,12},{5,37},{6,14},{7,39},{8,16},{9,4... | collective-permute-start | bytes 3194888 | tf_op jit(solution)/shard_map/ppermute | solution.py:90
  26.7 2.2 %collective-permute-start.4 = (bf16[4160,128]{1,0:T(8,128)(2,1)S(1)}, bf16[4160,128]{1,0:T(8,128)(2,1)S(1)}, u32[]{:S(2)}, u32[]{:S(2)}) collective-permute-start(bf16[4160,128]{1,0:T(8,128)(2,1)S(1)} %join1.1.refs_0_), channel_id=1, source_target_pairs={{0,24},{1,97},{2,26},{3,99},{4,28},{5,101},{6,30},{7,103},{8,0},{9... | collective-permute-start | bytes 3194888 | tf_op jit(solution)/shard_map/ppermute | solution.py:90
  28.9 1.2 %collective-permute-start.5 = (bf16[4160,128]{1,0:T(8,128)(2,1)S(1)}, bf16[4160,128]{1,0:T(8,128)(2,1)S(1)}, u32[]{:S(2)}, u32[]{:S(2)}) collective-permute-start(bf16[4160,128]{1,0:T(8,128)(2,1)S(1)} %join1.1.refs_0_), channel_id=1, source_target_pairs={{0,16},{1,65},{2,18},{3,67},{4,20},{5,69},{6,22},{7,71},{8,24},{9,... | collective-permute-start | bytes 3194888 | tf_op jit(solution)/shard_map/ppermute | solution.py:90
  30.7 2.1 %collective-permute-start.8 = (bf16[4096,128]{1,0:T(8,128)(2,1)S(1)}, bf16[4096,128]{1,0:T(8,128)(2,1)S(1)}, u32[]{:S(2)}, u32[]{:S(2)}) collective-permute-start(bf16[4096,128]{1,0:T(8,128)(2,1)S(1)} %bitcast.19), channel_id=1, source_target_pairs={{0,6},{1,7},{2,0},{3,1},{4,2},{5,3},{6,4},{7,5},{8,14},{9,15},{10,... | collective-permute-start | bytes 3145736 | tf_op jit(solution)/shard_map/ppermute | solution.py:90
  32.8 8.7 %collective-permute-done.3.refs_1_.refs_5_ = bf16[4160,128]{1,0:T(8,128)(2,1)S(1)} collective-permute-done((bf16[4160,128]{1,0:T(8,128)(2,1)S(1)}, bf16[4160,128]{1,0:T(8,128)(2,1)S(1)}, u32[]{:S(2)}, u32[]{:S(2)}) %collective-permute-start.3) | collective-permute-done | bytes 1064992 | tf_op jit(solution)/shard_map/ppermute | solution.py:90
  41.5 10.8 %collective-permute-done.4.refs_2_.refs_6_ = bf16[4160,128]{1,0:T(8,128)(2,1)S(1)} collective-permute-done((bf16[4160,128]{1,0:T(8,128)(2,1)S(1)}, bf16[4160,128]{1,0:T(8,128)(2,1)S(1)}, u32[]{:S(2)}, u32[]{:S(2)}) %collective-permute-start.4) | collective-permute-done | bytes 1064992 | tf_op jit(solution)/shard_map/ppermute | solution.py:90
  52.2 1.8 %collective-permute-done.5.refs_3_.refs_7_ = bf16[4160,128]{1,0:T(8,128)(2,1)S(1)} collective-permute-done((bf16[4160,128]{1,0:T(8,128)(2,1)S(1)}, bf16[4160,128]{1,0:T(8,128)(2,1)S(1)}, u32[]{:S(2)}, u32[]{:S(2)}) %collective-permute-start.5) | collective-permute-done | bytes 1064992 | tf_op jit(solution)/shard_map/ppermute | solution.py:90
  54.2 1.2 %collective-permute-start.6 = (bf16[512,1024]{1,0:T(8,128)(2,1)S(1)}, bf16[512,1024]{1,0:T(8,128)(2,1)S(1)}, u32[]{:S(2)}, u32[]{:S(2)}) collective-permute-start(bf16[512,1024]{1,0:T(8,128)(2,1)S(1)} %attend.1.refs_0_.normed), channel_id=1, source_target_pairs={{0,1},{1,0},{2,3},{3,2},{4,5},{5,4},{6,7},{7,6},{8,9},{9,8},{10,11... | collective-permute-start | bytes 3145736 | tf_op jit(solution)/shard_map/ppermute | solution.py:90
  55.3 1.1 %collective-permute-start.11 = (bf16[4352,128]{1,0:T(8,128)(2,1)S(1)}, bf16[4352,128]{1,0:T(8,128)(2,1)S(1)}, u32[]{:S(2)}, u32[]{:S(2)}) collective-permute-start(bf16[4352,128]{1,0:T(8,128)(2,1)S(1)} %join2.1), channel_id=1, source_target_pairs={{0,32},{1,9},{2,34},{3,11},{4,36},{5,13},{6,38},{7,15},{8,40},{9,1... | collective-permute-start | bytes 3342344 | tf_op jit(solution)/shard_map/ppermute | solution.py:90
  56.5 1.5 %collective-permute-start.12 = (bf16[4352,128]{1,0:T(8,128)(2,1)S(1)}, bf16[4352,128]{1,0:T(8,128)(2,1)S(1)}, u32[]{:S(2)}, u32[]{:S(2)}) collective-permute-start(bf16[4352,128]{1,0:T(8,128)(2,1)S(1)} %join2.1), channel_id=1, source_target_pairs={{0,96},{1,25},{2,98},{3,27},{4,100},{5,29},{6,102},{7,31},{8,104},... | collective-permute-start | bytes 3342344 | tf_op jit(solution)/shard_map/ppermute | solution.py:90
  58.1 0.9 collective-permute-start.9
  59.0 2.1 %collective-permute-start.10 = (bf16[2048,128]{1,0:T(8,128)(2,1)S(1)}, bf16[2048,128]{1,0:T(8,128)(2,1)S(1)}, u32[]{:S(2)}, u32[]{:S(2)}) collective-permute-start(bf16[2048,128]{1,0:T(8,128)(2,1)S(1)} %join4.1), channel_id=1, source_target_pairs={{0,6},{1,7},{2,0},{3,1},{4,2},{5,3},{6,4},{7,5},{8,14},{9,15},{10,... | collective-permute-start | bytes 1572872 | tf_op jit(solution)/shard_map/ppermute | solution.py:90
  61.3 2.5 %ffn1.1.refs_1_ = f32[1024,1024]{1,0:T(8,128)S(1)} custom-call(bf16[1024,1024]{1,0:T(8,128)(2,1)S(1)} %pad_maximum_fusion.refs_0_, bf16[4096,128]{1,0:T(8,128)(2,1)S(1)} %bitcast.20, bf16[4096,128]{1,0:T(8,128)(2,1)S(1)} %bitcast.21), custom_call_target="tpu_custom_call" | custom-call | flops 1 | bytes 1 | tf_op jit(solution)/shard_map/ffn1/pallas_call | solution.py:261
  63.7 5.1 %ffn2.1.refs_1_ = f32[1024,1024]{1,0:T(8,128)S(1)} custom-call(bf16[1024,1024]{1,0:T(8,128)(2,1)S(1)} %pad_maximum_fusion.refs_0_, f32[1024,1024]{1,0:T(8,128)S(1)} %ffn1.1.refs_1_, bf16[1296,128]{1,0:T(8,128)(2,1)S(1)} %collective-permute-done.refs_0_.refs_2_, ...), custom_call_target="tpu_custom_call", output_to_operand_aliasing={{}: (1, {})} | custom-call | flops 1 | bytes 1 | tf_op jit(solution)/shard_map/ffn2/pallas_call | solution.py:261
  68.8 4.6 %ffn3.1 = f32[1024,1024]{1,0:T(8,128)S(1)} custom-call(bf16[1024,1024]{1,0:T(8,128)(2,1)S(1)} %pad_maximum_fusion.refs_0_, f32[1024,1024]{1,0:T(8,128)S(1)} %ffn2.1.refs_1_, bf16[4096,128]{1,0:T(8,128)(2,1)S(1)} %collective-permute-done.7.refs_2_.refs_0_, bf16[4096,128]{1,0:T(8,128)(2,1)S(1)} %collective-permute-done.8.refs_3_.refs_0_), custom_call_target="tpu_custom_call", output_to_operand_aliasing={{}: (1, {})} | custom-call | flops 1 | bytes 1 | tf_op jit(solution)/shard_map/ffn3/pallas_call | solution.py:261
  74.0 1.3 %ffn4.1 = f32[512,1024]{1,0:T(8,128)S(1)} custom-call(bf16[512,1024]{1,0:T(8,128)(2,1)S(1)} %collective-permute-done.6.refs_0_, f32[512,1024]{1,0:T(8,128)S(1)} %get-tuple-element.28.refs_1_, bf16[2048,128]{1,0:T(8,128)(2,1)S(1)} %collective-permute-done.9.refs_2_, bf16[2048,128]{1,0:T(8,128)(2,1)S(1)} %collective-permute-done.10.refs_3_), custom_call_target="tpu_custom_call", output_to_operand_aliasing={{}: (1, {})} | custom-call | flops 1 | bytes 1 | tf_op jit(solution)/shard_map/ffn4/pallas_call | solution.py:261
  75.3 2.2 %collective-permute-start.13 = (f32[512,1024]{1,0:T(8,128)S(1)}, f32[512,1024]{1,0:T(8,128)S(1)}, u32[]{:S(2)}, u32[]{:S(2)}) collective-permute-start(f32[512,1024]{1,0:T(8,128)S(1)} %ffn4.1), channel_id=1, source_target_pairs={{0,1},{1,0},{2,3},{3,2},{4,5},{5,4},{6,7},{7,6},{8,9},{9,8},{10,11... | collective-permute-start | bytes 6291464 | tf_op jit(solution)/shard_map/ppermute | solution.py:90
  78.4 1.1 %collective-permute-start.16 = (bf16[2176,128]{1,0:T(8,128)(2,1)}, bf16[2176,128]{1,0:T(8,128)(2,1)}, u32[]{:S(2)}, u32[]{:S(2)}) collective-permute-start(bf16[2176,128]{1,0:T(8,128)(2,1)} %slice.26), channel_id=1, source_target_pairs={{0,32},{1,9},{2,34},{3,11},{4,36},{5,13},{6,38},{7,15},{8,40},{9,1... | collective-permute-start | bytes 1671176 | tf_op jit(solution)/shard_map/ppermute | solution.py:90
  80.4 1.5 %collective-permute-start.17 = (bf16[2176,128]{1,0:T(8,128)(2,1)}, bf16[2176,128]{1,0:T(8,128)(2,1)}, u32[]{:S(2)}, u32[]{:S(2)}) collective-permute-start(bf16[2176,128]{1,0:T(8,128)(2,1)} %slice.27), channel_id=1, source_target_pairs={{0,96},{1,25},{2,98},{3,27},{4,100},{5,29},{6,102},{7,31},{8,104},... | collective-permute-start | bytes 1671176 | tf_op jit(solution)/shard_map/ppermute | solution.py:90
  81.9 1.3 %ffn5.1.mine = f32[512,1024]{1,0:T(8,128)S(1)} custom-call(bf16[512,1024]{1,0:T(8,128)(2,1)S(1)} %attend.1.refs_0_.normed, f32[512,1024]{1,0:T(8,128)S(1)} %get-tuple-element.29.refs_1_, bf16[2048,128]{1,0:T(8,128)(2,1)S(1)} %collective-permute-done.9.refs_2_, bf16[2048,128]{1,0:T(8,128)(2,1)S(1)} %collective-permute-done.10.refs_3_), custom_call_target="tpu_custom_call", output_to_operand_aliasing={{}: (1, {})} | custom-call | flops 1 | bytes 1 | tf_op jit(solution)/shard_map/ffn5/pallas_call | solution.py:261
  83.3 2.3 %embed.1.emb = bf16[512,128]{1,0:T(8,128)(2,1)} custom-call(s32[4]{0:T(128)S(1)} %copy-done.10, bf16[512,1024]{1,0:T(8,128)(2,1)S(1)} %attend.1.refs_0_.normed, f32[512,1024]{1,0:T(8,128)S(1)} %ffn5.1.mine, f32[512,1024]{1,0:T(8,128)S(1)} %collective-permute-done.13.other, f32[1,1024]{1,0:T(1,128)S(1)} %bitcast.24, bf16[1024,128]{1,0:T(8,128)(2,1)S(1)} %copy-done.6), custom_call_target="tpu_custom_call" | custom-call | flops 1 | bytes 1 | tf_op jit(solution)/shard_map/embed/pallas_call | solution.py:284
  86.3 1.1 %collective-permute-done.14 = s32[4,8]{1,0:T(4,128)S(1)} collective-permute-done((s32[4,8]{1,0:T(4,128)S(1)}, s32[4,8]{1,0:T(4,128)S(1)}, u32[]{:S(2)}, u32[]{:S(2)}) %collective-permute-start.14) | collective-permute-done | bytes 160 | tf_op jit(solution)/shard_map/ppermute | solution.py:90
  87.4 1.2 %collective-permute-done.16 = bf16[2176,128]{1,0:T(8,128)(2,1)} collective-permute-done((bf16[2176,128]{1,0:T(8,128)(2,1)}, bf16[2176,128]{1,0:T(8,128)(2,1)}, u32[]{:S(2)}, u32[]{:S(2)}) %collective-permute-start.16) | collective-permute-done | bytes 557088 | tf_op jit(solution)/shard_map/ppermute | solution.py:90
  90.0 3.9 %score.1 = f32[64,128]{1,0:T(8,128)S(1)} custom-call(s32[5]{0:T(128)S(1)} %stack.23.where, s32[32]{0:T(128)S(1)} %reshape.48.cand, s32[32]{0:T(128)S(1)} %reshape.49.pair, bf16[512,128]{1,0:T(8,128)(2,1)S(1)} %copy-done.5, bf16[512,128]{1,0:T(8,128)(2,1)S(1)} %collective-permute-done.15.sib, bf16[4,4,272,128]{3,2,1,0:T(8,128)(2,1)S(1)} %bitcast.15, ...), custom_call_target="tpu_custom_call" | custom-call | flops 1 | bytes 1 | tf_op jit(solution)/shard_map/score/pallas_call | solution.py:334
  (56 shorter events, 10.1 us)
Async XLA Ops:
  0.8 1.2 %copy-start.1 = (bf16[1024,512]{1,0:T(8,128)(2,1)S(1)}, bf16[1024,512]{1,0:T(8,128)(2,1)}, u32[]{:S(2)}) copy-start(bf16[1024,512]{1,0:T(8,128)(2,1)} %up.3) | copy-start | bytes 3145732
  2.0 1.2 %copy-start.2 = (bf16[1024,512]{1,0:T(8,128)(2,1)S(1)}, bf16[1024,512]{1,0:T(8,128)(2,1)}, u32[]{:S(2)}) copy-start(bf16[1024,512]{1,0:T(8,128)(2,1)} %down.3) | copy-start | bytes 3145732
  3.2 0.8 copy-start.7
  4.0 0.7 copy-start.11
  4.7 7.0 %copy-start.3 = (bf16[1024,1024]{1,0:T(8,128)(2,1)S(1)}, bf16[1024,1024]{1,0:T(8,128)(2,1)}, u32[]{:S(2)}) copy-start(bf16[1024,1024]{1,0:T(8,128)(2,1)} %wo.1) | copy-start | bytes 6291460
  4.7 7.0 %copy-start.4 = (bf16[512,1024]{1,0:T(8,128)(2,1)S(1)}, bf16[512,1024]{1,0:T(8,128)(2,1)}, u32[]{:S(2)}) copy-start(bf16[512,1024]{1,0:T(8,128)(2,1)} %tok) | copy-start | bytes 3145732
  4.7 7.0 %copy-start.8 = (f32[1024]{0:T(1024)S(1)}, f32[1024]{0:T(1024)}, u32[]{:S(2)}) copy-start(f32[1024]{0:T(1024)} %param.15) | copy-start | bytes 12292
  4.7 7.0 %copy-start.10 = (s32[4]{0:T(128)S(1)}, s32[4]{0:T(128)}, u32[]{:S(2)}) copy-start(s32[4]{0:T(128)} %length.3) | copy-start | bytes 52
  5.8 19.0 %collective-permute-start = (bf16[1296,128]{1,0:T(8,128)(2,1)S(1)}, bf16[1296,128]{1,0:T(8,128)(2,1)S(1)}, u32[]{:S(2)}, u32[]{:S(2)}) collective-permute-start(bf16[1296,128]{1,0:T(8,128)(2,1)S(1)} %first.1.refs_3_), channel_id=1, source_target_pairs={{0,2},{1,3},{2,4},{3,5},{4,6},{5,7},{6,0},{7,1},{8,10},{9,11},{10,... | collective-permute-start | bytes 995336 | tf_op jit(solution)/shard_map/ppermute | solution.py:90
  8.0 16.8 %collective-permute-start.1 = (bf16[1296,128]{1,0:T(8,128)(2,1)S(1)}, bf16[1296,128]{1,0:T(8,128)(2,1)S(1)}, u32[]{:S(2)}, u32[]{:S(2)}) collective-permute-start(bf16[1296,128]{1,0:T(8,128)(2,1)S(1)} %first.1.refs_3_), channel_id=1, source_target_pairs={{0,6},{1,7},{2,0},{3,1},{4,2},{5,3},{6,4},{7,5},{8,14},{9,15},{10,... | collective-permute-start | bytes 995336 | tf_op jit(solution)/shard_map/ppermute | solution.py:90
  9.5 15.4 %collective-permute-start.2 = (bf16[1296,128]{1,0:T(8,128)(2,1)S(1)}, bf16[1296,128]{1,0:T(8,128)(2,1)S(1)}, u32[]{:S(2)}, u32[]{:S(2)}) collective-permute-start(bf16[1296,128]{1,0:T(8,128)(2,1)S(1)} %first.1.refs_3_), channel_id=1, source_target_pairs={{0,4},{1,5},{2,6},{3,7},{4,0},{5,1},{6,2},{7,3},{8,12},{9,13},{10,... | collective-permute-start | bytes 995336 | tf_op jit(solution)/shard_map/ppermute | solution.py:90
  11.7 2.8 %copy-start = (bf16[1024,3072]{1,0:T(8,128)(2,1)S(1)}, bf16[1024,3072]{1,0:T(8,128)(2,1)}, u32[]{:S(2)}) copy-start(bf16[1024,3072]{1,0:T(8,128)(2,1)} %qkv.1) | copy-start | bytes 18874372
  25.0 16.5 %collective-permute-start.3 = (bf16[4160,128]{1,0:T(8,128)(2,1)S(1)}, bf16[4160,128]{1,0:T(8,128)(2,1)S(1)}, u32[]{:S(2)}, u32[]{:S(2)}) collective-permute-start(bf16[4160,128]{1,0:T(8,128)(2,1)S(1)} %join1.1.refs_0_), channel_id=1, source_target_pairs={{0,8},{1,33},{2,10},{3,35},{4,12},{5,37},{6,14},{7,39},{8,16},{9,4... | collective-permute-start | bytes 3194888 | tf_op jit(solution)/shard_map/ppermute | solution.py:90
  26.7 25.5 %collective-permute-start.4 = (bf16[4160,128]{1,0:T(8,128)(2,1)S(1)}, bf16[4160,128]{1,0:T(8,128)(2,1)S(1)}, u32[]{:S(2)}, u32[]{:S(2)}) collective-permute-start(bf16[4160,128]{1,0:T(8,128)(2,1)S(1)} %join1.1.refs_0_), channel_id=1, source_target_pairs={{0,24},{1,97},{2,26},{3,99},{4,28},{5,101},{6,30},{7,103},{8,0},{9... | collective-permute-start | bytes 3194888 | tf_op jit(solution)/shard_map/ppermute | solution.py:90
  28.9 25.2 %collective-permute-start.5 = (bf16[4160,128]{1,0:T(8,128)(2,1)S(1)}, bf16[4160,128]{1,0:T(8,128)(2,1)S(1)}, u32[]{:S(2)}, u32[]{:S(2)}) collective-permute-start(bf16[4160,128]{1,0:T(8,128)(2,1)S(1)} %join1.1.refs_0_), channel_id=1, source_target_pairs={{0,16},{1,65},{2,18},{3,67},{4,20},{5,69},{6,22},{7,71},{8,24},{9,... | collective-permute-start | bytes 3194888 | tf_op jit(solution)/shard_map/ppermute | solution.py:90
  30.1 27.9 %collective-permute-start.7 = (bf16[4096,128]{1,0:T(8,128)(2,1)S(1)}, bf16[4096,128]{1,0:T(8,128)(2,1)S(1)}, u32[]{:S(2)}, u32[]{:S(2)}) collective-permute-start(bf16[4096,128]{1,0:T(8,128)(2,1)S(1)} %bitcast.18), channel_id=1, source_target_pairs={{0,2},{1,3},{2,4},{3,5},{4,6},{5,7},{6,0},{7,1},{8,10},{9,11},{10,... | collective-permute-start | bytes 3145736 | tf_op jit(solution)/shard_map/ppermute | solution.py:90
  30.7 27.4 %collective-permute-start.8 = (bf16[4096,128]{1,0:T(8,128)(2,1)S(1)}, bf16[4096,128]{1,0:T(8,128)(2,1)S(1)}, u32[]{:S(2)}, u32[]{:S(2)}) collective-permute-start(bf16[4096,128]{1,0:T(8,128)(2,1)S(1)} %bitcast.19), channel_id=1, source_target_pairs={{0,6},{1,7},{2,0},{3,1},{4,2},{5,3},{6,4},{7,5},{8,14},{9,15},{10,... | collective-permute-start | bytes 3145736 | tf_op jit(solution)/shard_map/ppermute | solution.py:90
  54.2 6.9 %collective-permute-start.6 = (bf16[512,1024]{1,0:T(8,128)(2,1)S(1)}, bf16[512,1024]{1,0:T(8,128)(2,1)S(1)}, u32[]{:S(2)}, u32[]{:S(2)}) collective-permute-start(bf16[512,1024]{1,0:T(8,128)(2,1)S(1)} %attend.1.refs_0_.normed), channel_id=1, source_target_pairs={{0,1},{1,0},{2,3},{3,2},{4,5},{5,4},{6,7},{7,6},{8,9},{9,8},{10,11... | collective-permute-start | bytes 3145736 | tf_op jit(solution)/shard_map/ppermute | solution.py:90
  55.3 18.7 %collective-permute-start.11 = (bf16[4352,128]{1,0:T(8,128)(2,1)S(1)}, bf16[4352,128]{1,0:T(8,128)(2,1)S(1)}, u32[]{:S(2)}, u32[]{:S(2)}) collective-permute-start(bf16[4352,128]{1,0:T(8,128)(2,1)S(1)} %join2.1), channel_id=1, source_target_pairs={{0,32},{1,9},{2,34},{3,11},{4,36},{5,13},{6,38},{7,15},{8,40},{9,1... | collective-permute-start | bytes 3342344 | tf_op jit(solution)/shard_map/ppermute | solution.py:90
  56.5 17.5 %collective-permute-start.12 = (bf16[4352,128]{1,0:T(8,128)(2,1)S(1)}, bf16[4352,128]{1,0:T(8,128)(2,1)S(1)}, u32[]{:S(2)}, u32[]{:S(2)}) collective-permute-start(bf16[4352,128]{1,0:T(8,128)(2,1)S(1)} %join2.1), channel_id=1, source_target_pairs={{0,96},{1,25},{2,98},{3,27},{4,100},{5,29},{6,102},{7,31},{8,104},... | collective-permute-start | bytes 3342344 | tf_op jit(solution)/shard_map/ppermute | solution.py:90
  58.1 15.9 %collective-permute-start.9 = (bf16[2048,128]{1,0:T(8,128)(2,1)S(1)}, bf16[2048,128]{1,0:T(8,128)(2,1)S(1)}, u32[]{:S(2)}, u32[]{:S(2)}) collective-permute-start(bf16[2048,128]{1,0:T(8,128)(2,1)S(1)} %join3.1), channel_id=1, source_target_pairs={{0,2},{1,3},{2,4},{3,5},{4,6},{5,7},{6,0},{7,1},{8,10},{9,11},{10,... | collective-permute-start | bytes 1572872 | tf_op jit(solution)/shard_map/ppermute | solution.py:90
  59.0 15.0 %collective-permute-start.10 = (bf16[2048,128]{1,0:T(8,128)(2,1)S(1)}, bf16[2048,128]{1,0:T(8,128)(2,1)S(1)}, u32[]{:S(2)}, u32[]{:S(2)}) collective-permute-start(bf16[2048,128]{1,0:T(8,128)(2,1)S(1)} %join4.1), channel_id=1, source_target_pairs={{0,6},{1,7},{2,0},{3,1},{4,2},{5,3},{6,4},{7,5},{8,14},{9,15},{10,... | collective-permute-start | bytes 1572872 | tf_op jit(solution)/shard_map/ppermute | solution.py:90
  75.3 7.9 %collective-permute-start.13 = (f32[512,1024]{1,0:T(8,128)S(1)}, f32[512,1024]{1,0:T(8,128)S(1)}, u32[]{:S(2)}, u32[]{:S(2)}) collective-permute-start(f32[512,1024]{1,0:T(8,128)S(1)} %ffn4.1), channel_id=1, source_target_pairs={{0,1},{1,0},{2,3},{3,2},{4,5},{5,4},{6,7},{7,6},{8,9},{9,8},{10,11... | collective-permute-start | bytes 6291464 | tf_op jit(solution)/shard_map/ppermute | solution.py:90
  78.4 10.2 %collective-permute-start.16 = (bf16[2176,128]{1,0:T(8,128)(2,1)}, bf16[2176,128]{1,0:T(8,128)(2,1)}, u32[]{:S(2)}, u32[]{:S(2)}) collective-permute-start(bf16[2176,128]{1,0:T(8,128)(2,1)} %slice.26), channel_id=1, source_target_pairs={{0,32},{1,9},{2,34},{3,11},{4,36},{5,13},{6,38},{7,15},{8,40},{9,1... | collective-permute-start | bytes 1671176 | tf_op jit(solution)/shard_map/ppermute | solution.py:90
  80.4 8.7 %collective-permute-start.17 = (bf16[2176,128]{1,0:T(8,128)(2,1)}, bf16[2176,128]{1,0:T(8,128)(2,1)}, u32[]{:S(2)}, u32[]{:S(2)}) collective-permute-start(bf16[2176,128]{1,0:T(8,128)(2,1)} %slice.27), channel_id=1, source_target_pairs={{0,96},{1,25},{2,98},{3,27},{4,100},{5,29},{6,102},{7,31},{8,104},... | collective-permute-start | bytes 1671176 | tf_op jit(solution)/shard_map/ppermute | solution.py:90
  81.9 1.3 %copy-start.6 = (bf16[1024,128]{1,0:T(8,128)(2,1)S(1)}, bf16[1024,128]{1,0:T(8,128)(2,1)}, u32[]{:S(2)}) copy-start(bf16[1024,128]{1,0:T(8,128)(2,1)} %we.1) | copy-start | bytes 786436
  81.9 1.3 %copy-start.9 = (f32[1024]{0:T(1024)S(1)}, f32[1024]{0:T(1024)}, u32[]{:S(2)}) copy-start(f32[1024]{0:T(1024)} %param.18) | copy-start | bytes 12292
  83.3 2.9 %copy-start.12 = (s32[4,8]{1,0:T(4,128)S(1)}, s32[4,8]{1,0:T(4,128)}, u32[]{:S(2)}) copy-start(s32[4,8]{1,0:T(4,128)} %param.23) | copy-start | bytes 388
  85.6 3.5 %collective-permute-start.15 = (bf16[512,128]{1,0:T(8,128)(2,1)}, bf16[512,128]{1,0:T(8,128)(2,1)S(1)}, u32[]{:S(2)}, u32[]{:S(2)}) collective-permute-start(bf16[512,128]{1,0:T(8,128)(2,1)} %embed.1.emb), channel_id=1, source_target_pairs={{0,1},{1,0},{2,3},{3,2},{4,5},{5,4},{6,7},{7,6},{8,9},{9,8},{10,11... | collective-permute-start | bytes 393224 | tf_op jit(solution)/shard_map/ppermute | solution.py:90
  86.2 1.2 %collective-permute-start.14 = (s32[4,8]{1,0:T(4,128)S(1)}, s32[4,8]{1,0:T(4,128)S(1)}, u32[]{:S(2)}, u32[]{:S(2)}) collective-permute-start(s32[4,8]{1,0:T(4,128)S(1)} %copy-done.12), channel_id=1, source_target_pairs={{0,1},{1,0},{2,3},{3,2},{4,5},{5,4},{6,7},{7,6},{8,9},{9,8},{10,11... | collective-permute-start | bytes 392 | tf_op jit(solution)/shard_map/ppermute | solution.py:90
  89.1 0.9 copy-start.5
  93.9 1.7 %collective-permute-start.18 = (f32[32,128]{1,0:T(8,128)S(1)}, f32[32,128]{1,0:T(8,128)S(1)}, u32[]{:S(2)}, u32[]{:S(2)}) collective-permute-start(f32[32,128]{1,0:T(8,128)S(1)} %slice.29), channel_id=1, source_target_pairs={{0,1},{1,0},{2,3},{3,2},{4,5},{5,4},{6,7},{7,6},{8,9},{9,8},{10,11... | collective-permute-start | bytes 49160 | tf_op jit(solution)/shard_map/ppermute | solution.py:90

commit v4 on v3

--- a/solution.py
+++ b/solution.py
@@ -98,22 +98,26 @@
     return [pl.BlockSpec(memory_space=pl.ANY)] * n
 
 
+def pinned(*arrays):
+    return [pltpu.with_memory_space_constraint(a, pltpu.HBM) for a in arrays]
+
+
+def hbm(n=1):
+    return [pl.BlockSpec(memory_space=pltpu.HBM)] * n
+
+
 SMEM = pl.BlockSpec(memory_space=pltpu.SMEM)
 
 
-def first_body(where, limits, up, down, docs, out, held, turned, sems):
+def first_body(where, up, down, docs, lengths, out, held, turned, limits, sems):
     index = where[4]
     lanes = pl.ds(pl.multiple_of(256 + (index >> 1) * LANES, LANES), LANES)
     copies = [pltpu.make_async_copy(w.at[:, lanes], held.at[k], sems.at[k]) for k, w in enumerate((up, down))]
     tokens = DOC_ROWS - 16
     copies.append(pltpu.make_async_copy(docs, out.at[PART : PART + tokens], sems.at[2]))
+    copies.append(pltpu.make_async_copy(lengths, limits, sems.at[3]))
     for copy in copies:
         copy.start()
-    row = lax.broadcasted_iota(jnp.int32, (16, LANES), 0)
-    limit = jnp.zeros((16, LANES), f32)
-    for j in range(8):
-        limit = jnp.where(row == j, limits[j].astype(f32), limit)
-    out[PART + tokens : BLOCK, :] = limit.astype(bf16)
     start = pl.multiple_of((index & 1) * SLICE, SLICE)
     for k in range(2):
         copies[k].wait()
@@ -121,33 +125,48 @@
             slab = k * HALF + j
             turned[slab] = held[k, j * LANES : (j + 1) * LANES, :].T
             out[slab * SLICE : (slab + 1) * SLICE, :] = turned[slab, pl.ds(start, SLICE), :]
+    copies[3].wait()
+    row = lax.broadcasted_iota(jnp.int32, (16, LANES), 0)
+    limit = jnp.zeros((16, LANES), f32)
+    for j in range(8):
+        limit = jnp.where(row == j, limits[j].astype(f32), limit)
+    out[PART + tokens : BLOCK, :] = limit.astype(bf16)
     copies[2].wait()
 
 
-def first(where, up, down, docs, limits):
+def first(where, up, down, docs, lengths):
     return pl.pallas_call(
         first_body,
         out_shape=jax.ShapeDtypeStruct((BLOCK, LANES), bf16),
-        in_specs=[SMEM] * 2 + any_spec(3),
+        in_specs=[SMEM] + hbm(4),
         out_specs=vmem()[0],
         scratch_shapes=[
             pltpu.VMEM((2, D, LANES), bf16),
             pltpu.VMEM((SLABS, LANES, LANES), bf16),
-            pltpu.SemaphoreType.DMA((3,)),
+            pltpu.SMEM((8,), jnp.int32),
+            pltpu.SemaphoreType.DMA((4,)),
         ],
         compiler_params=params(16),
         cost_estimate=LIGHT,
         name="first",
-    )(where, limits, up, down, docs)
-
-
-def pack_body(up, down, low, high):
-    for j in range(HALF):
-        rows = slice(j * LANES, (j + 1) * LANES)
-        low[j] = up[rows, :256].T
-        low[HALF + j] = down[rows, :256].T
-        high[j] = up[rows, 256:].T
-        high[HALF + j] = down[rows, 256:].T
+    )(where, *pinned(up, down, docs, lengths))
+
+
+def pack_body(up, down, low, high, held, sems):
+    copies = [
+        pltpu.make_async_copy(w.at[h * 512 : (h + 1) * 512], held.at[k, h * 512 : (h + 1) * 512], sems.at[2 * k + h])
+        for k, w in enumerate((up, down))
+        for h in range(2)
+    ]
+    for copy in copies:
+        copy.start()
+    for k in range(2):
+        for j in range(HALF):
+            if j % 4 == 0:
+                copies[2 * k + j // 4].wait()
+            rows = slice(j * LANES, (j + 1) * LANES)
+            low[k * HALF + j] = held[k, rows, :256].T
+            high[k * HALF + j] = held[k, rows, 256:].T
 
 
 def pack(up, down):
@@ -155,12 +174,13 @@
     low, high = pl.pallas_call(
         pack_body,
         out_shape=(piece, piece),
-        in_specs=vmem(2),
+        in_specs=hbm(2),
         out_specs=tuple(vmem(2)),
+        scratch_shapes=[pltpu.VMEM((2, D, 512), bf16), pltpu.SemaphoreType.DMA((4,))],
         compiler_params=params(16),
         cost_estimate=LIGHT,
         name="pack",
-    )(up, down)
+    )(*pinned(up, down))
     return low.reshape(-1, LANES), high.reshape(-1, LANES)
 
 
@@ -183,10 +203,21 @@
     )(*arrays)
 
 
-def attend_body(length, tok, qkv, wo, gain, out, packed, context):
+def attend_body(length, tok_hbm, qkv, wo_hbm, gain, out, packed, context, tok, held, wo, sems):
     rows_all = tok.shape[0]
-    for c in range(0, 3 * D, 512):
-        packed[:, c : c + 512] = dot(tok[...], qkv[:, c : c + 512]).astype(bf16)
+    step = 512
+    copies = [pltpu.make_async_copy(tok_hbm, tok, sems.at[6])]
+    for i in range(6):
+        columns = slice(i * step, (i + 1) * step)
+        copies.append(pltpu.make_async_copy(qkv.at[:, columns], held.at[:, columns], sems.at[i]))
+    copies.append(pltpu.make_async_copy(wo_hbm, wo, sems.at[7]))
+    for copy in copies:
+        copy.start()
+    copies[0].wait()
+    for i in range(6):
+        columns = slice(i * step, (i + 1) * step)
+        copies[1 + i].wait()
+        packed[:, columns] = dot(tok[...], held[:, columns]).astype(bf16)
     lane = lax.broadcasted_iota(jnp.int32, (2 * SEQ, LANES), 1)
     low = lax.broadcasted_iota(jnp.int32, (SEQ, LANES), 1) < HD
 
@@ -208,6 +239,7 @@
         return carry
 
     lax.fori_loop(0, rows_all // SEQ, request, 0)
+    copies[7].wait()
     attended = dot(context[...], wo[...])
     out[...] = norm_rows(tok[...].astype(f32) + attended, gain[...]).astype(bf16)
 
@@ -217,13 +249,20 @@
     return pl.pallas_call(
         attend_body,
         out_shape=jax.ShapeDtypeStruct((rows, D), bf16),
-        in_specs=[pl.BlockSpec(memory_space=pltpu.SMEM)] + vmem(4),
+        in_specs=[SMEM] + hbm(3) + vmem(1),
         out_specs=vmem()[0],
-        scratch_shapes=[pltpu.VMEM((rows, 3 * D), bf16), pltpu.VMEM((rows, D), bf16)],
+        scratch_shapes=[
+            pltpu.VMEM((rows, 3 * D), bf16),
+            pltpu.VMEM((rows, D), bf16),
+            pltpu.VMEM((rows, D), bf16),
+            pltpu.VMEM((D, 3 * D), bf16),
+            pltpu.VMEM((D, D), bf16),
+            pltpu.SemaphoreType.DMA((8,)),
+        ],
         compiler_params=params(32),
         cost_estimate=LIGHT,
         name="attend",
-    )(length, tokens, qkv, wo, gain.reshape(1, D))
+    )(length, *pinned(tokens, qkv, wo), gain.reshape(1, D))
 
 
 def units(refs, half, start, size):
@@ -240,60 +279,86 @@
     return jnp.concatenate(slabs, axis=1)
 
 
-def ffn_body(pieces, arrays, fresh, *refs):
-    tokens, out = refs[0], refs[-1]
-    held = refs[-1 - arrays : -1]
+def ffn_body(pieces, arrays, sets, fresh, *refs):
+    inner, outs = refs[-1], refs[-1 - sets : -1]
+    tokens, olds = refs[:sets], refs[sets : 2 * sets]
+    held = refs[-1 - sets - arrays : -1 - sets]
     laid = [(held[k], base, count) for k, base, count in pieces]
     total = sum(count for _, _, count in pieces)
-    x = tokens[...]
-    acc = None if fresh else refs[1][...]
-    for s in range(0, total, 256):
-        n = min(256, total - s)
-        inner = gelu(dot_t(x, units(laid, 0, s, n))).astype(bf16)
-        more = dot(inner, units(laid, 1, s, n))
-        acc = more if acc is None else acc + more
-    out[...] = acc
-
-
-def ffn(tokens, old, arrays, pieces, name):
-    rows = tokens.shape[0]
-    tail = ((tokens,) if old is None else (tokens, old)) + tuple(arrays)
-    return pl.pallas_call(
-        functools.partial(ffn_body, tuple(pieces), len(arrays), old is None),
-        out_shape=jax.ShapeDtypeStruct((rows, D), f32),
+    for t in range(sets):
+        x = tokens[t][...]
+        for s in range(0, total, 256):
+            n = min(256, total - s)
+            inner[t, :, s : s + n] = gelu(dot_t(x, units(laid, 0, s, n))).astype(bf16)
+    down = units(laid, 1, 0, total)
+    for t in range(sets):
+        for c in range(0, D, 256):
+            more = dot(inner[t], down[:, c : c + 256])
+            outs[t][:, c : c + 256] = more if fresh else olds[t][:, c : c + 256] + more
+
+
+def ffn(tokens, olds, arrays, pieces, name):
+    sets, rows = len(tokens), tokens[0].shape[0]
+    total = sum(count for _, _, count in pieces)
+    tail = tuple(tokens) + tuple(olds) + tuple(arrays)
+    return pl.pallas_call(
+        functools.partial(ffn_body, tuple(pieces), len(arrays), sets, not olds),
+        out_shape=(jax.ShapeDtypeStruct((rows, D), f32),) * sets,
         in_specs=vmem(len(tail)),
-        out_specs=vmem()[0],
-        input_output_aliases={} if old is None else {1: 0},
-        compiler_params=params(32),
+        out_specs=tuple(vmem(sets)),
+        input_output_aliases={sets + t: t for t in range(len(olds))},
+        scratch_shapes=[pltpu.VMEM((sets, rows, total), bf16)],
+        compiler_params=params(20),
         cost_estimate=LIGHT,
         name=name,
     )(*tail)
 
 
-def embed_body(length, normed, mine, other, gain, we, out):
+def embed_body(length, normed, mine, other, gain, we, out, kept):
     layer = norm_rows(normed[...].astype(f32) + (mine[...] + other[...]), gain[...]).astype(bf16)
     projected = dot(layer, we[...])
     unit = projected * lax.rsqrt(jnp.sum(projected * projected, axis=-1, keepdims=True) + 1e-06)
     slot = lax.broadcasted_iota(jnp.int32, (SEQ, P_SIZE), 0)
     for r in range(normed.shape[0] // SEQ):
         rows = slice(r * SEQ, (r + 1) * SEQ)
-        out[rows, :] = jnp.where(slot < length[r], unit[rows], 0.0).astype(bf16)
+        live = jnp.where(slot < length[r], unit[rows], 0.0).astype(bf16)
+        out[rows, :] = live
+        kept[rows, :] = live
 
 
 def embed(length, normed, mine, other, gain, we):
+    shape = jax.ShapeDtypeStruct((normed.shape[0], P_SIZE), bf16)
     return pl.pallas_call(
         embed_body,
-        out_shape=jax.ShapeDtypeStruct((normed.shape[0], P_SIZE), bf16),
-        in_specs=[pl.BlockSpec(memory_space=pltpu.SMEM)] + vmem(5),
-        out_specs=vmem()[0],
+        out_shape=(shape, shape),
+        in_specs=[SMEM] + vmem(5),
+        out_specs=tuple(vmem(2)),
         compiler_params=params(24),
         cost_estimate=LIGHT,
         name="embed",
     )(length, normed, mine, other, gain.reshape(1, D), we)
 
 
+def final_body(mine, other, out):
+    out[...] = jnp.sum(jnp.maximum(mine[...], other[...]), axis=-1)
+
+
+def final(mine, other, requests):
+    picks = mine.shape[0] // requests
+    shape = (requests, picks, mine.shape[1])
+    return pl.pallas_call(
+        final_body,
+        out_shape=jax.ShapeDtypeStruct((requests, picks), f32),
+        in_specs=vmem(2),
+        out_specs=vmem()[0],
+        compiler_params=params(8),
+        cost_estimate=LIGHT,
+        name="final",
+    )(mine.reshape(shape), other.reshape(shape))
+
+
 def score_body(where, cand, pair, emb, sib, *refs):
-    docs, out, held, sem = refs[:5], refs[5], refs[6], refs[7]
+    docs, outs, held, sem = refs[:5], refs[5:7], refs[7], refs[8]
     copies = [pltpu.make_async_copy(docs[i], held.at[i], sem.at[i]) for i in range(3)]
     copies += [
         pltpu.make_async_copy(docs[3 + i], held.at[3, 2 * i : 2 * i + 2], sem.at[3 + i]) for i in range(2)
@@ -325,17 +390,18 @@
         limit = jnp.sum(jnp.where(row == j, lens, 0.0), axis=0, keepdims=True)
         r = (i % per) // 8
         sims = dot_t(block.reshape(4 * TOKS, P_SIZE), tokens[r * SEQ : (r + 1) * SEQ, :])
-        out[i : i + 1, :] = jnp.max(jnp.where(pos < limit, sims, DEAD), axis=0, keepdims=True)
+        at = i % per
+        outs[i // per][at : at + 1, :] = jnp.max(jnp.where(pos < limit, sims, DEAD), axis=0, keepdims=True)
 
 
 def score(where, cand, pair, emb, sib, docs):
-    total = 2 * cand.size
+    total = cand.size
     docs = [d.reshape(-1, 4, DOC_ROWS, P_SIZE) for d in docs]
     return pl.pallas_call(
         score_body,
-        out_shape=jax.ShapeDtypeStruct((total, SEQ), f32),
+        out_shape=(jax.ShapeDtypeStruct((total, SEQ), f32),) * 2,
         in_specs=[SMEM] * 3 + vmem(2) + any_spec(5),
-        out_specs=vmem()[0],
+        out_specs=tuple(vmem(2)),
         scratch_shapes=[
             pltpu.VMEM((4, 4, 4, DOC_ROWS, P_SIZE), bf16),
             pltpu.SemaphoreType.DMA((5,)),
@@ -366,43 +432,45 @@
     start = first(where, up_weight, down_weight, documents.reshape(-1, P_SIZE), document_length)
     near = [send(start, way) for way in ("y+", "y-", "y2")]
     low, high = pack(up_weight, down_weight)
-    normed = attend(after(tokens, start), attend_weight, output_weight, attend_gain, query_length)
+    normed = attend(tokens, attend_weight, output_weight, after(attend_gain, start), query_length)
     near = after(tuple(near), normed, high)
 
     whole = [(k, 0, BLOCK) for k in range(3)] + [(3, PART, DOC_ROWS)]
     go = join([*near, start], whole, "join1")
     came = [send(go, way) for way in ("f+", "f-", "f2")]
-    low_go = after(low, go)
+    pair_normed = send(after(normed, go), "c")
+    pair = send(after(candidates, go), "c")
+    low_go = after(low, pair_normed, pair)
     low_near = [send(low_go, "y+"), send(low_go, "y-")]
-    parts = [(k, i * BLOCK, SLICE) for k in range(3) for i in range(3)]
+    sets = (normed, pair_normed)
+    total = ffn(sets, (), [low, high], [(0, 0, 256), (1, 0, 256)], "ffn1")
+    parts = [(i * BLOCK, SLICE) for i in range(3)]
+    pieces = [(k, 0, SLICE) for k in range(3)] + [(3,) + p for p in parts]
+    total = ffn(sets, total, [*near, came[0]], pieces, "ffn2")
+    came, low_near, total = after((came, low_near, total), *total)
     takes = [(k, at, DOC_ROWS) for k in range(4) for at in [i * BLOCK + PART for i in range(3)] + [3 * BLOCK]]
     docs = join([go, *came], takes, "join2")
     last = [send(docs, way) for way in ("g+", "g-")]
-    pair_normed = send(after(normed, docs), "c")
-    both = jnp.concatenate([normed, pair_normed], axis=0)
-    low_near = after(tuple(low_near), docs)
     mid = 128
-    ahead = join([low_near[0]], [(0, k * 256, mid) for k in range(SLABS)], "join3")
-    behind = join([low_near[1]], [(0, k * 256 + mid, mid) for k in range(SLABS)], "join4")
+    ahead = join([low_near[0]], [(0, k * 256, mid) for k in range(SLABS)], "join5")
+    behind = join([low_near[1]], [(0, k * 256 + mid, mid) for k in range(SLABS)], "join6")
     low_far = [send(ahead, "y+"), send(behind, "y-")]
-    total = ffn(both, None, [low, high], [(0, 0, 256), (1, 0, 256)], "ffn1")
-    total = ffn(both, total, tuple(near) + tuple(came), [(k, 0, SLICE) for k in range(3)] + [(k + 3, b, n) for k, b, n in parts], "ffn2")
-    total = ffn(both, total, low_near, [(0, 0, 256), (1, 0, 256)], "ffn3")
+    pieces = [(k,) + p for k in range(2) for p in parts] + [(2, 0, 256), (3, 0, 256)]
+    total = ffn(sets, total, [*came[1:], *low_near], pieces, "ffn3")
     cut = docs.shape[0] // 2
-    low_far = after(tuple(low_far), *last)
-    last += [send(last[0][:cut], "g+"), send(last[1][cut:], "g-")]
-    rows = normed.shape[0]
+    last += [
+        send(join([last[0]], [(0, 0, cut)], "join3"), "g+"),
+        send(join([last[1]], [(0, cut, cut)], "join4"), "g-"),
+    ]
+    low_far = after(low_far, *last[:2])
     rest = [(0, 0, mid), (1, 0, mid)]
-    away = ffn(pair_normed, total[rows:], low_far, rest, "ffn4")
+    away, = ffn(sets[1:], total[1:], low_far, rest, "ffn4")
     other = send(away, "c")
-    mine = ffn(normed, total[:rows], low_far, rest, "ffn5")
-    embedded = embed(query_length, normed, mine, other, mlp_gain, embed_weight)
-    sib = send(embedded, "c")
-    pair = send(after(candidates, total), "c")
-    best = score(where, candidates, pair, embedded, sib, [docs] + last)
-    half = best.shape[0] // 2
-    best = jnp.maximum(best[:half], send(best[half:], "c"))
-    scores = jnp.sum(best, axis=1).reshape(candidates.shape)
+    mine, = ffn(sets[:1], total[:1], low_far, rest, "ffn5")
+    embedded, kept = embed(query_length, normed, mine, other, mlp_gain, embed_weight)
+    sib = send(kept, "c")
+    best, best_pair = score(where, candidates, pair, kept, sib, [docs] + last)
+    scores = final(best, send(best_pair, "c"), candidates.shape[0])
     return (embedded, scores)
 
 

time: 96.7 us -> 101 us (1.044)
  local copies, waits for them, and re-layouts: 10.8 us -> 0.27 us
  waiting for transfers between devices: 25 us -> 34.5 us
  Pallas kernels: 33.2 us -> 38.4 us
    ppermute x19, waiting for transfers between devices: 25 us -> 34.5 us  [send(): return lax.ppermute(value, ('req', 'mlp'), STEPS[way])]
    unnamed x26 -> x10, local copies, waits for them, and re-layouts: 7.66 us -> 0.02 us
    pallas_call x1, Pallas kernels: 10.3 us -> 12.8 us  [attend(): pl.pallas_call(attend_body, out_shape=jax.ShapeDtypeStruct((rows, D), bf1...]
    slice x4 -> x0, local copies, waits for them, and re-layouts: 2.23 us -> none  [the longest x2 1.7 us: on_device(): last += [send(last[0][:cut], 'g+'), send(last[1][cut:], 'g-')]]
    pallas_call x4 -> x6, Pallas kernels: 0.21 us -> 1.89 us  [join(): pl.pallas_call(functools.partial(join_body, takes), out_shape=jax.ShapeDt...]
    pallas_call x8 -> x9, Pallas kernels: 21.6 us -> 21.9 us  [the longest x5 12.8 us: ffn(): pl.pallas_call(functools.partial(ffn_body, tuple(pieces), len(arrays), se...]
  transfers between devices with their start and end apart: 19 -> 19, of which waited for: 8 -> 11; matrix products, arithmetic and copies ran while one was open for 3% -> 0% of each run, Pallas kernels for 28% -> 30%
where the time goes in v4:
time: 101 us
  Pallas kernels  38.4 us (38%)
  waiting for transfers between devices  34.5 us (34%)
  starting transfers between devices  26.5 us (26%)
    ppermute x19, waiting for transfers between devices, send(): return lax.ppermute(value, ('req', 'mlp'), STEPS[way])  34.5 us
    ppermute x19, starting transfers between devices, send(): return lax.ppermute(value, ('req', 'mlp'), STEPS[way])  26.5 us
    pallas_call x1, Pallas kernels, attend(): pl.pallas_call(attend_body, out_shape=jax.ShapeDtypeStruct((rows, D), bf1...  12.8 us
    pallas_call x5, Pallas kernels, ffn(): pl.pallas_call(functools.partial(ffn_body, tuple(pieces), len(arrays), se...  12.8 us
    pallas_call x1, Pallas kernels, score(): pl.pallas_call(score_body, out_shape=(jax.ShapeDtypeStruct((total, SEQ),...  4.24 us
    pallas_call x1, Pallas kernels, embed(): pl.pallas_call(embed_body, out_shape=(shape, shape), in_specs=[SMEM] + vm...  2.34 us
  transfers between devices with their start and end apart: 19, of which 11 were waited for; matrix products, arithmetic and copies ran while one was open for 0% of the time, Pallas kernels for 30%

profile of v4, /device:TPU:1, one launch (start us, length us, event | category | flops | bytes accessed | tf_op | source)
XLA Modules:
  0.0 100.5 jit_solution(6914047102552698845)
XLA Ops:
  0.8 1.8 %first.1.refs_3_ = bf16[1296,128]{1,0:T(8,128)(2,1)S(1)} custom-call(s32[5]{0:T(128)S(1)} %stack.23.where, bf16[1024,512]{1,0:T(8,128)(2,1)} %up.3, bf16[1024,512]{1,0:T(8,128)(2,1)} %down.3, bf16[256,128]{1,0:T(8,128)(2,1)} %bitcast.28, s32[8]{0:T(128)} %lengths.1), custom_call_target="tpu_custom_call" | custom-call | flops 1 | bytes 1 | tf_op jit(solution)/shard_map/first/pallas_call | solution.py:138
  2.6 3.8 %collective-permute-start.2 = (bf16[1296,128]{1,0:T(8,128)(2,1)S(1)}, bf16[1296,128]{1,0:T(8,128)(2,1)S(1)}, u32[]{:S(2)}, u32[]{:S(2)}) collective-permute-start(bf16[1296,128]{1,0:T(8,128)(2,1)S(1)} %first.1.refs_3_), channel_id=1, source_target_pairs={{0,4},{1,5},{2,6},{3,7},{4,0},{5,1},{6,2},{7,3},{8,12},{9,13},{10,... | collective-permute-start | bytes 995336 | tf_op jit(solution)/shard_map/ppermute | solution.py:90
  7.9 1.8 %pack.1 = (bf16[16,256,128]{2,1,0:T(8,128)(2,1)S(1)}, bf16[16,256,128]{2,1,0:T(8,128)(2,1)S(1)}) custom-call(bf16[1024,512]{1,0:T(8,128)(2,1)} %up.3, bf16[1024,512]{1,0:T(8,128)(2,1)} %down.3), custom_call_target="tpu_custom_call" | custom-call | flops 1 | bytes 1 | tf_op jit(solution)/shard_map/pack/pallas_call | solution.py:174
  9.8 12.8 %attend.1.refs_0_.normed = bf16[512,1024]{1,0:T(8,128)(2,1)S(1)} custom-call(s32[4]{0:T(128)S(1)} %copy-done.3, bf16[512,1024]{1,0:T(8,128)(2,1)} %tok_hbm.1, bf16[1024,3072]{1,0:T(8,128)(2,1)} %qkv.1, bf16[1024,1024]{1,0:T(8,128)(2,1)} %wo_hbm.1, f32[1,1024]{1,0:T(1,128)S(1)} %bitcast.26), custom_call_target="tpu_custom_call" | custom-call | flops 1 | bytes 1 | tf_op jit(solution)/shard_map/attend/pallas_call | solution.py:249
  22.7 1.6 %collective-permute-start.3 = (bf16[512,1024]{1,0:T(8,128)(2,1)S(1)}, bf16[512,1024]{1,0:T(8,128)(2,1)S(1)}, u32[]{:S(2)}, u32[]{:S(2)}) collective-permute-start(bf16[512,1024]{1,0:T(8,128)(2,1)S(1)} %attend.1.refs_0_.normed), channel_id=1, source_target_pairs={{0,1},{1,0},{2,3},{3,2},{4,5},{5,4},{6,7},{7,6},{8,9},{9,8},{10,11... | collective-permute-start | bytes 3145736 | tf_op jit(solution)/shard_map/ppermute | solution.py:90
  24.3 1.6 %collective-permute-start.4 = (bf16[4160,128]{1,0:T(8,128)(2,1)S(1)}, bf16[4160,128]{1,0:T(8,128)(2,1)S(1)}, u32[]{:S(2)}, u32[]{:S(2)}) collective-permute-start(bf16[4160,128]{1,0:T(8,128)(2,1)S(1)} %join1.1.refs_0_), channel_id=1, source_target_pairs={{0,8},{1,33},{2,10},{3,35},{4,12},{5,37},{6,14},{7,39},{8,16},{9,4... | collective-permute-start | bytes 3194888 | tf_op jit(solution)/shard_map/ppermute | solution.py:90
  25.9 3.3 %collective-permute-start.6 = (bf16[4160,128]{1,0:T(8,128)(2,1)S(1)}, bf16[4160,128]{1,0:T(8,128)(2,1)S(1)}, u32[]{:S(2)}, u32[]{:S(2)}) collective-permute-start(bf16[4160,128]{1,0:T(8,128)(2,1)S(1)} %join1.1.refs_0_), channel_id=1, source_target_pairs={{0,16},{1,65},{2,18},{3,67},{4,20},{5,69},{6,22},{7,71},{8,24},{9,... | collective-permute-start | bytes 3194888 | tf_op jit(solution)/shard_map/ppermute | solution.py:90
  30.0 1.1 %collective-permute-done.7 = s32[4,8]{1,0:T(4,128)S(1)} collective-permute-done((s32[4,8]{1,0:T(4,128)S(1)}, s32[4,8]{1,0:T(4,128)S(1)}, u32[]{:S(2)}, u32[]{:S(2)}) %collective-permute-start.7) | collective-permute-done | bytes 160 | tf_op jit(solution)/shard_map/ppermute | solution.py:90
  31.1 2.0 %collective-permute-start.9 = (bf16[4096,128]{1,0:T(8,128)(2,1)S(1)}, bf16[4096,128]{1,0:T(8,128)(2,1)S(1)}, u32[]{:S(2)}, u32[]{:S(2)}) collective-permute-start(bf16[4096,128]{1,0:T(8,128)(2,1)S(1)} %bitcast.20), channel_id=1, source_target_pairs={{0,6},{1,7},{2,0},{3,1},{4,2},{5,3},{6,4},{7,5},{8,14},{9,15},{10,... | collective-permute-start | bytes 3145736 | tf_op jit(solution)/shard_map/ppermute | solution.py:90
  33.1 2.4 %ffn1.1 = (f32[512,1024]{1,0:T(8,128)S(1)}, f32[512,1024]{1,0:T(8,128)S(1)}) custom-call(bf16[512,1024]{1,0:T(8,128)(2,1)S(1)} %attend.1.refs_0_.normed, bf16[512,1024]{1,0:T(8,128)(2,1)S(1)} %collective-permute-done.3.refs_1_.refs_0_, bf16[4096,128]{1,0:T(8,128)(2,1)S(1)} %bitcast.22, bf16[4096,128]{1,0:T(8,128)(2,1)S(1)} %bitcast.23), custom_call_target="tpu_custom_call" | custom-call | flops 1 | bytes 1 | tf_op jit(solution)/shard_map/ffn1/pallas_call | solution.py:304
  35.6 5.1 %collective-permute-done.4.refs_7_.refs_1_ = bf16[4160,128]{1,0:T(8,128)(2,1)S(1)} collective-permute-done((bf16[4160,128]{1,0:T(8,128)(2,1)S(1)}, bf16[4160,128]{1,0:T(8,128)(2,1)S(1)}, u32[]{:S(2)}, u32[]{:S(2)}) %collective-permute-start.4) | collective-permute-done | bytes 1064992 | tf_op jit(solution)/shard_map/ppermute | solution.py:90
  40.7 3.0 %ffn2.1 = (f32[512,1024]{1,0:T(8,128)S(1)}, f32[512,1024]{1,0:T(8,128)S(1)}) custom-call(bf16[512,1024]{1,0:T(8,128)(2,1)S(1)} %attend.1.refs_0_.normed, bf16[512,1024]{1,0:T(8,128)(2,1)S(1)} %collective-permute-done.3.refs_1_.refs_0_, f32[512,1024]{1,0:T(8,128)S(1)} %get-tuple-element.39.refs_2_, ...), custom_call_target="tpu_custom_call", output_to_operand_aliasing={{0}: (2, {}), {1}: (3, {})} | custom-call | flops 1 | bytes 1 | tf_op jit(solution)/shard_map/ffn2/pallas_call | solution.py:304
  43.8 9.2 %collective-permute-done.6.refs_5_.refs_3_ = bf16[4160,128]{1,0:T(8,128)(2,1)S(1)} collective-permute-done((bf16[4160,128]{1,0:T(8,128)(2,1)S(1)}, bf16[4160,128]{1,0:T(8,128)(2,1)S(1)}, u32[]{:S(2)}, u32[]{:S(2)}) %collective-permute-start.6) | collective-permute-done | bytes 1064992 | tf_op jit(solution)/shard_map/ppermute | solution.py:90
  53.0 2.7 %collective-permute-done.9.refs_7_.refs_0_ = bf16[4096,128]{1,0:T(8,128)(2,1)S(1)} collective-permute-done((bf16[4096,128]{1,0:T(8,128)(2,1)S(1)}, bf16[4096,128]{1,0:T(8,128)(2,1)S(1)}, u32[]{:S(2)}, u32[]{:S(2)}) %collective-permute-start.9) | collective-permute-done | bytes 1048608 | tf_op jit(solution)/shard_map/ppermute | solution.py:90
  55.7 2.9 %collective-permute-done.8.refs_6_.refs_0_ = bf16[4096,128]{1,0:T(8,128)(2,1)S(1)} collective-permute-done((bf16[4096,128]{1,0:T(8,128)(2,1)S(1)}, bf16[4096,128]{1,0:T(8,128)(2,1)S(1)}, u32[]{:S(2)}, u32[]{:S(2)}) %collective-permute-start.8) | collective-permute-done | bytes 1048608 | tf_op jit(solution)/shard_map/ppermute | solution.py:90
  58.7 2.6 %collective-permute-start.13 = (bf16[4352,128]{1,0:T(8,128)(2,1)S(1)}, bf16[4352,128]{1,0:T(8,128)(2,1)S(1)}, u32[]{:S(2)}, u32[]{:S(2)}) collective-permute-start(bf16[4352,128]{1,0:T(8,128)(2,1)S(1)} %join2.1), channel_id=1, source_target_pairs={{0,96},{1,25},{2,98},{3,27},{4,100},{5,29},{6,102},{7,31},{8,104},... | collective-permute-start | bytes 3342344 | tf_op jit(solution)/shard_map/ppermute | solution.py:90
  61.4 2.7 %collective-permute-start.11 = (bf16[2048,128]{1,0:T(8,128)(2,1)S(1)}, bf16[2048,128]{1,0:T(8,128)(2,1)S(1)}, u32[]{:S(2)}, u32[]{:S(2)}) collective-permute-start(bf16[2048,128]{1,0:T(8,128)(2,1)S(1)} %join6.1), channel_id=1, source_target_pairs={{0,6},{1,7},{2,0},{3,1},{4,2},{5,3},{6,4},{7,5},{8,14},{9,15},{10,... | collective-permute-start | bytes 1572872 | tf_op jit(solution)/shard_map/ppermute | solution.py:90
  64.1 4.7 %ffn3.1 = (f32[512,1024]{1,0:T(8,128)S(1)}, f32[512,1024]{1,0:T(8,128)S(1)}) custom-call(bf16[512,1024]{1,0:T(8,128)(2,1)S(1)} %attend.1.refs_0_.normed, bf16[512,1024]{1,0:T(8,128)(2,1)S(1)} %collective-permute-done.3.refs_1_.refs_0_, f32[512,1024]{1,0:T(8,128)S(1)} %get-tuple-element.43.refs_2_, ...), custom_call_target="tpu_custom_call", output_to_operand_aliasing={{0}: (2, {}), {1}: (3, {})} | custom-call | flops 1 | bytes 1 | tf_op jit(solution)/shard_map/ffn3/pallas_call | solution.py:304
  68.8 4.6 %collective-permute-done.10.refs_2_ = bf16[2048,128]{1,0:T(8,128)(2,1)S(1)} collective-permute-done((bf16[2048,128]{1,0:T(8,128)(2,1)S(1)}, bf16[2048,128]{1,0:T(8,128)(2,1)S(1)}, u32[]{:S(2)}, u32[]{:S(2)}) %collective-permute-start.10) | collective-permute-done | bytes 524320 | tf_op jit(solution)/shard_map/ppermute | solution.py:90
  73.7 3.4 %collective-permute-done.12.refs_0_ = bf16[4352,128]{1,0:T(8,128)(2,1)S(1)} collective-permute-done((bf16[4352,128]{1,0:T(8,128)(2,1)S(1)}, bf16[4352,128]{1,0:T(8,128)(2,1)S(1)}, u32[]{:S(2)}, u32[]{:S(2)}) %collective-permute-start.12) | collective-permute-done | bytes 1114144 | tf_op jit(solution)/shard_map/ppermute | solution.py:90
  77.1 1.3 %ffn4.1 = f32[512,1024]{1,0:T(8,128)S(1)} custom-call(bf16[512,1024]{1,0:T(8,128)(2,1)S(1)} %collective-permute-done.3.refs_1_.refs_0_, f32[512,1024]{1,0:T(8,128)S(1)} %get-tuple-element.53.refs_1_, bf16[2048,128]{1,0:T(8,128)(2,1)S(1)} %collective-permute-done.10.refs_2_, ...), custom_call_target="tpu_custom_call", output_to_operand_aliasing={{}: (1, {})} | custom-call | flops 1 | bytes 1 | tf_op jit(solution)/shard_map/ffn4/pallas_call | solution.py:304
  78.4 3.5 %collective-permute-start.14 = (f32[512,1024]{1,0:T(8,128)S(1)}, f32[512,1024]{1,0:T(8,128)S(1)}, u32[]{:S(2)}, u32[]{:S(2)}) collective-permute-start(f32[512,1024]{1,0:T(8,128)S(1)} %ffn4.1), channel_id=1, source_target_pairs={{0,1},{1,0},{2,3},{3,2},{4,5},{5,4},{6,7},{7,6},{8,9},{9,8},{10,11... | collective-permute-start | bytes 6291464 | tf_op jit(solution)/shard_map/ppermute | solution.py:90
  81.9 0.8 join4.1
  82.8 0.8 join3.1
  83.6 1.5 %collective-permute-start.16 = (bf16[2176,128]{1,0:T(8,128)(2,1)}, bf16[2176,128]{1,0:T(8,128)(2,1)}, u32[]{:S(2)}, u32[]{:S(2)}) collective-permute-start(bf16[2176,128]{1,0:T(8,128)(2,1)} %join3.1), channel_id=1, source_target_pairs={{0,32},{1,9},{2,34},{3,11},{4,36},{5,13},{6,38},{7,15},{8,40},{9,1... | collective-permute-start | bytes 1671176 | tf_op jit(solution)/shard_map/ppermute | solution.py:90
  85.1 1.3 %ffn5.1.mine = f32[512,1024]{1,0:T(8,128)S(1)} custom-call(bf16[512,1024]{1,0:T(8,128)(2,1)S(1)} %attend.1.refs_0_.normed, f32[512,1024]{1,0:T(8,128)S(1)} %get-tuple-element.49.refs_1_, bf16[2048,128]{1,0:T(8,128)(2,1)S(1)} %collective-permute-done.10.refs_2_, bf16[2048,128]{1,0:T(8,128)(2,1)S(1)} %collective-permute-done.11.refs_3_), custom_call_target="tpu_custom_call", output_to_operand_aliasing={{}: (1, {})} | custom-call | flops 1 | bytes 1 | tf_op jit(solution)/shard_map/ffn5/pallas_call | solution.py:304
  86.4 2.3 %embed.1 = (bf16[512,128]{1,0:T(8,128)(2,1)}, bf16[512,128]{1,0:T(8,128)(2,1)S(1)}) custom-call(s32[4]{0:T(128)S(1)} %copy-done.3, bf16[512,1024]{1,0:T(8,128)(2,1)S(1)} %attend.1.refs_0_.normed, f32[512,1024]{1,0:T(8,128)S(1)} %ffn5.1.mine, f32[512,1024]{1,0:T(8,128)S(1)} %collective-permute-done.14.other, f32[1,1024]{1,0:T(1,128)S(1)} %bitcast.27, ...), custom_call_target="tpu_custom_call" | custom-call | flops 1 | bytes 1 | tf_op jit(solution)/shard_map/embed/pallas_call | solution.py:331
  89.5 2.3 %collective-permute-done.17 = bf16[2176,128]{1,0:T(8,128)(2,1)} collective-permute-done((bf16[2176,128]{1,0:T(8,128)(2,1)}, bf16[2176,128]{1,0:T(8,128)(2,1)}, u32[]{:S(2)}, u32[]{:S(2)}) %collective-permute-start.17) | collective-permute-done | bytes 557088 | tf_op jit(solution)/shard_map/ppermute | solution.py:90
  91.8 2.1 %collective-permute-done.16 = bf16[2176,128]{1,0:T(8,128)(2,1)} collective-permute-done((bf16[2176,128]{1,0:T(8,128)(2,1)}, bf16[2176,128]{1,0:T(8,128)(2,1)}, u32[]{:S(2)}, u32[]{:S(2)}) %collective-permute-start.16) | collective-permute-done | bytes 557088 | tf_op jit(solution)/shard_map/ppermute | solution.py:90
  93.8 4.2 %score.1 = (f32[32,128]{1,0:T(8,128)S(1)}, f32[32,128]{1,0:T(8,128)S(1)}) custom-call(s32[5]{0:T(128)S(1)} %stack.23.where, s32[32]{0:T(128)S(1)} %reshape.51.cand, s32[32]{0:T(128)S(1)} %reshape.52.pair, bf16[512,128]{1,0:T(8,128)(2,1)S(1)} %get-tuple-element.55.emb, bf16[512,128]{1,0:T(8,128)(2,1)} %collective-permute-done.15.sib, ...), custom_call_target="tpu_custom_call" | custom-call | flops 1 | bytes 1 | tf_op jit(solution)/shard_map/score/pallas_call | solution.py:400
  98.1 1.0 collective-permute-start.18
  99.0 0.8 collective-permute-done.18
  (36 shorter events, 4.4 us)
Async XLA Ops:
  0.8 9.0 %copy-start.1 = (f32[1024]{0:T(1024)S(1)}, f32[1024]{0:T(1024)}, u32[]{:S(2)}) copy-start(f32[1024]{0:T(1024)} %param.15) | copy-start | bytes 12292
  0.8 9.0 %copy-start.3 = (s32[4]{0:T(128)S(1)}, s32[4]{0:T(128)}, u32[]{:S(2)}) copy-start(s32[4]{0:T(128)} %length.3) | copy-start | bytes 52
  2.6 20.0 %collective-permute-start.2 = (bf16[1296,128]{1,0:T(8,128)(2,1)S(1)}, bf16[1296,128]{1,0:T(8,128)(2,1)S(1)}, u32[]{:S(2)}, u32[]{:S(2)}) collective-permute-start(bf16[1296,128]{1,0:T(8,128)(2,1)S(1)} %first.1.refs_3_), channel_id=1, source_target_pairs={{0,4},{1,5},{2,6},{3,7},{4,0},{5,1},{6,2},{7,3},{8,12},{9,13},{10,... | collective-permute-start | bytes 995336 | tf_op jit(solution)/shard_map/ppermute | solution.py:90
  6.4 16.2 %collective-permute-start.1 = (bf16[1296,128]{1,0:T(8,128)(2,1)S(1)}, bf16[1296,128]{1,0:T(8,128)(2,1)S(1)}, u32[]{:S(2)}, u32[]{:S(2)}) collective-permute-start(bf16[1296,128]{1,0:T(8,128)(2,1)S(1)} %first.1.refs_3_), channel_id=1, source_target_pairs={{0,6},{1,7},{2,0},{3,1},{4,2},{5,3},{6,4},{7,5},{8,14},{9,15},{10,... | collective-permute-start | bytes 995336 | tf_op jit(solution)/shard_map/ppermute | solution.py:90
  7.2 15.4 %collective-permute-start = (bf16[1296,128]{1,0:T(8,128)(2,1)S(1)}, bf16[1296,128]{1,0:T(8,128)(2,1)S(1)}, u32[]{:S(2)}, u32[]{:S(2)}) collective-permute-start(bf16[1296,128]{1,0:T(8,128)(2,1)S(1)} %first.1.refs_3_), channel_id=1, source_target_pairs={{0,2},{1,3},{2,4},{3,5},{4,6},{5,7},{6,0},{7,1},{8,10},{9,11},{10,... | collective-permute-start | bytes 995336 | tf_op jit(solution)/shard_map/ppermute | solution.py:90
  22.6 7.4 %copy-start.4 = (s32[4,8]{1,0:T(4,128)S(1)}, s32[4,8]{1,0:T(4,128)}, u32[]{:S(2)}) copy-start(s32[4,8]{1,0:T(4,128)} %param.23) | copy-start | bytes 388
  22.7 8.4 %collective-permute-start.3 = (bf16[512,1024]{1,0:T(8,128)(2,1)S(1)}, bf16[512,1024]{1,0:T(8,128)(2,1)S(1)}, u32[]{:S(2)}, u32[]{:S(2)}) collective-permute-start(bf16[512,1024]{1,0:T(8,128)(2,1)S(1)} %attend.1.refs_0_.normed), channel_id=1, source_target_pairs={{0,1},{1,0},{2,3},{3,2},{4,5},{5,4},{6,7},{7,6},{8,9},{9,8},{10,11... | collective-permute-start | bytes 3145736 | tf_op jit(solution)/shard_map/ppermute | solution.py:90
  24.3 16.4 %collective-permute-start.4 = (bf16[4160,128]{1,0:T(8,128)(2,1)S(1)}, bf16[4160,128]{1,0:T(8,128)(2,1)S(1)}, u32[]{:S(2)}, u32[]{:S(2)}) collective-permute-start(bf16[4160,128]{1,0:T(8,128)(2,1)S(1)} %join1.1.refs_0_), channel_id=1, source_target_pairs={{0,8},{1,33},{2,10},{3,35},{4,12},{5,37},{6,14},{7,39},{8,16},{9,4... | collective-permute-start | bytes 3194888 | tf_op jit(solution)/shard_map/ppermute | solution.py:90
  25.9 27.1 %collective-permute-start.6 = (bf16[4160,128]{1,0:T(8,128)(2,1)S(1)}, bf16[4160,128]{1,0:T(8,128)(2,1)S(1)}, u32[]{:S(2)}, u32[]{:S(2)}) collective-permute-start(bf16[4160,128]{1,0:T(8,128)(2,1)S(1)} %join1.1.refs_0_), channel_id=1, source_target_pairs={{0,16},{1,65},{2,18},{3,67},{4,20},{5,69},{6,22},{7,71},{8,24},{9,... | collective-permute-start | bytes 3194888 | tf_op jit(solution)/shard_map/ppermute | solution.py:90
  29.2 23.8 %collective-permute-start.5 = (bf16[4160,128]{1,0:T(8,128)(2,1)S(1)}, bf16[4160,128]{1,0:T(8,128)(2,1)S(1)}, u32[]{:S(2)}, u32[]{:S(2)}) collective-permute-start(bf16[4160,128]{1,0:T(8,128)(2,1)S(1)} %join1.1.refs_0_), channel_id=1, source_target_pairs={{0,24},{1,97},{2,26},{3,99},{4,28},{5,101},{6,30},{7,103},{8,0},{9... | collective-permute-start | bytes 3194888 | tf_op jit(solution)/shard_map/ppermute | solution.py:90
  30.0 1.2 %collective-permute-start.7 = (s32[4,8]{1,0:T(4,128)S(1)}, s32[4,8]{1,0:T(4,128)S(1)}, u32[]{:S(2)}, u32[]{:S(2)}) collective-permute-start(s32[4,8]{1,0:T(4,128)S(1)} %copy-done.4), channel_id=1, source_target_pairs={{0,1},{1,0},{2,3},{3,2},{4,5},{5,4},{6,7},{7,6},{8,9},{9,8},{10,11... | collective-permute-start | bytes 392 | tf_op jit(solution)/shard_map/ppermute | solution.py:90
  31.1 24.6 %collective-permute-start.9 = (bf16[4096,128]{1,0:T(8,128)(2,1)S(1)}, bf16[4096,128]{1,0:T(8,128)(2,1)S(1)}, u32[]{:S(2)}, u32[]{:S(2)}) collective-permute-start(bf16[4096,128]{1,0:T(8,128)(2,1)S(1)} %bitcast.20), channel_id=1, source_target_pairs={{0,6},{1,7},{2,0},{3,1},{4,2},{5,3},{6,4},{7,5},{8,14},{9,15},{10,... | collective-permute-start | bytes 3145736 | tf_op jit(solution)/shard_map/ppermute | solution.py:90
  33.1 25.5 %collective-permute-start.8 = (bf16[4096,128]{1,0:T(8,128)(2,1)S(1)}, bf16[4096,128]{1,0:T(8,128)(2,1)S(1)}, u32[]{:S(2)}, u32[]{:S(2)}) collective-permute-start(bf16[4096,128]{1,0:T(8,128)(2,1)S(1)} %bitcast.21), channel_id=1, source_target_pairs={{0,2},{1,3},{2,4},{3,5},{4,6},{5,7},{6,0},{7,1},{8,10},{9,11},{10,... | collective-permute-start | bytes 3145736 | tf_op jit(solution)/shard_map/ppermute | solution.py:90
  58.7 15.0 %collective-permute-start.13 = (bf16[4352,128]{1,0:T(8,128)(2,1)S(1)}, bf16[4352,128]{1,0:T(8,128)(2,1)S(1)}, u32[]{:S(2)}, u32[]{:S(2)}) collective-permute-start(bf16[4352,128]{1,0:T(8,128)(2,1)S(1)} %join2.1), channel_id=1, source_target_pairs={{0,96},{1,25},{2,98},{3,27},{4,100},{5,29},{6,102},{7,31},{8,104},... | collective-permute-start | bytes 3342344 | tf_op jit(solution)/shard_map/ppermute | solution.py:90
  61.2 15.9 %collective-permute-start.12 = (bf16[4352,128]{1,0:T(8,128)(2,1)S(1)}, bf16[4352,128]{1,0:T(8,128)(2,1)S(1)}, u32[]{:S(2)}, u32[]{:S(2)}) collective-permute-start(bf16[4352,128]{1,0:T(8,128)(2,1)S(1)} %join2.1), channel_id=1, source_target_pairs={{0,32},{1,9},{2,34},{3,11},{4,36},{5,13},{6,38},{7,15},{8,40},{9,1... | collective-permute-start | bytes 3342344 | tf_op jit(solution)/shard_map/ppermute | solution.py:90
  61.3 12.1 %collective-permute-start.10 = (bf16[2048,128]{1,0:T(8,128)(2,1)S(1)}, bf16[2048,128]{1,0:T(8,128)(2,1)S(1)}, u32[]{:S(2)}, u32[]{:S(2)}) collective-permute-start(bf16[2048,128]{1,0:T(8,128)(2,1)S(1)} %join5.1), channel_id=1, source_target_pairs={{0,2},{1,3},{2,4},{3,5},{4,6},{5,7},{6,0},{7,1},{8,10},{9,11},{10,... | collective-permute-start | bytes 1572872 | tf_op jit(solution)/shard_map/ppermute | solution.py:90
  61.4 12.0 %collective-permute-start.11 = (bf16[2048,128]{1,0:T(8,128)(2,1)S(1)}, bf16[2048,128]{1,0:T(8,128)(2,1)S(1)}, u32[]{:S(2)}, u32[]{:S(2)}) collective-permute-start(bf16[2048,128]{1,0:T(8,128)(2,1)S(1)} %join6.1), channel_id=1, source_target_pairs={{0,6},{1,7},{2,0},{3,1},{4,2},{5,3},{6,4},{7,5},{8,14},{9,15},{10,... | collective-permute-start | bytes 1572872 | tf_op jit(solution)/shard_map/ppermute | solution.py:90
  78.4 8.0 %collective-permute-start.14 = (f32[512,1024]{1,0:T(8,128)S(1)}, f32[512,1024]{1,0:T(8,128)S(1)}, u32[]{:S(2)}, u32[]{:S(2)}) collective-permute-start(f32[512,1024]{1,0:T(8,128)S(1)} %ffn4.1), channel_id=1, source_target_pairs={{0,1},{1,0},{2,3},{3,2},{4,5},{5,4},{6,7},{7,6},{8,9},{9,8},{10,11... | collective-permute-start | bytes 6291464 | tf_op jit(solution)/shard_map/ppermute | solution.py:90
  82.8 9.0 %collective-permute-start.17 = (bf16[2176,128]{1,0:T(8,128)(2,1)}, bf16[2176,128]{1,0:T(8,128)(2,1)}, u32[]{:S(2)}, u32[]{:S(2)}) collective-permute-start(bf16[2176,128]{1,0:T(8,128)(2,1)} %join4.1), channel_id=1, source_target_pairs={{0,96},{1,25},{2,98},{3,27},{4,100},{5,29},{6,102},{7,31},{8,104},... | collective-permute-start | bytes 1671176 | tf_op jit(solution)/shard_map/ppermute | solution.py:90
  83.6 10.2 %collective-permute-start.16 = (bf16[2176,128]{1,0:T(8,128)(2,1)}, bf16[2176,128]{1,0:T(8,128)(2,1)}, u32[]{:S(2)}, u32[]{:S(2)}) collective-permute-start(bf16[2176,128]{1,0:T(8,128)(2,1)} %join3.1), channel_id=1, source_target_pairs={{0,32},{1,9},{2,34},{3,11},{4,36},{5,13},{6,38},{7,15},{8,40},{9,1... | collective-permute-start | bytes 1671176 | tf_op jit(solution)/shard_map/ppermute | solution.py:90
  85.1 1.3 %copy-start = (bf16[1024,128]{1,0:T(8,128)(2,1)S(1)}, bf16[1024,128]{1,0:T(8,128)(2,1)}, u32[]{:S(2)}) copy-start(bf16[1024,128]{1,0:T(8,128)(2,1)} %we.1) | copy-start | bytes 786436
  85.1 1.3 %copy-start.2 = (f32[1024]{0:T(1024)S(1)}, f32[1024]{0:T(1024)}, u32[]{:S(2)}) copy-start(f32[1024]{0:T(1024)} %param.18) | copy-start | bytes 12292
  88.8 5.1 %collective-permute-start.15 = (bf16[512,128]{1,0:T(8,128)(2,1)S(1)}, bf16[512,128]{1,0:T(8,128)(2,1)}, u32[]{:S(2)}, u32[]{:S(2)}) collective-permute-start(bf16[512,128]{1,0:T(8,128)(2,1)S(1)} %get-tuple-element.55.emb), channel_id=1, source_target_pairs={{0,1},{1,0},{2,3},{3,2},{4,5},{5,4},{6,7},{7,6},{8,9},{9,8},{10,11... | collective-permute-start | bytes 393224 | tf_op jit(solution)/shard_map/ppermute | solution.py:90
  98.1 1.8 %collective-permute-start.18 = (f32[32,128]{1,0:T(8,128)S(1)}, f32[32,128]{1,0:T(8,128)S(1)}, u32[]{:S(2)}, u32[]{:S(2)}) collective-permute-start(f32[32,128]{1,0:T(8,128)S(1)} %get-tuple-element.57), channel_id=1, source_target_pairs={{0,1},{1,0},{2,3},{3,2},{4,5},{5,4},{6,7},{7,6},{8,9},{9,8},{10,11... | collective-permute-start | bytes 49160 | tf_op jit(solution)/shard_map/ppermute | solution.py:90

commit v5 on v4

--- a/solution.py
+++ b/solution.py
@@ -146,7 +146,7 @@
             pltpu.SMEM((8,), jnp.int32),
             pltpu.SemaphoreType.DMA((4,)),
         ],
-        compiler_params=params(16),
+        compiler_params=params(8),
         cost_estimate=LIGHT,
         name="first",
     )(where, *pinned(up, down, docs, lengths))
@@ -177,7 +177,7 @@
         in_specs=hbm(2),
         out_specs=tuple(vmem(2)),
         scratch_shapes=[pltpu.VMEM((2, D, 512), bf16), pltpu.SemaphoreType.DMA((4,))],
-        compiler_params=params(16),
+        compiler_params=params(8),
         cost_estimate=LIGHT,
         name="pack",
     )(*pinned(up, down))
@@ -211,12 +211,14 @@
         columns = slice(i * step, (i + 1) * step)
         copies.append(pltpu.make_async_copy(qkv.at[:, columns], held.at[:, columns], sems.at[i]))
     copies.append(pltpu.make_async_copy(wo_hbm, wo, sems.at[7]))
-    for copy in copies:
+    for copy in copies[:3]:
         copy.start()
     copies[0].wait()
     for i in range(6):
         columns = slice(i * step, (i + 1) * step)
         copies[1 + i].wait()
+        if i < 5:
+            copies[3 + i].start()
         packed[:, columns] = dot(tok[...], held[:, columns]).astype(bf16)
     lane = lax.broadcasted_iota(jnp.int32, (2 * SEQ, LANES), 1)
     low = lax.broadcasted_iota(jnp.int32, (SEQ, LANES), 1) < HD
@@ -259,7 +261,7 @@
             pltpu.VMEM((D, D), bf16),
             pltpu.SemaphoreType.DMA((8,)),
         ],
-        compiler_params=params(32),
+        compiler_params=params(24),
         cost_estimate=LIGHT,
         name="attend",
     )(length, *pinned(tokens, qkv, wo), gain.reshape(1, D))
@@ -308,7 +310,7 @@
         out_specs=tuple(vmem(sets)),
         input_output_aliases={sets + t: t for t in range(len(olds))},
         scratch_shapes=[pltpu.VMEM((sets, rows, total), bf16)],
-        compiler_params=params(20),
+        compiler_params=params(16),
         cost_estimate=LIGHT,
         name=name,
     )(*tail)
@@ -333,7 +335,7 @@
         out_shape=(shape, shape),
         in_specs=[SMEM] + vmem(5),
         out_specs=tuple(vmem(2)),
-        compiler_params=params(24),
+        compiler_params=params(12),
         cost_estimate=LIGHT,
         name="embed",
     )(length, normed, mine, other, gain.reshape(1, D), we)
@@ -406,7 +408,7 @@
             pltpu.VMEM((4, 4, 4, DOC_ROWS, P_SIZE), bf16),
             pltpu.SemaphoreType.DMA((5,)),
         ],
-        compiler_params=params(16),
+        compiler_params=params(8),
         cost_estimate=LIGHT,
         name="score",
     )(where, cand.reshape(-1), pair.reshape(-1), emb, sib, *docs)
@@ -433,36 +435,35 @@
     near = [send(start, way) for way in ("y+", "y-", "y2")]
     low, high = pack(up_weight, down_weight)
     normed = attend(tokens, attend_weight, output_weight, after(attend_gain, start), query_length)
-    near = after(tuple(near), normed, high)
+    pair = send(after(candidates, start), "c")
+    near, pair = after((tuple(near), pair), normed, high)
 
     whole = [(k, 0, BLOCK) for k in range(3)] + [(3, PART, DOC_ROWS)]
     go = join([*near, start], whole, "join1")
     came = [send(go, way) for way in ("f+", "f-", "f2")]
     pair_normed = send(after(normed, go), "c")
-    pair = send(after(candidates, go), "c")
-    low_go = after(low, pair_normed, pair)
+    low_go = after(low, pair_normed)
     low_near = [send(low_go, "y+"), send(low_go, "y-")]
     sets = (normed, pair_normed)
     total = ffn(sets, (), [low, high], [(0, 0, 256), (1, 0, 256)], "ffn1")
     parts = [(i * BLOCK, SLICE) for i in range(3)]
     pieces = [(k, 0, SLICE) for k in range(3)] + [(3,) + p for p in parts]
     total = ffn(sets, total, [*near, came[0]], pieces, "ffn2")
-    came, low_near, total = after((came, low_near, total), *total)
+    came, total = after((came, total), *total)
     takes = [(k, at, DOC_ROWS) for k in range(4) for at in [i * BLOCK + PART for i in range(3)] + [3 * BLOCK]]
     docs = join([go, *came], takes, "join2")
     last = [send(docs, way) for way in ("g+", "g-")]
     mid = 128
+    low_near = after(tuple(low_near), docs)
     ahead = join([low_near[0]], [(0, k * 256, mid) for k in range(SLABS)], "join5")
     behind = join([low_near[1]], [(0, k * 256 + mid, mid) for k in range(SLABS)], "join6")
     low_far = [send(ahead, "y+"), send(behind, "y-")]
     pieces = [(k,) + p for k in range(2) for p in parts] + [(2, 0, 256), (3, 0, 256)]
     total = ffn(sets, total, [*came[1:], *low_near], pieces, "ffn3")
     cut = docs.shape[0] // 2
-    last += [
-        send(join([last[0]], [(0, 0, cut)], "join3"), "g+"),
-        send(join([last[1]], [(0, cut, cut)], "join4"), "g-"),
-    ]
-    low_far = after(low_far, *last[:2])
+    halves = [join([last[0]], [(0, 0, cut)], "join3"), join([last[1]], [(0, cut, cut)], "join4")]
+    last += [send(halves[0], "g+"), send(halves[1], "g-")]
+    low_far = after(tuple(low_far), *halves)
     rest = [(0, 0, mid), (1, 0, mid)]
     away, = ffn(sets[1:], total[1:], low_far, rest, "ffn4")
     other = send(away, "c")

time: 101 us -> 91.4 us (0.905)
  waiting for transfers between devices: 34.5 us -> 25 us
    ppermute x19, waiting for transfers between devices: 34.5 us -> 25 us  [send(): return lax.ppermute(value, ('req', 'mlp'), STEPS[way])]
  transfers between devices with their start and end apart: 19 -> 19, of which waited for: 11 -> 6; matrix products, arithmetic and copies ran while one was open for 0% -> 0% of each run, Pallas kernels for 30% -> 33%
where the time goes in v5:
time: 91.4 us; the launch traced here: 91.2 us
  Pallas kernels  38.4 us (42%)
  starting transfers between devices  26.7 us (29%)
  waiting for transfers between devices  25 us (27%)
    ppermute x19, starting transfers between devices, send(): return lax.ppermute(value, ('req', 'mlp'), STEPS[way])  26.7 us
    ppermute x19, waiting for transfers between devices, send(): return lax.ppermute(value, ('req', 'mlp'), STEPS[way])  25 us
    pallas_call x1, Pallas kernels, attend(): pl.pallas_call(attend_body, out_shape=jax.ShapeDtypeStruct((rows, D), bf1...  12.8 us
    pallas_call x5, Pallas kernels, ffn(): pl.pallas_call(functools.partial(ffn_body, tuple(pieces), len(arrays), se...  12.8 us
    pallas_call x1, Pallas kernels, score(): pl.pallas_call(score_body, out_shape=(jax.ShapeDtypeStruct((total, SEQ),...  4.24 us
    pallas_call x1, Pallas kernels, embed(): pl.pallas_call(embed_body, out_shape=(shape, shape), in_specs=[SMEM] + vm...  2.35 us
    pallas_call x6, Pallas kernels, join(): pl.pallas_call(functools.partial(join_body, takes), out_shape=jax.ShapeDt...  1.92 us
    pallas_call x1, Pallas kernels, first(): pl.pallas_call(first_body, out_shape=jax.ShapeDtypeStruct((BLOCK, LANES),...  1.84 us
  transfers between devices with their start and end apart: 19, of which 6 were waited for; matrix products, arithmetic and copies ran while one was open for 0% of the time, Pallas kernels for 33%

profile of v5, /device:TPU:1, one launch (start us, length us, event | category | flops | bytes accessed | tf_op | source)
XLA Modules:
  0.0 91.2 jit_solution(10583210955325796173)
XLA Ops:
  0.8 1.8 %first.1.refs_3_ = bf16[1296,128]{1,0:T(8,128)(2,1)S(1)} custom-call(s32[5]{0:T(128)S(1)} %stack.23.where, bf16[1024,512]{1,0:T(8,128)(2,1)} %up.3, bf16[1024,512]{1,0:T(8,128)(2,1)} %down.3, bf16[256,128]{1,0:T(8,128)(2,1)} %bitcast.28, s32[8]{0:T(128)} %lengths.1), custom_call_target="tpu_custom_call" | custom-call | flops 1 | bytes 1 | tf_op jit(solution)/shard_map/first/pallas_call | solution.py:138
  2.6 2.2 %collective-permute-start = (bf16[1296,128]{1,0:T(8,128)(2,1)S(1)}, bf16[1296,128]{1,0:T(8,128)(2,1)S(1)}, u32[]{:S(2)}, u32[]{:S(2)}) collective-permute-start(bf16[1296,128]{1,0:T(8,128)(2,1)S(1)} %first.1.refs_3_), channel_id=1, source_target_pairs={{0,2},{1,3},{2,4},{3,5},{4,6},{5,7},{6,0},{7,1},{8,10},{9,11},{10,... | collective-permute-start | bytes 995336 | tf_op jit(solution)/shard_map/ppermute | solution.py:90
  4.8 1.5 %collective-permute-start.1 = (bf16[1296,128]{1,0:T(8,128)(2,1)S(1)}, bf16[1296,128]{1,0:T(8,128)(2,1)S(1)}, u32[]{:S(2)}, u32[]{:S(2)}) collective-permute-start(bf16[1296,128]{1,0:T(8,128)(2,1)S(1)} %first.1.refs_3_), channel_id=1, source_target_pairs={{0,6},{1,7},{2,0},{3,1},{4,2},{5,3},{6,4},{7,5},{8,14},{9,15},{10,... | collective-permute-start | bytes 995336 | tf_op jit(solution)/shard_map/ppermute | solution.py:90
  6.3 1.6 %collective-permute-start.2 = (bf16[1296,128]{1,0:T(8,128)(2,1)S(1)}, bf16[1296,128]{1,0:T(8,128)(2,1)S(1)}, u32[]{:S(2)}, u32[]{:S(2)}) collective-permute-start(bf16[1296,128]{1,0:T(8,128)(2,1)S(1)} %first.1.refs_3_), channel_id=1, source_target_pairs={{0,4},{1,5},{2,6},{3,7},{4,0},{5,1},{6,2},{7,3},{8,12},{9,13},{10,... | collective-permute-start | bytes 995336 | tf_op jit(solution)/shard_map/ppermute | solution.py:90
  7.9 1.5 %collective-permute-start.3 = (s32[4,8]{1,0:T(4,128)S(1)}, s32[4,8]{1,0:T(4,128)S(1)}, u32[]{:S(2)}, u32[]{:S(2)}) collective-permute-start(s32[4,8]{1,0:T(4,128)S(1)} %copy-done.4), channel_id=1, source_target_pairs={{0,1},{1,0},{2,3},{3,2},{4,5},{5,4},{6,7},{7,6},{8,9},{9,8},{10,11... | collective-permute-start | bytes 392 | tf_op jit(solution)/shard_map/ppermute | solution.py:90
  9.4 1.8 %pack.1 = (bf16[16,256,128]{2,1,0:T(8,128)(2,1)S(1)}, bf16[16,256,128]{2,1,0:T(8,128)(2,1)S(1)}) custom-call(bf16[1024,512]{1,0:T(8,128)(2,1)} %up.3, bf16[1024,512]{1,0:T(8,128)(2,1)} %down.3), custom_call_target="tpu_custom_call" | custom-call | flops 1 | bytes 1 | tf_op jit(solution)/shard_map/pack/pallas_call | solution.py:174
  11.3 12.8 %attend.1.refs_0_.normed = bf16[512,1024]{1,0:T(8,128)(2,1)S(1)} custom-call(s32[4]{0:T(128)S(1)} %copy-done.3, bf16[512,1024]{1,0:T(8,128)(2,1)} %tok_hbm.1, bf16[1024,3072]{1,0:T(8,128)(2,1)} %qkv.1, bf16[1024,1024]{1,0:T(8,128)(2,1)} %wo_hbm.1, f32[1,1024]{1,0:T(1,128)S(1)} %bitcast.26), custom_call_target="tpu_custom_call" | custom-call | flops 1 | bytes 1 | tf_op jit(solution)/shard_map/attend/pallas_call | solution.py:251
  24.3 1.7 %collective-permute-start.5 = (bf16[4160,128]{1,0:T(8,128)(2,1)S(1)}, bf16[4160,128]{1,0:T(8,128)(2,1)S(1)}, u32[]{:S(2)}, u32[]{:S(2)}) collective-permute-start(bf16[4160,128]{1,0:T(8,128)(2,1)S(1)} %join1.1.refs_0_), channel_id=1, source_target_pairs={{0,8},{1,33},{2,10},{3,35},{4,12},{5,37},{6,14},{7,39},{8,16},{9,4... | collective-permute-start | bytes 3194888 | tf_op jit(solution)/shard_map/ppermute | solution.py:90
  26.0 2.2 %collective-permute-start.6 = (bf16[4160,128]{1,0:T(8,128)(2,1)S(1)}, bf16[4160,128]{1,0:T(8,128)(2,1)S(1)}, u32[]{:S(2)}, u32[]{:S(2)}) collective-permute-start(bf16[4160,128]{1,0:T(8,128)(2,1)S(1)} %join1.1.refs_0_), channel_id=1, source_target_pairs={{0,24},{1,97},{2,26},{3,99},{4,28},{5,101},{6,30},{7,103},{8,0},{9... | collective-permute-start | bytes 3194888 | tf_op jit(solution)/shard_map/ppermute | solution.py:90
  28.2 1.2 %collective-permute-start.7 = (bf16[4160,128]{1,0:T(8,128)(2,1)S(1)}, bf16[4160,128]{1,0:T(8,128)(2,1)S(1)}, u32[]{:S(2)}, u32[]{:S(2)}) collective-permute-start(bf16[4160,128]{1,0:T(8,128)(2,1)S(1)} %join1.1.refs_0_), channel_id=1, source_target_pairs={{0,16},{1,65},{2,18},{3,67},{4,20},{5,69},{6,22},{7,71},{8,24},{9,... | collective-permute-start | bytes 3194888 | tf_op jit(solution)/shard_map/ppermute | solution.py:90
  29.8 2.3 %collective-permute-start.9 = (bf16[4096,128]{1,0:T(8,128)(2,1)S(1)}, bf16[4096,128]{1,0:T(8,128)(2,1)S(1)}, u32[]{:S(2)}, u32[]{:S(2)}) collective-permute-start(bf16[4096,128]{1,0:T(8,128)(2,1)S(1)} %bitcast.21), channel_id=1, source_target_pairs={{0,6},{1,7},{2,0},{3,1},{4,2},{5,3},{6,4},{7,5},{8,14},{9,15},{10,... | collective-permute-start | bytes 3145736 | tf_op jit(solution)/shard_map/ppermute | solution.py:90
  32.1 2.4 %ffn1.1 = (f32[512,1024]{1,0:T(8,128)S(1)}, f32[512,1024]{1,0:T(8,128)S(1)}) custom-call(bf16[512,1024]{1,0:T(8,128)(2,1)S(1)} %attend.1.refs_0_.normed, bf16[512,1024]{1,0:T(8,128)(2,1)S(1)} %collective-permute-done.4.refs_1_.refs_0_, bf16[4096,128]{1,0:T(8,128)(2,1)S(1)} %bitcast.22, bf16[4096,128]{1,0:T(8,128)(2,1)S(1)} %bitcast.23), custom_call_target="tpu_custom_call" | custom-call | flops 1 | bytes 1 | tf_op jit(solution)/shard_map/ffn1/pallas_call | solution.py:306
  34.6 6.2 %collective-permute-done.5.refs_7_.refs_1_ = bf16[4160,128]{1,0:T(8,128)(2,1)S(1)} collective-permute-done((bf16[4160,128]{1,0:T(8,128)(2,1)S(1)}, bf16[4160,128]{1,0:T(8,128)(2,1)S(1)}, u32[]{:S(2)}, u32[]{:S(2)}) %collective-permute-start.5) | collective-permute-done | bytes 1064992 | tf_op jit(solution)/shard_map/ppermute | solution.py:90
  40.8 3.0 %ffn2.1 = (f32[512,1024]{1,0:T(8,128)S(1)}, f32[512,1024]{1,0:T(8,128)S(1)}) custom-call(bf16[512,1024]{1,0:T(8,128)(2,1)S(1)} %attend.1.refs_0_.normed, bf16[512,1024]{1,0:T(8,128)(2,1)S(1)} %collective-permute-done.4.refs_1_.refs_0_, f32[512,1024]{1,0:T(8,128)S(1)} %get-tuple-element.39.refs_2_, ...), custom_call_target="tpu_custom_call", output_to_operand_aliasing={{0}: (2, {}), {1}: (3, {})} | custom-call | flops 1 | bytes 1 | tf_op jit(solution)/shard_map/ffn2/pallas_call | solution.py:306
  43.8 7.7 %collective-permute-done.6.refs_2_.refs_4_ = bf16[4160,128]{1,0:T(8,128)(2,1)S(1)} collective-permute-done((bf16[4160,128]{1,0:T(8,128)(2,1)S(1)}, bf16[4160,128]{1,0:T(8,128)(2,1)S(1)}, u32[]{:S(2)}, u32[]{:S(2)}) %collective-permute-start.6) | collective-permute-done | bytes 1064992 | tf_op jit(solution)/shard_map/ppermute | solution.py:90
  51.6 1.5 %collective-permute-done.7.refs_3_.refs_5_ = bf16[4160,128]{1,0:T(8,128)(2,1)S(1)} collective-permute-done((bf16[4160,128]{1,0:T(8,128)(2,1)S(1)}, bf16[4160,128]{1,0:T(8,128)(2,1)S(1)}, u32[]{:S(2)}, u32[]{:S(2)}) %collective-permute-start.7) | collective-permute-done | bytes 1064992 | tf_op jit(solution)/shard_map/ppermute | solution.py:90
  53.2 1.3 %collective-permute-start.12 = (bf16[4352,128]{1,0:T(8,128)(2,1)S(1)}, bf16[4352,128]{1,0:T(8,128)(2,1)S(1)}, u32[]{:S(2)}, u32[]{:S(2)}) collective-permute-start(bf16[4352,128]{1,0:T(8,128)(2,1)S(1)} %join2.1), channel_id=1, source_target_pairs={{0,32},{1,9},{2,34},{3,11},{4,36},{5,13},{6,38},{7,15},{8,40},{9,1... | collective-permute-start | bytes 3342344 | tf_op jit(solution)/shard_map/ppermute | solution.py:90
  54.5 1.4 %collective-permute-start.13 = (bf16[4352,128]{1,0:T(8,128)(2,1)S(1)}, bf16[4352,128]{1,0:T(8,128)(2,1)S(1)}, u32[]{:S(2)}, u32[]{:S(2)}) collective-permute-start(bf16[4352,128]{1,0:T(8,128)(2,1)S(1)} %join2.1), channel_id=1, source_target_pairs={{0,96},{1,25},{2,98},{3,27},{4,100},{5,29},{6,102},{7,31},{8,104},... | collective-permute-start | bytes 3342344 | tf_op jit(solution)/shard_map/ppermute | solution.py:90
  56.5 2.3 %collective-permute-start.11 = (bf16[2048,128]{1,0:T(8,128)(2,1)S(1)}, bf16[2048,128]{1,0:T(8,128)(2,1)S(1)}, u32[]{:S(2)}, u32[]{:S(2)}) collective-permute-start(bf16[2048,128]{1,0:T(8,128)(2,1)S(1)} %join6.1), channel_id=1, source_target_pairs={{0,6},{1,7},{2,0},{3,1},{4,2},{5,3},{6,4},{7,5},{8,14},{9,15},{10,... | collective-permute-start | bytes 1572872 | tf_op jit(solution)/shard_map/ppermute | solution.py:90
  58.8 4.7 %ffn3.1 = (f32[512,1024]{1,0:T(8,128)S(1)}, f32[512,1024]{1,0:T(8,128)S(1)}) custom-call(bf16[512,1024]{1,0:T(8,128)(2,1)S(1)} %attend.1.refs_0_.normed, bf16[512,1024]{1,0:T(8,128)(2,1)S(1)} %collective-permute-done.4.refs_1_.refs_0_, f32[512,1024]{1,0:T(8,128)S(1)} %get-tuple-element.43.refs_2_, ...), custom_call_target="tpu_custom_call", output_to_operand_aliasing={{0}: (2, {}), {1}: (3, {})} | custom-call | flops 1 | bytes 1 | tf_op jit(solution)/shard_map/ffn3/pallas_call | solution.py:306
  63.5 5.6 %collective-permute-done.12.refs_0_ = bf16[4352,128]{1,0:T(8,128)(2,1)S(1)} collective-permute-done((bf16[4352,128]{1,0:T(8,128)(2,1)S(1)}, bf16[4352,128]{1,0:T(8,128)(2,1)S(1)}, u32[]{:S(2)}, u32[]{:S(2)}) %collective-permute-start.12) | collective-permute-done | bytes 1114144 | tf_op jit(solution)/shard_map/ppermute | solution.py:90
  69.1 0.9 join3.1
  70.8 1.3 %ffn4.1 = f32[512,1024]{1,0:T(8,128)S(1)} custom-call(bf16[512,1024]{1,0:T(8,128)(2,1)S(1)} %collective-permute-done.4.refs_1_.refs_0_, f32[512,1024]{1,0:T(8,128)S(1)} %get-tuple-element.54.refs_1_, bf16[2048,128]{1,0:T(8,128)(2,1)S(1)} %collective-permute-done.10.refs_2_, ...), custom_call_target="tpu_custom_call", output_to_operand_aliasing={{}: (1, {})} | custom-call | flops 1 | bytes 1 | tf_op jit(solution)/shard_map/ffn4/pallas_call | solution.py:306
  72.1 2.1 %collective-permute-start.14 = (f32[512,1024]{1,0:T(8,128)S(1)}, f32[512,1024]{1,0:T(8,128)S(1)}, u32[]{:S(2)}, u32[]{:S(2)}) collective-permute-start(f32[512,1024]{1,0:T(8,128)S(1)} %ffn4.1), channel_id=1, source_target_pairs={{0,1},{1,0},{2,3},{3,2},{4,5},{5,4},{6,7},{7,6},{8,9},{9,8},{10,11... | collective-permute-start | bytes 6291464 | tf_op jit(solution)/shard_map/ppermute | solution.py:90
  74.2 1.1 %collective-permute-start.16 = (bf16[2176,128]{1,0:T(8,128)(2,1)}, bf16[2176,128]{1,0:T(8,128)(2,1)}, u32[]{:S(2)}, u32[]{:S(2)}) collective-permute-start(bf16[2176,128]{1,0:T(8,128)(2,1)} %join3.1), channel_id=1, source_target_pairs={{0,32},{1,9},{2,34},{3,11},{4,36},{5,13},{6,38},{7,15},{8,40},{9,1... | collective-permute-start | bytes 1671176 | tf_op jit(solution)/shard_map/ppermute | solution.py:90
  75.3 1.5 %collective-permute-start.17 = (bf16[2176,128]{1,0:T(8,128)(2,1)}, bf16[2176,128]{1,0:T(8,128)(2,1)}, u32[]{:S(2)}, u32[]{:S(2)}) collective-permute-start(bf16[2176,128]{1,0:T(8,128)(2,1)} %join4.1), channel_id=1, source_target_pairs={{0,96},{1,25},{2,98},{3,27},{4,100},{5,29},{6,102},{7,31},{8,104},... | collective-permute-start | bytes 1671176 | tf_op jit(solution)/shard_map/ppermute | solution.py:90
  76.9 1.3 %ffn5.1.mine = f32[512,1024]{1,0:T(8,128)S(1)} custom-call(bf16[512,1024]{1,0:T(8,128)(2,1)S(1)} %attend.1.refs_0_.normed, f32[512,1024]{1,0:T(8,128)S(1)} %get-tuple-element.51.refs_1_, bf16[2048,128]{1,0:T(8,128)(2,1)S(1)} %collective-permute-done.10.refs_2_, bf16[2048,128]{1,0:T(8,128)(2,1)S(1)} %collective-permute-done.11.refs_3_), custom_call_target="tpu_custom_call", output_to_operand_aliasing={{}: (1, {})} | custom-call | flops 1 | bytes 1 | tf_op jit(solution)/shard_map/ffn5/pallas_call | solution.py:306
  78.2 2.3 %embed.1 = (bf16[512,128]{1,0:T(8,128)(2,1)}, bf16[512,128]{1,0:T(8,128)(2,1)S(1)}) custom-call(s32[4]{0:T(128)S(1)} %copy-done.3, bf16[512,1024]{1,0:T(8,128)(2,1)S(1)} %attend.1.refs_0_.normed, f32[512,1024]{1,0:T(8,128)S(1)} %ffn5.1.mine, f32[512,1024]{1,0:T(8,128)S(1)} %collective-permute-done.14.other, f32[1,1024]{1,0:T(1,128)S(1)} %bitcast.27, ...), custom_call_target="tpu_custom_call" | custom-call | flops 1 | bytes 1 | tf_op jit(solution)/shard_map/embed/pallas_call | solution.py:333
  81.4 3.0 %collective-permute-done.16 = bf16[2176,128]{1,0:T(8,128)(2,1)} collective-permute-done((bf16[2176,128]{1,0:T(8,128)(2,1)}, bf16[2176,128]{1,0:T(8,128)(2,1)}, u32[]{:S(2)}, u32[]{:S(2)}) %collective-permute-start.16) | collective-permute-done | bytes 557088 | tf_op jit(solution)/shard_map/ppermute | solution.py:90
  84.4 4.2 %score.1 = (f32[32,128]{1,0:T(8,128)S(1)}, f32[32,128]{1,0:T(8,128)S(1)}) custom-call(s32[5]{0:T(128)S(1)} %stack.23.where, s32[32]{0:T(128)S(1)} %reshape.51.cand, s32[32]{0:T(128)S(1)} %reshape.52.pair, bf16[512,128]{1,0:T(8,128)(2,1)S(1)} %get-tuple-element.57.emb, bf16[512,128]{1,0:T(8,128)(2,1)} %collective-permute-done.15.sib, ...), custom_call_target="tpu_custom_call" | custom-call | flops 1 | bytes 1 | tf_op jit(solution)/shard_map/score/pallas_call | solution.py:402
  88.6 1.0 %collective-permute-start.18 = (f32[32,128]{1,0:T(8,128)S(1)}, f32[32,128]{1,0:T(8,128)S(1)}, u32[]{:S(2)}, u32[]{:S(2)}) collective-permute-start(f32[32,128]{1,0:T(8,128)S(1)} %get-tuple-element.59), channel_id=1, source_target_pairs={{0,1},{1,0},{2,3},{3,2},{4,5},{5,4},{6,7},{7,6},{8,9},{9,8},{10,11... | collective-permute-start | bytes 49160 | tf_op jit(solution)/shard_map/ppermute | solution.py:90
  89.7 0.8 collective-permute-done.18
  (36 shorter events, 3.6 us)
Async XLA Ops:
  0.6 7.3 %copy-start.4 = (s32[4,8]{1,0:T(4,128)S(1)}, s32[4,8]{1,0:T(4,128)}, u32[]{:S(2)}) copy-start(s32[4,8]{1,0:T(4,128)} %param.23) | copy-start | bytes 388
  0.8 10.5 %copy-start.1 = (f32[1024]{0:T(1024)S(1)}, f32[1024]{0:T(1024)}, u32[]{:S(2)}) copy-start(f32[1024]{0:T(1024)} %param.15) | copy-start | bytes 12292
  0.8 10.5 %copy-start.3 = (s32[4]{0:T(128)S(1)}, s32[4]{0:T(128)}, u32[]{:S(2)}) copy-start(s32[4]{0:T(128)} %length.3) | copy-start | bytes 52
  2.6 21.5 %collective-permute-start = (bf16[1296,128]{1,0:T(8,128)(2,1)S(1)}, bf16[1296,128]{1,0:T(8,128)(2,1)S(1)}, u32[]{:S(2)}, u32[]{:S(2)}) collective-permute-start(bf16[1296,128]{1,0:T(8,128)(2,1)S(1)} %first.1.refs_3_), channel_id=1, source_target_pairs={{0,2},{1,3},{2,4},{3,5},{4,6},{5,7},{6,0},{7,1},{8,10},{9,11},{10,... | collective-permute-start | bytes 995336 | tf_op jit(solution)/shard_map/ppermute | solution.py:90
  4.8 19.3 %collective-permute-start.1 = (bf16[1296,128]{1,0:T(8,128)(2,1)S(1)}, bf16[1296,128]{1,0:T(8,128)(2,1)S(1)}, u32[]{:S(2)}, u32[]{:S(2)}) collective-permute-start(bf16[1296,128]{1,0:T(8,128)(2,1)S(1)} %first.1.refs_3_), channel_id=1, source_target_pairs={{0,6},{1,7},{2,0},{3,1},{4,2},{5,3},{6,4},{7,5},{8,14},{9,15},{10,... | collective-permute-start | bytes 995336 | tf_op jit(solution)/shard_map/ppermute | solution.py:90
  6.3 17.8 %collective-permute-start.2 = (bf16[1296,128]{1,0:T(8,128)(2,1)S(1)}, bf16[1296,128]{1,0:T(8,128)(2,1)S(1)}, u32[]{:S(2)}, u32[]{:S(2)}) collective-permute-start(bf16[1296,128]{1,0:T(8,128)(2,1)S(1)} %first.1.refs_3_), channel_id=1, source_target_pairs={{0,4},{1,5},{2,6},{3,7},{4,0},{5,1},{6,2},{7,3},{8,12},{9,13},{10,... | collective-permute-start | bytes 995336 | tf_op jit(solution)/shard_map/ppermute | solution.py:90
  7.9 16.2 %collective-permute-start.3 = (s32[4,8]{1,0:T(4,128)S(1)}, s32[4,8]{1,0:T(4,128)S(1)}, u32[]{:S(2)}, u32[]{:S(2)}) collective-permute-start(s32[4,8]{1,0:T(4,128)S(1)} %copy-done.4), channel_id=1, source_target_pairs={{0,1},{1,0},{2,3},{3,2},{4,5},{5,4},{6,7},{7,6},{8,9},{9,8},{10,11... | collective-permute-start | bytes 392 | tf_op jit(solution)/shard_map/ppermute | solution.py:90
  24.2 5.2 %collective-permute-start.4 = (bf16[512,1024]{1,0:T(8,128)(2,1)S(1)}, bf16[512,1024]{1,0:T(8,128)(2,1)S(1)}, u32[]{:S(2)}, u32[]{:S(2)}) collective-permute-start(bf16[512,1024]{1,0:T(8,128)(2,1)S(1)} %attend.1.refs_0_.normed), channel_id=1, source_target_pairs={{0,1},{1,0},{2,3},{3,2},{4,5},{5,4},{6,7},{7,6},{8,9},{9,8},{10,11... | collective-permute-start | bytes 3145736 | tf_op jit(solution)/shard_map/ppermute | solution.py:90
  24.3 16.5 %collective-permute-start.5 = (bf16[4160,128]{1,0:T(8,128)(2,1)S(1)}, bf16[4160,128]{1,0:T(8,128)(2,1)S(1)}, u32[]{:S(2)}, u32[]{:S(2)}) collective-permute-start(bf16[4160,128]{1,0:T(8,128)(2,1)S(1)} %join1.1.refs_0_), channel_id=1, source_target_pairs={{0,8},{1,33},{2,10},{3,35},{4,12},{5,37},{6,14},{7,39},{8,16},{9,4... | collective-permute-start | bytes 3194888 | tf_op jit(solution)/shard_map/ppermute | solution.py:90
  26.0 25.5 %collective-permute-start.6 = (bf16[4160,128]{1,0:T(8,128)(2,1)S(1)}, bf16[4160,128]{1,0:T(8,128)(2,1)S(1)}, u32[]{:S(2)}, u32[]{:S(2)}) collective-permute-start(bf16[4160,128]{1,0:T(8,128)(2,1)S(1)} %join1.1.refs_0_), channel_id=1, source_target_pairs={{0,24},{1,97},{2,26},{3,99},{4,28},{5,101},{6,30},{7,103},{8,0},{9... | collective-permute-start | bytes 3194888 | tf_op jit(solution)/shard_map/ppermute | solution.py:90
  28.2 24.9 %collective-permute-start.7 = (bf16[4160,128]{1,0:T(8,128)(2,1)S(1)}, bf16[4160,128]{1,0:T(8,128)(2,1)S(1)}, u32[]{:S(2)}, u32[]{:S(2)}) collective-permute-start(bf16[4160,128]{1,0:T(8,128)(2,1)S(1)} %join1.1.refs_0_), channel_id=1, source_target_pairs={{0,16},{1,65},{2,18},{3,67},{4,20},{5,69},{6,22},{7,71},{8,24},{9,... | collective-permute-start | bytes 3194888 | tf_op jit(solution)/shard_map/ppermute | solution.py:90
  29.4 26.5 %collective-permute-start.8 = (bf16[4096,128]{1,0:T(8,128)(2,1)S(1)}, bf16[4096,128]{1,0:T(8,128)(2,1)S(1)}, u32[]{:S(2)}, u32[]{:S(2)}) collective-permute-start(bf16[4096,128]{1,0:T(8,128)(2,1)S(1)} %bitcast.20), channel_id=1, source_target_pairs={{0,2},{1,3},{2,4},{3,5},{4,6},{5,7},{6,0},{7,1},{8,10},{9,11},{10,... | collective-permute-start | bytes 3145736 | tf_op jit(solution)/shard_map/ppermute | solution.py:90
  29.8 26.1 %collective-permute-start.9 = (bf16[4096,128]{1,0:T(8,128)(2,1)S(1)}, bf16[4096,128]{1,0:T(8,128)(2,1)S(1)}, u32[]{:S(2)}, u32[]{:S(2)}) collective-permute-start(bf16[4096,128]{1,0:T(8,128)(2,1)S(1)} %bitcast.21), channel_id=1, source_target_pairs={{0,6},{1,7},{2,0},{3,1},{4,2},{5,3},{6,4},{7,5},{8,14},{9,15},{10,... | collective-permute-start | bytes 3145736 | tf_op jit(solution)/shard_map/ppermute | solution.py:90
  53.2 15.9 %collective-permute-start.12 = (bf16[4352,128]{1,0:T(8,128)(2,1)S(1)}, bf16[4352,128]{1,0:T(8,128)(2,1)S(1)}, u32[]{:S(2)}, u32[]{:S(2)}) collective-permute-start(bf16[4352,128]{1,0:T(8,128)(2,1)S(1)} %join2.1), channel_id=1, source_target_pairs={{0,32},{1,9},{2,34},{3,11},{4,36},{5,13},{6,38},{7,15},{8,40},{9,1... | collective-permute-start | bytes 3342344 | tf_op jit(solution)/shard_map/ppermute | solution.py:90
  54.5 15.5 %collective-permute-start.13 = (bf16[4352,128]{1,0:T(8,128)(2,1)S(1)}, bf16[4352,128]{1,0:T(8,128)(2,1)S(1)}, u32[]{:S(2)}, u32[]{:S(2)}) collective-permute-start(bf16[4352,128]{1,0:T(8,128)(2,1)S(1)} %join2.1), channel_id=1, source_target_pairs={{0,96},{1,25},{2,98},{3,27},{4,100},{5,29},{6,102},{7,31},{8,104},... | collective-permute-start | bytes 3342344 | tf_op jit(solution)/shard_map/ppermute | solution.py:90
  56.0 14.8 %collective-permute-start.10 = (bf16[2048,128]{1,0:T(8,128)(2,1)S(1)}, bf16[2048,128]{1,0:T(8,128)(2,1)S(1)}, u32[]{:S(2)}, u32[]{:S(2)}) collective-permute-start(bf16[2048,128]{1,0:T(8,128)(2,1)S(1)} %join5.1), channel_id=1, source_target_pairs={{0,2},{1,3},{2,4},{3,5},{4,6},{5,7},{6,0},{7,1},{8,10},{9,11},{10,... | collective-permute-start | bytes 1572872 | tf_op jit(solution)/shard_map/ppermute | solution.py:90
  56.5 14.3 %collective-permute-start.11 = (bf16[2048,128]{1,0:T(8,128)(2,1)S(1)}, bf16[2048,128]{1,0:T(8,128)(2,1)S(1)}, u32[]{:S(2)}, u32[]{:S(2)}) collective-permute-start(bf16[2048,128]{1,0:T(8,128)(2,1)S(1)} %join6.1), channel_id=1, source_target_pairs={{0,6},{1,7},{2,0},{3,1},{4,2},{5,3},{6,4},{7,5},{8,14},{9,15},{10,... | collective-permute-start | bytes 1572872 | tf_op jit(solution)/shard_map/ppermute | solution.py:90
  72.1 6.1 %collective-permute-start.14 = (f32[512,1024]{1,0:T(8,128)S(1)}, f32[512,1024]{1,0:T(8,128)S(1)}, u32[]{:S(2)}, u32[]{:S(2)}) collective-permute-start(f32[512,1024]{1,0:T(8,128)S(1)} %ffn4.1), channel_id=1, source_target_pairs={{0,1},{1,0},{2,3},{3,2},{4,5},{5,4},{6,7},{7,6},{8,9},{9,8},{10,11... | collective-permute-start | bytes 6291464 | tf_op jit(solution)/shard_map/ppermute | solution.py:90
  74.2 10.2 %collective-permute-start.16 = (bf16[2176,128]{1,0:T(8,128)(2,1)}, bf16[2176,128]{1,0:T(8,128)(2,1)}, u32[]{:S(2)}, u32[]{:S(2)}) collective-permute-start(bf16[2176,128]{1,0:T(8,128)(2,1)} %join3.1), channel_id=1, source_target_pairs={{0,32},{1,9},{2,34},{3,11},{4,36},{5,13},{6,38},{7,15},{8,40},{9,1... | collective-permute-start | bytes 1671176 | tf_op jit(solution)/shard_map/ppermute | solution.py:90
  75.3 9.1 %collective-permute-start.17 = (bf16[2176,128]{1,0:T(8,128)(2,1)}, bf16[2176,128]{1,0:T(8,128)(2,1)}, u32[]{:S(2)}, u32[]{:S(2)}) collective-permute-start(bf16[2176,128]{1,0:T(8,128)(2,1)} %join4.1), channel_id=1, source_target_pairs={{0,96},{1,25},{2,98},{3,27},{4,100},{5,29},{6,102},{7,31},{8,104},... | collective-permute-start | bytes 1671176 | tf_op jit(solution)/shard_map/ppermute | solution.py:90
  76.9 1.3 %copy-start = (bf16[1024,128]{1,0:T(8,128)(2,1)S(1)}, bf16[1024,128]{1,0:T(8,128)(2,1)}, u32[]{:S(2)}) copy-start(bf16[1024,128]{1,0:T(8,128)(2,1)} %we.1) | copy-start | bytes 786436
  76.9 1.3 %copy-start.2 = (f32[1024]{0:T(1024)S(1)}, f32[1024]{0:T(1024)}, u32[]{:S(2)}) copy-start(f32[1024]{0:T(1024)} %param.18) | copy-start | bytes 12292
  80.6 3.8 %collective-permute-start.15 = (bf16[512,128]{1,0:T(8,128)(2,1)S(1)}, bf16[512,128]{1,0:T(8,128)(2,1)}, u32[]{:S(2)}, u32[]{:S(2)}) collective-permute-start(bf16[512,128]{1,0:T(8,128)(2,1)S(1)} %get-tuple-element.57.emb), channel_id=1, source_target_pairs={{0,1},{1,0},{2,3},{3,2},{4,5},{5,4},{6,7},{7,6},{8,9},{9,8},{10,11... | collective-permute-start | bytes 393224 | tf_op jit(solution)/shard_map/ppermute | solution.py:90
  88.6 1.9 %collective-permute-start.18 = (f32[32,128]{1,0:T(8,128)S(1)}, f32[32,128]{1,0:T(8,128)S(1)}, u32[]{:S(2)}, u32[]{:S(2)}) collective-permute-start(f32[32,128]{1,0:T(8,128)S(1)} %get-tuple-element.59), channel_id=1, source_target_pairs={{0,1},{1,0},{2,3},{3,2},{4,5},{5,4},{6,7},{7,6},{8,9},{9,8},{10,11... | collective-permute-start | bytes 49160 | tf_op jit(solution)/shard_map/ppermute | solution.py:90

commit v6 on v5

--- a/solution.py
+++ b/solution.py
@@ -152,38 +152,6 @@
     )(where, *pinned(up, down, docs, lengths))
 
 
-def pack_body(up, down, low, high, held, sems):
-    copies = [
-        pltpu.make_async_copy(w.at[h * 512 : (h + 1) * 512], held.at[k, h * 512 : (h + 1) * 512], sems.at[2 * k + h])
-        for k, w in enumerate((up, down))
-        for h in range(2)
-    ]
-    for copy in copies:
-        copy.start()
-    for k in range(2):
-        for j in range(HALF):
-            if j % 4 == 0:
-                copies[2 * k + j // 4].wait()
-            rows = slice(j * LANES, (j + 1) * LANES)
-            low[k * HALF + j] = held[k, rows, :256].T
-            high[k * HALF + j] = held[k, rows, 256:].T
-
-
-def pack(up, down):
-    piece = jax.ShapeDtypeStruct((SLABS, 256, LANES), bf16)
-    low, high = pl.pallas_call(
-        pack_body,
-        out_shape=(piece, piece),
-        in_specs=hbm(2),
-        out_specs=tuple(vmem(2)),
-        scratch_shapes=[pltpu.VMEM((2, D, 512), bf16), pltpu.SemaphoreType.DMA((4,))],
-        compiler_params=params(8),
-        cost_estimate=LIGHT,
-        name="pack",
-    )(*pinned(up, down))
-    return low.reshape(-1, LANES), high.reshape(-1, LANES)
-
-
 def join_body(takes, *refs):
     out, at = refs[-1], 0
     for k, start, size in takes:
@@ -203,23 +171,33 @@
     )(*arrays)
 
 
-def attend_body(length, tok_hbm, qkv, wo_hbm, gain, out, packed, context, tok, held, wo, sems):
+def attend_body(
+    length, tok_hbm, qkv, wo_hbm, up, down, gain, out, low_out, high_out, packed, context, tok, held, wo, wide, sems
+):
     rows_all = tok.shape[0]
     step = 512
-    copies = [pltpu.make_async_copy(tok_hbm, tok, sems.at[6])]
+    copies = [pltpu.make_async_copy(tok_hbm, tok, sems.at[0])]
     for i in range(6):
         columns = slice(i * step, (i + 1) * step)
-        copies.append(pltpu.make_async_copy(qkv.at[:, columns], held.at[:, columns], sems.at[i]))
-    copies.append(pltpu.make_async_copy(wo_hbm, wo, sems.at[7]))
+        copies.append(pltpu.make_async_copy(qkv.at[:, columns], held.at[:, columns], sems.at[1 + i]))
+    copies.append(pltpu.make_async_copy(up, wide.at[0], sems.at[7]))
+    copies.append(pltpu.make_async_copy(down, wide.at[1], sems.at[8]))
+    copies.append(pltpu.make_async_copy(wo_hbm, wo, sems.at[9]))
     for copy in copies[:3]:
         copy.start()
     copies[0].wait()
     for i in range(6):
         columns = slice(i * step, (i + 1) * step)
         copies[1 + i].wait()
-        if i < 5:
-            copies[3 + i].start()
+        copies[3 + i].start()
         packed[:, columns] = dot(tok[...], held[:, columns]).astype(bf16)
+    copies[9].start()
+    for k in range(2):
+        copies[7 + k].wait()
+        for j in range(HALF):
+            rows = slice(j * LANES, (j + 1) * LANES)
+            low_out[k * HALF + j] = wide[k, rows, :256].T
+            high_out[k * HALF + j] = wide[k, rows, 256:].T
     lane = lax.broadcasted_iota(jnp.int32, (2 * SEQ, LANES), 1)
     low = lax.broadcasted_iota(jnp.int32, (SEQ, LANES), 1) < HD
 
@@ -241,30 +219,59 @@
         return carry
 
     lax.fori_loop(0, rows_all // SEQ, request, 0)
-    copies[7].wait()
+    copies[9].wait()
     attended = dot(context[...], wo[...])
     out[...] = norm_rows(tok[...].astype(f32) + attended, gain[...]).astype(bf16)
 
 
-def attend(tokens, qkv, wo, gain, length):
+def attend(tokens, qkv, wo, gain, length, up, down):
     rows = tokens.shape[0]
-    return pl.pallas_call(
+    piece = jax.ShapeDtypeStruct((SLABS, 256, LANES), bf16)
+    normed, low, high = pl.pallas_call(
         attend_body,
-        out_shape=jax.ShapeDtypeStruct((rows, D), bf16),
-        in_specs=[SMEM] + hbm(3) + vmem(1),
-        out_specs=vmem()[0],
+        out_shape=(jax.ShapeDtypeStruct((rows, D), bf16), piece, piece),
+        in_specs=[SMEM] + hbm(5) + vmem(1),
+        out_specs=tuple(vmem(3)),
         scratch_shapes=[
             pltpu.VMEM((rows, 3 * D), bf16),
             pltpu.VMEM((rows, D), bf16),
             pltpu.VMEM((rows, D), bf16),
             pltpu.VMEM((D, 3 * D), bf16),
             pltpu.VMEM((D, D), bf16),
-            pltpu.SemaphoreType.DMA((8,)),
+            pltpu.VMEM((2, D, 512), bf16),
+            pltpu.SemaphoreType.DMA((10,)),
         ],
-        compiler_params=params(24),
+        compiler_params=params(28),
         cost_estimate=LIGHT,
         name="attend",
-    )(length, *pinned(tokens, qkv, wo), gain.reshape(1, D))
+    )(length, *pinned(tokens, qkv, wo, up, down), gain.reshape(1, D))
+    return normed, low.reshape(-1, LANES), high.reshape(-1, LANES)
+
+
+def halves_body(plus, minus, low, high, sems):
+    rows = low.shape[0]
+    copies = [
+        pltpu.make_async_copy(plus.at[:rows], low, sems.at[0]),
+        pltpu.make_async_copy(minus.at[rows:], high, sems.at[1]),
+    ]
+    for copy in copies:
+        copy.start()
+    for copy in copies:
+        copy.wait()
+
+
+def halves(plus, minus):
+    half = jax.ShapeDtypeStruct((plus.shape[0] // 2, LANES), bf16)
+    return pl.pallas_call(
+        halves_body,
+        out_shape=(half, half),
+        in_specs=any_spec(2),
+        out_specs=tuple(any_spec(2)),
+        scratch_shapes=[pltpu.SemaphoreType.DMA((2,))],
+        compiler_params=params(8),
+        cost_estimate=LIGHT,
+        name="halves",
+    )(plus, minus)
 
 
 def units(refs, half, start, size):
@@ -433,10 +440,11 @@
     where = jnp.stack([z, x, y, c, jnp.where(c == 0, x, z)]).astype(jnp.int32)
     start = first(where, up_weight, down_weight, documents.reshape(-1, P_SIZE), document_length)
     near = [send(start, way) for way in ("y+", "y-", "y2")]
-    low, high = pack(up_weight, down_weight)
-    normed = attend(tokens, attend_weight, output_weight, after(attend_gain, start), query_length)
+    normed, low, high = attend(
+        tokens, attend_weight, output_weight, after(attend_gain, start), query_length, up_weight, down_weight
+    )
     pair = send(after(candidates, start), "c")
-    near, pair = after((tuple(near), pair), normed, high)
+    near, pair = after((tuple(near), pair), normed)
 
     whole = [(k, 0, BLOCK) for k in range(3)] + [(3, PART, DOC_ROWS)]
     go = join([*near, start], whole, "join1")
@@ -460,17 +468,16 @@
     low_far = [send(ahead, "y+"), send(behind, "y-")]
     pieces = [(k,) + p for k in range(2) for p in parts] + [(2, 0, 256), (3, 0, 256)]
     total = ffn(sets, total, [*came[1:], *low_near], pieces, "ffn3")
-    cut = docs.shape[0] // 2
-    halves = [join([last[0]], [(0, 0, cut)], "join3"), join([last[1]], [(0, cut, cut)], "join4")]
-    last += [send(halves[0], "g+"), send(halves[1], "g-")]
-    low_far = after(tuple(low_far), *halves)
+    parted = halves(*last)
+    far_docs = [send(parted[0], "g+"), send(parted[1], "g-")]
+    low_far = after(tuple(low_far), *parted)
     rest = [(0, 0, mid), (1, 0, mid)]
     away, = ffn(sets[1:], total[1:], low_far, rest, "ffn4")
     other = send(away, "c")
-    mine, = ffn(sets[:1], total[:1], low_far, rest, "ffn5")
+    mine, = ffn((normed,), total[:1], low_far, rest, "ffn5")
     embedded, kept = embed(query_length, normed, mine, other, mlp_gain, embed_weight)
     sib = send(kept, "c")
-    best, best_pair = score(where, candidates, pair, kept, sib, [docs] + last)
+    best, best_pair = score(where, candidates, pair, kept, sib, [docs, *last, *far_docs])
     scores = final(best, send(best_pair, "c"), candidates.shape[0])
     return (embedded, scores)
 

time: 91.4 us -> 90.4 us (0.989)
  Pallas kernels: 38.4 us -> 36.9 us
    pallas_call x6 -> x4, Pallas kernels: 1.92 us -> 0.21 us  [join(): pl.pallas_call(functools.partial(join_body, takes), out_shape=jax.ShapeDt...]
    ppermute x19, starting transfers between devices: 26.7 us -> 27.6 us  [send(): return lax.ppermute(value, ('req', 'mlp'), STEPS[way])]
  transfers between devices with their start and end apart: 19 -> 19, of which waited for: 6 -> 6; matrix products, arithmetic and copies ran while one was open for 0% -> 0% of each run, Pallas kernels for 33% -> 32%
where the time goes in v6:
time: 90.4 us; the launch traced here: 90.2 us
  Pallas kernels  36.9 us (41%)
  starting transfers between devices  27.6 us (31%)
  waiting for transfers between devices  24.5 us (27%)
    ppermute x19, starting transfers between devices, send(): return lax.ppermute(value, ('req', 'mlp'), STEPS[way])  27.6 us
    ppermute x19, waiting for transfers between devices, send(): return lax.ppermute(value, ('req', 'mlp'), STEPS[way])  24.5 us
    pallas_call x1, Pallas kernels, attend(): pl.pallas_call(attend_body, out_shape=(jax.ShapeDtypeStruct((rows, D), bf...  13.7 us
    pallas_call x5, Pallas kernels, ffn(): pl.pallas_call(functools.partial(ffn_body, tuple(pieces), len(arrays), se...  12.8 us
    pallas_call x1, Pallas kernels, score(): pl.pallas_call(score_body, out_shape=(jax.ShapeDtypeStruct((total, SEQ),...  4.24 us
    pallas_call x1, Pallas kernels, embed(): pl.pallas_call(embed_body, out_shape=(shape, shape), in_specs=[SMEM] + vm...  2.36 us
    pallas_call x1, Pallas kernels, first(): pl.pallas_call(first_body, out_shape=jax.ShapeDtypeStruct((BLOCK, LANES),...  1.84 us
  transfers between devices with their start and end apart: 19, of which 6 were waited for; matrix products, arithmetic and copies ran while one was open for 0% of the time, Pallas kernels for 32%

profile of v6, /device:TPU:1, one launch (start us, length us, event | category | flops | bytes accessed | tf_op | source)
XLA Modules:
  0.0 90.2 jit_solution(1018356648018346081)
XLA Ops:
  0.8 1.8 %first.1.refs_3_ = bf16[1296,128]{1,0:T(8,128)(2,1)S(1)} custom-call(s32[5]{0:T(128)S(1)} %stack.23.where, bf16[1024,512]{1,0:T(8,128)(2,1)} %up.3, bf16[1024,512]{1,0:T(8,128)(2,1)} %down.3, bf16[256,128]{1,0:T(8,128)(2,1)} %bitcast.28, s32[8]{0:T(128)} %lengths.1), custom_call_target="tpu_custom_call" | custom-call | flops 1 | bytes 1 | tf_op jit(solution)/shard_map/first/pallas_call | solution.py:138
  2.6 2.2 %collective-permute-start = (bf16[1296,128]{1,0:T(8,128)(2,1)S(1)}, bf16[1296,128]{1,0:T(8,128)(2,1)S(1)}, u32[]{:S(2)}, u32[]{:S(2)}) collective-permute-start(bf16[1296,128]{1,0:T(8,128)(2,1)S(1)} %first.1.refs_3_), channel_id=1, source_target_pairs={{0,2},{1,3},{2,4},{3,5},{4,6},{5,7},{6,0},{7,1},{8,10},{9,11},{10,... | collective-permute-start | bytes 995336 | tf_op jit(solution)/shard_map/ppermute | solution.py:90
  4.8 1.5 %collective-permute-start.1 = (bf16[1296,128]{1,0:T(8,128)(2,1)S(1)}, bf16[1296,128]{1,0:T(8,128)(2,1)S(1)}, u32[]{:S(2)}, u32[]{:S(2)}) collective-permute-start(bf16[1296,128]{1,0:T(8,128)(2,1)S(1)} %first.1.refs_3_), channel_id=1, source_target_pairs={{0,6},{1,7},{2,0},{3,1},{4,2},{5,3},{6,4},{7,5},{8,14},{9,15},{10,... | collective-permute-start | bytes 995336 | tf_op jit(solution)/shard_map/ppermute | solution.py:90
  6.3 1.6 %collective-permute-start.2 = (bf16[1296,128]{1,0:T(8,128)(2,1)S(1)}, bf16[1296,128]{1,0:T(8,128)(2,1)S(1)}, u32[]{:S(2)}, u32[]{:S(2)}) collective-permute-start(bf16[1296,128]{1,0:T(8,128)(2,1)S(1)} %first.1.refs_3_), channel_id=1, source_target_pairs={{0,4},{1,5},{2,6},{3,7},{4,0},{5,1},{6,2},{7,3},{8,12},{9,13},{10,... | collective-permute-start | bytes 995336 | tf_op jit(solution)/shard_map/ppermute | solution.py:90
  7.9 1.5 %collective-permute-start.3 = (s32[4,8]{1,0:T(4,128)S(1)}, s32[4,8]{1,0:T(4,128)S(1)}, u32[]{:S(2)}, u32[]{:S(2)}) collective-permute-start(s32[4,8]{1,0:T(4,128)S(1)} %copy-done.4), channel_id=1, source_target_pairs={{0,1},{1,0},{2,3},{3,2},{4,5},{5,4},{6,7},{7,6},{8,9},{9,8},{10,11... | collective-permute-start | bytes 392 | tf_op jit(solution)/shard_map/ppermute | solution.py:90
  9.4 13.7 %attend.1 = (bf16[512,1024]{1,0:T(8,128)(2,1)S(1)}, bf16[16,256,128]{2,1,0:T(8,128)(2,1)S(1)}, bf16[16,256,128]{2,1,0:T(8,128)(2,1)S(1)}) custom-call(s32[4]{0:T(128)S(1)} %copy-done.3, bf16[512,1024]{1,0:T(8,128)(2,1)} %tok_hbm.1, bf16[1024,3072]{1,0:T(8,128)(2,1)} %qkv.1, bf16[1024,1024]{1,0:T(8,128)(2,1)} %wo_hbm.1, bf16[1024,512]{1,0:T(8,128)(2,1)} %up.3, ...), custom_call_target="tpu_custom_call" | custom-call | flops 1 | bytes 1 | tf_op jit(solution)/shard_map/attend/pallas_call | solution.py:230
  23.5 1.7 %collective-permute-start.5 = (bf16[4160,128]{1,0:T(8,128)(2,1)S(1)}, bf16[4160,128]{1,0:T(8,128)(2,1)S(1)}, u32[]{:S(2)}, u32[]{:S(2)}) collective-permute-start(bf16[4160,128]{1,0:T(8,128)(2,1)S(1)} %join1.1.refs_0_), channel_id=1, source_target_pairs={{0,8},{1,33},{2,10},{3,35},{4,12},{5,37},{6,14},{7,39},{8,16},{9,4... | collective-permute-start | bytes 3194888 | tf_op jit(solution)/shard_map/ppermute | solution.py:90
  25.1 2.2 %collective-permute-start.6 = (bf16[4160,128]{1,0:T(8,128)(2,1)S(1)}, bf16[4160,128]{1,0:T(8,128)(2,1)S(1)}, u32[]{:S(2)}, u32[]{:S(2)}) collective-permute-start(bf16[4160,128]{1,0:T(8,128)(2,1)S(1)} %join1.1.refs_0_), channel_id=1, source_target_pairs={{0,24},{1,97},{2,26},{3,99},{4,28},{5,101},{6,30},{7,103},{8,0},{9... | collective-permute-start | bytes 3194888 | tf_op jit(solution)/shard_map/ppermute | solution.py:90
  27.3 1.2 %collective-permute-start.7 = (bf16[4160,128]{1,0:T(8,128)(2,1)S(1)}, bf16[4160,128]{1,0:T(8,128)(2,1)S(1)}, u32[]{:S(2)}, u32[]{:S(2)}) collective-permute-start(bf16[4160,128]{1,0:T(8,128)(2,1)S(1)} %join1.1.refs_0_), channel_id=1, source_target_pairs={{0,16},{1,65},{2,18},{3,67},{4,20},{5,69},{6,22},{7,71},{8,24},{9,... | collective-permute-start | bytes 3194888 | tf_op jit(solution)/shard_map/ppermute | solution.py:90
  29.4 1.8 %collective-permute-start.9 = (bf16[4096,128]{1,0:T(8,128)(2,1)S(1)}, bf16[4096,128]{1,0:T(8,128)(2,1)S(1)}, u32[]{:S(2)}, u32[]{:S(2)}) collective-permute-start(bf16[4096,128]{1,0:T(8,128)(2,1)S(1)} %bitcast.21), channel_id=1, source_target_pairs={{0,6},{1,7},{2,0},{3,1},{4,2},{5,3},{6,4},{7,5},{8,14},{9,15},{10,... | collective-permute-start | bytes 3145736 | tf_op jit(solution)/shard_map/ppermute | solution.py:90
  31.2 2.5 %ffn1.1 = (f32[512,1024]{1,0:T(8,128)S(1)}, f32[512,1024]{1,0:T(8,128)S(1)}) custom-call(bf16[512,1024]{1,0:T(8,128)(2,1)S(1)} %get-tuple-element.40.refs_0_.normed, bf16[512,1024]{1,0:T(8,128)(2,1)S(1)} %collective-permute-done.4.refs_1_.refs_0_, bf16[4096,128]{1,0:T(8,128)(2,1)S(1)} %bitcast.22, bf16[4096,128]{1,0:T(8,128)(2,1)S(1)} %bitcast.23), custom_call_target="tpu_custom_call" | custom-call | flops 1 | bytes 1 | tf_op jit(solution)/shard_map/ffn1/pallas_call | solution.py:313
  33.7 6.2 %collective-permute-done.5.refs_7_.refs_1_ = bf16[4160,128]{1,0:T(8,128)(2,1)S(1)} collective-permute-done((bf16[4160,128]{1,0:T(8,128)(2,1)S(1)}, bf16[4160,128]{1,0:T(8,128)(2,1)S(1)}, u32[]{:S(2)}, u32[]{:S(2)}) %collective-permute-start.5) | collective-permute-done | bytes 1064992 | tf_op jit(solution)/shard_map/ppermute | solution.py:90
  39.9 3.0 %ffn2.1 = (f32[512,1024]{1,0:T(8,128)S(1)}, f32[512,1024]{1,0:T(8,128)S(1)}) custom-call(bf16[512,1024]{1,0:T(8,128)(2,1)S(1)} %get-tuple-element.40.refs_0_.normed, bf16[512,1024]{1,0:T(8,128)(2,1)S(1)} %collective-permute-done.4.refs_1_.refs_0_, f32[512,1024]{1,0:T(8,128)S(1)} %get-tuple-element.43.refs_2_, ...), custom_call_target="tpu_custom_call", output_to_operand_aliasing={{0}: (2, {}), {1}: (3, {})} | custom-call | flops 1 | bytes 1 | tf_op jit(solution)/shard_map/ffn2/pallas_call | solution.py:313
  42.9 7.7 %collective-permute-done.6.refs_2_.refs_4_ = bf16[4160,128]{1,0:T(8,128)(2,1)S(1)} collective-permute-done((bf16[4160,128]{1,0:T(8,128)(2,1)S(1)}, bf16[4160,128]{1,0:T(8,128)(2,1)S(1)}, u32[]{:S(2)}, u32[]{:S(2)}) %collective-permute-start.6) | collective-permute-done | bytes 1064992 | tf_op jit(solution)/shard_map/ppermute | solution.py:90
  50.6 1.5 %collective-permute-done.7.refs_3_.refs_5_ = bf16[4160,128]{1,0:T(8,128)(2,1)S(1)} collective-permute-done((bf16[4160,128]{1,0:T(8,128)(2,1)S(1)}, bf16[4160,128]{1,0:T(8,128)(2,1)S(1)}, u32[]{:S(2)}, u32[]{:S(2)}) %collective-permute-start.7) | collective-permute-done | bytes 1064992 | tf_op jit(solution)/shard_map/ppermute | solution.py:90
  52.3 1.3 %collective-permute-start.12 = (bf16[4352,128]{1,0:T(8,128)(2,1)S(1)}, bf16[4352,128]{1,0:T(8,128)(2,1)S(1)}, u32[]{:S(2)}, u32[]{:S(2)}) collective-permute-start(bf16[4352,128]{1,0:T(8,128)(2,1)S(1)} %join2.1), channel_id=1, source_target_pairs={{0,32},{1,9},{2,34},{3,11},{4,36},{5,13},{6,38},{7,15},{8,40},{9,1... | collective-permute-start | bytes 3342344 | tf_op jit(solution)/shard_map/ppermute | solution.py:90
  53.6 1.5 %collective-permute-start.13 = (bf16[4352,128]{1,0:T(8,128)(2,1)S(1)}, bf16[4352,128]{1,0:T(8,128)(2,1)S(1)}, u32[]{:S(2)}, u32[]{:S(2)}) collective-permute-start(bf16[4352,128]{1,0:T(8,128)(2,1)S(1)} %join2.1), channel_id=1, source_target_pairs={{0,96},{1,25},{2,98},{3,27},{4,100},{5,29},{6,102},{7,31},{8,104},... | collective-permute-start | bytes 3342344 | tf_op jit(solution)/shard_map/ppermute | solution.py:90
  55.1 0.9 %collective-permute-start.10 = (bf16[2048,128]{1,0:T(8,128)(2,1)S(1)}, bf16[2048,128]{1,0:T(8,128)(2,1)S(1)}, u32[]{:S(2)}, u32[]{:S(2)}) collective-permute-start(bf16[2048,128]{1,0:T(8,128)(2,1)S(1)} %join5.1), channel_id=1, source_target_pairs={{0,2},{1,3},{2,4},{3,5},{4,6},{5,7},{6,0},{7,1},{8,10},{9,11},{10,... | collective-permute-start | bytes 1572872 | tf_op jit(solution)/shard_map/ppermute | solution.py:90
  56.0 1.9 %collective-permute-start.11 = (bf16[2048,128]{1,0:T(8,128)(2,1)S(1)}, bf16[2048,128]{1,0:T(8,128)(2,1)S(1)}, u32[]{:S(2)}, u32[]{:S(2)}) collective-permute-start(bf16[2048,128]{1,0:T(8,128)(2,1)S(1)} %join6.1), channel_id=1, source_target_pairs={{0,6},{1,7},{2,0},{3,1},{4,2},{5,3},{6,4},{7,5},{8,14},{9,15},{10,... | collective-permute-start | bytes 1572872 | tf_op jit(solution)/shard_map/ppermute | solution.py:90
  57.9 4.7 %ffn3.1 = (f32[512,1024]{1,0:T(8,128)S(1)}, f32[512,1024]{1,0:T(8,128)S(1)}) custom-call(bf16[512,1024]{1,0:T(8,128)(2,1)S(1)} %get-tuple-element.40.refs_0_.normed, bf16[512,1024]{1,0:T(8,128)(2,1)S(1)} %collective-permute-done.4.refs_1_.refs_0_, f32[512,1024]{1,0:T(8,128)S(1)} %get-tuple-element.47.refs_2_, ...), custom_call_target="tpu_custom_call", output_to_operand_aliasing={{0}: (2, {}), {1}: (3, {})} | custom-call | flops 1 | bytes 1 | tf_op jit(solution)/shard_map/ffn3/pallas_call | solution.py:313
  62.6 5.6 %collective-permute-done.12.plus = bf16[4352,128]{1,0:T(8,128)(2,1)S(1)} collective-permute-done((bf16[4352,128]{1,0:T(8,128)(2,1)S(1)}, bf16[4352,128]{1,0:T(8,128)(2,1)S(1)}, u32[]{:S(2)}, u32[]{:S(2)}) %collective-permute-start.12) | collective-permute-done | bytes 1114144 | tf_op jit(solution)/shard_map/ppermute | solution.py:90
  68.2 1.0 %halves.1 = (bf16[2176,128]{1,0:T(8,128)(2,1)}, bf16[2176,128]{1,0:T(8,128)(2,1)}) custom-call(bf16[4352,128]{1,0:T(8,128)(2,1)S(1)} %collective-permute-done.12.plus, bf16[4352,128]{1,0:T(8,128)(2,1)S(1)} %collective-permute-done.13.minus), custom_call_target="tpu_custom_call" | custom-call | flops 1 | bytes 1 | tf_op jit(solution)/shard_map/halves/pallas_call | solution.py:265
  69.3 1.3 %ffn4.1 = f32[512,1024]{1,0:T(8,128)S(1)} custom-call(bf16[512,1024]{1,0:T(8,128)(2,1)S(1)} %collective-permute-done.4.refs_1_.refs_0_, f32[512,1024]{1,0:T(8,128)S(1)} %get-tuple-element.60.refs_1_, bf16[2048,128]{1,0:T(8,128)(2,1)S(1)} %collective-permute-done.10.refs_2_, ...), custom_call_target="tpu_custom_call", output_to_operand_aliasing={{}: (1, {})} | custom-call | flops 1 | bytes 1 | tf_op jit(solution)/shard_map/ffn4/pallas_call | solution.py:313
  70.6 2.0 %collective-permute-start.14 = (f32[512,1024]{1,0:T(8,128)S(1)}, f32[512,1024]{1,0:T(8,128)S(1)}, u32[]{:S(2)}, u32[]{:S(2)}) collective-permute-start(f32[512,1024]{1,0:T(8,128)S(1)} %ffn4.1), channel_id=1, source_target_pairs={{0,1},{1,0},{2,3},{3,2},{4,5},{5,4},{6,7},{7,6},{8,9},{9,8},{10,11... | collective-permute-start | bytes 6291464 | tf_op jit(solution)/shard_map/ppermute | solution.py:90
  72.6 1.1 %collective-permute-start.16 = (bf16[2176,128]{1,0:T(8,128)(2,1)}, bf16[2176,128]{1,0:T(8,128)(2,1)}, u32[]{:S(2)}, u32[]{:S(2)}) collective-permute-start(bf16[2176,128]{1,0:T(8,128)(2,1)} %get-tuple-element.56), channel_id=1, source_target_pairs={{0,32},{1,9},{2,34},{3,11},{4,36},{5,13},{6,38},{7,15},{8,40},{9,1... | collective-permute-start | bytes 1671176 | tf_op jit(solution)/shard_map/ppermute | solution.py:90
  73.8 1.5 %collective-permute-start.17 = (bf16[2176,128]{1,0:T(8,128)(2,1)}, bf16[2176,128]{1,0:T(8,128)(2,1)}, u32[]{:S(2)}, u32[]{:S(2)}) collective-permute-start(bf16[2176,128]{1,0:T(8,128)(2,1)} %get-tuple-element.57), channel_id=1, source_target_pairs={{0,96},{1,25},{2,98},{3,27},{4,100},{5,29},{6,102},{7,31},{8,104},... | collective-permute-start | bytes 1671176 | tf_op jit(solution)/shard_map/ppermute | solution.py:90
  75.3 1.3 %ffn5.1.mine = f32[512,1024]{1,0:T(8,128)S(1)} custom-call(bf16[512,1024]{1,0:T(8,128)(2,1)S(1)} %get-tuple-element.40.refs_0_.normed, f32[512,1024]{1,0:T(8,128)S(1)} %get-tuple-element.55.refs_1_, bf16[2048,128]{1,0:T(8,128)(2,1)S(1)} %collective-permute-done.10.refs_2_, ...), custom_call_target="tpu_custom_call", output_to_operand_aliasing={{}: (1, {})} | custom-call | flops 1 | bytes 1 | tf_op jit(solution)/shard_map/ffn5/pallas_call | solution.py:313
  76.7 2.4 %embed.1 = (bf16[512,128]{1,0:T(8,128)(2,1)}, bf16[512,128]{1,0:T(8,128)(2,1)S(1)}) custom-call(s32[4]{0:T(128)S(1)} %copy-done.3, bf16[512,1024]{1,0:T(8,128)(2,1)S(1)} %get-tuple-element.40.refs_0_.normed, f32[512,1024]{1,0:T(8,128)S(1)} %ffn5.1.mine, f32[512,1024]{1,0:T(8,128)S(1)} %collective-permute-done.14.other, f32[1,1024]{1,0:T(1,128)S(1)} %bitcast.27, ...), custom_call_target="tpu_custom_call" | custom-call | flops 1 | bytes 1 | tf_op jit(solution)/shard_map/embed/pallas_call | solution.py:340
  79.0 1.0 %collective-permute-start.15 = (bf16[512,128]{1,0:T(8,128)(2,1)S(1)}, bf16[512,128]{1,0:T(8,128)(2,1)}, u32[]{:S(2)}, u32[]{:S(2)}) collective-permute-start(bf16[512,128]{1,0:T(8,128)(2,1)S(1)} %get-tuple-element.63.emb), channel_id=1, source_target_pairs={{0,1},{1,0},{2,3},{3,2},{4,5},{5,4},{6,7},{7,6},{8,9},{9,8},{10,11... | collective-permute-start | bytes 393224 | tf_op jit(solution)/shard_map/ppermute | solution.py:90
  80.2 2.6 %collective-permute-done.16 = bf16[2176,128]{1,0:T(8,128)(2,1)} collective-permute-done((bf16[2176,128]{1,0:T(8,128)(2,1)}, bf16[2176,128]{1,0:T(8,128)(2,1)}, u32[]{:S(2)}, u32[]{:S(2)}) %collective-permute-start.16) | collective-permute-done | bytes 557088 | tf_op jit(solution)/shard_map/ppermute | solution.py:90
  82.8 4.2 %score.1 = (f32[32,128]{1,0:T(8,128)S(1)}, f32[32,128]{1,0:T(8,128)S(1)}) custom-call(s32[5]{0:T(128)S(1)} %stack.23.where, s32[32]{0:T(128)S(1)} %reshape.51.cand, s32[32]{0:T(128)S(1)} %reshape.52.pair, bf16[512,128]{1,0:T(8,128)(2,1)S(1)} %get-tuple-element.63.emb, bf16[512,128]{1,0:T(8,128)(2,1)} %collective-permute-done.15.sib, ...), custom_call_target="tpu_custom_call" | custom-call | flops 1 | bytes 1 | tf_op jit(solution)/shard_map/score/pallas_call | solution.py:409
  87.1 1.6 %collective-permute-start.18 = (f32[32,128]{1,0:T(8,128)S(1)}, f32[32,128]{1,0:T(8,128)S(1)}, u32[]{:S(2)}, u32[]{:S(2)}) collective-permute-start(f32[32,128]{1,0:T(8,128)S(1)} %get-tuple-element.65), channel_id=1, source_target_pairs={{0,1},{1,0},{2,3},{3,2},{4,5},{5,4},{6,7},{7,6},{8,9},{9,8},{10,11... | collective-permute-start | bytes 49160 | tf_op jit(solution)/shard_map/ppermute | solution.py:90
  (34 shorter events, 3.0 us)
Async XLA Ops:
  0.6 7.3 %copy-start.4 = (s32[4,8]{1,0:T(4,128)S(1)}, s32[4,8]{1,0:T(4,128)}, u32[]{:S(2)}) copy-start(s32[4,8]{1,0:T(4,128)} %param.23) | copy-start | bytes 388
  0.6 8.8 %copy-start.1 = (f32[1024]{0:T(1024)S(1)}, f32[1024]{0:T(1024)}, u32[]{:S(2)}) copy-start(f32[1024]{0:T(1024)} %param.15) | copy-start | bytes 12292
  0.7 8.8 %copy-start.3 = (s32[4]{0:T(128)S(1)}, s32[4]{0:T(128)}, u32[]{:S(2)}) copy-start(s32[4]{0:T(128)} %length.3) | copy-start | bytes 52
  2.6 20.6 %collective-permute-start = (bf16[1296,128]{1,0:T(8,128)(2,1)S(1)}, bf16[1296,128]{1,0:T(8,128)(2,1)S(1)}, u32[]{:S(2)}, u32[]{:S(2)}) collective-permute-start(bf16[1296,128]{1,0:T(8,128)(2,1)S(1)} %first.1.refs_3_), channel_id=1, source_target_pairs={{0,2},{1,3},{2,4},{3,5},{4,6},{5,7},{6,0},{7,1},{8,10},{9,11},{10,... | collective-permute-start | bytes 995336 | tf_op jit(solution)/shard_map/ppermute | solution.py:90
  4.8 18.4 %collective-permute-start.1 = (bf16[1296,128]{1,0:T(8,128)(2,1)S(1)}, bf16[1296,128]{1,0:T(8,128)(2,1)S(1)}, u32[]{:S(2)}, u32[]{:S(2)}) collective-permute-start(bf16[1296,128]{1,0:T(8,128)(2,1)S(1)} %first.1.refs_3_), channel_id=1, source_target_pairs={{0,6},{1,7},{2,0},{3,1},{4,2},{5,3},{6,4},{7,5},{8,14},{9,15},{10,... | collective-permute-start | bytes 995336 | tf_op jit(solution)/shard_map/ppermute | solution.py:90
  6.3 16.9 %collective-permute-start.2 = (bf16[1296,128]{1,0:T(8,128)(2,1)S(1)}, bf16[1296,128]{1,0:T(8,128)(2,1)S(1)}, u32[]{:S(2)}, u32[]{:S(2)}) collective-permute-start(bf16[1296,128]{1,0:T(8,128)(2,1)S(1)} %first.1.refs_3_), channel_id=1, source_target_pairs={{0,4},{1,5},{2,6},{3,7},{4,0},{5,1},{6,2},{7,3},{8,12},{9,13},{10,... | collective-permute-start | bytes 995336 | tf_op jit(solution)/shard_map/ppermute | solution.py:90
  7.9 15.3 %collective-permute-start.3 = (s32[4,8]{1,0:T(4,128)S(1)}, s32[4,8]{1,0:T(4,128)S(1)}, u32[]{:S(2)}, u32[]{:S(2)}) collective-permute-start(s32[4,8]{1,0:T(4,128)S(1)} %copy-done.4), channel_id=1, source_target_pairs={{0,1},{1,0},{2,3},{3,2},{4,5},{5,4},{6,7},{7,6},{8,9},{9,8},{10,11... | collective-permute-start | bytes 392 | tf_op jit(solution)/shard_map/ppermute | solution.py:90
  23.3 5.2 %collective-permute-start.4 = (bf16[512,1024]{1,0:T(8,128)(2,1)S(1)}, bf16[512,1024]{1,0:T(8,128)(2,1)S(1)}, u32[]{:S(2)}, u32[]{:S(2)}) collective-permute-start(bf16[512,1024]{1,0:T(8,128)(2,1)S(1)} %get-tuple-element.40.refs_0_.normed), channel_id=1, source_target_pairs={{0,1},{1,0},{2,3},{3,2},{4,5},{5,4},{6,7},{7,6},{8,9},{9,8},{10,11... | collective-permute-start | bytes 3145736 | tf_op jit(solution)/shard_map/ppermute | solution.py:90
  23.5 16.4 %collective-permute-start.5 = (bf16[4160,128]{1,0:T(8,128)(2,1)S(1)}, bf16[4160,128]{1,0:T(8,128)(2,1)S(1)}, u32[]{:S(2)}, u32[]{:S(2)}) collective-permute-start(bf16[4160,128]{1,0:T(8,128)(2,1)S(1)} %join1.1.refs_0_), channel_id=1, source_target_pairs={{0,8},{1,33},{2,10},{3,35},{4,12},{5,37},{6,14},{7,39},{8,16},{9,4... | collective-permute-start | bytes 3194888 | tf_op jit(solution)/shard_map/ppermute | solution.py:90
  25.1 25.5 %collective-permute-start.6 = (bf16[4160,128]{1,0:T(8,128)(2,1)S(1)}, bf16[4160,128]{1,0:T(8,128)(2,1)S(1)}, u32[]{:S(2)}, u32[]{:S(2)}) collective-permute-start(bf16[4160,128]{1,0:T(8,128)(2,1)S(1)} %join1.1.refs_0_), channel_id=1, source_target_pairs={{0,24},{1,97},{2,26},{3,99},{4,28},{5,101},{6,30},{7,103},{8,0},{9... | collective-permute-start | bytes 3194888 | tf_op jit(solution)/shard_map/ppermute | solution.py:90
  27.3 24.9 %collective-permute-start.7 = (bf16[4160,128]{1,0:T(8,128)(2,1)S(1)}, bf16[4160,128]{1,0:T(8,128)(2,1)S(1)}, u32[]{:S(2)}, u32[]{:S(2)}) collective-permute-start(bf16[4160,128]{1,0:T(8,128)(2,1)S(1)} %join1.1.refs_0_), channel_id=1, source_target_pairs={{0,16},{1,65},{2,18},{3,67},{4,20},{5,69},{6,22},{7,71},{8,24},{9,... | collective-permute-start | bytes 3194888 | tf_op jit(solution)/shard_map/ppermute | solution.py:90
  28.5 26.5 %collective-permute-start.8 = (bf16[4096,128]{1,0:T(8,128)(2,1)S(1)}, bf16[4096,128]{1,0:T(8,128)(2,1)S(1)}, u32[]{:S(2)}, u32[]{:S(2)}) collective-permute-start(bf16[4096,128]{1,0:T(8,128)(2,1)S(1)} %bitcast.20), channel_id=1, source_target_pairs={{0,2},{1,3},{2,4},{3,5},{4,6},{5,7},{6,0},{7,1},{8,10},{9,11},{10,... | collective-permute-start | bytes 3145736 | tf_op jit(solution)/shard_map/ppermute | solution.py:90
  29.4 25.6 %collective-permute-start.9 = (bf16[4096,128]{1,0:T(8,128)(2,1)S(1)}, bf16[4096,128]{1,0:T(8,128)(2,1)S(1)}, u32[]{:S(2)}, u32[]{:S(2)}) collective-permute-start(bf16[4096,128]{1,0:T(8,128)(2,1)S(1)} %bitcast.21), channel_id=1, source_target_pairs={{0,6},{1,7},{2,0},{3,1},{4,2},{5,3},{6,4},{7,5},{8,14},{9,15},{10,... | collective-permute-start | bytes 3145736 | tf_op jit(solution)/shard_map/ppermute | solution.py:90
  52.3 15.9 %collective-permute-start.12 = (bf16[4352,128]{1,0:T(8,128)(2,1)S(1)}, bf16[4352,128]{1,0:T(8,128)(2,1)S(1)}, u32[]{:S(2)}, u32[]{:S(2)}) collective-permute-start(bf16[4352,128]{1,0:T(8,128)(2,1)S(1)} %join2.1), channel_id=1, source_target_pairs={{0,32},{1,9},{2,34},{3,11},{4,36},{5,13},{6,38},{7,15},{8,40},{9,1... | collective-permute-start | bytes 3342344 | tf_op jit(solution)/shard_map/ppermute | solution.py:90
  53.6 14.6 %collective-permute-start.13 = (bf16[4352,128]{1,0:T(8,128)(2,1)S(1)}, bf16[4352,128]{1,0:T(8,128)(2,1)S(1)}, u32[]{:S(2)}, u32[]{:S(2)}) collective-permute-start(bf16[4352,128]{1,0:T(8,128)(2,1)S(1)} %join2.1), channel_id=1, source_target_pairs={{0,96},{1,25},{2,98},{3,27},{4,100},{5,29},{6,102},{7,31},{8,104},... | collective-permute-start | bytes 3342344 | tf_op jit(solution)/shard_map/ppermute | solution.py:90
  55.1 14.2 %collective-permute-start.10 = (bf16[2048,128]{1,0:T(8,128)(2,1)S(1)}, bf16[2048,128]{1,0:T(8,128)(2,1)S(1)}, u32[]{:S(2)}, u32[]{:S(2)}) collective-permute-start(bf16[2048,128]{1,0:T(8,128)(2,1)S(1)} %join5.1), channel_id=1, source_target_pairs={{0,2},{1,3},{2,4},{3,5},{4,6},{5,7},{6,0},{7,1},{8,10},{9,11},{10,... | collective-permute-start | bytes 1572872 | tf_op jit(solution)/shard_map/ppermute | solution.py:90
  56.0 13.2 %collective-permute-start.11 = (bf16[2048,128]{1,0:T(8,128)(2,1)S(1)}, bf16[2048,128]{1,0:T(8,128)(2,1)S(1)}, u32[]{:S(2)}, u32[]{:S(2)}) collective-permute-start(bf16[2048,128]{1,0:T(8,128)(2,1)S(1)} %join6.1), channel_id=1, source_target_pairs={{0,6},{1,7},{2,0},{3,1},{4,2},{5,3},{6,4},{7,5},{8,14},{9,15},{10,... | collective-permute-start | bytes 1572872 | tf_op jit(solution)/shard_map/ppermute | solution.py:90
  70.6 6.0 %collective-permute-start.14 = (f32[512,1024]{1,0:T(8,128)S(1)}, f32[512,1024]{1,0:T(8,128)S(1)}, u32[]{:S(2)}, u32[]{:S(2)}) collective-permute-start(f32[512,1024]{1,0:T(8,128)S(1)} %ffn4.1), channel_id=1, source_target_pairs={{0,1},{1,0},{2,3},{3,2},{4,5},{5,4},{6,7},{7,6},{8,9},{9,8},{10,11... | collective-permute-start | bytes 6291464 | tf_op jit(solution)/shard_map/ppermute | solution.py:90
  72.6 10.2 %collective-permute-start.16 = (bf16[2176,128]{1,0:T(8,128)(2,1)}, bf16[2176,128]{1,0:T(8,128)(2,1)}, u32[]{:S(2)}, u32[]{:S(2)}) collective-permute-start(bf16[2176,128]{1,0:T(8,128)(2,1)} %get-tuple-element.56), channel_id=1, source_target_pairs={{0,32},{1,9},{2,34},{3,11},{4,36},{5,13},{6,38},{7,15},{8,40},{9,1... | collective-permute-start | bytes 1671176 | tf_op jit(solution)/shard_map/ppermute | solution.py:90
  73.8 9.1 %collective-permute-start.17 = (bf16[2176,128]{1,0:T(8,128)(2,1)}, bf16[2176,128]{1,0:T(8,128)(2,1)}, u32[]{:S(2)}, u32[]{:S(2)}) collective-permute-start(bf16[2176,128]{1,0:T(8,128)(2,1)} %get-tuple-element.57), channel_id=1, source_target_pairs={{0,96},{1,25},{2,98},{3,27},{4,100},{5,29},{6,102},{7,31},{8,104},... | collective-permute-start | bytes 1671176 | tf_op jit(solution)/shard_map/ppermute | solution.py:90
  75.3 1.3 %copy-start = (bf16[1024,128]{1,0:T(8,128)(2,1)S(1)}, bf16[1024,128]{1,0:T(8,128)(2,1)}, u32[]{:S(2)}) copy-start(bf16[1024,128]{1,0:T(8,128)(2,1)} %we.1) | copy-start | bytes 786436
  75.3 1.3 %copy-start.2 = (f32[1024]{0:T(1024)S(1)}, f32[1024]{0:T(1024)}, u32[]{:S(2)}) copy-start(f32[1024]{0:T(1024)} %param.18) | copy-start | bytes 12292
  79.0 3.8 %collective-permute-start.15 = (bf16[512,128]{1,0:T(8,128)(2,1)S(1)}, bf16[512,128]{1,0:T(8,128)(2,1)}, u32[]{:S(2)}, u32[]{:S(2)}) collective-permute-start(bf16[512,128]{1,0:T(8,128)(2,1)S(1)} %get-tuple-element.63.emb), channel_id=1, source_target_pairs={{0,1},{1,0},{2,3},{3,2},{4,5},{5,4},{6,7},{7,6},{8,9},{9,8},{10,11... | collective-permute-start | bytes 393224 | tf_op jit(solution)/shard_map/ppermute | solution.py:90
  87.1 2.5 %collective-permute-start.18 = (f32[32,128]{1,0:T(8,128)S(1)}, f32[32,128]{1,0:T(8,128)S(1)}, u32[]{:S(2)}, u32[]{:S(2)}) collective-permute-start(f32[32,128]{1,0:T(8,128)S(1)} %get-tuple-element.65), channel_id=1, source_target_pairs={{0,1},{1,0},{2,3},{3,2},{4,5},{5,4},{6,7},{7,6},{8,9},{9,8},{10,11... | collective-permute-start | bytes 49160 | tf_op jit(solution)/shard_map/ppermute | solution.py:90

commit v7 on v6

--- a/solution.py
+++ b/solution.py
@@ -109,13 +109,14 @@
 SMEM = pl.BlockSpec(memory_space=pltpu.SMEM)
 
 
-def first_body(where, up, down, docs, lengths, out, held, turned, limits, sems):
+def first_body(where, up, down, docs, lengths, qkv, out, query, held, turned, limits, sems):
     index = where[4]
     lanes = pl.ds(pl.multiple_of(256 + (index >> 1) * LANES, LANES), LANES)
     copies = [pltpu.make_async_copy(w.at[:, lanes], held.at[k], sems.at[k]) for k, w in enumerate((up, down))]
     tokens = DOC_ROWS - 16
     copies.append(pltpu.make_async_copy(docs, out.at[PART : PART + tokens], sems.at[2]))
     copies.append(pltpu.make_async_copy(lengths, limits, sems.at[3]))
+    copies.append(pltpu.make_async_copy(qkv.at[:, :D], query, sems.at[4]))
     for copy in copies:
         copy.start()
     start = pl.multiple_of((index & 1) * SLICE, SLICE)
@@ -132,24 +133,25 @@
         limit = jnp.where(row == j, limits[j].astype(f32), limit)
     out[PART + tokens : BLOCK, :] = limit.astype(bf16)
     copies[2].wait()
-
-
-def first(where, up, down, docs, lengths):
+    copies[4].wait()
+
+
+def first(where, up, down, docs, lengths, qkv):
     return pl.pallas_call(
         first_body,
-        out_shape=jax.ShapeDtypeStruct((BLOCK, LANES), bf16),
-        in_specs=[SMEM] + hbm(4),
-        out_specs=vmem()[0],
+        out_shape=(jax.ShapeDtypeStruct((BLOCK, LANES), bf16), jax.ShapeDtypeStruct((D, D), bf16)),
+        in_specs=[SMEM] + hbm(5),
+        out_specs=tuple(vmem(2)),
         scratch_shapes=[
             pltpu.VMEM((2, D, LANES), bf16),
             pltpu.VMEM((SLABS, LANES, LANES), bf16),
             pltpu.SMEM((8,), jnp.int32),
-            pltpu.SemaphoreType.DMA((4,)),
+            pltpu.SemaphoreType.DMA((5,)),
         ],
         compiler_params=params(8),
         cost_estimate=LIGHT,
         name="first",
-    )(where, *pinned(up, down, docs, lengths))
+    )(where, *pinned(up, down, docs, lengths, qkv))
 
 
 def join_body(takes, *refs):
@@ -171,29 +173,31 @@
     )(*arrays)
 
 
+def norm_into(out, values, gain, block=32):
+    for at in range(0, out.shape[0], block):
+        rows = slice(at, at + block)
+        out[rows, :] = norm_rows(values(rows), gain).astype(bf16)
+
+
 def attend_body(
-    length, tok_hbm, qkv, wo_hbm, up, down, gain, out, low_out, high_out, packed, context, tok, held, wo, wide, sems
+    length, qkv, wo_hbm, up, down, tok, query, gain, out, low_out, high_out, packed, context, held, wo, wide, added, sems
 ):
     rows_all = tok.shape[0]
     step = 512
-    copies = [pltpu.make_async_copy(tok_hbm, tok, sems.at[0])]
-    for i in range(6):
+    sources = [(qkv.at[:, D + c : D + c + step], held.at[:, c : c + step]) for c in range(0, 2 * D, step)]
+    sources += [(up, wide.at[0]), (down, wide.at[1]), (wo_hbm, wo)]
+    copies = [pltpu.make_async_copy(source, target, sems.at[i]) for i, (source, target) in enumerate(sources)]
+    for copy in copies[:4]:
+        copy.start()
+    packed[:, :D] = dot(tok[...], query[...]).astype(bf16)
+    for copy in copies[4:]:
+        copy.start()
+    for i in range(4):
+        copies[i].wait()
         columns = slice(i * step, (i + 1) * step)
-        copies.append(pltpu.make_async_copy(qkv.at[:, columns], held.at[:, columns], sems.at[1 + i]))
-    copies.append(pltpu.make_async_copy(up, wide.at[0], sems.at[7]))
-    copies.append(pltpu.make_async_copy(down, wide.at[1], sems.at[8]))
-    copies.append(pltpu.make_async_copy(wo_hbm, wo, sems.at[9]))
-    for copy in copies[:3]:
-        copy.start()
-    copies[0].wait()
-    for i in range(6):
-        columns = slice(i * step, (i + 1) * step)
-        copies[1 + i].wait()
-        copies[3 + i].start()
-        packed[:, columns] = dot(tok[...], held[:, columns]).astype(bf16)
-    copies[9].start()
+        packed[:, D + i * step : D + (i + 1) * step] = dot(tok[...], held[:, columns]).astype(bf16)
     for k in range(2):
-        copies[7 + k].wait()
+        copies[4 + k].wait()
         for j in range(HALF):
             rows = slice(j * LANES, (j + 1) * LANES)
             low_out[k * HALF + j] = wide[k, rows, :256].T
@@ -219,32 +223,32 @@
         return carry
 
     lax.fori_loop(0, rows_all // SEQ, request, 0)
-    copies[9].wait()
-    attended = dot(context[...], wo[...])
-    out[...] = norm_rows(tok[...].astype(f32) + attended, gain[...]).astype(bf16)
-
-
-def attend(tokens, qkv, wo, gain, length, up, down):
+    copies[6].wait()
+    added[...] = dot(context[...], wo[...])
+    norm_into(out, lambda rows: tok[rows, :].astype(f32) + added[rows, :], gain[...])
+
+
+def attend(tokens, qkv, query, wo, gain, length, up, down):
     rows = tokens.shape[0]
     piece = jax.ShapeDtypeStruct((SLABS, 256, LANES), bf16)
     normed, low, high = pl.pallas_call(
         attend_body,
         out_shape=(jax.ShapeDtypeStruct((rows, D), bf16), piece, piece),
-        in_specs=[SMEM] + hbm(5) + vmem(1),
+        in_specs=[SMEM] + hbm(4) + vmem(3),
         out_specs=tuple(vmem(3)),
         scratch_shapes=[
             pltpu.VMEM((rows, 3 * D), bf16),
             pltpu.VMEM((rows, D), bf16),
-            pltpu.VMEM((rows, D), bf16),
-            pltpu.VMEM((D, 3 * D), bf16),
+            pltpu.VMEM((D, 2 * D), bf16),
             pltpu.VMEM((D, D), bf16),
             pltpu.VMEM((2, D, 512), bf16),
-            pltpu.SemaphoreType.DMA((10,)),
+            pltpu.VMEM((rows, D), f32),
+            pltpu.SemaphoreType.DMA((7,)),
         ],
         compiler_params=params(28),
         cost_estimate=LIGHT,
         name="attend",
-    )(length, *pinned(tokens, qkv, wo, up, down), gain.reshape(1, D))
+    )(length, *pinned(qkv, wo, up, down), tokens, query, gain.reshape(1, D))
     return normed, low.reshape(-1, LANES), high.reshape(-1, LANES)
 
 
@@ -323,9 +327,11 @@
     )(*tail)
 
 
-def embed_body(length, normed, mine, other, gain, we, out, kept):
-    layer = norm_rows(normed[...].astype(f32) + (mine[...] + other[...]), gain[...]).astype(bf16)
-    projected = dot(layer, we[...])
+def embed_body(length, normed, mine, other, gain, we, out, kept, layer):
+    norm_into(
+        layer, lambda rows: normed[rows, :].astype(f32) + (mine[rows, :] + other[rows, :]), gain[...]
+    )
+    projected = dot(layer[...], we[...])
     unit = projected * lax.rsqrt(jnp.sum(projected * projected, axis=-1, keepdims=True) + 1e-06)
     slot = lax.broadcasted_iota(jnp.int32, (SEQ, P_SIZE), 0)
     for r in range(normed.shape[0] // SEQ):
@@ -342,6 +348,7 @@
         out_shape=(shape, shape),
         in_specs=[SMEM] + vmem(5),
         out_specs=tuple(vmem(2)),
+        scratch_shapes=[pltpu.VMEM(normed.shape, bf16)],
         compiler_params=params(12),
         cost_estimate=LIGHT,
         name="embed",
@@ -387,20 +394,26 @@
     for copy in copies:
         copy.wait()
     per = cand.shape[0]
-    for i in range(2 * per):
-        e = cand[i] if i < per else pair[i - per]
-        tokens = emb if i < per else sib
-        j, req = e & 7, e >> 3
-        sz, sx = slot(((req >> 2) - z) & 3), slot(((req & 3) - x) & 3)
-        outer = jnp.where(c == 0, sz, sx)
-        within = jnp.where(c == 0, sx, sz)
-        block = held[outer, within, :, pl.ds(pl.multiple_of(j * TOKS, TOKS), TOKS), :]
-        lens = held[outer, within, 0, 8 * TOKS : DOC_ROWS, :].astype(f32)
-        limit = jnp.sum(jnp.where(row == j, lens, 0.0), axis=0, keepdims=True)
-        r = (i % per) // 8
-        sims = dot_t(block.reshape(4 * TOKS, P_SIZE), tokens[r * SEQ : (r + 1) * SEQ, :])
-        at = i % per
-        outs[i // per][at : at + 1, :] = jnp.max(jnp.where(pos < limit, sims, DEAD), axis=0, keepdims=True)
+    picks = 8
+    for first_pick in range(0, 2 * per, picks):
+        blocks, limits = [], []
+        for i in range(first_pick, first_pick + picks):
+            e = cand[i] if i < per else pair[i - per]
+            j, req = e & 7, e >> 3
+            sz, sx = slot(((req >> 2) - z) & 3), slot(((req & 3) - x) & 3)
+            outer = jnp.where(c == 0, sz, sx)
+            within = jnp.where(c == 0, sx, sz)
+            block = held[outer, within, :, pl.ds(pl.multiple_of(j * TOKS, TOKS), TOKS), :]
+            blocks.append(block.reshape(4 * TOKS, P_SIZE))
+            lens = held[outer, within, 0, 8 * TOKS : DOC_ROWS, :].astype(f32)
+            limits.append(jnp.sum(jnp.where(row == j, lens, 0.0), axis=0, keepdims=True))
+        at = first_pick % per
+        tokens = emb if first_pick < per else sib
+        r = at // picks
+        sims = dot_t(jnp.concatenate(blocks, axis=0), tokens[r * SEQ : (r + 1) * SEQ, :])
+        for k in range(picks):
+            some = jnp.where(pos < limits[k], sims[k * 4 * TOKS : (k + 1) * 4 * TOKS], DEAD)
+            outs[first_pick // per][at + k : at + k + 1, :] = jnp.max(some, axis=0, keepdims=True)
 
 
 def score(where, cand, pair, emb, sib, docs):
@@ -438,10 +451,12 @@
     req, mlp = lax.axis_index("req"), lax.axis_index("mlp")
     z, x, y, c = req // 4, req % 4, mlp // 2, mlp % 2
     where = jnp.stack([z, x, y, c, jnp.where(c == 0, x, z)]).astype(jnp.int32)
-    start = first(where, up_weight, down_weight, documents.reshape(-1, P_SIZE), document_length)
+    start, query = first(
+        where, up_weight, down_weight, documents.reshape(-1, P_SIZE), document_length, attend_weight
+    )
     near = [send(start, way) for way in ("y+", "y-", "y2")]
     normed, low, high = attend(
-        tokens, attend_weight, output_weight, after(attend_gain, start), query_length, up_weight, down_weight
+        tokens, attend_weight, query, output_weight, attend_gain, query_length, up_weight, down_weight
     )
     pair = send(after(candidates, start), "c")
     near, pair = after((tuple(near), pair), normed)

time: 90.4 us -> 89.8 us (level)
  Pallas kernels: 36.9 us -> 35.7 us
    pallas_call x1, Pallas kernels: 13.7 us -> 12.7 us  [attend(): pl.pallas_call(attend_body, out_shape=(jax.ShapeDtypeStruct((rows, D), bf...]
  transfers between devices with their start and end apart: 19 -> 19, of which waited for: 6 -> 6; matrix products, arithmetic and copies ran while one was open for 0% -> 0% of each run, Pallas kernels for 32% -> 31%
where the time goes in v7:
time: 89.8 us; the launch traced here: 89.6 us
  Pallas kernels  35.7 us (40%)
  starting transfers between devices  28.3 us (32%)
  waiting for transfers between devices  24.5 us (27%)
    ppermute x19, starting transfers between devices, send(): return lax.ppermute(value, ('req', 'mlp'), STEPS[way])  28.3 us
    ppermute x19, waiting for transfers between devices, send(): return lax.ppermute(value, ('req', 'mlp'), STEPS[way])  24.5 us
    pallas_call x5, Pallas kernels, ffn(): pl.pallas_call(functools.partial(ffn_body, tuple(pieces), len(arrays), se...  12.9 us
    pallas_call x1, Pallas kernels, attend(): pl.pallas_call(attend_body, out_shape=(jax.ShapeDtypeStruct((rows, D), bf...  12.7 us
    pallas_call x1, Pallas kernels, score(): pl.pallas_call(score_body, out_shape=(jax.ShapeDtypeStruct((total, SEQ),...  3.53 us
    pallas_call x1, Pallas kernels, first(): pl.pallas_call(first_body, out_shape=(jax.ShapeDtypeStruct((BLOCK, LANES)...  2.4 us
    pallas_call x1, Pallas kernels, embed(): pl.pallas_call(embed_body, out_shape=(shape, shape), in_specs=[SMEM] + vm...  2.36 us
  transfers between devices with their start and end apart: 19, of which 6 were waited for; matrix products, arithmetic and copies ran while one was open for 0% of the time, Pallas kernels for 31%

profile of v7, /device:TPU:1, one launch (start us, length us, event | category | flops | bytes accessed | tf_op | source)
XLA Modules:
  0.0 89.6 jit_solution(4397151456854970527)
XLA Ops:
  0.8 2.4 %first.1 = (bf16[1296,128]{1,0:T(8,128)(2,1)S(1)}, bf16[1024,1024]{1,0:T(8,128)(2,1)S(1)}) custom-call(s32[5]{0:T(128)S(1)} %stack.23.where, bf16[1024,512]{1,0:T(8,128)(2,1)} %up.3, bf16[1024,512]{1,0:T(8,128)(2,1)} %down.3, bf16[256,128]{1,0:T(8,128)(2,1)} %bitcast.28, s32[8]{0:T(128)} %lengths.1, bf16[1024,3072]{1,0:T(8,128)(2,1)} %qkv.3), custom_call_target="tpu_custom_call" | custom-call | flops 1 | bytes 1 | tf_op jit(solution)/shard_map/first/pallas_call | solution.py:140
  3.2 2.2 %collective-permute-start = (bf16[1296,128]{1,0:T(8,128)(2,1)S(1)}, bf16[1296,128]{1,0:T(8,128)(2,1)S(1)}, u32[]{:S(2)}, u32[]{:S(2)}) collective-permute-start(bf16[1296,128]{1,0:T(8,128)(2,1)S(1)} %get-tuple-element.37.refs_3_), channel_id=1, source_target_pairs={{0,2},{1,3},{2,4},{3,5},{4,6},{5,7},{6,0},{7,1},{8,10},{9,11},{10,... | collective-permute-start | bytes 995336 | tf_op jit(solution)/shard_map/ppermute | solution.py:90
  5.4 1.5 %collective-permute-start.1 = (bf16[1296,128]{1,0:T(8,128)(2,1)S(1)}, bf16[1296,128]{1,0:T(8,128)(2,1)S(1)}, u32[]{:S(2)}, u32[]{:S(2)}) collective-permute-start(bf16[1296,128]{1,0:T(8,128)(2,1)S(1)} %get-tuple-element.37.refs_3_), channel_id=1, source_target_pairs={{0,6},{1,7},{2,0},{3,1},{4,2},{5,3},{6,4},{7,5},{8,14},{9,15},{10,... | collective-permute-start | bytes 995336 | tf_op jit(solution)/shard_map/ppermute | solution.py:90
  6.9 1.6 %collective-permute-start.2 = (bf16[1296,128]{1,0:T(8,128)(2,1)S(1)}, bf16[1296,128]{1,0:T(8,128)(2,1)S(1)}, u32[]{:S(2)}, u32[]{:S(2)}) collective-permute-start(bf16[1296,128]{1,0:T(8,128)(2,1)S(1)} %get-tuple-element.37.refs_3_), channel_id=1, source_target_pairs={{0,4},{1,5},{2,6},{3,7},{4,0},{5,1},{6,2},{7,3},{8,12},{9,13},{10,... | collective-permute-start | bytes 995336 | tf_op jit(solution)/shard_map/ppermute | solution.py:90
  8.5 1.5 %collective-permute-start.3 = (s32[4,8]{1,0:T(4,128)S(1)}, s32[4,8]{1,0:T(4,128)S(1)}, u32[]{:S(2)}, u32[]{:S(2)}) collective-permute-start(s32[4,8]{1,0:T(4,128)S(1)} %copy-done.5), channel_id=1, source_target_pairs={{0,1},{1,0},{2,3},{3,2},{4,5},{5,4},{6,7},{7,6},{8,9},{9,8},{10,11... | collective-permute-start | bytes 392 | tf_op jit(solution)/shard_map/ppermute | solution.py:90
  10.0 12.7 %attend.1 = (bf16[512,1024]{1,0:T(8,128)(2,1)S(1)}, bf16[16,256,128]{2,1,0:T(8,128)(2,1)S(1)}, bf16[16,256,128]{2,1,0:T(8,128)(2,1)S(1)}) custom-call(s32[4]{0:T(128)S(1)} %copy-done.4, bf16[1024,3072]{1,0:T(8,128)(2,1)} %qkv.3, bf16[1024,1024]{1,0:T(8,128)(2,1)} %wo_hbm.1, bf16[1024,512]{1,0:T(8,128)(2,1)} %up.3, bf16[1024,512]{1,0:T(8,128)(2,1)} %down.3, ...), custom_call_target="tpu_custom_call" | custom-call | flops 1 | bytes 1 | tf_op jit(solution)/shard_map/attend/pallas_call | solution.py:234
  22.8 1.2 %collective-permute-start.4 = (bf16[512,1024]{1,0:T(8,128)(2,1)S(1)}, bf16[512,1024]{1,0:T(8,128)(2,1)S(1)}, u32[]{:S(2)}, u32[]{:S(2)}) collective-permute-start(bf16[512,1024]{1,0:T(8,128)(2,1)S(1)} %get-tuple-element.42.refs_0_.normed), channel_id=1, source_target_pairs={{0,1},{1,0},{2,3},{3,2},{4,5},{5,4},{6,7},{7,6},{8,9},{9,8},{10,11... | collective-permute-start | bytes 3145736 | tf_op jit(solution)/shard_map/ppermute | solution.py:90
  24.0 1.6 %collective-permute-start.5 = (bf16[4160,128]{1,0:T(8,128)(2,1)S(1)}, bf16[4160,128]{1,0:T(8,128)(2,1)S(1)}, u32[]{:S(2)}, u32[]{:S(2)}) collective-permute-start(bf16[4160,128]{1,0:T(8,128)(2,1)S(1)} %join1.1.refs_0_), channel_id=1, source_target_pairs={{0,8},{1,33},{2,10},{3,35},{4,12},{5,37},{6,14},{7,39},{8,16},{9,4... | collective-permute-start | bytes 3194888 | tf_op jit(solution)/shard_map/ppermute | solution.py:90
  25.6 2.1 %collective-permute-start.6 = (bf16[4160,128]{1,0:T(8,128)(2,1)S(1)}, bf16[4160,128]{1,0:T(8,128)(2,1)S(1)}, u32[]{:S(2)}, u32[]{:S(2)}) collective-permute-start(bf16[4160,128]{1,0:T(8,128)(2,1)S(1)} %join1.1.refs_0_), channel_id=1, source_target_pairs={{0,24},{1,97},{2,26},{3,99},{4,28},{5,101},{6,30},{7,103},{8,0},{9... | collective-permute-start | bytes 3194888 | tf_op jit(solution)/shard_map/ppermute | solution.py:90
  27.8 1.3 %collective-permute-start.7 = (bf16[4160,128]{1,0:T(8,128)(2,1)S(1)}, bf16[4160,128]{1,0:T(8,128)(2,1)S(1)}, u32[]{:S(2)}, u32[]{:S(2)}) collective-permute-start(bf16[4160,128]{1,0:T(8,128)(2,1)S(1)} %join1.1.refs_0_), channel_id=1, source_target_pairs={{0,16},{1,65},{2,18},{3,67},{4,20},{5,69},{6,22},{7,71},{8,24},{9,... | collective-permute-start | bytes 3194888 | tf_op jit(solution)/shard_map/ppermute | solution.py:90
  29.9 1.8 %collective-permute-start.9 = (bf16[4096,128]{1,0:T(8,128)(2,1)S(1)}, bf16[4096,128]{1,0:T(8,128)(2,1)S(1)}, u32[]{:S(2)}, u32[]{:S(2)}) collective-permute-start(bf16[4096,128]{1,0:T(8,128)(2,1)S(1)} %bitcast.21), channel_id=1, source_target_pairs={{0,6},{1,7},{2,0},{3,1},{4,2},{5,3},{6,4},{7,5},{8,14},{9,15},{10,... | collective-permute-start | bytes 3145736 | tf_op jit(solution)/shard_map/ppermute | solution.py:90
  31.7 2.5 %ffn1.1 = (f32[512,1024]{1,0:T(8,128)S(1)}, f32[512,1024]{1,0:T(8,128)S(1)}) custom-call(bf16[512,1024]{1,0:T(8,128)(2,1)S(1)} %get-tuple-element.42.refs_0_.normed, bf16[512,1024]{1,0:T(8,128)(2,1)S(1)} %collective-permute-done.4.refs_1_.refs_0_, bf16[4096,128]{1,0:T(8,128)(2,1)S(1)} %bitcast.22, bf16[4096,128]{1,0:T(8,128)(2,1)S(1)} %bitcast.23), custom_call_target="tpu_custom_call" | custom-call | flops 1 | bytes 1 | tf_op jit(solution)/shard_map/ffn1/pallas_call | solution.py:317
  34.2 6.2 %collective-permute-done.5.refs_7_.refs_1_ = bf16[4160,128]{1,0:T(8,128)(2,1)S(1)} collective-permute-done((bf16[4160,128]{1,0:T(8,128)(2,1)S(1)}, bf16[4160,128]{1,0:T(8,128)(2,1)S(1)}, u32[]{:S(2)}, u32[]{:S(2)}) %collective-permute-start.5) | collective-permute-done | bytes 1064992 | tf_op jit(solution)/shard_map/ppermute | solution.py:90
  40.4 3.0 %ffn2.1 = (f32[512,1024]{1,0:T(8,128)S(1)}, f32[512,1024]{1,0:T(8,128)S(1)}) custom-call(bf16[512,1024]{1,0:T(8,128)(2,1)S(1)} %get-tuple-element.42.refs_0_.normed, bf16[512,1024]{1,0:T(8,128)(2,1)S(1)} %collective-permute-done.4.refs_1_.refs_0_, f32[512,1024]{1,0:T(8,128)S(1)} %get-tuple-element.45.refs_2_, ...), custom_call_target="tpu_custom_call", output_to_operand_aliasing={{0}: (2, {}), {1}: (3, {})} | custom-call | flops 1 | bytes 1 | tf_op jit(solution)/shard_map/ffn2/pallas_call | solution.py:317
  43.5 7.6 %collective-permute-done.6.refs_2_.refs_4_ = bf16[4160,128]{1,0:T(8,128)(2,1)S(1)} collective-permute-done((bf16[4160,128]{1,0:T(8,128)(2,1)S(1)}, bf16[4160,128]{1,0:T(8,128)(2,1)S(1)}, u32[]{:S(2)}, u32[]{:S(2)}) %collective-permute-start.6) | collective-permute-done | bytes 1064992 | tf_op jit(solution)/shard_map/ppermute | solution.py:90
  51.1 1.6 %collective-permute-done.7.refs_3_.refs_5_ = bf16[4160,128]{1,0:T(8,128)(2,1)S(1)} collective-permute-done((bf16[4160,128]{1,0:T(8,128)(2,1)S(1)}, bf16[4160,128]{1,0:T(8,128)(2,1)S(1)}, u32[]{:S(2)}, u32[]{:S(2)}) %collective-permute-start.7) | collective-permute-done | bytes 1064992 | tf_op jit(solution)/shard_map/ppermute | solution.py:90
  52.8 1.3 %collective-permute-start.12 = (bf16[4352,128]{1,0:T(8,128)(2,1)S(1)}, bf16[4352,128]{1,0:T(8,128)(2,1)S(1)}, u32[]{:S(2)}, u32[]{:S(2)}) collective-permute-start(bf16[4352,128]{1,0:T(8,128)(2,1)S(1)} %join2.1), channel_id=1, source_target_pairs={{0,32},{1,9},{2,34},{3,11},{4,36},{5,13},{6,38},{7,15},{8,40},{9,1... | collective-permute-start | bytes 3342344 | tf_op jit(solution)/shard_map/ppermute | solution.py:90
  54.1 1.5 %collective-permute-start.13 = (bf16[4352,128]{1,0:T(8,128)(2,1)S(1)}, bf16[4352,128]{1,0:T(8,128)(2,1)S(1)}, u32[]{:S(2)}, u32[]{:S(2)}) collective-permute-start(bf16[4352,128]{1,0:T(8,128)(2,1)S(1)} %join2.1), channel_id=1, source_target_pairs={{0,96},{1,25},{2,98},{3,27},{4,100},{5,29},{6,102},{7,31},{8,104},... | collective-permute-start | bytes 3342344 | tf_op jit(solution)/shard_map/ppermute | solution.py:90
  56.5 1.9 %collective-permute-start.11 = (bf16[2048,128]{1,0:T(8,128)(2,1)S(1)}, bf16[2048,128]{1,0:T(8,128)(2,1)S(1)}, u32[]{:S(2)}, u32[]{:S(2)}) collective-permute-start(bf16[2048,128]{1,0:T(8,128)(2,1)S(1)} %join6.1), channel_id=1, source_target_pairs={{0,6},{1,7},{2,0},{3,1},{4,2},{5,3},{6,4},{7,5},{8,14},{9,15},{10,... | collective-permute-start | bytes 1572872 | tf_op jit(solution)/shard_map/ppermute | solution.py:90
  58.4 4.7 %ffn3.1 = (f32[512,1024]{1,0:T(8,128)S(1)}, f32[512,1024]{1,0:T(8,128)S(1)}) custom-call(bf16[512,1024]{1,0:T(8,128)(2,1)S(1)} %get-tuple-element.42.refs_0_.normed, bf16[512,1024]{1,0:T(8,128)(2,1)S(1)} %collective-permute-done.4.refs_1_.refs_0_, f32[512,1024]{1,0:T(8,128)S(1)} %get-tuple-element.49.refs_2_, ...), custom_call_target="tpu_custom_call", output_to_operand_aliasing={{0}: (2, {}), {1}: (3, {})} | custom-call | flops 1 | bytes 1 | tf_op jit(solution)/shard_map/ffn3/pallas_call | solution.py:317
  63.2 5.5 %collective-permute-done.12.plus = bf16[4352,128]{1,0:T(8,128)(2,1)S(1)} collective-permute-done((bf16[4352,128]{1,0:T(8,128)(2,1)S(1)}, bf16[4352,128]{1,0:T(8,128)(2,1)S(1)}, u32[]{:S(2)}, u32[]{:S(2)}) %collective-permute-start.12) | collective-permute-done | bytes 1114144 | tf_op jit(solution)/shard_map/ppermute | solution.py:90
  68.7 1.0 %halves.1 = (bf16[2176,128]{1,0:T(8,128)(2,1)}, bf16[2176,128]{1,0:T(8,128)(2,1)}) custom-call(bf16[4352,128]{1,0:T(8,128)(2,1)S(1)} %collective-permute-done.12.plus, bf16[4352,128]{1,0:T(8,128)(2,1)S(1)} %collective-permute-done.13.minus), custom_call_target="tpu_custom_call" | custom-call | flops 1 | bytes 1 | tf_op jit(solution)/shard_map/halves/pallas_call | solution.py:269
  69.8 1.3 %ffn4.1 = f32[512,1024]{1,0:T(8,128)S(1)} custom-call(bf16[512,1024]{1,0:T(8,128)(2,1)S(1)} %collective-permute-done.4.refs_1_.refs_0_, f32[512,1024]{1,0:T(8,128)S(1)} %get-tuple-element.62.refs_1_, bf16[2048,128]{1,0:T(8,128)(2,1)S(1)} %collective-permute-done.10.refs_2_, ...), custom_call_target="tpu_custom_call", output_to_operand_aliasing={{}: (1, {})} | custom-call | flops 1 | bytes 1 | tf_op jit(solution)/shard_map/ffn4/pallas_call | solution.py:317
  71.1 1.7 %collective-permute-start.14 = (f32[512,1024]{1,0:T(8,128)S(1)}, f32[512,1024]{1,0:T(8,128)S(1)}, u32[]{:S(2)}, u32[]{:S(2)}) collective-permute-start(f32[512,1024]{1,0:T(8,128)S(1)} %ffn4.1), channel_id=1, source_target_pairs={{0,1},{1,0},{2,3},{3,2},{4,5},{5,4},{6,7},{7,6},{8,9},{9,8},{10,11... | collective-permute-start | bytes 6291464 | tf_op jit(solution)/shard_map/ppermute | solution.py:90
  72.8 1.1 %collective-permute-start.16 = (bf16[2176,128]{1,0:T(8,128)(2,1)}, bf16[2176,128]{1,0:T(8,128)(2,1)}, u32[]{:S(2)}, u32[]{:S(2)}) collective-permute-start(bf16[2176,128]{1,0:T(8,128)(2,1)} %get-tuple-element.58), channel_id=1, source_target_pairs={{0,32},{1,9},{2,34},{3,11},{4,36},{5,13},{6,38},{7,15},{8,40},{9,1... | collective-permute-start | bytes 1671176 | tf_op jit(solution)/shard_map/ppermute | solution.py:90
  73.9 1.5 %collective-permute-start.17 = (bf16[2176,128]{1,0:T(8,128)(2,1)}, bf16[2176,128]{1,0:T(8,128)(2,1)}, u32[]{:S(2)}, u32[]{:S(2)}) collective-permute-start(bf16[2176,128]{1,0:T(8,128)(2,1)} %get-tuple-element.59), channel_id=1, source_target_pairs={{0,96},{1,25},{2,98},{3,27},{4,100},{5,29},{6,102},{7,31},{8,104},... | collective-permute-start | bytes 1671176 | tf_op jit(solution)/shard_map/ppermute | solution.py:90
  75.5 1.3 %ffn5.1.mine = f32[512,1024]{1,0:T(8,128)S(1)} custom-call(bf16[512,1024]{1,0:T(8,128)(2,1)S(1)} %get-tuple-element.42.refs_0_.normed, f32[512,1024]{1,0:T(8,128)S(1)} %get-tuple-element.57.refs_1_, bf16[2048,128]{1,0:T(8,128)(2,1)S(1)} %collective-permute-done.10.refs_2_, ...), custom_call_target="tpu_custom_call", output_to_operand_aliasing={{}: (1, {})} | custom-call | flops 1 | bytes 1 | tf_op jit(solution)/shard_map/ffn5/pallas_call | solution.py:317
  76.8 2.4 %embed.1 = (bf16[512,128]{1,0:T(8,128)(2,1)}, bf16[512,128]{1,0:T(8,128)(2,1)S(1)}) custom-call(s32[4]{0:T(128)S(1)} %copy-done.4, bf16[512,1024]{1,0:T(8,128)(2,1)S(1)} %get-tuple-element.42.refs_0_.normed, f32[512,1024]{1,0:T(8,128)S(1)} %ffn5.1.mine, f32[512,1024]{1,0:T(8,128)S(1)} %collective-permute-done.14.other, f32[1,1024]{1,0:T(1,128)S(1)} %bitcast.27, ...), custom_call_target="tpu_custom_call" | custom-call | flops 1 | bytes 1 | tf_op jit(solution)/shard_map/embed/pallas_call | solution.py:346
  79.2 1.0 %collective-permute-start.15 = (bf16[512,128]{1,0:T(8,128)(2,1)S(1)}, bf16[512,128]{1,0:T(8,128)(2,1)}, u32[]{:S(2)}, u32[]{:S(2)}) collective-permute-start(bf16[512,128]{1,0:T(8,128)(2,1)S(1)} %get-tuple-element.65.emb), channel_id=1, source_target_pairs={{0,1},{1,0},{2,3},{3,2},{4,5},{5,4},{6,7},{7,6},{8,9},{9,8},{10,11... | collective-permute-start | bytes 393224 | tf_op jit(solution)/shard_map/ppermute | solution.py:90
  80.4 2.6 %collective-permute-done.16 = bf16[2176,128]{1,0:T(8,128)(2,1)} collective-permute-done((bf16[2176,128]{1,0:T(8,128)(2,1)}, bf16[2176,128]{1,0:T(8,128)(2,1)}, u32[]{:S(2)}, u32[]{:S(2)}) %collective-permute-start.16) | collective-permute-done | bytes 557088 | tf_op jit(solution)/shard_map/ppermute | solution.py:90
  83.0 3.5 %score.1 = (f32[32,128]{1,0:T(8,128)S(1)}, f32[32,128]{1,0:T(8,128)S(1)}) custom-call(s32[5]{0:T(128)S(1)} %stack.23.where, s32[32]{0:T(128)S(1)} %reshape.51.cand, s32[32]{0:T(128)S(1)} %reshape.52.pair, bf16[512,128]{1,0:T(8,128)(2,1)S(1)} %get-tuple-element.65.emb, bf16[512,128]{1,0:T(8,128)(2,1)} %collective-permute-done.15.sib, ...), custom_call_target="tpu_custom_call" | custom-call | flops 1 | bytes 1 | tf_op jit(solution)/shard_map/score/pallas_call | solution.py:422
  86.5 1.6 %collective-permute-start.18 = (f32[32,128]{1,0:T(8,128)S(1)}, f32[32,128]{1,0:T(8,128)S(1)}, u32[]{:S(2)}, u32[]{:S(2)}) collective-permute-start(f32[32,128]{1,0:T(8,128)S(1)} %get-tuple-element.67), channel_id=1, source_target_pairs={{0,1},{1,0},{2,3},{3,2},{4,5},{5,4},{6,7},{7,6},{8,9},{9,8},{10,11... | collective-permute-start | bytes 49160 | tf_op jit(solution)/shard_map/ppermute | solution.py:90
  (36 shorter events, 3.8 us)
Async XLA Ops:
  0.8 7.7 %copy-start.5 = (s32[4,8]{1,0:T(4,128)S(1)}, s32[4,8]{1,0:T(4,128)}, u32[]{:S(2)}) copy-start(s32[4,8]{1,0:T(4,128)} %param.23) | copy-start | bytes 388
  0.8 9.2 %copy-start = (bf16[512,1024]{1,0:T(8,128)(2,1)S(1)}, bf16[512,1024]{1,0:T(8,128)(2,1)}, u32[]{:S(2)}) copy-start(bf16[512,1024]{1,0:T(8,128)(2,1)} %tok.1) | copy-start | bytes 3145732
  0.8 9.2 %copy-start.2 = (f32[1024]{0:T(1024)S(1)}, f32[1024]{0:T(1024)}, u32[]{:S(2)}) copy-start(f32[1024]{0:T(1024)} %param.15) | copy-start | bytes 12292
  0.8 9.2 %copy-start.4 = (s32[4]{0:T(128)S(1)}, s32[4]{0:T(128)}, u32[]{:S(2)}) copy-start(s32[4]{0:T(128)} %length.3) | copy-start | bytes 52
  3.2 19.5 %collective-permute-start = (bf16[1296,128]{1,0:T(8,128)(2,1)S(1)}, bf16[1296,128]{1,0:T(8,128)(2,1)S(1)}, u32[]{:S(2)}, u32[]{:S(2)}) collective-permute-start(bf16[1296,128]{1,0:T(8,128)(2,1)S(1)} %get-tuple-element.37.refs_3_), channel_id=1, source_target_pairs={{0,2},{1,3},{2,4},{3,5},{4,6},{5,7},{6,0},{7,1},{8,10},{9,11},{10,... | collective-permute-start | bytes 995336 | tf_op jit(solution)/shard_map/ppermute | solution.py:90
  5.4 17.3 %collective-permute-start.1 = (bf16[1296,128]{1,0:T(8,128)(2,1)S(1)}, bf16[1296,128]{1,0:T(8,128)(2,1)S(1)}, u32[]{:S(2)}, u32[]{:S(2)}) collective-permute-start(bf16[1296,128]{1,0:T(8,128)(2,1)S(1)} %get-tuple-element.37.refs_3_), channel_id=1, source_target_pairs={{0,6},{1,7},{2,0},{3,1},{4,2},{5,3},{6,4},{7,5},{8,14},{9,15},{10,... | collective-permute-start | bytes 995336 | tf_op jit(solution)/shard_map/ppermute | solution.py:90
  6.9 15.8 %collective-permute-start.2 = (bf16[1296,128]{1,0:T(8,128)(2,1)S(1)}, bf16[1296,128]{1,0:T(8,128)(2,1)S(1)}, u32[]{:S(2)}, u32[]{:S(2)}) collective-permute-start(bf16[1296,128]{1,0:T(8,128)(2,1)S(1)} %get-tuple-element.37.refs_3_), channel_id=1, source_target_pairs={{0,4},{1,5},{2,6},{3,7},{4,0},{5,1},{6,2},{7,3},{8,12},{9,13},{10,... | collective-permute-start | bytes 995336 | tf_op jit(solution)/shard_map/ppermute | solution.py:90
  8.5 14.2 %collective-permute-start.3 = (s32[4,8]{1,0:T(4,128)S(1)}, s32[4,8]{1,0:T(4,128)S(1)}, u32[]{:S(2)}, u32[]{:S(2)}) collective-permute-start(s32[4,8]{1,0:T(4,128)S(1)} %copy-done.5), channel_id=1, source_target_pairs={{0,1},{1,0},{2,3},{3,2},{4,5},{5,4},{6,7},{7,6},{8,9},{9,8},{10,11... | collective-permute-start | bytes 392 | tf_op jit(solution)/shard_map/ppermute | solution.py:90
  22.8 6.3 %collective-permute-start.4 = (bf16[512,1024]{1,0:T(8,128)(2,1)S(1)}, bf16[512,1024]{1,0:T(8,128)(2,1)S(1)}, u32[]{:S(2)}, u32[]{:S(2)}) collective-permute-start(bf16[512,1024]{1,0:T(8,128)(2,1)S(1)} %get-tuple-element.42.refs_0_.normed), channel_id=1, source_target_pairs={{0,1},{1,0},{2,3},{3,2},{4,5},{5,4},{6,7},{7,6},{8,9},{9,8},{10,11... | collective-permute-start | bytes 3145736 | tf_op jit(solution)/shard_map/ppermute | solution.py:90
  24.0 16.4 %collective-permute-start.5 = (bf16[4160,128]{1,0:T(8,128)(2,1)S(1)}, bf16[4160,128]{1,0:T(8,128)(2,1)S(1)}, u32[]{:S(2)}, u32[]{:S(2)}) collective-permute-start(bf16[4160,128]{1,0:T(8,128)(2,1)S(1)} %join1.1.refs_0_), channel_id=1, source_target_pairs={{0,8},{1,33},{2,10},{3,35},{4,12},{5,37},{6,14},{7,39},{8,16},{9,4... | collective-permute-start | bytes 3194888 | tf_op jit(solution)/shard_map/ppermute | solution.py:90
  25.6 25.5 %collective-permute-start.6 = (bf16[4160,128]{1,0:T(8,128)(2,1)S(1)}, bf16[4160,128]{1,0:T(8,128)(2,1)S(1)}, u32[]{:S(2)}, u32[]{:S(2)}) collective-permute-start(bf16[4160,128]{1,0:T(8,128)(2,1)S(1)} %join1.1.refs_0_), channel_id=1, source_target_pairs={{0,24},{1,97},{2,26},{3,99},{4,28},{5,101},{6,30},{7,103},{8,0},{9... | collective-permute-start | bytes 3194888 | tf_op jit(solution)/shard_map/ppermute | solution.py:90
  27.8 24.9 %collective-permute-start.7 = (bf16[4160,128]{1,0:T(8,128)(2,1)S(1)}, bf16[4160,128]{1,0:T(8,128)(2,1)S(1)}, u32[]{:S(2)}, u32[]{:S(2)}) collective-permute-start(bf16[4160,128]{1,0:T(8,128)(2,1)S(1)} %join1.1.refs_0_), channel_id=1, source_target_pairs={{0,16},{1,65},{2,18},{3,67},{4,20},{5,69},{6,22},{7,71},{8,24},{9,... | collective-permute-start | bytes 3194888 | tf_op jit(solution)/shard_map/ppermute | solution.py:90
  29.1 26.5 %collective-permute-start.8 = (bf16[4096,128]{1,0:T(8,128)(2,1)S(1)}, bf16[4096,128]{1,0:T(8,128)(2,1)S(1)}, u32[]{:S(2)}, u32[]{:S(2)}) collective-permute-start(bf16[4096,128]{1,0:T(8,128)(2,1)S(1)} %bitcast.20), channel_id=1, source_target_pairs={{0,2},{1,3},{2,4},{3,5},{4,6},{5,7},{6,0},{7,1},{8,10},{9,11},{10,... | collective-permute-start | bytes 3145736 | tf_op jit(solution)/shard_map/ppermute | solution.py:90
  29.9 25.6 %collective-permute-start.9 = (bf16[4096,128]{1,0:T(8,128)(2,1)S(1)}, bf16[4096,128]{1,0:T(8,128)(2,1)S(1)}, u32[]{:S(2)}, u32[]{:S(2)}) collective-permute-start(bf16[4096,128]{1,0:T(8,128)(2,1)S(1)} %bitcast.21), channel_id=1, source_target_pairs={{0,6},{1,7},{2,0},{3,1},{4,2},{5,3},{6,4},{7,5},{8,14},{9,15},{10,... | collective-permute-start | bytes 3145736 | tf_op jit(solution)/shard_map/ppermute | solution.py:90
  52.8 15.9 %collective-permute-start.12 = (bf16[4352,128]{1,0:T(8,128)(2,1)S(1)}, bf16[4352,128]{1,0:T(8,128)(2,1)S(1)}, u32[]{:S(2)}, u32[]{:S(2)}) collective-permute-start(bf16[4352,128]{1,0:T(8,128)(2,1)S(1)} %join2.1), channel_id=1, source_target_pairs={{0,32},{1,9},{2,34},{3,11},{4,36},{5,13},{6,38},{7,15},{8,40},{9,1... | collective-permute-start | bytes 3342344 | tf_op jit(solution)/shard_map/ppermute | solution.py:90
  54.1 14.6 %collective-permute-start.13 = (bf16[4352,128]{1,0:T(8,128)(2,1)S(1)}, bf16[4352,128]{1,0:T(8,128)(2,1)S(1)}, u32[]{:S(2)}, u32[]{:S(2)}) collective-permute-start(bf16[4352,128]{1,0:T(8,128)(2,1)S(1)} %join2.1), channel_id=1, source_target_pairs={{0,96},{1,25},{2,98},{3,27},{4,100},{5,29},{6,102},{7,31},{8,104},... | collective-permute-start | bytes 3342344 | tf_op jit(solution)/shard_map/ppermute | solution.py:90
  55.6 14.2 %collective-permute-start.10 = (bf16[2048,128]{1,0:T(8,128)(2,1)S(1)}, bf16[2048,128]{1,0:T(8,128)(2,1)S(1)}, u32[]{:S(2)}, u32[]{:S(2)}) collective-permute-start(bf16[2048,128]{1,0:T(8,128)(2,1)S(1)} %join5.1), channel_id=1, source_target_pairs={{0,2},{1,3},{2,4},{3,5},{4,6},{5,7},{6,0},{7,1},{8,10},{9,11},{10,... | collective-permute-start | bytes 1572872 | tf_op jit(solution)/shard_map/ppermute | solution.py:90
  56.5 13.2 %collective-permute-start.11 = (bf16[2048,128]{1,0:T(8,128)(2,1)S(1)}, bf16[2048,128]{1,0:T(8,128)(2,1)S(1)}, u32[]{:S(2)}, u32[]{:S(2)}) collective-permute-start(bf16[2048,128]{1,0:T(8,128)(2,1)S(1)} %join6.1), channel_id=1, source_target_pairs={{0,6},{1,7},{2,0},{3,1},{4,2},{5,3},{6,4},{7,5},{8,14},{9,15},{10,... | collective-permute-start | bytes 1572872 | tf_op jit(solution)/shard_map/ppermute | solution.py:90
  71.1 5.7 %collective-permute-start.14 = (f32[512,1024]{1,0:T(8,128)S(1)}, f32[512,1024]{1,0:T(8,128)S(1)}, u32[]{:S(2)}, u32[]{:S(2)}) collective-permute-start(f32[512,1024]{1,0:T(8,128)S(1)} %ffn4.1), channel_id=1, source_target_pairs={{0,1},{1,0},{2,3},{3,2},{4,5},{5,4},{6,7},{7,6},{8,9},{9,8},{10,11... | collective-permute-start | bytes 6291464 | tf_op jit(solution)/shard_map/ppermute | solution.py:90
  72.8 10.2 %collective-permute-start.16 = (bf16[2176,128]{1,0:T(8,128)(2,1)}, bf16[2176,128]{1,0:T(8,128)(2,1)}, u32[]{:S(2)}, u32[]{:S(2)}) collective-permute-start(bf16[2176,128]{1,0:T(8,128)(2,1)} %get-tuple-element.58), channel_id=1, source_target_pairs={{0,32},{1,9},{2,34},{3,11},{4,36},{5,13},{6,38},{7,15},{8,40},{9,1... | collective-permute-start | bytes 1671176 | tf_op jit(solution)/shard_map/ppermute | solution.py:90
  73.9 9.1 %collective-permute-start.17 = (bf16[2176,128]{1,0:T(8,128)(2,1)}, bf16[2176,128]{1,0:T(8,128)(2,1)}, u32[]{:S(2)}, u32[]{:S(2)}) collective-permute-start(bf16[2176,128]{1,0:T(8,128)(2,1)} %get-tuple-element.59), channel_id=1, source_target_pairs={{0,96},{1,25},{2,98},{3,27},{4,100},{5,29},{6,102},{7,31},{8,104},... | collective-permute-start | bytes 1671176 | tf_op jit(solution)/shard_map/ppermute | solution.py:90
  75.5 1.3 %copy-start.1 = (bf16[1024,128]{1,0:T(8,128)(2,1)S(1)}, bf16[1024,128]{1,0:T(8,128)(2,1)}, u32[]{:S(2)}) copy-start(bf16[1024,128]{1,0:T(8,128)(2,1)} %we.1) | copy-start | bytes 786436
  75.5 1.3 %copy-start.3 = (f32[1024]{0:T(1024)S(1)}, f32[1024]{0:T(1024)}, u32[]{:S(2)}) copy-start(f32[1024]{0:T(1024)} %param.18) | copy-start | bytes 12292
  79.2 3.8 %collective-permute-start.15 = (bf16[512,128]{1,0:T(8,128)(2,1)S(1)}, bf16[512,128]{1,0:T(8,128)(2,1)}, u32[]{:S(2)}, u32[]{:S(2)}) collective-permute-start(bf16[512,128]{1,0:T(8,128)(2,1)S(1)} %get-tuple-element.65.emb), channel_id=1, source_target_pairs={{0,1},{1,0},{2,3},{3,2},{4,5},{5,4},{6,7},{7,6},{8,9},{9,8},{10,11... | collective-permute-start | bytes 393224 | tf_op jit(solution)/shard_map/ppermute | solution.py:90
  86.5 2.5 %collective-permute-start.18 = (f32[32,128]{1,0:T(8,128)S(1)}, f32[32,128]{1,0:T(8,128)S(1)}, u32[]{:S(2)}, u32[]{:S(2)}) collective-permute-start(f32[32,128]{1,0:T(8,128)S(1)} %get-tuple-element.67), channel_id=1, source_target_pairs={{0,1},{1,0},{2,3},{3,2},{4,5},{5,4},{6,7},{7,6},{8,9},{9,8},{10,11... | collective-permute-start | bytes 49160 | tf_op jit(solution)/shard_map/ppermute | solution.py:90

commit v8 on v7

--- a/solution.py
+++ b/solution.py
@@ -252,32 +252,6 @@
     return normed, low.reshape(-1, LANES), high.reshape(-1, LANES)
 
 
-def halves_body(plus, minus, low, high, sems):
-    rows = low.shape[0]
-    copies = [
-        pltpu.make_async_copy(plus.at[:rows], low, sems.at[0]),
-        pltpu.make_async_copy(minus.at[rows:], high, sems.at[1]),
-    ]
-    for copy in copies:
-        copy.start()
-    for copy in copies:
-        copy.wait()
-
-
-def halves(plus, minus):
-    half = jax.ShapeDtypeStruct((plus.shape[0] // 2, LANES), bf16)
-    return pl.pallas_call(
-        halves_body,
-        out_shape=(half, half),
-        in_specs=any_spec(2),
-        out_specs=tuple(any_spec(2)),
-        scratch_shapes=[pltpu.SemaphoreType.DMA((2,))],
-        compiler_params=params(8),
-        cost_estimate=LIGHT,
-        name="halves",
-    )(plus, minus)
-
-
 def units(refs, half, start, size):
     slabs = []
     for j in range(HALF):
@@ -292,10 +266,10 @@
     return jnp.concatenate(slabs, axis=1)
 
 
-def ffn_body(pieces, arrays, sets, fresh, *refs):
-    inner, outs = refs[-1], refs[-1 - sets : -1]
+def ffn_body(pieces, arrays, sets, fresh, split, *refs):
+    inner, outs = refs[-1], refs[-1 - sets * split : -1]
     tokens, olds = refs[:sets], refs[sets : 2 * sets]
-    held = refs[-1 - sets - arrays : -1 - sets]
+    held = refs[-1 - sets * split - arrays : -1 - sets * split]
     laid = [(held[k], base, count) for k, base, count in pieces]
     total = sum(count for _, _, count in pieces)
     for t in range(sets):
@@ -307,19 +281,22 @@
     for t in range(sets):
         for c in range(0, D, 256):
             more = dot(inner[t], down[:, c : c + 256])
-            outs[t][:, c : c + 256] = more if fresh else olds[t][:, c : c + 256] + more
-
-
-def ffn(tokens, olds, arrays, pieces, name):
+            more = more if fresh else olds[t][:, c : c + 256] + more
+            rows = more.shape[0] // split
+            for k in range(split):
+                outs[t * split + k][:, c : c + 256] = more[k * rows : (k + 1) * rows]
+
+
+def ffn(tokens, olds, arrays, pieces, name, split=1):
     sets, rows = len(tokens), tokens[0].shape[0]
     total = sum(count for _, _, count in pieces)
     tail = tuple(tokens) + tuple(olds) + tuple(arrays)
     return pl.pallas_call(
-        functools.partial(ffn_body, tuple(pieces), len(arrays), sets, not olds),
-        out_shape=(jax.ShapeDtypeStruct((rows, D), f32),) * sets,
+        functools.partial(ffn_body, tuple(pieces), len(arrays), sets, not olds, split),
+        out_shape=(jax.ShapeDtypeStruct((rows // split, D), f32),) * (sets * split),
         in_specs=vmem(len(tail)),
-        out_specs=tuple(vmem(sets)),
-        input_output_aliases={sets + t: t for t in range(len(olds))},
+        out_specs=tuple(vmem(sets * split)),
+        input_output_aliases={sets + t: t for t in range(len(olds))} if split == 1 else {},
         scratch_shapes=[pltpu.VMEM((sets, rows, total), bf16)],
         compiler_params=params(16),
         cost_estimate=LIGHT,
@@ -327,10 +304,15 @@
     )(*tail)
 
 
-def embed_body(length, normed, mine, other, gain, we, out, kept, layer):
-    norm_into(
-        layer, lambda rows: normed[rows, :].astype(f32) + (mine[rows, :] + other[rows, :]), gain[...]
-    )
+def embed_body(length, normed, mine, other0, other1, gain, we, out, kept, layer):
+    half = other0.shape[0]
+    for k, other in enumerate((other0, other1)):
+        norm_into(
+            layer.at[k * half : (k + 1) * half],
+            lambda rows: normed[k * half + rows.start : k * half + rows.stop, :].astype(f32)
+            + (mine[k * half + rows.start : k * half + rows.stop, :] + other[rows, :]),
+            gain[...],
+        )
     projected = dot(layer[...], we[...])
     unit = projected * lax.rsqrt(jnp.sum(projected * projected, axis=-1, keepdims=True) + 1e-06)
     slot = lax.broadcasted_iota(jnp.int32, (SEQ, P_SIZE), 0)
@@ -341,18 +323,18 @@
         kept[rows, :] = live
 
 
-def embed(length, normed, mine, other, gain, we):
+def embed(length, normed, mine, other0, other1, gain, we):
     shape = jax.ShapeDtypeStruct((normed.shape[0], P_SIZE), bf16)
     return pl.pallas_call(
         embed_body,
         out_shape=(shape, shape),
-        in_specs=[SMEM] + vmem(5),
+        in_specs=[SMEM] + vmem(6),
         out_specs=tuple(vmem(2)),
         scratch_shapes=[pltpu.VMEM(normed.shape, bf16)],
         compiler_params=params(12),
         cost_estimate=LIGHT,
         name="embed",
-    )(length, normed, mine, other, gain.reshape(1, D), we)
+    )(length, normed, mine, other0, other1, gain.reshape(1, D), we)
 
 
 def final_body(mine, other, out):
@@ -374,11 +356,8 @@
 
 
 def score_body(where, cand, pair, emb, sib, *refs):
-    docs, outs, held, sem = refs[:5], refs[5:7], refs[7], refs[8]
-    copies = [pltpu.make_async_copy(docs[i], held.at[i], sem.at[i]) for i in range(3)]
-    copies += [
-        pltpu.make_async_copy(docs[3 + i], held.at[3, 2 * i : 2 * i + 2], sem.at[3 + i]) for i in range(2)
-    ]
+    docs, outs, held, sem = refs[:4], refs[4:6], refs[6], refs[7]
+    copies = [pltpu.make_async_copy(docs[i], held.at[i], sem.at[i]) for i in range(4)]
     for copy in copies:
         copy.start()
     z, x, y, c = where[0], where[1], where[2], where[3]
@@ -422,16 +401,16 @@
     return pl.pallas_call(
         score_body,
         out_shape=(jax.ShapeDtypeStruct((total, SEQ), f32),) * 2,
-        in_specs=[SMEM] * 3 + vmem(2) + any_spec(5),
+        in_specs=[SMEM] * 3 + vmem(2) + any_spec(4),
         out_specs=tuple(vmem(2)),
         scratch_shapes=[
             pltpu.VMEM((4, 4, 4, DOC_ROWS, P_SIZE), bf16),
-            pltpu.SemaphoreType.DMA((5,)),
+            pltpu.SemaphoreType.DMA((4,)),
         ],
         compiler_params=params(8),
         cost_estimate=LIGHT,
         name="score",
-    )(where, cand.reshape(-1), pair.reshape(-1), emb, sib, *docs)
+    )(where, cand.reshape(-1), pair.reshape(-1), emb, sib, *docs[:3], *pinned(docs[3]))
 
 
 def on_device(
@@ -483,16 +462,15 @@
     low_far = [send(ahead, "y+"), send(behind, "y-")]
     pieces = [(k,) + p for k in range(2) for p in parts] + [(2, 0, 256), (3, 0, 256)]
     total = ffn(sets, total, [*came[1:], *low_near], pieces, "ffn3")
-    parted = halves(*last)
-    far_docs = [send(parted[0], "g+"), send(parted[1], "g-")]
-    low_far = after(tuple(low_far), *parted)
+    far_docs = send(docs, "g2")
+    low_far = after(tuple(low_far), *last)
     rest = [(0, 0, mid), (1, 0, mid)]
-    away, = ffn(sets[1:], total[1:], low_far, rest, "ffn4")
-    other = send(away, "c")
-    mine, = ffn((normed,), total[:1], low_far, rest, "ffn5")
-    embedded, kept = embed(query_length, normed, mine, other, mlp_gain, embed_weight)
-    sib = send(kept, "c")
-    best, best_pair = score(where, candidates, pair, kept, sib, [docs, *last, *far_docs])
+    away = ffn(sets[1:], total[1:], low_far, rest, "ffn4", split=2)
+    other = [send(a, "c") for a in away]
+    mine, = ffn(sets[:1], total[:1], low_far, rest, "ffn5")
+    embedded, kept = embed(query_length, normed, mine, *other, mlp_gain, embed_weight)
+    sib = send(after(kept, far_docs), "c")
+    best, best_pair = score(where, candidates, pair, kept, sib, [docs, *last, far_docs])
     scores = final(best, send(best_pair, "c"), candidates.shape[0])
     return (embedded, scores)
 

time: 89.8 us -> 97.6 us (1.087)
  starting transfers between devices: 28.3 us -> 37.8 us
  waiting for transfers between devices: 24.5 us -> 23 us
  Pallas kernels: 35.7 us -> 34.6 us
  local copies, waits for them, and re-layouts: 0.27 us -> 1.26 us
    ppermute x19, starting transfers between devices: 28.3 us -> 37.8 us  [send(): return lax.ppermute(value, ('req', 'mlp'), STEPS[way])]
    ppermute x19, waiting for transfers between devices: 24.5 us -> 23 us  [send(): return lax.ppermute(value, ('req', 'mlp'), STEPS[way])]
    pallas_call x1 -> x0, Pallas kernels: 1.03 us -> none  [halves(): pl.pallas_call(halves_body, out_shape=(half, half), in_specs=any_spec(2),...]
    unnamed x12 -> x14, local copies, waits for them, and re-layouts: 0.02 us -> 1.01 us
  transfers between devices with their start and end apart: 19 -> 19, of which waited for: 6 -> 9; matrix products, arithmetic and copies ran while one was open for 0% -> 0% of each run, Pallas kernels for 31% -> 29%
where the time goes in v8:
time: 97.6 us; the launch traced here: 97.4 us
  starting transfers between devices  37.8 us (39%)
  Pallas kernels  34.6 us (35%)
  waiting for transfers between devices  23 us (24%)
  local copies, waits for them, and re-layouts  1.26 us (1%)
    ppermute x19, starting transfers between devices, send(): return lax.ppermute(value, ('req', 'mlp'), STEPS[way])  37.8 us
    ppermute x19, waiting for transfers between devices, send(): return lax.ppermute(value, ('req', 'mlp'), STEPS[way])  23 us
    pallas_call x5, Pallas kernels, ffn(): pl.pallas_call(functools.partial(ffn_body, tuple(pieces), len(arrays), se...  12.8 us
    pallas_call x1, Pallas kernels, attend(): pl.pallas_call(attend_body, out_shape=(jax.ShapeDtypeStruct((rows, D), bf...  12.7 us
    pallas_call x1, Pallas kernels, score(): pl.pallas_call(score_body, out_shape=(jax.ShapeDtypeStruct((total, SEQ),...  3.54 us
    pallas_call x1, Pallas kernels, first(): pl.pallas_call(first_body, out_shape=(jax.ShapeDtypeStruct((BLOCK, LANES)...  2.4 us
    pallas_call x1, Pallas kernels, embed(): pl.pallas_call(embed_body, out_shape=(shape, shape), in_specs=[SMEM] + vm...  2.34 us
  transfers between devices with their start and end apart: 19, of which 9 were waited for; matrix products, arithmetic and copies ran while one was open for 0% of the time, Pallas kernels for 29%

profile of v8, /device:TPU:1, one launch (start us, length us, event | category | flops | bytes accessed | tf_op | source)
XLA Modules:
  0.0 97.4 jit_solution(11810124170454277639)
XLA Ops:
  0.8 2.4 %first.1 = (bf16[1296,128]{1,0:T(8,128)(2,1)S(1)}, bf16[1024,1024]{1,0:T(8,128)(2,1)S(1)}) custom-call(s32[5]{0:T(128)S(1)} %stack.23.where, bf16[1024,512]{1,0:T(8,128)(2,1)} %up.3, bf16[1024,512]{1,0:T(8,128)(2,1)} %down.3, bf16[256,128]{1,0:T(8,128)(2,1)} %bitcast.28, s32[8]{0:T(128)} %lengths.1, bf16[1024,3072]{1,0:T(8,128)(2,1)} %qkv.3), custom_call_target="tpu_custom_call" | custom-call | flops 1 | bytes 1 | tf_op jit(solution)/shard_map/first/pallas_call | solution.py:140
  3.2 2.2 %collective-permute-start = (bf16[1296,128]{1,0:T(8,128)(2,1)S(1)}, bf16[1296,128]{1,0:T(8,128)(2,1)S(1)}, u32[]{:S(2)}, u32[]{:S(2)}) collective-permute-start(bf16[1296,128]{1,0:T(8,128)(2,1)S(1)} %get-tuple-element.38.refs_3_), channel_id=1, source_target_pairs={{0,2},{1,3},{2,4},{3,5},{4,6},{5,7},{6,0},{7,1},{8,10},{9,11},{10,... | collective-permute-start | bytes 995336 | tf_op jit(solution)/shard_map/ppermute | solution.py:90
  5.4 1.5 %collective-permute-start.1 = (bf16[1296,128]{1,0:T(8,128)(2,1)S(1)}, bf16[1296,128]{1,0:T(8,128)(2,1)S(1)}, u32[]{:S(2)}, u32[]{:S(2)}) collective-permute-start(bf16[1296,128]{1,0:T(8,128)(2,1)S(1)} %get-tuple-element.38.refs_3_), channel_id=1, source_target_pairs={{0,6},{1,7},{2,0},{3,1},{4,2},{5,3},{6,4},{7,5},{8,14},{9,15},{10,... | collective-permute-start | bytes 995336 | tf_op jit(solution)/shard_map/ppermute | solution.py:90
  6.9 1.6 %collective-permute-start.2 = (bf16[1296,128]{1,0:T(8,128)(2,1)S(1)}, bf16[1296,128]{1,0:T(8,128)(2,1)S(1)}, u32[]{:S(2)}, u32[]{:S(2)}) collective-permute-start(bf16[1296,128]{1,0:T(8,128)(2,1)S(1)} %get-tuple-element.38.refs_3_), channel_id=1, source_target_pairs={{0,4},{1,5},{2,6},{3,7},{4,0},{5,1},{6,2},{7,3},{8,12},{9,13},{10,... | collective-permute-start | bytes 995336 | tf_op jit(solution)/shard_map/ppermute | solution.py:90
  8.5 1.5 %collective-permute-start.3 = (s32[4,8]{1,0:T(4,128)S(1)}, s32[4,8]{1,0:T(4,128)S(1)}, u32[]{:S(2)}, u32[]{:S(2)}) collective-permute-start(s32[4,8]{1,0:T(4,128)S(1)} %copy-done.6), channel_id=1, source_target_pairs={{0,1},{1,0},{2,3},{3,2},{4,5},{5,4},{6,7},{7,6},{8,9},{9,8},{10,11... | collective-permute-start | bytes 392 | tf_op jit(solution)/shard_map/ppermute | solution.py:90
  10.0 12.7 %attend.1 = (bf16[512,1024]{1,0:T(8,128)(2,1)S(1)}, bf16[16,256,128]{2,1,0:T(8,128)(2,1)S(1)}, bf16[16,256,128]{2,1,0:T(8,128)(2,1)S(1)}) custom-call(s32[4]{0:T(128)S(1)} %copy-done.4, bf16[1024,3072]{1,0:T(8,128)(2,1)} %qkv.3, bf16[1024,1024]{1,0:T(8,128)(2,1)} %wo_hbm.1, bf16[1024,512]{1,0:T(8,128)(2,1)} %up.3, bf16[1024,512]{1,0:T(8,128)(2,1)} %down.3, ...), custom_call_target="tpu_custom_call" | custom-call | flops 1 | bytes 1 | tf_op jit(solution)/shard_map/attend/pallas_call | solution.py:234
  22.8 1.2 %collective-permute-start.4 = (bf16[512,1024]{1,0:T(8,128)(2,1)S(1)}, bf16[512,1024]{1,0:T(8,128)(2,1)S(1)}, u32[]{:S(2)}, u32[]{:S(2)}) collective-permute-start(bf16[512,1024]{1,0:T(8,128)(2,1)S(1)} %get-tuple-element.43.refs_0_.normed), channel_id=1, source_target_pairs={{0,1},{1,0},{2,3},{3,2},{4,5},{5,4},{6,7},{7,6},{8,9},{9,8},{10,11... | collective-permute-start | bytes 3145736 | tf_op jit(solution)/shard_map/ppermute | solution.py:90
  24.0 1.6 %collective-permute-start.5 = (bf16[4160,128]{1,0:T(8,128)(2,1)S(1)}, bf16[4160,128]{1,0:T(8,128)(2,1)S(1)}, u32[]{:S(2)}, u32[]{:S(2)}) collective-permute-start(bf16[4160,128]{1,0:T(8,128)(2,1)S(1)} %join1.1.refs_0_), channel_id=1, source_target_pairs={{0,8},{1,33},{2,10},{3,35},{4,12},{5,37},{6,14},{7,39},{8,16},{9,4... | collective-permute-start | bytes 3194888 | tf_op jit(solution)/shard_map/ppermute | solution.py:90
  25.6 2.1 %collective-permute-start.6 = (bf16[4160,128]{1,0:T(8,128)(2,1)S(1)}, bf16[4160,128]{1,0:T(8,128)(2,1)S(1)}, u32[]{:S(2)}, u32[]{:S(2)}) collective-permute-start(bf16[4160,128]{1,0:T(8,128)(2,1)S(1)} %join1.1.refs_0_), channel_id=1, source_target_pairs={{0,24},{1,97},{2,26},{3,99},{4,28},{5,101},{6,30},{7,103},{8,0},{9... | collective-permute-start | bytes 3194888 | tf_op jit(solution)/shard_map/ppermute | solution.py:90
  27.8 1.3 %collective-permute-start.7 = (bf16[4160,128]{1,0:T(8,128)(2,1)S(1)}, bf16[4160,128]{1,0:T(8,128)(2,1)S(1)}, u32[]{:S(2)}, u32[]{:S(2)}) collective-permute-start(bf16[4160,128]{1,0:T(8,128)(2,1)S(1)} %join1.1.refs_0_), channel_id=1, source_target_pairs={{0,16},{1,65},{2,18},{3,67},{4,20},{5,69},{6,22},{7,71},{8,24},{9,... | collective-permute-start | bytes 3194888 | tf_op jit(solution)/shard_map/ppermute | solution.py:90
  29.1 0.9 collective-permute-start.8
  29.9 1.8 %collective-permute-start.9 = (bf16[4096,128]{1,0:T(8,128)(2,1)S(1)}, bf16[4096,128]{1,0:T(8,128)(2,1)S(1)}, u32[]{:S(2)}, u32[]{:S(2)}) collective-permute-start(bf16[4096,128]{1,0:T(8,128)(2,1)S(1)} %bitcast.20), channel_id=1, source_target_pairs={{0,6},{1,7},{2,0},{3,1},{4,2},{5,3},{6,4},{7,5},{8,14},{9,15},{10,... | collective-permute-start | bytes 3145736 | tf_op jit(solution)/shard_map/ppermute | solution.py:90
  31.7 2.5 %ffn1.1 = (f32[512,1024]{1,0:T(8,128)S(1)}, f32[512,1024]{1,0:T(8,128)S(1)}) custom-call(bf16[512,1024]{1,0:T(8,128)(2,1)S(1)} %get-tuple-element.43.refs_0_.normed, bf16[512,1024]{1,0:T(8,128)(2,1)S(1)} %collective-permute-done.4.refs_1_.refs_0_, bf16[4096,128]{1,0:T(8,128)(2,1)S(1)} %bitcast.21, bf16[4096,128]{1,0:T(8,128)(2,1)S(1)} %bitcast.22), custom_call_target="tpu_custom_call" | custom-call | flops 1 | bytes 1 | tf_op jit(solution)/shard_map/ffn1/pallas_call | solution.py:294
  34.2 6.2 %collective-permute-done.5.refs_7_.refs_1_ = bf16[4160,128]{1,0:T(8,128)(2,1)S(1)} collective-permute-done((bf16[4160,128]{1,0:T(8,128)(2,1)S(1)}, bf16[4160,128]{1,0:T(8,128)(2,1)S(1)}, u32[]{:S(2)}, u32[]{:S(2)}) %collective-permute-start.5) | collective-permute-done | bytes 1064992 | tf_op jit(solution)/shard_map/ppermute | solution.py:90
  40.4 3.0 %ffn2.1 = (f32[512,1024]{1,0:T(8,128)S(1)}, f32[512,1024]{1,0:T(8,128)S(1)}) custom-call(bf16[512,1024]{1,0:T(8,128)(2,1)S(1)} %get-tuple-element.43.refs_0_.normed, bf16[512,1024]{1,0:T(8,128)(2,1)S(1)} %collective-permute-done.4.refs_1_.refs_0_, f32[512,1024]{1,0:T(8,128)S(1)} %get-tuple-element.46.refs_2_, ...), custom_call_target="tpu_custom_call", output_to_operand_aliasing={{0}: (2, {}), {1}: (3, {})} | custom-call | flops 1 | bytes 1 | tf_op jit(solution)/shard_map/ffn2/pallas_call | solution.py:294
  43.5 7.6 %collective-permute-done.6.refs_2_.refs_4_ = bf16[4160,128]{1,0:T(8,128)(2,1)S(1)} collective-permute-done((bf16[4160,128]{1,0:T(8,128)(2,1)S(1)}, bf16[4160,128]{1,0:T(8,128)(2,1)S(1)}, u32[]{:S(2)}, u32[]{:S(2)}) %collective-permute-start.6) | collective-permute-done | bytes 1064992 | tf_op jit(solution)/shard_map/ppermute | solution.py:90
  51.1 1.6 %collective-permute-done.7.refs_3_.refs_5_ = bf16[4160,128]{1,0:T(8,128)(2,1)S(1)} collective-permute-done((bf16[4160,128]{1,0:T(8,128)(2,1)S(1)}, bf16[4160,128]{1,0:T(8,128)(2,1)S(1)}, u32[]{:S(2)}, u32[]{:S(2)}) %collective-permute-start.7) | collective-permute-done | bytes 1064992 | tf_op jit(solution)/shard_map/ppermute | solution.py:90
  52.8 1.3 %collective-permute-start.12 = (bf16[4352,128]{1,0:T(8,128)(2,1)S(1)}, bf16[4352,128]{1,0:T(8,128)(2,1)S(1)}, u32[]{:S(2)}, u32[]{:S(2)}) collective-permute-start(bf16[4352,128]{1,0:T(8,128)(2,1)S(1)} %join2.1), channel_id=1, source_target_pairs={{0,32},{1,9},{2,34},{3,11},{4,36},{5,13},{6,38},{7,15},{8,40},{9,1... | collective-permute-start | bytes 3342344 | tf_op jit(solution)/shard_map/ppermute | solution.py:90
  54.1 1.5 %collective-permute-start.13 = (bf16[4352,128]{1,0:T(8,128)(2,1)S(1)}, bf16[4352,128]{1,0:T(8,128)(2,1)S(1)}, u32[]{:S(2)}, u32[]{:S(2)}) collective-permute-start(bf16[4352,128]{1,0:T(8,128)(2,1)S(1)} %join2.1), channel_id=1, source_target_pairs={{0,96},{1,25},{2,98},{3,27},{4,100},{5,29},{6,102},{7,31},{8,104},... | collective-permute-start | bytes 3342344 | tf_op jit(solution)/shard_map/ppermute | solution.py:90
  55.6 0.9 collective-permute-start.10
  56.5 1.9 %collective-permute-start.11 = (bf16[2048,128]{1,0:T(8,128)(2,1)S(1)}, bf16[2048,128]{1,0:T(8,128)(2,1)S(1)}, u32[]{:S(2)}, u32[]{:S(2)}) collective-permute-start(bf16[2048,128]{1,0:T(8,128)(2,1)S(1)} %join6.1), channel_id=1, source_target_pairs={{0,6},{1,7},{2,0},{3,1},{4,2},{5,3},{6,4},{7,5},{8,14},{9,15},{10,... | collective-permute-start | bytes 1572872 | tf_op jit(solution)/shard_map/ppermute | solution.py:90
  58.4 2.2 %collective-permute-start.16 = (bf16[4352,128]{1,0:T(8,128)(2,1)S(1)}, bf16[4352,128]{1,0:T(8,128)(2,1)S(1)}, u32[]{:S(2)}, u32[]{:S(2)}) collective-permute-start(bf16[4352,128]{1,0:T(8,128)(2,1)S(1)} %join2.1), channel_id=1, source_target_pairs={{0,64},{1,17},{2,66},{3,19},{4,68},{5,21},{6,70},{7,23},{8,72},{9,... | collective-permute-start | bytes 3342344 | tf_op jit(solution)/shard_map/ppermute | solution.py:90
  60.6 4.7 %ffn3.1 = (f32[512,1024]{1,0:T(8,128)S(1)}, f32[512,1024]{1,0:T(8,128)S(1)}) custom-call(bf16[512,1024]{1,0:T(8,128)(2,1)S(1)} %get-tuple-element.43.refs_0_.normed, bf16[512,1024]{1,0:T(8,128)(2,1)S(1)} %collective-permute-done.4.refs_1_.refs_0_, f32[512,1024]{1,0:T(8,128)S(1)} %get-tuple-element.50.refs_2_, ...), custom_call_target="tpu_custom_call", output_to_operand_aliasing={{0}: (2, {}), {1}: (3, {})} | custom-call | flops 1 | bytes 1 | tf_op jit(solution)/shard_map/ffn3/pallas_call | solution.py:294
  65.3 3.4 %collective-permute-done.12 = bf16[4352,128]{1,0:T(8,128)(2,1)S(1)} collective-permute-done((bf16[4352,128]{1,0:T(8,128)(2,1)S(1)}, bf16[4352,128]{1,0:T(8,128)(2,1)S(1)}, u32[]{:S(2)}, u32[]{:S(2)}) %collective-permute-start.12) | collective-permute-done | bytes 1114144 | tf_op jit(solution)/shard_map/ppermute | solution.py:90
  68.9 1.3 %ffn4.1 = (f32[256,1024]{1,0:T(8,128)S(1)}, f32[256,1024]{1,0:T(8,128)S(1)}) custom-call(bf16[512,1024]{1,0:T(8,128)(2,1)S(1)} %collective-permute-done.4.refs_1_.refs_0_, f32[512,1024]{1,0:T(8,128)S(1)} %get-tuple-element.61.refs_1_, bf16[2048,128]{1,0:T(8,128)(2,1)S(1)} %collective-permute-done.10.refs_2_, ...), custom_call_target="tpu_custom_call" | custom-call | flops 1 | bytes 1 | tf_op jit(solution)/shard_map/ffn4/pallas_call | solution.py:294
  70.2 13.1 %collective-permute-start.14 = (f32[256,1024]{1,0:T(8,128)S(1)}, f32[256,1024]{1,0:T(8,128)S(1)}, u32[]{:S(2)}, u32[]{:S(2)}) collective-permute-start(f32[256,1024]{1,0:T(8,128)S(1)} %get-tuple-element.62), channel_id=1, source_target_pairs={{0,1},{1,0},{2,3},{3,2},{4,5},{5,4},{6,7},{7,6},{8,9},{9,8},{10,11... | collective-permute-start | bytes 3145736 | tf_op jit(solution)/shard_map/ppermute | solution.py:90
  83.6 1.3 %ffn5.1.mine = f32[512,1024]{1,0:T(8,128)S(1)} custom-call(bf16[512,1024]{1,0:T(8,128)(2,1)S(1)} %get-tuple-element.43.refs_0_.normed, f32[512,1024]{1,0:T(8,128)S(1)} %get-tuple-element.58.refs_1_, bf16[2048,128]{1,0:T(8,128)(2,1)S(1)} %collective-permute-done.10.refs_2_, ...), custom_call_target="tpu_custom_call", output_to_operand_aliasing={{}: (1, {})} | custom-call | flops 1 | bytes 1 | tf_op jit(solution)/shard_map/ffn5/pallas_call | solution.py:294
  85.6 1.5 %collective-permute-done.15.other1 = f32[256,1024]{1,0:T(8,128)S(1)} collective-permute-done((f32[256,1024]{1,0:T(8,128)S(1)}, f32[256,1024]{1,0:T(8,128)S(1)}, u32[]{:S(2)}, u32[]{:S(2)}) %collective-permute-start.15) | collective-permute-done | bytes 1048608 | tf_op jit(solution)/shard_map/ppermute | solution.py:90
  87.1 2.3 %embed.1 = (bf16[512,128]{1,0:T(8,128)(2,1)}, bf16[512,128]{1,0:T(8,128)(2,1)S(1)}) custom-call(s32[4]{0:T(128)S(1)} %copy-done.4, bf16[512,1024]{1,0:T(8,128)(2,1)S(1)} %get-tuple-element.43.refs_0_.normed, f32[512,1024]{1,0:T(8,128)S(1)} %ffn5.1.mine, f32[256,1024]{1,0:T(8,128)S(1)} %collective-permute-done.14.other0, ...), custom_call_target="tpu_custom_call" | custom-call | flops 1 | bytes 1 | tf_op jit(solution)/shard_map/embed/pallas_call | solution.py:328
  89.4 1.0 %copy-done.5 = bf16[4352,128]{1,0:T(8,128)(2,1)} copy-done((bf16[4352,128]{1,0:T(8,128)(2,1)}, bf16[4352,128]{1,0:T(8,128)(2,1)S(1)}, u32[]{:S(2)}) %copy-start.5) | copy-done | bytes 1114136
  90.9 1.0 collective-permute-done.17.sib
  91.9 3.5 %score.1 = (f32[32,128]{1,0:T(8,128)S(1)}, f32[32,128]{1,0:T(8,128)S(1)}) custom-call(s32[5]{0:T(128)S(1)} %stack.23.where, s32[32]{0:T(128)S(1)} %reshape.48.cand, s32[32]{0:T(128)S(1)} %reshape.49.pair, bf16[512,128]{1,0:T(8,128)(2,1)S(1)} %get-tuple-element.67.emb, bf16[512,128]{1,0:T(8,128)(2,1)} %collective-permute-done.17.sib, ...), custom_call_target="tpu_custom_call" | custom-call | flops 1 | bytes 1 | tf_op jit(solution)/shard_map/score/pallas_call | solution.py:401
  (37 shorter events, 4.0 us)
Async XLA Ops:
  0.8 7.7 %copy-start.6 = (s32[4,8]{1,0:T(4,128)S(1)}, s32[4,8]{1,0:T(4,128)}, u32[]{:S(2)}) copy-start(s32[4,8]{1,0:T(4,128)} %param.23) | copy-start | bytes 388
  0.8 9.2 %copy-start = (bf16[512,1024]{1,0:T(8,128)(2,1)S(1)}, bf16[512,1024]{1,0:T(8,128)(2,1)}, u32[]{:S(2)}) copy-start(bf16[512,1024]{1,0:T(8,128)(2,1)} %tok.1) | copy-start | bytes 3145732
  0.8 9.2 %copy-start.2 = (f32[1024]{0:T(1024)S(1)}, f32[1024]{0:T(1024)}, u32[]{:S(2)}) copy-start(f32[1024]{0:T(1024)} %param.15) | copy-start | bytes 12292
  0.8 9.2 %copy-start.4 = (s32[4]{0:T(128)S(1)}, s32[4]{0:T(128)}, u32[]{:S(2)}) copy-start(s32[4]{0:T(128)} %length.3) | copy-start | bytes 52
  3.2 19.5 %collective-permute-start = (bf16[1296,128]{1,0:T(8,128)(2,1)S(1)}, bf16[1296,128]{1,0:T(8,128)(2,1)S(1)}, u32[]{:S(2)}, u32[]{:S(2)}) collective-permute-start(bf16[1296,128]{1,0:T(8,128)(2,1)S(1)} %get-tuple-element.38.refs_3_), channel_id=1, source_target_pairs={{0,2},{1,3},{2,4},{3,5},{4,6},{5,7},{6,0},{7,1},{8,10},{9,11},{10,... | collective-permute-start | bytes 995336 | tf_op jit(solution)/shard_map/ppermute | solution.py:90
  5.4 17.3 %collective-permute-start.1 = (bf16[1296,128]{1,0:T(8,128)(2,1)S(1)}, bf16[1296,128]{1,0:T(8,128)(2,1)S(1)}, u32[]{:S(2)}, u32[]{:S(2)}) collective-permute-start(bf16[1296,128]{1,0:T(8,128)(2,1)S(1)} %get-tuple-element.38.refs_3_), channel_id=1, source_target_pairs={{0,6},{1,7},{2,0},{3,1},{4,2},{5,3},{6,4},{7,5},{8,14},{9,15},{10,... | collective-permute-start | bytes 995336 | tf_op jit(solution)/shard_map/ppermute | solution.py:90
  6.9 15.8 %collective-permute-start.2 = (bf16[1296,128]{1,0:T(8,128)(2,1)S(1)}, bf16[1296,128]{1,0:T(8,128)(2,1)S(1)}, u32[]{:S(2)}, u32[]{:S(2)}) collective-permute-start(bf16[1296,128]{1,0:T(8,128)(2,1)S(1)} %get-tuple-element.38.refs_3_), channel_id=1, source_target_pairs={{0,4},{1,5},{2,6},{3,7},{4,0},{5,1},{6,2},{7,3},{8,12},{9,13},{10,... | collective-permute-start | bytes 995336 | tf_op jit(solution)/shard_map/ppermute | solution.py:90
  8.5 14.2 %collective-permute-start.3 = (s32[4,8]{1,0:T(4,128)S(1)}, s32[4,8]{1,0:T(4,128)S(1)}, u32[]{:S(2)}, u32[]{:S(2)}) collective-permute-start(s32[4,8]{1,0:T(4,128)S(1)} %copy-done.6), channel_id=1, source_target_pairs={{0,1},{1,0},{2,3},{3,2},{4,5},{5,4},{6,7},{7,6},{8,9},{9,8},{10,11... | collective-permute-start | bytes 392 | tf_op jit(solution)/shard_map/ppermute | solution.py:90
  22.8 6.3 %collective-permute-start.4 = (bf16[512,1024]{1,0:T(8,128)(2,1)S(1)}, bf16[512,1024]{1,0:T(8,128)(2,1)S(1)}, u32[]{:S(2)}, u32[]{:S(2)}) collective-permute-start(bf16[512,1024]{1,0:T(8,128)(2,1)S(1)} %get-tuple-element.43.refs_0_.normed), channel_id=1, source_target_pairs={{0,1},{1,0},{2,3},{3,2},{4,5},{5,4},{6,7},{7,6},{8,9},{9,8},{10,11... | collective-permute-start | bytes 3145736 | tf_op jit(solution)/shard_map/ppermute | solution.py:90
  24.0 16.4 %collective-permute-start.5 = (bf16[4160,128]{1,0:T(8,128)(2,1)S(1)}, bf16[4160,128]{1,0:T(8,128)(2,1)S(1)}, u32[]{:S(2)}, u32[]{:S(2)}) collective-permute-start(bf16[4160,128]{1,0:T(8,128)(2,1)S(1)} %join1.1.refs_0_), channel_id=1, source_target_pairs={{0,8},{1,33},{2,10},{3,35},{4,12},{5,37},{6,14},{7,39},{8,16},{9,4... | collective-permute-start | bytes 3194888 | tf_op jit(solution)/shard_map/ppermute | solution.py:90
  25.6 25.5 %collective-permute-start.6 = (bf16[4160,128]{1,0:T(8,128)(2,1)S(1)}, bf16[4160,128]{1,0:T(8,128)(2,1)S(1)}, u32[]{:S(2)}, u32[]{:S(2)}) collective-permute-start(bf16[4160,128]{1,0:T(8,128)(2,1)S(1)} %join1.1.refs_0_), channel_id=1, source_target_pairs={{0,24},{1,97},{2,26},{3,99},{4,28},{5,101},{6,30},{7,103},{8,0},{9... | collective-permute-start | bytes 3194888 | tf_op jit(solution)/shard_map/ppermute | solution.py:90
  27.8 24.9 %collective-permute-start.7 = (bf16[4160,128]{1,0:T(8,128)(2,1)S(1)}, bf16[4160,128]{1,0:T(8,128)(2,1)S(1)}, u32[]{:S(2)}, u32[]{:S(2)}) collective-permute-start(bf16[4160,128]{1,0:T(8,128)(2,1)S(1)} %join1.1.refs_0_), channel_id=1, source_target_pairs={{0,16},{1,65},{2,18},{3,67},{4,20},{5,69},{6,22},{7,71},{8,24},{9,... | collective-permute-start | bytes 3194888 | tf_op jit(solution)/shard_map/ppermute | solution.py:90
  29.1 26.5 %collective-permute-start.8 = (bf16[4096,128]{1,0:T(8,128)(2,1)S(1)}, bf16[4096,128]{1,0:T(8,128)(2,1)S(1)}, u32[]{:S(2)}, u32[]{:S(2)}) collective-permute-start(bf16[4096,128]{1,0:T(8,128)(2,1)S(1)} %bitcast.19), channel_id=1, source_target_pairs={{0,2},{1,3},{2,4},{3,5},{4,6},{5,7},{6,0},{7,1},{8,10},{9,11},{10,... | collective-permute-start | bytes 3145736 | tf_op jit(solution)/shard_map/ppermute | solution.py:90
  29.9 25.6 %collective-permute-start.9 = (bf16[4096,128]{1,0:T(8,128)(2,1)S(1)}, bf16[4096,128]{1,0:T(8,128)(2,1)S(1)}, u32[]{:S(2)}, u32[]{:S(2)}) collective-permute-start(bf16[4096,128]{1,0:T(8,128)(2,1)S(1)} %bitcast.20), channel_id=1, source_target_pairs={{0,6},{1,7},{2,0},{3,1},{4,2},{5,3},{6,4},{7,5},{8,14},{9,15},{10,... | collective-permute-start | bytes 3145736 | tf_op jit(solution)/shard_map/ppermute | solution.py:90
  52.8 15.9 %collective-permute-start.12 = (bf16[4352,128]{1,0:T(8,128)(2,1)S(1)}, bf16[4352,128]{1,0:T(8,128)(2,1)S(1)}, u32[]{:S(2)}, u32[]{:S(2)}) collective-permute-start(bf16[4352,128]{1,0:T(8,128)(2,1)S(1)} %join2.1), channel_id=1, source_target_pairs={{0,32},{1,9},{2,34},{3,11},{4,36},{5,13},{6,38},{7,15},{8,40},{9,1... | collective-permute-start | bytes 3342344 | tf_op jit(solution)/shard_map/ppermute | solution.py:90
  54.1 14.6 %collective-permute-start.13 = (bf16[4352,128]{1,0:T(8,128)(2,1)S(1)}, bf16[4352,128]{1,0:T(8,128)(2,1)S(1)}, u32[]{:S(2)}, u32[]{:S(2)}) collective-permute-start(bf16[4352,128]{1,0:T(8,128)(2,1)S(1)} %join2.1), channel_id=1, source_target_pairs={{0,96},{1,25},{2,98},{3,27},{4,100},{5,29},{6,102},{7,31},{8,104},... | collective-permute-start | bytes 3342344 | tf_op jit(solution)/shard_map/ppermute | solution.py:90
  55.6 13.3 %collective-permute-start.10 = (bf16[2048,128]{1,0:T(8,128)(2,1)S(1)}, bf16[2048,128]{1,0:T(8,128)(2,1)S(1)}, u32[]{:S(2)}, u32[]{:S(2)}) collective-permute-start(bf16[2048,128]{1,0:T(8,128)(2,1)S(1)} %join5.1), channel_id=1, source_target_pairs={{0,2},{1,3},{2,4},{3,5},{4,6},{5,7},{6,0},{7,1},{8,10},{9,11},{10,... | collective-permute-start | bytes 1572872 | tf_op jit(solution)/shard_map/ppermute | solution.py:90
  56.5 12.3 %collective-permute-start.11 = (bf16[2048,128]{1,0:T(8,128)(2,1)S(1)}, bf16[2048,128]{1,0:T(8,128)(2,1)S(1)}, u32[]{:S(2)}, u32[]{:S(2)}) collective-permute-start(bf16[2048,128]{1,0:T(8,128)(2,1)S(1)} %join6.1), channel_id=1, source_target_pairs={{0,6},{1,7},{2,0},{3,1},{4,2},{5,3},{6,4},{7,5},{8,14},{9,15},{10,... | collective-permute-start | bytes 1572872 | tf_op jit(solution)/shard_map/ppermute | solution.py:90
  58.4 31.0 %collective-permute-start.16 = (bf16[4352,128]{1,0:T(8,128)(2,1)S(1)}, bf16[4352,128]{1,0:T(8,128)(2,1)S(1)}, u32[]{:S(2)}, u32[]{:S(2)}) collective-permute-start(bf16[4352,128]{1,0:T(8,128)(2,1)S(1)} %join2.1), channel_id=1, source_target_pairs={{0,64},{1,17},{2,66},{3,19},{4,68},{5,21},{6,70},{7,23},{8,72},{9,... | collective-permute-start | bytes 3342344 | tf_op jit(solution)/shard_map/ppermute | solution.py:90
  70.2 15.4 %collective-permute-start.14 = (f32[256,1024]{1,0:T(8,128)S(1)}, f32[256,1024]{1,0:T(8,128)S(1)}, u32[]{:S(2)}, u32[]{:S(2)}) collective-permute-start(f32[256,1024]{1,0:T(8,128)S(1)} %get-tuple-element.62), channel_id=1, source_target_pairs={{0,1},{1,0},{2,3},{3,2},{4,5},{5,4},{6,7},{7,6},{8,9},{9,8},{10,11... | collective-permute-start | bytes 3145736 | tf_op jit(solution)/shard_map/ppermute | solution.py:90
  83.3 3.8 %collective-permute-start.15 = (f32[256,1024]{1,0:T(8,128)S(1)}, f32[256,1024]{1,0:T(8,128)S(1)}, u32[]{:S(2)}, u32[]{:S(2)}) collective-permute-start(f32[256,1024]{1,0:T(8,128)S(1)} %get-tuple-element.63), channel_id=1, source_target_pairs={{0,1},{1,0},{2,3},{3,2},{4,5},{5,4},{6,7},{7,6},{8,9},{9,8},{10,11... | collective-permute-start | bytes 3145736 | tf_op jit(solution)/shard_map/ppermute | solution.py:90
  83.6 3.5 %copy-start.1 = (bf16[1024,128]{1,0:T(8,128)(2,1)S(1)}, bf16[1024,128]{1,0:T(8,128)(2,1)}, u32[]{:S(2)}) copy-start(bf16[1024,128]{1,0:T(8,128)(2,1)} %we.1) | copy-start | bytes 786436
  83.6 3.5 %copy-start.3 = (f32[1024]{0:T(1024)S(1)}, f32[1024]{0:T(1024)}, u32[]{:S(2)}) copy-start(f32[1024]{0:T(1024)} %param.18) | copy-start | bytes 12292
  89.4 1.0 %copy-start.5 = (bf16[4352,128]{1,0:T(8,128)(2,1)}, bf16[4352,128]{1,0:T(8,128)(2,1)S(1)}, u32[]{:S(2)}) copy-start(bf16[4352,128]{1,0:T(8,128)(2,1)S(1)} %collective-permute-done.16) | copy-start | bytes 3342340
  90.4 1.5 %collective-permute-start.17 = (bf16[512,128]{1,0:T(8,128)(2,1)S(1)}, bf16[512,128]{1,0:T(8,128)(2,1)}, u32[]{:S(2)}, u32[]{:S(2)}) collective-permute-start(bf16[512,128]{1,0:T(8,128)(2,1)S(1)} %get-tuple-element.67.emb), channel_id=1, source_target_pairs={{0,1},{1,0},{2,3},{3,2},{4,5},{5,4},{6,7},{7,6},{8,9},{9,8},{10,11... | collective-permute-start | bytes 393224 | tf_op jit(solution)/shard_map/ppermute | solution.py:90
  95.4 1.3 %collective-permute-start.18 = (f32[32,128]{1,0:T(8,128)S(1)}, f32[32,128]{1,0:T(8,128)S(1)}, u32[]{:S(2)}, u32[]{:S(2)}) collective-permute-start(f32[32,128]{1,0:T(8,128)S(1)} %get-tuple-element.69), channel_id=1, source_target_pairs={{0,1},{1,0},{2,3},{3,2},{4,5},{5,4},{6,7},{7,6},{8,9},{9,8},{10,11... | collective-permute-start | bytes 49160 | tf_op jit(solution)/shard_map/ppermute | solution.py:90

commit v9 on v7

--- a/solution.py
+++ b/solution.py
@@ -21,7 +21,7 @@
 PART = SLABS * SLICE
 BLOCK = PART + DOC_ROWS
 AROUND = (0, 3, 1, 2)
-AROUND_Y = (3, 1, 2, 0)
+AROUND_Y = (2, 3, 1, 0)
 DEAD = -1e30
 f32 = jnp.float32
 bf16 = jnp.bfloat16
@@ -375,12 +375,13 @@
 
 def score_body(where, cand, pair, emb, sib, *refs):
     docs, outs, held, sem = refs[:5], refs[5:7], refs[7], refs[8]
-    copies = [pltpu.make_async_copy(docs[i], held.at[i], sem.at[i]) for i in range(3)]
-    copies += [
-        pltpu.make_async_copy(docs[3 + i], held.at[3, 2 * i : 2 * i + 2], sem.at[3 + i]) for i in range(2)
+    copies = [
+        pltpu.make_async_copy(docs[3 + i], held.at[3, 2 * i : 2 * i + 2], sem.at[i]) for i in range(2)
     ]
     for copy in copies:
         copy.start()
+    for i in range(3):
+        held[i] = docs[i][...]
     z, x, y, c = where[0], where[1], where[2], where[3]
     local = lax.broadcasted_iota(jnp.int32, (TOKS, LANES), 0)
     pos = jnp.concatenate(
@@ -422,11 +423,11 @@
     return pl.pallas_call(
         score_body,
         out_shape=(jax.ShapeDtypeStruct((total, SEQ), f32),) * 2,
-        in_specs=[SMEM] * 3 + vmem(2) + any_spec(5),
+        in_specs=[SMEM] * 3 + vmem(5) + any_spec(2),
         out_specs=tuple(vmem(2)),
         scratch_shapes=[
             pltpu.VMEM((4, 4, 4, DOC_ROWS, P_SIZE), bf16),
-            pltpu.SemaphoreType.DMA((5,)),
+            pltpu.SemaphoreType.DMA((2,)),
         ],
         compiler_params=params(8),
         cost_estimate=LIGHT,
@@ -454,7 +455,7 @@
     start, query = first(
         where, up_weight, down_weight, documents.reshape(-1, P_SIZE), document_length, attend_weight
     )
-    near = [send(start, way) for way in ("y+", "y-", "y2")]
+    near = [send(start, way) for way in ("y2", "y+", "y-")]
     normed, low, high = attend(
         tokens, attend_weight, query, output_weight, attend_gain, query_length, up_weight, down_weight
     )

time: 89.8 us -> 89.8 us (level)
  no operation moved by 1% of the time
where the time goes in v9:
time: 89.8 us; the launch traced here: 89.6 us
  Pallas kernels  35.2 us (39%)
  starting transfers between devices  28.8 us (32%)
  waiting for transfers between devices  24.5 us (27%)
    ppermute x19, starting transfers between devices, send(): return lax.ppermute(value, ('req', 'mlp'), STEPS[way])  28.8 us
    ppermute x19, waiting for transfers between devices, send(): return lax.ppermute(value, ('req', 'mlp'), STEPS[way])  24.5 us
    pallas_call x5, Pallas kernels, ffn(): pl.pallas_call(functools.partial(ffn_body, tuple(pieces), len(arrays), se...  12.8 us
    pallas_call x1, Pallas kernels, attend(): pl.pallas_call(attend_body, out_shape=(jax.ShapeDtypeStruct((rows, D), bf...  12.6 us
    pallas_call x1, Pallas kernels, score(): pl.pallas_call(score_body, out_shape=(jax.ShapeDtypeStruct((total, SEQ),...  3.03 us
    pallas_call x1, Pallas kernels, first(): pl.pallas_call(first_body, out_shape=(jax.ShapeDtypeStruct((BLOCK, LANES)...  2.4 us
    pallas_call x1, Pallas kernels, embed(): pl.pallas_call(embed_body, out_shape=(shape, shape), in_specs=[SMEM] + vm...  2.36 us
  transfers between devices with their start and end apart: 19, of which 6 were waited for; matrix products, arithmetic and copies ran while one was open for 0% of the time, Pallas kernels for 31%

profile of v9, /device:TPU:1, one launch (start us, length us, event | category | flops | bytes accessed | tf_op | source)
XLA Modules:
  0.0 89.6 jit_solution(13638700113719433209)
XLA Ops:
  0.8 2.4 %first.1 = (bf16[1296,128]{1,0:T(8,128)(2,1)S(1)}, bf16[1024,1024]{1,0:T(8,128)(2,1)S(1)}) custom-call(s32[5]{0:T(128)S(1)} %stack.23.where, bf16[1024,512]{1,0:T(8,128)(2,1)} %up.3, bf16[1024,512]{1,0:T(8,128)(2,1)} %down.3, bf16[256,128]{1,0:T(8,128)(2,1)} %bitcast.28, s32[8]{0:T(128)} %lengths.1, bf16[1024,3072]{1,0:T(8,128)(2,1)} %qkv.3), custom_call_target="tpu_custom_call" | custom-call | flops 1 | bytes 1 | tf_op jit(solution)/shard_map/first/pallas_call | solution.py:140
  3.2 3.8 %collective-permute-start = (bf16[1296,128]{1,0:T(8,128)(2,1)S(1)}, bf16[1296,128]{1,0:T(8,128)(2,1)S(1)}, u32[]{:S(2)}, u32[]{:S(2)}) collective-permute-start(bf16[1296,128]{1,0:T(8,128)(2,1)S(1)} %get-tuple-element.37.refs_3_), channel_id=1, source_target_pairs={{0,4},{1,5},{2,6},{3,7},{4,0},{5,1},{6,2},{7,3},{8,12},{9,13},{10,... | collective-permute-start | bytes 995336 | tf_op jit(solution)/shard_map/ppermute | solution.py:90
  7.4 2.3 %collective-permute-start.2 = (bf16[1296,128]{1,0:T(8,128)(2,1)S(1)}, bf16[1296,128]{1,0:T(8,128)(2,1)S(1)}, u32[]{:S(2)}, u32[]{:S(2)}) collective-permute-start(bf16[1296,128]{1,0:T(8,128)(2,1)S(1)} %get-tuple-element.37.refs_3_), channel_id=1, source_target_pairs={{0,6},{1,7},{2,0},{3,1},{4,2},{5,3},{6,4},{7,5},{8,14},{9,15},{10,... | collective-permute-start | bytes 995336 | tf_op jit(solution)/shard_map/ppermute | solution.py:90
  9.7 1.5 %collective-permute-start.3 = (s32[4,8]{1,0:T(4,128)S(1)}, s32[4,8]{1,0:T(4,128)S(1)}, u32[]{:S(2)}, u32[]{:S(2)}) collective-permute-start(s32[4,8]{1,0:T(4,128)S(1)} %copy-done.5), channel_id=1, source_target_pairs={{0,1},{1,0},{2,3},{3,2},{4,5},{5,4},{6,7},{7,6},{8,9},{9,8},{10,11... | collective-permute-start | bytes 392 | tf_op jit(solution)/shard_map/ppermute | solution.py:90
  11.2 12.6 %attend.1 = (bf16[512,1024]{1,0:T(8,128)(2,1)S(1)}, bf16[16,256,128]{2,1,0:T(8,128)(2,1)S(1)}, bf16[16,256,128]{2,1,0:T(8,128)(2,1)S(1)}) custom-call(s32[4]{0:T(128)S(1)} %copy-done.4, bf16[1024,3072]{1,0:T(8,128)(2,1)} %qkv.3, bf16[1024,1024]{1,0:T(8,128)(2,1)} %wo_hbm.1, bf16[1024,512]{1,0:T(8,128)(2,1)} %up.3, bf16[1024,512]{1,0:T(8,128)(2,1)} %down.3, ...), custom_call_target="tpu_custom_call" | custom-call | flops 1 | bytes 1 | tf_op jit(solution)/shard_map/attend/pallas_call | solution.py:234
  24.1 1.7 %collective-permute-start.5 = (bf16[4160,128]{1,0:T(8,128)(2,1)S(1)}, bf16[4160,128]{1,0:T(8,128)(2,1)S(1)}, u32[]{:S(2)}, u32[]{:S(2)}) collective-permute-start(bf16[4160,128]{1,0:T(8,128)(2,1)S(1)} %join1.1.refs_0_), channel_id=1, source_target_pairs={{0,8},{1,33},{2,10},{3,35},{4,12},{5,37},{6,14},{7,39},{8,16},{9,4... | collective-permute-start | bytes 3194888 | tf_op jit(solution)/shard_map/ppermute | solution.py:90
  25.8 2.2 %collective-permute-start.6 = (bf16[4160,128]{1,0:T(8,128)(2,1)S(1)}, bf16[4160,128]{1,0:T(8,128)(2,1)S(1)}, u32[]{:S(2)}, u32[]{:S(2)}) collective-permute-start(bf16[4160,128]{1,0:T(8,128)(2,1)S(1)} %join1.1.refs_0_), channel_id=1, source_target_pairs={{0,24},{1,97},{2,26},{3,99},{4,28},{5,101},{6,30},{7,103},{8,0},{9... | collective-permute-start | bytes 3194888 | tf_op jit(solution)/shard_map/ppermute | solution.py:90
  28.0 1.2 %collective-permute-start.7 = (bf16[4160,128]{1,0:T(8,128)(2,1)S(1)}, bf16[4160,128]{1,0:T(8,128)(2,1)S(1)}, u32[]{:S(2)}, u32[]{:S(2)}) collective-permute-start(bf16[4160,128]{1,0:T(8,128)(2,1)S(1)} %join1.1.refs_0_), channel_id=1, source_target_pairs={{0,16},{1,65},{2,18},{3,67},{4,20},{5,69},{6,22},{7,71},{8,24},{9,... | collective-permute-start | bytes 3194888 | tf_op jit(solution)/shard_map/ppermute | solution.py:90
  29.6 2.3 %collective-permute-start.9 = (bf16[4096,128]{1,0:T(8,128)(2,1)S(1)}, bf16[4096,128]{1,0:T(8,128)(2,1)S(1)}, u32[]{:S(2)}, u32[]{:S(2)}) collective-permute-start(bf16[4096,128]{1,0:T(8,128)(2,1)S(1)} %bitcast.21), channel_id=1, source_target_pairs={{0,6},{1,7},{2,0},{3,1},{4,2},{5,3},{6,4},{7,5},{8,14},{9,15},{10,... | collective-permute-start | bytes 3145736 | tf_op jit(solution)/shard_map/ppermute | solution.py:90
  31.9 2.5 %ffn1.1 = (f32[512,1024]{1,0:T(8,128)S(1)}, f32[512,1024]{1,0:T(8,128)S(1)}) custom-call(bf16[512,1024]{1,0:T(8,128)(2,1)S(1)} %get-tuple-element.42.refs_0_.normed, bf16[512,1024]{1,0:T(8,128)(2,1)S(1)} %collective-permute-done.4.refs_1_.refs_0_, bf16[4096,128]{1,0:T(8,128)(2,1)S(1)} %bitcast.22, bf16[4096,128]{1,0:T(8,128)(2,1)S(1)} %bitcast.23), custom_call_target="tpu_custom_call" | custom-call | flops 1 | bytes 1 | tf_op jit(solution)/shard_map/ffn1/pallas_call | solution.py:317
  34.3 6.2 %collective-permute-done.5.refs_7_.refs_1_ = bf16[4160,128]{1,0:T(8,128)(2,1)S(1)} collective-permute-done((bf16[4160,128]{1,0:T(8,128)(2,1)S(1)}, bf16[4160,128]{1,0:T(8,128)(2,1)S(1)}, u32[]{:S(2)}, u32[]{:S(2)}) %collective-permute-start.5) | collective-permute-done | bytes 1064992 | tf_op jit(solution)/shard_map/ppermute | solution.py:90
  40.5 3.0 %ffn2.1 = (f32[512,1024]{1,0:T(8,128)S(1)}, f32[512,1024]{1,0:T(8,128)S(1)}) custom-call(bf16[512,1024]{1,0:T(8,128)(2,1)S(1)} %get-tuple-element.42.refs_0_.normed, bf16[512,1024]{1,0:T(8,128)(2,1)S(1)} %collective-permute-done.4.refs_1_.refs_0_, f32[512,1024]{1,0:T(8,128)S(1)} %get-tuple-element.45.refs_2_, ...), custom_call_target="tpu_custom_call", output_to_operand_aliasing={{0}: (2, {}), {1}: (3, {})} | custom-call | flops 1 | bytes 1 | tf_op jit(solution)/shard_map/ffn2/pallas_call | solution.py:317
  43.6 7.7 %collective-permute-done.6.refs_2_.refs_4_ = bf16[4160,128]{1,0:T(8,128)(2,1)S(1)} collective-permute-done((bf16[4160,128]{1,0:T(8,128)(2,1)S(1)}, bf16[4160,128]{1,0:T(8,128)(2,1)S(1)}, u32[]{:S(2)}, u32[]{:S(2)}) %collective-permute-start.6) | collective-permute-done | bytes 1064992 | tf_op jit(solution)/shard_map/ppermute | solution.py:90
  51.3 1.5 %collective-permute-done.7.refs_3_.refs_5_ = bf16[4160,128]{1,0:T(8,128)(2,1)S(1)} collective-permute-done((bf16[4160,128]{1,0:T(8,128)(2,1)S(1)}, bf16[4160,128]{1,0:T(8,128)(2,1)S(1)}, u32[]{:S(2)}, u32[]{:S(2)}) %collective-permute-start.7) | collective-permute-done | bytes 1064992 | tf_op jit(solution)/shard_map/ppermute | solution.py:90
  52.9 1.3 %collective-permute-start.12 = (bf16[4352,128]{1,0:T(8,128)(2,1)S(1)}, bf16[4352,128]{1,0:T(8,128)(2,1)S(1)}, u32[]{:S(2)}, u32[]{:S(2)}) collective-permute-start(bf16[4352,128]{1,0:T(8,128)(2,1)S(1)} %join2.1), channel_id=1, source_target_pairs={{0,32},{1,9},{2,34},{3,11},{4,36},{5,13},{6,38},{7,15},{8,40},{9,1... | collective-permute-start | bytes 3342344 | tf_op jit(solution)/shard_map/ppermute | solution.py:90
  54.2 1.5 %collective-permute-start.13 = (bf16[4352,128]{1,0:T(8,128)(2,1)S(1)}, bf16[4352,128]{1,0:T(8,128)(2,1)S(1)}, u32[]{:S(2)}, u32[]{:S(2)}) collective-permute-start(bf16[4352,128]{1,0:T(8,128)(2,1)S(1)} %join2.1), channel_id=1, source_target_pairs={{0,96},{1,25},{2,98},{3,27},{4,100},{5,29},{6,102},{7,31},{8,104},... | collective-permute-start | bytes 3342344 | tf_op jit(solution)/shard_map/ppermute | solution.py:90
  56.2 2.4 %collective-permute-start.11 = (bf16[2048,128]{1,0:T(8,128)(2,1)S(1)}, bf16[2048,128]{1,0:T(8,128)(2,1)S(1)}, u32[]{:S(2)}, u32[]{:S(2)}) collective-permute-start(bf16[2048,128]{1,0:T(8,128)(2,1)S(1)} %join6.1), channel_id=1, source_target_pairs={{0,6},{1,7},{2,0},{3,1},{4,2},{5,3},{6,4},{7,5},{8,14},{9,15},{10,... | collective-permute-start | bytes 1572872 | tf_op jit(solution)/shard_map/ppermute | solution.py:90
  58.6 4.7 %ffn3.1 = (f32[512,1024]{1,0:T(8,128)S(1)}, f32[512,1024]{1,0:T(8,128)S(1)}) custom-call(bf16[512,1024]{1,0:T(8,128)(2,1)S(1)} %get-tuple-element.42.refs_0_.normed, bf16[512,1024]{1,0:T(8,128)(2,1)S(1)} %collective-permute-done.4.refs_1_.refs_0_, f32[512,1024]{1,0:T(8,128)S(1)} %get-tuple-element.49.refs_2_, ...), custom_call_target="tpu_custom_call", output_to_operand_aliasing={{0}: (2, {}), {1}: (3, {})} | custom-call | flops 1 | bytes 1 | tf_op jit(solution)/shard_map/ffn3/pallas_call | solution.py:317
  63.3 5.6 %collective-permute-done.12.plus = bf16[4352,128]{1,0:T(8,128)(2,1)S(1)} collective-permute-done((bf16[4352,128]{1,0:T(8,128)(2,1)S(1)}, bf16[4352,128]{1,0:T(8,128)(2,1)S(1)}, u32[]{:S(2)}, u32[]{:S(2)}) %collective-permute-start.12) | collective-permute-done | bytes 1114144 | tf_op jit(solution)/shard_map/ppermute | solution.py:90
  68.9 1.0 %halves.1 = (bf16[2176,128]{1,0:T(8,128)(2,1)}, bf16[2176,128]{1,0:T(8,128)(2,1)}) custom-call(bf16[4352,128]{1,0:T(8,128)(2,1)S(1)} %collective-permute-done.12.plus, bf16[4352,128]{1,0:T(8,128)(2,1)S(1)} %collective-permute-done.13.minus), custom_call_target="tpu_custom_call" | custom-call | flops 1 | bytes 1 | tf_op jit(solution)/shard_map/halves/pallas_call | solution.py:269
  69.9 1.3 %ffn4.1 = f32[512,1024]{1,0:T(8,128)S(1)} custom-call(bf16[512,1024]{1,0:T(8,128)(2,1)S(1)} %collective-permute-done.4.refs_1_.refs_0_, f32[512,1024]{1,0:T(8,128)S(1)} %get-tuple-element.62.refs_1_, bf16[2048,128]{1,0:T(8,128)(2,1)S(1)} %collective-permute-done.10.refs_2_, ...), custom_call_target="tpu_custom_call", output_to_operand_aliasing={{}: (1, {})} | custom-call | flops 1 | bytes 1 | tf_op jit(solution)/shard_map/ffn4/pallas_call | solution.py:317
  71.2 2.0 %collective-permute-start.14 = (f32[512,1024]{1,0:T(8,128)S(1)}, f32[512,1024]{1,0:T(8,128)S(1)}, u32[]{:S(2)}, u32[]{:S(2)}) collective-permute-start(f32[512,1024]{1,0:T(8,128)S(1)} %ffn4.1), channel_id=1, source_target_pairs={{0,1},{1,0},{2,3},{3,2},{4,5},{5,4},{6,7},{7,6},{8,9},{9,8},{10,11... | collective-permute-start | bytes 6291464 | tf_op jit(solution)/shard_map/ppermute | solution.py:90
  73.3 1.1 %collective-permute-start.16 = (bf16[2176,128]{1,0:T(8,128)(2,1)}, bf16[2176,128]{1,0:T(8,128)(2,1)}, u32[]{:S(2)}, u32[]{:S(2)}) collective-permute-start(bf16[2176,128]{1,0:T(8,128)(2,1)} %get-tuple-element.58), channel_id=1, source_target_pairs={{0,32},{1,9},{2,34},{3,11},{4,36},{5,13},{6,38},{7,15},{8,40},{9,1... | collective-permute-start | bytes 1671176 | tf_op jit(solution)/shard_map/ppermute | solution.py:90
  74.4 1.5 %collective-permute-start.17 = (bf16[2176,128]{1,0:T(8,128)(2,1)}, bf16[2176,128]{1,0:T(8,128)(2,1)}, u32[]{:S(2)}, u32[]{:S(2)}) collective-permute-start(bf16[2176,128]{1,0:T(8,128)(2,1)} %get-tuple-element.59), channel_id=1, source_target_pairs={{0,96},{1,25},{2,98},{3,27},{4,100},{5,29},{6,102},{7,31},{8,104},... | collective-permute-start | bytes 1671176 | tf_op jit(solution)/shard_map/ppermute | solution.py:90
  75.9 1.3 %ffn5.1.mine = f32[512,1024]{1,0:T(8,128)S(1)} custom-call(bf16[512,1024]{1,0:T(8,128)(2,1)S(1)} %get-tuple-element.42.refs_0_.normed, f32[512,1024]{1,0:T(8,128)S(1)} %get-tuple-element.57.refs_1_, bf16[2048,128]{1,0:T(8,128)(2,1)S(1)} %collective-permute-done.10.refs_2_, ...), custom_call_target="tpu_custom_call", output_to_operand_aliasing={{}: (1, {})} | custom-call | flops 1 | bytes 1 | tf_op jit(solution)/shard_map/ffn5/pallas_call | solution.py:317
  77.3 2.4 %embed.1 = (bf16[512,128]{1,0:T(8,128)(2,1)}, bf16[512,128]{1,0:T(8,128)(2,1)S(1)}) custom-call(s32[4]{0:T(128)S(1)} %copy-done.4, bf16[512,1024]{1,0:T(8,128)(2,1)S(1)} %get-tuple-element.42.refs_0_.normed, f32[512,1024]{1,0:T(8,128)S(1)} %ffn5.1.mine, f32[512,1024]{1,0:T(8,128)S(1)} %collective-permute-done.14.other, f32[1,1024]{1,0:T(1,128)S(1)} %bitcast.27, ...), custom_call_target="tpu_custom_call" | custom-call | flops 1 | bytes 1 | tf_op jit(solution)/shard_map/embed/pallas_call | solution.py:346
  79.7 1.0 %collective-permute-start.15 = (bf16[512,128]{1,0:T(8,128)(2,1)S(1)}, bf16[512,128]{1,0:T(8,128)(2,1)}, u32[]{:S(2)}, u32[]{:S(2)}) collective-permute-start(bf16[512,128]{1,0:T(8,128)(2,1)S(1)} %get-tuple-element.65.emb), channel_id=1, source_target_pairs={{0,1},{1,0},{2,3},{3,2},{4,5},{5,4},{6,7},{7,6},{8,9},{9,8},{10,11... | collective-permute-start | bytes 393224 | tf_op jit(solution)/shard_map/ppermute | solution.py:90
  80.8 2.6 %collective-permute-done.16 = bf16[2176,128]{1,0:T(8,128)(2,1)} collective-permute-done((bf16[2176,128]{1,0:T(8,128)(2,1)}, bf16[2176,128]{1,0:T(8,128)(2,1)}, u32[]{:S(2)}, u32[]{:S(2)}) %collective-permute-start.16) | collective-permute-done | bytes 557088 | tf_op jit(solution)/shard_map/ppermute | solution.py:90
  83.5 3.0 %score.1 = (f32[32,128]{1,0:T(8,128)S(1)}, f32[32,128]{1,0:T(8,128)S(1)}) custom-call(s32[5]{0:T(128)S(1)} %stack.23.where, s32[32]{0:T(128)S(1)} %reshape.51.cand, s32[32]{0:T(128)S(1)} %reshape.52.pair, bf16[512,128]{1,0:T(8,128)(2,1)S(1)} %get-tuple-element.65.emb, bf16[512,128]{1,0:T(8,128)(2,1)} %collective-permute-done.15.sib, ...), custom_call_target="tpu_custom_call" | custom-call | flops 1 | bytes 1 | tf_op jit(solution)/shard_map/score/pallas_call | solution.py:423
  86.5 1.6 %collective-permute-start.18 = (f32[32,128]{1,0:T(8,128)S(1)}, f32[32,128]{1,0:T(8,128)S(1)}, u32[]{:S(2)}, u32[]{:S(2)}) collective-permute-start(f32[32,128]{1,0:T(8,128)S(1)} %get-tuple-element.67), channel_id=1, source_target_pairs={{0,1},{1,0},{2,3},{3,2},{4,5},{5,4},{6,7},{7,6},{8,9},{9,8},{10,11... | collective-permute-start | bytes 49160 | tf_op jit(solution)/shard_map/ppermute | solution.py:90
  88.1 0.8 collective-permute-done.18
  89.0 0.7 final.1
  (36 shorter events, 1.9 us)
Async XLA Ops:
  0.8 8.9 %copy-start.5 = (s32[4,8]{1,0:T(4,128)S(1)}, s32[4,8]{1,0:T(4,128)}, u32[]{:S(2)}) copy-start(s32[4,8]{1,0:T(4,128)} %param.23) | copy-start | bytes 388
  0.8 10.4 %copy-start = (bf16[512,1024]{1,0:T(8,128)(2,1)S(1)}, bf16[512,1024]{1,0:T(8,128)(2,1)}, u32[]{:S(2)}) copy-start(bf16[512,1024]{1,0:T(8,128)(2,1)} %tok.1) | copy-start | bytes 3145732
  0.8 10.4 %copy-start.2 = (f32[1024]{0:T(1024)S(1)}, f32[1024]{0:T(1024)}, u32[]{:S(2)}) copy-start(f32[1024]{0:T(1024)} %param.15) | copy-start | bytes 12292
  0.8 10.4 %copy-start.4 = (s32[4]{0:T(128)S(1)}, s32[4]{0:T(128)}, u32[]{:S(2)}) copy-start(s32[4]{0:T(128)} %length.3) | copy-start | bytes 52
  3.2 20.7 %collective-permute-start = (bf16[1296,128]{1,0:T(8,128)(2,1)S(1)}, bf16[1296,128]{1,0:T(8,128)(2,1)S(1)}, u32[]{:S(2)}, u32[]{:S(2)}) collective-permute-start(bf16[1296,128]{1,0:T(8,128)(2,1)S(1)} %get-tuple-element.37.refs_3_), channel_id=1, source_target_pairs={{0,4},{1,5},{2,6},{3,7},{4,0},{5,1},{6,2},{7,3},{8,12},{9,13},{10,... | collective-permute-start | bytes 995336 | tf_op jit(solution)/shard_map/ppermute | solution.py:90
  7.0 16.9 %collective-permute-start.1 = (bf16[1296,128]{1,0:T(8,128)(2,1)S(1)}, bf16[1296,128]{1,0:T(8,128)(2,1)S(1)}, u32[]{:S(2)}, u32[]{:S(2)}) collective-permute-start(bf16[1296,128]{1,0:T(8,128)(2,1)S(1)} %get-tuple-element.37.refs_3_), channel_id=1, source_target_pairs={{0,2},{1,3},{2,4},{3,5},{4,6},{5,7},{6,0},{7,1},{8,10},{9,11},{10,... | collective-permute-start | bytes 995336 | tf_op jit(solution)/shard_map/ppermute | solution.py:90
  7.4 16.5 %collective-permute-start.2 = (bf16[1296,128]{1,0:T(8,128)(2,1)S(1)}, bf16[1296,128]{1,0:T(8,128)(2,1)S(1)}, u32[]{:S(2)}, u32[]{:S(2)}) collective-permute-start(bf16[1296,128]{1,0:T(8,128)(2,1)S(1)} %get-tuple-element.37.refs_3_), channel_id=1, source_target_pairs={{0,6},{1,7},{2,0},{3,1},{4,2},{5,3},{6,4},{7,5},{8,14},{9,15},{10,... | collective-permute-start | bytes 995336 | tf_op jit(solution)/shard_map/ppermute | solution.py:90
  9.7 14.2 %collective-permute-start.3 = (s32[4,8]{1,0:T(4,128)S(1)}, s32[4,8]{1,0:T(4,128)S(1)}, u32[]{:S(2)}, u32[]{:S(2)}) collective-permute-start(s32[4,8]{1,0:T(4,128)S(1)} %copy-done.5), channel_id=1, source_target_pairs={{0,1},{1,0},{2,3},{3,2},{4,5},{5,4},{6,7},{7,6},{8,9},{9,8},{10,11... | collective-permute-start | bytes 392 | tf_op jit(solution)/shard_map/ppermute | solution.py:90
  24.0 5.2 %collective-permute-start.4 = (bf16[512,1024]{1,0:T(8,128)(2,1)S(1)}, bf16[512,1024]{1,0:T(8,128)(2,1)S(1)}, u32[]{:S(2)}, u32[]{:S(2)}) collective-permute-start(bf16[512,1024]{1,0:T(8,128)(2,1)S(1)} %get-tuple-element.42.refs_0_.normed), channel_id=1, source_target_pairs={{0,1},{1,0},{2,3},{3,2},{4,5},{5,4},{6,7},{7,6},{8,9},{9,8},{10,11... | collective-permute-start | bytes 3145736 | tf_op jit(solution)/shard_map/ppermute | solution.py:90
  24.1 16.5 %collective-permute-start.5 = (bf16[4160,128]{1,0:T(8,128)(2,1)S(1)}, bf16[4160,128]{1,0:T(8,128)(2,1)S(1)}, u32[]{:S(2)}, u32[]{:S(2)}) collective-permute-start(bf16[4160,128]{1,0:T(8,128)(2,1)S(1)} %join1.1.refs_0_), channel_id=1, source_target_pairs={{0,8},{1,33},{2,10},{3,35},{4,12},{5,37},{6,14},{7,39},{8,16},{9,4... | collective-permute-start | bytes 3194888 | tf_op jit(solution)/shard_map/ppermute | solution.py:90
  25.8 25.5 %collective-permute-start.6 = (bf16[4160,128]{1,0:T(8,128)(2,1)S(1)}, bf16[4160,128]{1,0:T(8,128)(2,1)S(1)}, u32[]{:S(2)}, u32[]{:S(2)}) collective-permute-start(bf16[4160,128]{1,0:T(8,128)(2,1)S(1)} %join1.1.refs_0_), channel_id=1, source_target_pairs={{0,24},{1,97},{2,26},{3,99},{4,28},{5,101},{6,30},{7,103},{8,0},{9... | collective-permute-start | bytes 3194888 | tf_op jit(solution)/shard_map/ppermute | solution.py:90
  28.0 24.9 %collective-permute-start.7 = (bf16[4160,128]{1,0:T(8,128)(2,1)S(1)}, bf16[4160,128]{1,0:T(8,128)(2,1)S(1)}, u32[]{:S(2)}, u32[]{:S(2)}) collective-permute-start(bf16[4160,128]{1,0:T(8,128)(2,1)S(1)} %join1.1.refs_0_), channel_id=1, source_target_pairs={{0,16},{1,65},{2,18},{3,67},{4,20},{5,69},{6,22},{7,71},{8,24},{9,... | collective-permute-start | bytes 3194888 | tf_op jit(solution)/shard_map/ppermute | solution.py:90
  29.2 26.5 %collective-permute-start.8 = (bf16[4096,128]{1,0:T(8,128)(2,1)S(1)}, bf16[4096,128]{1,0:T(8,128)(2,1)S(1)}, u32[]{:S(2)}, u32[]{:S(2)}) collective-permute-start(bf16[4096,128]{1,0:T(8,128)(2,1)S(1)} %bitcast.20), channel_id=1, source_target_pairs={{0,2},{1,3},{2,4},{3,5},{4,6},{5,7},{6,0},{7,1},{8,10},{9,11},{10,... | collective-permute-start | bytes 3145736 | tf_op jit(solution)/shard_map/ppermute | solution.py:90
  29.6 26.1 %collective-permute-start.9 = (bf16[4096,128]{1,0:T(8,128)(2,1)S(1)}, bf16[4096,128]{1,0:T(8,128)(2,1)S(1)}, u32[]{:S(2)}, u32[]{:S(2)}) collective-permute-start(bf16[4096,128]{1,0:T(8,128)(2,1)S(1)} %bitcast.21), channel_id=1, source_target_pairs={{0,6},{1,7},{2,0},{3,1},{4,2},{5,3},{6,4},{7,5},{8,14},{9,15},{10,... | collective-permute-start | bytes 3145736 | tf_op jit(solution)/shard_map/ppermute | solution.py:90
  52.9 15.9 %collective-permute-start.12 = (bf16[4352,128]{1,0:T(8,128)(2,1)S(1)}, bf16[4352,128]{1,0:T(8,128)(2,1)S(1)}, u32[]{:S(2)}, u32[]{:S(2)}) collective-permute-start(bf16[4352,128]{1,0:T(8,128)(2,1)S(1)} %join2.1), channel_id=1, source_target_pairs={{0,32},{1,9},{2,34},{3,11},{4,36},{5,13},{6,38},{7,15},{8,40},{9,1... | collective-permute-start | bytes 3342344 | tf_op jit(solution)/shard_map/ppermute | solution.py:90
  54.2 14.6 %collective-permute-start.13 = (bf16[4352,128]{1,0:T(8,128)(2,1)S(1)}, bf16[4352,128]{1,0:T(8,128)(2,1)S(1)}, u32[]{:S(2)}, u32[]{:S(2)}) collective-permute-start(bf16[4352,128]{1,0:T(8,128)(2,1)S(1)} %join2.1), channel_id=1, source_target_pairs={{0,96},{1,25},{2,98},{3,27},{4,100},{5,29},{6,102},{7,31},{8,104},... | collective-permute-start | bytes 3342344 | tf_op jit(solution)/shard_map/ppermute | solution.py:90
  55.7 14.2 %collective-permute-start.10 = (bf16[2048,128]{1,0:T(8,128)(2,1)S(1)}, bf16[2048,128]{1,0:T(8,128)(2,1)S(1)}, u32[]{:S(2)}, u32[]{:S(2)}) collective-permute-start(bf16[2048,128]{1,0:T(8,128)(2,1)S(1)} %join5.1), channel_id=1, source_target_pairs={{0,2},{1,3},{2,4},{3,5},{4,6},{5,7},{6,0},{7,1},{8,10},{9,11},{10,... | collective-permute-start | bytes 1572872 | tf_op jit(solution)/shard_map/ppermute | solution.py:90
  56.2 13.7 %collective-permute-start.11 = (bf16[2048,128]{1,0:T(8,128)(2,1)S(1)}, bf16[2048,128]{1,0:T(8,128)(2,1)S(1)}, u32[]{:S(2)}, u32[]{:S(2)}) collective-permute-start(bf16[2048,128]{1,0:T(8,128)(2,1)S(1)} %join6.1), channel_id=1, source_target_pairs={{0,6},{1,7},{2,0},{3,1},{4,2},{5,3},{6,4},{7,5},{8,14},{9,15},{10,... | collective-permute-start | bytes 1572872 | tf_op jit(solution)/shard_map/ppermute | solution.py:90
  71.2 6.0 %collective-permute-start.14 = (f32[512,1024]{1,0:T(8,128)S(1)}, f32[512,1024]{1,0:T(8,128)S(1)}, u32[]{:S(2)}, u32[]{:S(2)}) collective-permute-start(f32[512,1024]{1,0:T(8,128)S(1)} %ffn4.1), channel_id=1, source_target_pairs={{0,1},{1,0},{2,3},{3,2},{4,5},{5,4},{6,7},{7,6},{8,9},{9,8},{10,11... | collective-permute-start | bytes 6291464 | tf_op jit(solution)/shard_map/ppermute | solution.py:90
  73.3 10.2 %collective-permute-start.16 = (bf16[2176,128]{1,0:T(8,128)(2,1)}, bf16[2176,128]{1,0:T(8,128)(2,1)}, u32[]{:S(2)}, u32[]{:S(2)}) collective-permute-start(bf16[2176,128]{1,0:T(8,128)(2,1)} %get-tuple-element.58), channel_id=1, source_target_pairs={{0,32},{1,9},{2,34},{3,11},{4,36},{5,13},{6,38},{7,15},{8,40},{9,1... | collective-permute-start | bytes 1671176 | tf_op jit(solution)/shard_map/ppermute | solution.py:90
  74.4 9.1 %collective-permute-start.17 = (bf16[2176,128]{1,0:T(8,128)(2,1)}, bf16[2176,128]{1,0:T(8,128)(2,1)}, u32[]{:S(2)}, u32[]{:S(2)}) collective-permute-start(bf16[2176,128]{1,0:T(8,128)(2,1)} %get-tuple-element.59), channel_id=1, source_target_pairs={{0,96},{1,25},{2,98},{3,27},{4,100},{5,29},{6,102},{7,31},{8,104},... | collective-permute-start | bytes 1671176 | tf_op jit(solution)/shard_map/ppermute | solution.py:90
  75.9 1.3 %copy-start.1 = (bf16[1024,128]{1,0:T(8,128)(2,1)S(1)}, bf16[1024,128]{1,0:T(8,128)(2,1)}, u32[]{:S(2)}) copy-start(bf16[1024,128]{1,0:T(8,128)(2,1)} %we.1) | copy-start | bytes 786436
  75.9 1.3 %copy-start.3 = (f32[1024]{0:T(1024)S(1)}, f32[1024]{0:T(1024)}, u32[]{:S(2)}) copy-start(f32[1024]{0:T(1024)} %param.18) | copy-start | bytes 12292
  79.7 3.8 %collective-permute-start.15 = (bf16[512,128]{1,0:T(8,128)(2,1)S(1)}, bf16[512,128]{1,0:T(8,128)(2,1)}, u32[]{:S(2)}, u32[]{:S(2)}) collective-permute-start(bf16[512,128]{1,0:T(8,128)(2,1)S(1)} %get-tuple-element.65.emb), channel_id=1, source_target_pairs={{0,1},{1,0},{2,3},{3,2},{4,5},{5,4},{6,7},{7,6},{8,9},{9,8},{10,11... | collective-permute-start | bytes 393224 | tf_op jit(solution)/shard_map/ppermute | solution.py:90
  86.5 2.5 %collective-permute-start.18 = (f32[32,128]{1,0:T(8,128)S(1)}, f32[32,128]{1,0:T(8,128)S(1)}, u32[]{:S(2)}, u32[]{:S(2)}) collective-permute-start(f32[32,128]{1,0:T(8,128)S(1)} %get-tuple-element.67), channel_id=1, source_target_pairs={{0,1},{1,0},{2,3},{3,2},{4,5},{5,4},{6,7},{7,6},{8,9},{9,8},{10,11... | collective-permute-start | bytes 49160 | tf_op jit(solution)/shard_map/ppermute | solution.py:90

commit v10 on v9

--- a/solution.py
+++ b/solution.py
@@ -109,14 +109,13 @@
 SMEM = pl.BlockSpec(memory_space=pltpu.SMEM)
 
 
-def first_body(where, up, down, docs, lengths, qkv, out, query, held, turned, limits, sems):
+def first_body(where, up, down, docs, lengths, out, held, turned, limits, sems):
     index = where[4]
     lanes = pl.ds(pl.multiple_of(256 + (index >> 1) * LANES, LANES), LANES)
     copies = [pltpu.make_async_copy(w.at[:, lanes], held.at[k], sems.at[k]) for k, w in enumerate((up, down))]
     tokens = DOC_ROWS - 16
     copies.append(pltpu.make_async_copy(docs, out.at[PART : PART + tokens], sems.at[2]))
     copies.append(pltpu.make_async_copy(lengths, limits, sems.at[3]))
-    copies.append(pltpu.make_async_copy(qkv.at[:, :D], query, sems.at[4]))
     for copy in copies:
         copy.start()
     start = pl.multiple_of((index & 1) * SLICE, SLICE)
@@ -133,25 +132,24 @@
         limit = jnp.where(row == j, limits[j].astype(f32), limit)
     out[PART + tokens : BLOCK, :] = limit.astype(bf16)
     copies[2].wait()
-    copies[4].wait()
-
-
-def first(where, up, down, docs, lengths, qkv):
+
+
+def first(where, up, down, docs, lengths):
     return pl.pallas_call(
         first_body,
-        out_shape=(jax.ShapeDtypeStruct((BLOCK, LANES), bf16), jax.ShapeDtypeStruct((D, D), bf16)),
-        in_specs=[SMEM] + hbm(5),
-        out_specs=tuple(vmem(2)),
+        out_shape=jax.ShapeDtypeStruct((BLOCK, LANES), bf16),
+        in_specs=[SMEM] + hbm(4),
+        out_specs=vmem()[0],
         scratch_shapes=[
             pltpu.VMEM((2, D, LANES), bf16),
             pltpu.VMEM((SLABS, LANES, LANES), bf16),
             pltpu.SMEM((8,), jnp.int32),
-            pltpu.SemaphoreType.DMA((5,)),
+            pltpu.SemaphoreType.DMA((4,)),
         ],
         compiler_params=params(8),
         cost_estimate=LIGHT,
         name="first",
-    )(where, *pinned(up, down, docs, lengths, qkv))
+    )(where, *pinned(up, down, docs, lengths))
 
 
 def join_body(takes, *refs):
@@ -180,34 +178,32 @@
 
 
 def attend_body(
-    length, qkv, wo_hbm, up, down, tok, query, gain, out, low_out, high_out, packed, context, held, wo, wide, added, sems
+    length, qkv, wo_hbm, up, down, tok, gain, out, low_out, high_out, packed, context, held, wo, wide, added, sems
 ):
     rows_all = tok.shape[0]
     step = 512
-    sources = [(qkv.at[:, D + c : D + c + step], held.at[:, c : c + step]) for c in range(0, 2 * D, step)]
+    sources = [(qkv.at[:, c : c + step], held.at[:, c : c + step]) for c in range(0, 3 * D, step)]
     sources += [(up, wide.at[0]), (down, wide.at[1]), (wo_hbm, wo)]
     copies = [pltpu.make_async_copy(source, target, sems.at[i]) for i, (source, target) in enumerate(sources)]
-    for copy in copies[:4]:
+    for copy in copies[:3]:
         copy.start()
-    packed[:, :D] = dot(tok[...], query[...]).astype(bf16)
-    for copy in copies[4:]:
-        copy.start()
-    for i in range(4):
+    for i in range(6):
         copies[i].wait()
+        copies[3 + i].start()
         columns = slice(i * step, (i + 1) * step)
-        packed[:, D + i * step : D + (i + 1) * step] = dot(tok[...], held[:, columns]).astype(bf16)
+        packed[:, columns] = dot(tok[...], held[:, columns]).astype(bf16)
     for k in range(2):
-        copies[4 + k].wait()
+        copies[6 + k].wait()
         for j in range(HALF):
             rows = slice(j * LANES, (j + 1) * LANES)
             low_out[k * HALF + j] = wide[k, rows, :256].T
             high_out[k * HALF + j] = wide[k, rows, 256:].T
-    lane = lax.broadcasted_iota(jnp.int32, (2 * SEQ, LANES), 1)
+    key = lax.broadcasted_iota(jnp.int32, (SEQ, 2 * LANES), 0)
     low = lax.broadcasted_iota(jnp.int32, (SEQ, LANES), 1) < HD
 
     def request(r, carry):
         rows = pl.ds(pl.multiple_of(r * SEQ, SEQ), SEQ)
-        live = lane < length[r]
+        live = key < length[r]
         for p in range(HEADS // 2):
             at = p * LANES
             q = packed[rows, at : at + LANES]
@@ -215,40 +211,40 @@
             v = packed[rows, 2 * D + at : 2 * D + at + LANES]
             zero = jnp.zeros_like(q)
             both = jnp.concatenate([jnp.where(low, q, zero), jnp.where(low, zero, q)], axis=0)
-            logits = jnp.where(live, dot_t(both, k) * HD ** (-0.5), DEAD)
-            weights = jnp.exp(logits - jnp.max(logits, axis=-1, keepdims=True))
-            probs = (weights * (1.0 / jnp.sum(weights, axis=-1, keepdims=True))).astype(bf16)
-            ctx = dot(probs, v)
+            logits = jnp.where(live, dot_t(k, both) * HD ** (-0.5), DEAD)
+            weights = jnp.exp(logits - jnp.max(logits, axis=0, keepdims=True))
+            probs = (weights * (1.0 / jnp.sum(weights, axis=0, keepdims=True))).astype(bf16)
+            ctx = lax.dot_general(probs, v, (((0,), (0,)), ((), ())), preferred_element_type=f32)
             context[rows, at : at + LANES] = jnp.where(low, ctx[:SEQ], ctx[SEQ:]).astype(bf16)
         return carry
 
-    lax.fori_loop(0, rows_all // SEQ, request, 0)
-    copies[6].wait()
+    lax.fori_loop(0, rows_all // SEQ, request, 0, unroll=True)
+    copies[8].wait()
     added[...] = dot(context[...], wo[...])
     norm_into(out, lambda rows: tok[rows, :].astype(f32) + added[rows, :], gain[...])
 
 
-def attend(tokens, qkv, query, wo, gain, length, up, down):
+def attend(tokens, qkv, wo, gain, length, up, down):
     rows = tokens.shape[0]
     piece = jax.ShapeDtypeStruct((SLABS, 256, LANES), bf16)
     normed, low, high = pl.pallas_call(
         attend_body,
         out_shape=(jax.ShapeDtypeStruct((rows, D), bf16), piece, piece),
-        in_specs=[SMEM] + hbm(4) + vmem(3),
+        in_specs=[SMEM] + hbm(4) + vmem(2),
         out_specs=tuple(vmem(3)),
         scratch_shapes=[
             pltpu.VMEM((rows, 3 * D), bf16),
             pltpu.VMEM((rows, D), bf16),
-            pltpu.VMEM((D, 2 * D), bf16),
+            pltpu.VMEM((D, 3 * D), bf16),
             pltpu.VMEM((D, D), bf16),
             pltpu.VMEM((2, D, 512), bf16),
             pltpu.VMEM((rows, D), f32),
-            pltpu.SemaphoreType.DMA((7,)),
+            pltpu.SemaphoreType.DMA((9,)),
         ],
         compiler_params=params(28),
         cost_estimate=LIGHT,
         name="attend",
-    )(length, *pinned(qkv, wo, up, down), tokens, query, gain.reshape(1, D))
+    )(length, *pinned(qkv, wo, up, down), tokens, gain.reshape(1, D))
     return normed, low.reshape(-1, LANES), high.reshape(-1, LANES)
 
 
@@ -452,12 +448,10 @@
     req, mlp = lax.axis_index("req"), lax.axis_index("mlp")
     z, x, y, c = req // 4, req % 4, mlp // 2, mlp % 2
     where = jnp.stack([z, x, y, c, jnp.where(c == 0, x, z)]).astype(jnp.int32)
-    start, query = first(
-        where, up_weight, down_weight, documents.reshape(-1, P_SIZE), document_length, attend_weight
-    )
+    start = first(where, up_weight, down_weight, documents.reshape(-1, P_SIZE), document_length)
     near = [send(start, way) for way in ("y2", "y+", "y-")]
     normed, low, high = attend(
-        tokens, attend_weight, query, output_weight, attend_gain, query_length, up_weight, down_weight
+        tokens, attend_weight, output_weight, after(attend_gain, start), query_length, up_weight, down_weight
     )
     pair = send(after(candidates, start), "c")
     near, pair = after((tuple(near), pair), normed)

time: 89.8 us -> 88.2 us (0.982)
  Pallas kernels: 35.2 us -> 32.4 us
    pallas_call x1, Pallas kernels: 12.6 us -> 10.4 us  [attend(): pl.pallas_call(attend_body, out_shape=(jax.ShapeDtypeStruct((rows, D), bf...]
  transfers between devices with their start and end apart: 19 -> 19, of which waited for: 6 -> 7; matrix products, arithmetic and copies ran while one was open for 0% -> 0% of each run, Pallas kernels for 31% -> 29%
where the time goes in v10:
time: 88.2 us; the launch traced here: 88.1 us
  Pallas kernels  32.4 us (37%)
  starting transfers between devices  29.3 us (33%)
  waiting for transfers between devices  25.2 us (29%)
    ppermute x19, starting transfers between devices, send(): return lax.ppermute(value, ('req', 'mlp'), STEPS[way])  29.3 us
    ppermute x19, waiting for transfers between devices, send(): return lax.ppermute(value, ('req', 'mlp'), STEPS[way])  25.2 us
    pallas_call x5, Pallas kernels, ffn(): pl.pallas_call(functools.partial(ffn_body, tuple(pieces), len(arrays), se...  12.8 us
    pallas_call x1, Pallas kernels, attend(): pl.pallas_call(attend_body, out_shape=(jax.ShapeDtypeStruct((rows, D), bf...  10.4 us
    pallas_call x1, Pallas kernels, score(): pl.pallas_call(score_body, out_shape=(jax.ShapeDtypeStruct((total, SEQ),...  3.04 us
    pallas_call x1, Pallas kernels, embed(): pl.pallas_call(embed_body, out_shape=(shape, shape), in_specs=[SMEM] + vm...  2.36 us
    pallas_call x1, Pallas kernels, first(): pl.pallas_call(first_body, out_shape=jax.ShapeDtypeStruct((BLOCK, LANES),...  1.84 us
  transfers between devices with their start and end apart: 19, of which 7 were waited for; matrix products, arithmetic and copies ran while one was open for 0% of the time, Pallas kernels for 29%

profile of v10, /device:TPU:1, one launch (start us, length us, event | category | flops | bytes accessed | tf_op | source)
XLA Modules:
  0.0 88.1 jit_solution(4877343877073271095)
XLA Ops:
  0.8 1.8 %first.1.refs_3_ = bf16[1296,128]{1,0:T(8,128)(2,1)S(1)} custom-call(s32[5]{0:T(128)S(1)} %stack.23.where, bf16[1024,512]{1,0:T(8,128)(2,1)} %up.3, bf16[1024,512]{1,0:T(8,128)(2,1)} %down.3, bf16[256,128]{1,0:T(8,128)(2,1)} %bitcast.28, s32[8]{0:T(128)} %lengths.1), custom_call_target="tpu_custom_call" | custom-call | flops 1 | bytes 1 | tf_op jit(solution)/shard_map/first/pallas_call | solution.py:138
  2.6 3.8 %collective-permute-start = (bf16[1296,128]{1,0:T(8,128)(2,1)S(1)}, bf16[1296,128]{1,0:T(8,128)(2,1)S(1)}, u32[]{:S(2)}, u32[]{:S(2)}) collective-permute-start(bf16[1296,128]{1,0:T(8,128)(2,1)S(1)} %first.1.refs_3_), channel_id=1, source_target_pairs={{0,4},{1,5},{2,6},{3,7},{4,0},{5,1},{6,2},{7,3},{8,12},{9,13},{10,... | collective-permute-start | bytes 995336 | tf_op jit(solution)/shard_map/ppermute | solution.py:90
  6.9 2.3 %collective-permute-start.2 = (bf16[1296,128]{1,0:T(8,128)(2,1)S(1)}, bf16[1296,128]{1,0:T(8,128)(2,1)S(1)}, u32[]{:S(2)}, u32[]{:S(2)}) collective-permute-start(bf16[1296,128]{1,0:T(8,128)(2,1)S(1)} %first.1.refs_3_), channel_id=1, source_target_pairs={{0,6},{1,7},{2,0},{3,1},{4,2},{5,3},{6,4},{7,5},{8,14},{9,15},{10,... | collective-permute-start | bytes 995336 | tf_op jit(solution)/shard_map/ppermute | solution.py:90
  9.1 1.5 %collective-permute-start.3 = (s32[4,8]{1,0:T(4,128)S(1)}, s32[4,8]{1,0:T(4,128)S(1)}, u32[]{:S(2)}, u32[]{:S(2)}) collective-permute-start(s32[4,8]{1,0:T(4,128)S(1)} %copy-done.5), channel_id=1, source_target_pairs={{0,1},{1,0},{2,3},{3,2},{4,5},{5,4},{6,7},{7,6},{8,9},{9,8},{10,11... | collective-permute-start | bytes 392 | tf_op jit(solution)/shard_map/ppermute | solution.py:90
  10.7 10.4 %attend.1 = (bf16[512,1024]{1,0:T(8,128)(2,1)S(1)}, bf16[16,256,128]{2,1,0:T(8,128)(2,1)S(1)}, bf16[16,256,128]{2,1,0:T(8,128)(2,1)S(1)}) custom-call(s32[4]{0:T(128)S(1)} %copy-done.4, bf16[1024,3072]{1,0:T(8,128)(2,1)} %qkv.1, bf16[1024,1024]{1,0:T(8,128)(2,1)} %wo_hbm.1, bf16[1024,512]{1,0:T(8,128)(2,1)} %up.3, bf16[1024,512]{1,0:T(8,128)(2,1)} %down.3, ...), custom_call_target="tpu_custom_call" | custom-call | flops 1 | bytes 1 | tf_op jit(solution)/shard_map/attend/pallas_call | solution.py:230
  22.9 1.7 %collective-permute-start.5 = (bf16[4160,128]{1,0:T(8,128)(2,1)S(1)}, bf16[4160,128]{1,0:T(8,128)(2,1)S(1)}, u32[]{:S(2)}, u32[]{:S(2)}) collective-permute-start(bf16[4160,128]{1,0:T(8,128)(2,1)S(1)} %join1.1.refs_0_), channel_id=1, source_target_pairs={{0,8},{1,33},{2,10},{3,35},{4,12},{5,37},{6,14},{7,39},{8,16},{9,4... | collective-permute-start | bytes 3194888 | tf_op jit(solution)/shard_map/ppermute | solution.py:90
  24.6 2.1 %collective-permute-start.6 = (bf16[4160,128]{1,0:T(8,128)(2,1)S(1)}, bf16[4160,128]{1,0:T(8,128)(2,1)S(1)}, u32[]{:S(2)}, u32[]{:S(2)}) collective-permute-start(bf16[4160,128]{1,0:T(8,128)(2,1)S(1)} %join1.1.refs_0_), channel_id=1, source_target_pairs={{0,24},{1,97},{2,26},{3,99},{4,28},{5,101},{6,30},{7,103},{8,0},{9... | collective-permute-start | bytes 3194888 | tf_op jit(solution)/shard_map/ppermute | solution.py:90
  26.7 1.3 %collective-permute-start.7 = (bf16[4160,128]{1,0:T(8,128)(2,1)S(1)}, bf16[4160,128]{1,0:T(8,128)(2,1)S(1)}, u32[]{:S(2)}, u32[]{:S(2)}) collective-permute-start(bf16[4160,128]{1,0:T(8,128)(2,1)S(1)} %join1.1.refs_0_), channel_id=1, source_target_pairs={{0,16},{1,65},{2,18},{3,67},{4,20},{5,69},{6,22},{7,71},{8,24},{9,... | collective-permute-start | bytes 3194888 | tf_op jit(solution)/shard_map/ppermute | solution.py:90
  28.0 1.1 %collective-permute-start.8 = (bf16[4096,128]{1,0:T(8,128)(2,1)S(1)}, bf16[4096,128]{1,0:T(8,128)(2,1)S(1)}, u32[]{:S(2)}, u32[]{:S(2)}) collective-permute-start(bf16[4096,128]{1,0:T(8,128)(2,1)S(1)} %bitcast.20), channel_id=1, source_target_pairs={{0,2},{1,3},{2,4},{3,5},{4,6},{5,7},{6,0},{7,1},{8,10},{9,11},{10,... | collective-permute-start | bytes 3145736 | tf_op jit(solution)/shard_map/ppermute | solution.py:90
  29.1 1.6 %collective-permute-start.9 = (bf16[4096,128]{1,0:T(8,128)(2,1)S(1)}, bf16[4096,128]{1,0:T(8,128)(2,1)S(1)}, u32[]{:S(2)}, u32[]{:S(2)}) collective-permute-start(bf16[4096,128]{1,0:T(8,128)(2,1)S(1)} %bitcast.21), channel_id=1, source_target_pairs={{0,6},{1,7},{2,0},{3,1},{4,2},{5,3},{6,4},{7,5},{8,14},{9,15},{10,... | collective-permute-start | bytes 3145736 | tf_op jit(solution)/shard_map/ppermute | solution.py:90
  30.7 2.5 %ffn1.1 = (f32[512,1024]{1,0:T(8,128)S(1)}, f32[512,1024]{1,0:T(8,128)S(1)}) custom-call(bf16[512,1024]{1,0:T(8,128)(2,1)S(1)} %get-tuple-element.40.refs_0_.normed, bf16[512,1024]{1,0:T(8,128)(2,1)S(1)} %collective-permute-done.4.refs_1_.refs_0_, bf16[4096,128]{1,0:T(8,128)(2,1)S(1)} %bitcast.22, bf16[4096,128]{1,0:T(8,128)(2,1)S(1)} %bitcast.23), custom_call_target="tpu_custom_call" | custom-call | flops 1 | bytes 1 | tf_op jit(solution)/shard_map/ffn1/pallas_call | solution.py:313
  33.1 6.2 %collective-permute-done.5.refs_7_.refs_1_ = bf16[4160,128]{1,0:T(8,128)(2,1)S(1)} collective-permute-done((bf16[4160,128]{1,0:T(8,128)(2,1)S(1)}, bf16[4160,128]{1,0:T(8,128)(2,1)S(1)}, u32[]{:S(2)}, u32[]{:S(2)}) %collective-permute-start.5) | collective-permute-done | bytes 1064992 | tf_op jit(solution)/shard_map/ppermute | solution.py:90
  39.4 3.0 %ffn2.1 = (f32[512,1024]{1,0:T(8,128)S(1)}, f32[512,1024]{1,0:T(8,128)S(1)}) custom-call(bf16[512,1024]{1,0:T(8,128)(2,1)S(1)} %get-tuple-element.40.refs_0_.normed, bf16[512,1024]{1,0:T(8,128)(2,1)S(1)} %collective-permute-done.4.refs_1_.refs_0_, f32[512,1024]{1,0:T(8,128)S(1)} %get-tuple-element.43.refs_2_, ...), custom_call_target="tpu_custom_call", output_to_operand_aliasing={{0}: (2, {}), {1}: (3, {})} | custom-call | flops 1 | bytes 1 | tf_op jit(solution)/shard_map/ffn2/pallas_call | solution.py:313
  42.4 7.6 %collective-permute-done.6.refs_2_.refs_4_ = bf16[4160,128]{1,0:T(8,128)(2,1)S(1)} collective-permute-done((bf16[4160,128]{1,0:T(8,128)(2,1)S(1)}, bf16[4160,128]{1,0:T(8,128)(2,1)S(1)}, u32[]{:S(2)}, u32[]{:S(2)}) %collective-permute-start.6) | collective-permute-done | bytes 1064992 | tf_op jit(solution)/shard_map/ppermute | solution.py:90
  50.0 1.6 %collective-permute-done.7.refs_3_.refs_5_ = bf16[4160,128]{1,0:T(8,128)(2,1)S(1)} collective-permute-done((bf16[4160,128]{1,0:T(8,128)(2,1)S(1)}, bf16[4160,128]{1,0:T(8,128)(2,1)S(1)}, u32[]{:S(2)}, u32[]{:S(2)}) %collective-permute-start.7) | collective-permute-done | bytes 1064992 | tf_op jit(solution)/shard_map/ppermute | solution.py:90
  51.7 1.3 %collective-permute-start.12 = (bf16[4352,128]{1,0:T(8,128)(2,1)S(1)}, bf16[4352,128]{1,0:T(8,128)(2,1)S(1)}, u32[]{:S(2)}, u32[]{:S(2)}) collective-permute-start(bf16[4352,128]{1,0:T(8,128)(2,1)S(1)} %join2.1), channel_id=1, source_target_pairs={{0,32},{1,9},{2,34},{3,11},{4,36},{5,13},{6,38},{7,15},{8,40},{9,1... | collective-permute-start | bytes 3342344 | tf_op jit(solution)/shard_map/ppermute | solution.py:90
  53.0 1.5 %collective-permute-start.13 = (bf16[4352,128]{1,0:T(8,128)(2,1)S(1)}, bf16[4352,128]{1,0:T(8,128)(2,1)S(1)}, u32[]{:S(2)}, u32[]{:S(2)}) collective-permute-start(bf16[4352,128]{1,0:T(8,128)(2,1)S(1)} %join2.1), channel_id=1, source_target_pairs={{0,96},{1,25},{2,98},{3,27},{4,100},{5,29},{6,102},{7,31},{8,104},... | collective-permute-start | bytes 3342344 | tf_op jit(solution)/shard_map/ppermute | solution.py:90
  54.5 1.1 %collective-permute-start.10 = (bf16[2048,128]{1,0:T(8,128)(2,1)S(1)}, bf16[2048,128]{1,0:T(8,128)(2,1)S(1)}, u32[]{:S(2)}, u32[]{:S(2)}) collective-permute-start(bf16[2048,128]{1,0:T(8,128)(2,1)S(1)} %join5.1), channel_id=1, source_target_pairs={{0,2},{1,3},{2,4},{3,5},{4,6},{5,7},{6,0},{7,1},{8,10},{9,11},{10,... | collective-permute-start | bytes 1572872 | tf_op jit(solution)/shard_map/ppermute | solution.py:90
  55.7 1.7 %collective-permute-start.11 = (bf16[2048,128]{1,0:T(8,128)(2,1)S(1)}, bf16[2048,128]{1,0:T(8,128)(2,1)S(1)}, u32[]{:S(2)}, u32[]{:S(2)}) collective-permute-start(bf16[2048,128]{1,0:T(8,128)(2,1)S(1)} %join6.1), channel_id=1, source_target_pairs={{0,6},{1,7},{2,0},{3,1},{4,2},{5,3},{6,4},{7,5},{8,14},{9,15},{10,... | collective-permute-start | bytes 1572872 | tf_op jit(solution)/shard_map/ppermute | solution.py:90
  57.4 4.7 %ffn3.1 = (f32[512,1024]{1,0:T(8,128)S(1)}, f32[512,1024]{1,0:T(8,128)S(1)}) custom-call(bf16[512,1024]{1,0:T(8,128)(2,1)S(1)} %get-tuple-element.40.refs_0_.normed, bf16[512,1024]{1,0:T(8,128)(2,1)S(1)} %collective-permute-done.4.refs_1_.refs_0_, f32[512,1024]{1,0:T(8,128)S(1)} %get-tuple-element.47.refs_2_, ...), custom_call_target="tpu_custom_call", output_to_operand_aliasing={{0}: (2, {}), {1}: (3, {})} | custom-call | flops 1 | bytes 1 | tf_op jit(solution)/shard_map/ffn3/pallas_call | solution.py:313
  62.1 5.5 %collective-permute-done.12.plus = bf16[4352,128]{1,0:T(8,128)(2,1)S(1)} collective-permute-done((bf16[4352,128]{1,0:T(8,128)(2,1)S(1)}, bf16[4352,128]{1,0:T(8,128)(2,1)S(1)}, u32[]{:S(2)}, u32[]{:S(2)}) %collective-permute-start.12) | collective-permute-done | bytes 1114144 | tf_op jit(solution)/shard_map/ppermute | solution.py:90
  67.7 1.0 %halves.1 = (bf16[2176,128]{1,0:T(8,128)(2,1)}, bf16[2176,128]{1,0:T(8,128)(2,1)}) custom-call(bf16[4352,128]{1,0:T(8,128)(2,1)S(1)} %collective-permute-done.12.plus, bf16[4352,128]{1,0:T(8,128)(2,1)S(1)} %collective-permute-done.13.minus), custom_call_target="tpu_custom_call" | custom-call | flops 1 | bytes 1 | tf_op jit(solution)/shard_map/halves/pallas_call | solution.py:265
  68.7 1.3 %ffn4.1 = f32[512,1024]{1,0:T(8,128)S(1)} custom-call(bf16[512,1024]{1,0:T(8,128)(2,1)S(1)} %collective-permute-done.4.refs_1_.refs_0_, f32[512,1024]{1,0:T(8,128)S(1)} %get-tuple-element.60.refs_1_, bf16[2048,128]{1,0:T(8,128)(2,1)S(1)} %collective-permute-done.10.refs_2_, ...), custom_call_target="tpu_custom_call", output_to_operand_aliasing={{}: (1, {})} | custom-call | flops 1 | bytes 1 | tf_op jit(solution)/shard_map/ffn4/pallas_call | solution.py:313
  70.0 1.7 %collective-permute-start.14 = (f32[512,1024]{1,0:T(8,128)S(1)}, f32[512,1024]{1,0:T(8,128)S(1)}, u32[]{:S(2)}, u32[]{:S(2)}) collective-permute-start(f32[512,1024]{1,0:T(8,128)S(1)} %ffn4.1), channel_id=1, source_target_pairs={{0,1},{1,0},{2,3},{3,2},{4,5},{5,4},{6,7},{7,6},{8,9},{9,8},{10,11... | collective-permute-start | bytes 6291464 | tf_op jit(solution)/shard_map/ppermute | solution.py:90
  71.7 1.1 %collective-permute-start.16 = (bf16[2176,128]{1,0:T(8,128)(2,1)}, bf16[2176,128]{1,0:T(8,128)(2,1)}, u32[]{:S(2)}, u32[]{:S(2)}) collective-permute-start(bf16[2176,128]{1,0:T(8,128)(2,1)} %get-tuple-element.56), channel_id=1, source_target_pairs={{0,32},{1,9},{2,34},{3,11},{4,36},{5,13},{6,38},{7,15},{8,40},{9,1... | collective-permute-start | bytes 1671176 | tf_op jit(solution)/shard_map/ppermute | solution.py:90
  72.9 1.5 %collective-permute-start.17 = (bf16[2176,128]{1,0:T(8,128)(2,1)}, bf16[2176,128]{1,0:T(8,128)(2,1)}, u32[]{:S(2)}, u32[]{:S(2)}) collective-permute-start(bf16[2176,128]{1,0:T(8,128)(2,1)} %get-tuple-element.57), channel_id=1, source_target_pairs={{0,96},{1,25},{2,98},{3,27},{4,100},{5,29},{6,102},{7,31},{8,104},... | collective-permute-start | bytes 1671176 | tf_op jit(solution)/shard_map/ppermute | solution.py:90
  74.4 1.3 %ffn5.1.mine = f32[512,1024]{1,0:T(8,128)S(1)} custom-call(bf16[512,1024]{1,0:T(8,128)(2,1)S(1)} %get-tuple-element.40.refs_0_.normed, f32[512,1024]{1,0:T(8,128)S(1)} %get-tuple-element.55.refs_1_, bf16[2048,128]{1,0:T(8,128)(2,1)S(1)} %collective-permute-done.10.refs_2_, ...), custom_call_target="tpu_custom_call", output_to_operand_aliasing={{}: (1, {})} | custom-call | flops 1 | bytes 1 | tf_op jit(solution)/shard_map/ffn5/pallas_call | solution.py:313
  75.8 2.4 %embed.1 = (bf16[512,128]{1,0:T(8,128)(2,1)}, bf16[512,128]{1,0:T(8,128)(2,1)S(1)}) custom-call(s32[4]{0:T(128)S(1)} %copy-done.4, bf16[512,1024]{1,0:T(8,128)(2,1)S(1)} %get-tuple-element.40.refs_0_.normed, f32[512,1024]{1,0:T(8,128)S(1)} %ffn5.1.mine, f32[512,1024]{1,0:T(8,128)S(1)} %collective-permute-done.14.other, f32[1,1024]{1,0:T(1,128)S(1)} %bitcast.27, ...), custom_call_target="tpu_custom_call" | custom-call | flops 1 | bytes 1 | tf_op jit(solution)/shard_map/embed/pallas_call | solution.py:342
  78.1 1.0 %collective-permute-start.15 = (bf16[512,128]{1,0:T(8,128)(2,1)S(1)}, bf16[512,128]{1,0:T(8,128)(2,1)}, u32[]{:S(2)}, u32[]{:S(2)}) collective-permute-start(bf16[512,128]{1,0:T(8,128)(2,1)S(1)} %get-tuple-element.63.emb), channel_id=1, source_target_pairs={{0,1},{1,0},{2,3},{3,2},{4,5},{5,4},{6,7},{7,6},{8,9},{9,8},{10,11... | collective-permute-start | bytes 393224 | tf_op jit(solution)/shard_map/ppermute | solution.py:90
  79.3 2.6 %collective-permute-done.16 = bf16[2176,128]{1,0:T(8,128)(2,1)} collective-permute-done((bf16[2176,128]{1,0:T(8,128)(2,1)}, bf16[2176,128]{1,0:T(8,128)(2,1)}, u32[]{:S(2)}, u32[]{:S(2)}) %collective-permute-start.16) | collective-permute-done | bytes 557088 | tf_op jit(solution)/shard_map/ppermute | solution.py:90
  81.9 3.0 %score.1 = (f32[32,128]{1,0:T(8,128)S(1)}, f32[32,128]{1,0:T(8,128)S(1)}) custom-call(s32[5]{0:T(128)S(1)} %stack.23.where, s32[32]{0:T(128)S(1)} %reshape.51.cand, s32[32]{0:T(128)S(1)} %reshape.52.pair, bf16[512,128]{1,0:T(8,128)(2,1)S(1)} %get-tuple-element.63.emb, bf16[512,128]{1,0:T(8,128)(2,1)} %collective-permute-done.15.sib, ...), custom_call_target="tpu_custom_call" | custom-call | flops 1 | bytes 1 | tf_op jit(solution)/shard_map/score/pallas_call | solution.py:419
  85.0 1.6 %collective-permute-start.18 = (f32[32,128]{1,0:T(8,128)S(1)}, f32[32,128]{1,0:T(8,128)S(1)}, u32[]{:S(2)}, u32[]{:S(2)}) collective-permute-start(f32[32,128]{1,0:T(8,128)S(1)} %get-tuple-element.65), channel_id=1, source_target_pairs={{0,1},{1,0},{2,3},{3,2},{4,5},{5,4},{6,7},{7,6},{8,9},{9,8},{10,11... | collective-permute-start | bytes 49160 | tf_op jit(solution)/shard_map/ppermute | solution.py:90
  (36 shorter events, 4.1 us)
Async XLA Ops:
  0.6 8.5 %copy-start.5 = (s32[4,8]{1,0:T(4,128)S(1)}, s32[4,8]{1,0:T(4,128)}, u32[]{:S(2)}) copy-start(s32[4,8]{1,0:T(4,128)} %param.23) | copy-start | bytes 388
  0.6 10.0 %copy-start.2 = (f32[1024]{0:T(1024)S(1)}, f32[1024]{0:T(1024)}, u32[]{:S(2)}) copy-start(f32[1024]{0:T(1024)} %param.15) | copy-start | bytes 12292
  0.7 10.0 %copy-start.4 = (s32[4]{0:T(128)S(1)}, s32[4]{0:T(128)}, u32[]{:S(2)}) copy-start(s32[4]{0:T(128)} %length.3) | copy-start | bytes 52
  0.7 10.0 %copy-start = (bf16[512,1024]{1,0:T(8,128)(2,1)S(1)}, bf16[512,1024]{1,0:T(8,128)(2,1)}, u32[]{:S(2)}) copy-start(bf16[512,1024]{1,0:T(8,128)(2,1)} %tok.1) | copy-start | bytes 3145732
  2.6 18.5 %collective-permute-start = (bf16[1296,128]{1,0:T(8,128)(2,1)S(1)}, bf16[1296,128]{1,0:T(8,128)(2,1)S(1)}, u32[]{:S(2)}, u32[]{:S(2)}) collective-permute-start(bf16[1296,128]{1,0:T(8,128)(2,1)S(1)} %first.1.refs_3_), channel_id=1, source_target_pairs={{0,4},{1,5},{2,6},{3,7},{4,0},{5,1},{6,2},{7,3},{8,12},{9,13},{10,... | collective-permute-start | bytes 995336 | tf_op jit(solution)/shard_map/ppermute | solution.py:90
  6.5 15.4 %collective-permute-start.1 = (bf16[1296,128]{1,0:T(8,128)(2,1)S(1)}, bf16[1296,128]{1,0:T(8,128)(2,1)S(1)}, u32[]{:S(2)}, u32[]{:S(2)}) collective-permute-start(bf16[1296,128]{1,0:T(8,128)(2,1)S(1)} %first.1.refs_3_), channel_id=1, source_target_pairs={{0,2},{1,3},{2,4},{3,5},{4,6},{5,7},{6,0},{7,1},{8,10},{9,11},{10,... | collective-permute-start | bytes 995336 | tf_op jit(solution)/shard_map/ppermute | solution.py:90
  6.9 15.0 %collective-permute-start.2 = (bf16[1296,128]{1,0:T(8,128)(2,1)S(1)}, bf16[1296,128]{1,0:T(8,128)(2,1)S(1)}, u32[]{:S(2)}, u32[]{:S(2)}) collective-permute-start(bf16[1296,128]{1,0:T(8,128)(2,1)S(1)} %first.1.refs_3_), channel_id=1, source_target_pairs={{0,6},{1,7},{2,0},{3,1},{4,2},{5,3},{6,4},{7,5},{8,14},{9,15},{10,... | collective-permute-start | bytes 995336 | tf_op jit(solution)/shard_map/ppermute | solution.py:90
  9.1 12.0 %collective-permute-start.3 = (s32[4,8]{1,0:T(4,128)S(1)}, s32[4,8]{1,0:T(4,128)S(1)}, u32[]{:S(2)}, u32[]{:S(2)}) collective-permute-start(s32[4,8]{1,0:T(4,128)S(1)} %copy-done.5), channel_id=1, source_target_pairs={{0,1},{1,0},{2,3},{3,2},{4,5},{5,4},{6,7},{7,6},{8,9},{9,8},{10,11... | collective-permute-start | bytes 392 | tf_op jit(solution)/shard_map/ppermute | solution.py:90
  21.9 6.1 %collective-permute-start.4 = (bf16[512,1024]{1,0:T(8,128)(2,1)S(1)}, bf16[512,1024]{1,0:T(8,128)(2,1)S(1)}, u32[]{:S(2)}, u32[]{:S(2)}) collective-permute-start(bf16[512,1024]{1,0:T(8,128)(2,1)S(1)} %get-tuple-element.40.refs_0_.normed), channel_id=1, source_target_pairs={{0,1},{1,0},{2,3},{3,2},{4,5},{5,4},{6,7},{7,6},{8,9},{9,8},{10,11... | collective-permute-start | bytes 3145736 | tf_op jit(solution)/shard_map/ppermute | solution.py:90
  22.9 16.4 %collective-permute-start.5 = (bf16[4160,128]{1,0:T(8,128)(2,1)S(1)}, bf16[4160,128]{1,0:T(8,128)(2,1)S(1)}, u32[]{:S(2)}, u32[]{:S(2)}) collective-permute-start(bf16[4160,128]{1,0:T(8,128)(2,1)S(1)} %join1.1.refs_0_), channel_id=1, source_target_pairs={{0,8},{1,33},{2,10},{3,35},{4,12},{5,37},{6,14},{7,39},{8,16},{9,4... | collective-permute-start | bytes 3194888 | tf_op jit(solution)/shard_map/ppermute | solution.py:90
  24.6 25.5 %collective-permute-start.6 = (bf16[4160,128]{1,0:T(8,128)(2,1)S(1)}, bf16[4160,128]{1,0:T(8,128)(2,1)S(1)}, u32[]{:S(2)}, u32[]{:S(2)}) collective-permute-start(bf16[4160,128]{1,0:T(8,128)(2,1)S(1)} %join1.1.refs_0_), channel_id=1, source_target_pairs={{0,24},{1,97},{2,26},{3,99},{4,28},{5,101},{6,30},{7,103},{8,0},{9... | collective-permute-start | bytes 3194888 | tf_op jit(solution)/shard_map/ppermute | solution.py:90
  26.7 24.9 %collective-permute-start.7 = (bf16[4160,128]{1,0:T(8,128)(2,1)S(1)}, bf16[4160,128]{1,0:T(8,128)(2,1)S(1)}, u32[]{:S(2)}, u32[]{:S(2)}) collective-permute-start(bf16[4160,128]{1,0:T(8,128)(2,1)S(1)} %join1.1.refs_0_), channel_id=1, source_target_pairs={{0,16},{1,65},{2,18},{3,67},{4,20},{5,69},{6,22},{7,71},{8,24},{9,... | collective-permute-start | bytes 3194888 | tf_op jit(solution)/shard_map/ppermute | solution.py:90
  28.0 26.5 %collective-permute-start.8 = (bf16[4096,128]{1,0:T(8,128)(2,1)S(1)}, bf16[4096,128]{1,0:T(8,128)(2,1)S(1)}, u32[]{:S(2)}, u32[]{:S(2)}) collective-permute-start(bf16[4096,128]{1,0:T(8,128)(2,1)S(1)} %bitcast.20), channel_id=1, source_target_pairs={{0,2},{1,3},{2,4},{3,5},{4,6},{5,7},{6,0},{7,1},{8,10},{9,11},{10,... | collective-permute-start | bytes 3145736 | tf_op jit(solution)/shard_map/ppermute | solution.py:90
  29.1 25.4 %collective-permute-start.9 = (bf16[4096,128]{1,0:T(8,128)(2,1)S(1)}, bf16[4096,128]{1,0:T(8,128)(2,1)S(1)}, u32[]{:S(2)}, u32[]{:S(2)}) collective-permute-start(bf16[4096,128]{1,0:T(8,128)(2,1)S(1)} %bitcast.21), channel_id=1, source_target_pairs={{0,6},{1,7},{2,0},{3,1},{4,2},{5,3},{6,4},{7,5},{8,14},{9,15},{10,... | collective-permute-start | bytes 3145736 | tf_op jit(solution)/shard_map/ppermute | solution.py:90
  51.7 15.9 %collective-permute-start.12 = (bf16[4352,128]{1,0:T(8,128)(2,1)S(1)}, bf16[4352,128]{1,0:T(8,128)(2,1)S(1)}, u32[]{:S(2)}, u32[]{:S(2)}) collective-permute-start(bf16[4352,128]{1,0:T(8,128)(2,1)S(1)} %join2.1), channel_id=1, source_target_pairs={{0,32},{1,9},{2,34},{3,11},{4,36},{5,13},{6,38},{7,15},{8,40},{9,1... | collective-permute-start | bytes 3342344 | tf_op jit(solution)/shard_map/ppermute | solution.py:90
  53.0 14.6 %collective-permute-start.13 = (bf16[4352,128]{1,0:T(8,128)(2,1)S(1)}, bf16[4352,128]{1,0:T(8,128)(2,1)S(1)}, u32[]{:S(2)}, u32[]{:S(2)}) collective-permute-start(bf16[4352,128]{1,0:T(8,128)(2,1)S(1)} %join2.1), channel_id=1, source_target_pairs={{0,96},{1,25},{2,98},{3,27},{4,100},{5,29},{6,102},{7,31},{8,104},... | collective-permute-start | bytes 3342344 | tf_op jit(solution)/shard_map/ppermute | solution.py:90
  54.5 14.2 %collective-permute-start.10 = (bf16[2048,128]{1,0:T(8,128)(2,1)S(1)}, bf16[2048,128]{1,0:T(8,128)(2,1)S(1)}, u32[]{:S(2)}, u32[]{:S(2)}) collective-permute-start(bf16[2048,128]{1,0:T(8,128)(2,1)S(1)} %join5.1), channel_id=1, source_target_pairs={{0,2},{1,3},{2,4},{3,5},{4,6},{5,7},{6,0},{7,1},{8,10},{9,11},{10,... | collective-permute-start | bytes 1572872 | tf_op jit(solution)/shard_map/ppermute | solution.py:90
  55.7 13.0 %collective-permute-start.11 = (bf16[2048,128]{1,0:T(8,128)(2,1)S(1)}, bf16[2048,128]{1,0:T(8,128)(2,1)S(1)}, u32[]{:S(2)}, u32[]{:S(2)}) collective-permute-start(bf16[2048,128]{1,0:T(8,128)(2,1)S(1)} %join6.1), channel_id=1, source_target_pairs={{0,6},{1,7},{2,0},{3,1},{4,2},{5,3},{6,4},{7,5},{8,14},{9,15},{10,... | collective-permute-start | bytes 1572872 | tf_op jit(solution)/shard_map/ppermute | solution.py:90
  70.0 5.7 %collective-permute-start.14 = (f32[512,1024]{1,0:T(8,128)S(1)}, f32[512,1024]{1,0:T(8,128)S(1)}, u32[]{:S(2)}, u32[]{:S(2)}) collective-permute-start(f32[512,1024]{1,0:T(8,128)S(1)} %ffn4.1), channel_id=1, source_target_pairs={{0,1},{1,0},{2,3},{3,2},{4,5},{5,4},{6,7},{7,6},{8,9},{9,8},{10,11... | collective-permute-start | bytes 6291464 | tf_op jit(solution)/shard_map/ppermute | solution.py:90
  71.7 10.2 %collective-permute-start.16 = (bf16[2176,128]{1,0:T(8,128)(2,1)}, bf16[2176,128]{1,0:T(8,128)(2,1)}, u32[]{:S(2)}, u32[]{:S(2)}) collective-permute-start(bf16[2176,128]{1,0:T(8,128)(2,1)} %get-tuple-element.56), channel_id=1, source_target_pairs={{0,32},{1,9},{2,34},{3,11},{4,36},{5,13},{6,38},{7,15},{8,40},{9,1... | collective-permute-start | bytes 1671176 | tf_op jit(solution)/shard_map/ppermute | solution.py:90
  72.9 9.1 %collective-permute-start.17 = (bf16[2176,128]{1,0:T(8,128)(2,1)}, bf16[2176,128]{1,0:T(8,128)(2,1)}, u32[]{:S(2)}, u32[]{:S(2)}) collective-permute-start(bf16[2176,128]{1,0:T(8,128)(2,1)} %get-tuple-element.57), channel_id=1, source_target_pairs={{0,96},{1,25},{2,98},{3,27},{4,100},{5,29},{6,102},{7,31},{8,104},... | collective-permute-start | bytes 1671176 | tf_op jit(solution)/shard_map/ppermute | solution.py:90
  74.4 1.3 %copy-start.1 = (bf16[1024,128]{1,0:T(8,128)(2,1)S(1)}, bf16[1024,128]{1,0:T(8,128)(2,1)}, u32[]{:S(2)}) copy-start(bf16[1024,128]{1,0:T(8,128)(2,1)} %we.1) | copy-start | bytes 786436
  74.4 1.3 %copy-start.3 = (f32[1024]{0:T(1024)S(1)}, f32[1024]{0:T(1024)}, u32[]{:S(2)}) copy-start(f32[1024]{0:T(1024)} %param.18) | copy-start | bytes 12292
  78.1 3.8 %collective-permute-start.15 = (bf16[512,128]{1,0:T(8,128)(2,1)S(1)}, bf16[512,128]{1,0:T(8,128)(2,1)}, u32[]{:S(2)}, u32[]{:S(2)}) collective-permute-start(bf16[512,128]{1,0:T(8,128)(2,1)S(1)} %get-tuple-element.63.emb), channel_id=1, source_target_pairs={{0,1},{1,0},{2,3},{3,2},{4,5},{5,4},{6,7},{7,6},{8,9},{9,8},{10,11... | collective-permute-start | bytes 393224 | tf_op jit(solution)/shard_map/ppermute | solution.py:90
  85.0 2.4 %collective-permute-start.18 = (f32[32,128]{1,0:T(8,128)S(1)}, f32[32,128]{1,0:T(8,128)S(1)}, u32[]{:S(2)}, u32[]{:S(2)}) collective-permute-start(f32[32,128]{1,0:T(8,128)S(1)} %get-tuple-element.65), channel_id=1, source_target_pairs={{0,1},{1,0},{2,3},{3,2},{4,5},{5,4},{6,7},{7,6},{8,9},{9,8},{10,11... | collective-permute-start | bytes 49160 | tf_op jit(solution)/shard_map/ppermute | solution.py:90
